TPU v7x, 512 devices: a whole 4x8x8 slice. The times are simulated.
512 devices in a mesh: expert: 16 (over z, core), tensor: 32 (over x, y).
Axes of the slice: x: 4, y: 8, z: 8, core: 2. Of those that a mesh axis runs over, the one named last changes fastest.
Arguments:
- tokens: bfloat16 [2048, 5120], P('expert', 'tensor'), may hold values from -6 to 6
- routes: int32 [2048, 6], P('expert'), may hold values from 0 to 15, all different within a row; in each aligned block of 128 rows (0 to 127, 128 to 255, ...) at most 64 rows name the same one
- gates: float32 [2048, 6], P('expert'), may hold values from 0.05 to 0.35
- w_gate: bfloat16 [16, 1536, 5120], P('expert', 'tensor'), may hold values from -0.078125 to 0.078125
- w_up: bfloat16 [16, 1536, 5120], P('expert', 'tensor'), may hold values from -0.078125 to 0.078125
- w_down: bfloat16 [16, 1536, 5120], P('expert', None, 'tensor'), may hold values from -0.15625 to 0.15625
- shared_gate: bfloat16 [1536, 5120], P('tensor'), may hold values from -0.078125 to 0.078125
- shared_up: bfloat16 [1536, 5120], P('tensor'), may hold values from -0.078125 to 0.078125
- shared_down: bfloat16 [1536, 5120], P(None, 'tensor'), may hold values from -0.15625 to 0.15625
- vocab: bfloat16 [65536, 5120], P(('expert', 'tensor'))
- targets: int32 [64], replicated, may hold values from 0 to 65535
Outputs:
- layer_out: bfloat16 [2048, 5120], P('expert', 'tensor')
- loglik: float32 [64], replicated
Inputs may be any that keep to these rules, and one draw needn't show every extreme that they name: `routes`: the tokens of one group name one expert at most 64 times; in every draw some group names some expert exactly 64 times.
All inputs are finite; a program needn't handle non-finite values.
Results may differ from a plain program's by a relative error of at most 0.0041.
Values may be sent and summed in bfloat16 or wider, within the bound.
No kernel may reach another device: no remote copies, remote signals or barrier semaphores. Data moves between devices by JAX's collectives and lax.ppermute only.
A program may use at most 64 MiB of HBM per device.

v0:
```python
import jax
import jax.numpy as jnp
from jax import lax
from jax.sharding import PartitionSpec as P

EXPERTS = 16
SCORE_E = 4


def slot_tables(routes, gates, capacity):
    picks = (routes[:, :, None] == jnp.arange(EXPERTS, dtype=jnp.int32)[None, None, :]).astype(
        jnp.int32
    )
    per_token = jnp.sum(picks, axis=1)
    earlier = jnp.cumsum(per_token, axis=0) - per_token
    slots = jnp.sum(picks * earlier[:, None, :], axis=2)
    places = (slots[:, :, None] == jnp.arange(capacity, dtype=jnp.int32)[None, None, :]).astype(
        jnp.float32
    )
    picked = picks.astype(jnp.float32)
    select = jnp.einsum("ikr,iks->rsi", picked, places, precision=lax.Precision.HIGHEST)
    weigh = jnp.einsum("ikr,iks,ik->rsi", picked, places, gates, precision=lax.Precision.HIGHEST)
    return (select.astype(jnp.bfloat16), weigh)


def contract_last(left, right):
    return lax.dot_general(
        left, right, (((1,), (1,)), ((), ())), preferred_element_type=jnp.float32
    )


def shards(
    tokens, routes, gates, w_gate, w_up, w_down, shared_gate, shared_up, shared_down, vocab, targets
):
    tok_rows = tokens.shape[0]
    capacity = tok_rows // 2
    groups = lax.axis_size("expert")
    lanes = lax.axis_size("tensor")
    exp_dev = w_gate.shape[0]
    width = w_gate.shape[1]
    out_width = w_down.shape[2]
    select, weigh = slot_tables(routes, gates, capacity)
    outgoing = jnp.einsum("rsi,id->rsd", select, tokens, preferred_element_type=jnp.float32).astype(
        jnp.bfloat16
    )
    arrived = lax.all_to_all(outgoing, "expert", split_axis=0, concat_axis=1, tiled=True)
    slot_count = arrived.shape[1]
    flat_rows = arrived.reshape(exp_dev * slot_count, arrived.shape[2])
    pieces = (
        lax.all_gather(flat_rows, "tensor", axis=1, tiled=True),
        lax.all_gather(tokens, "tensor", axis=1, tiled=True),
    )
    span = pieces[0].shape[1]
    rows = pieces[0].reshape(exp_dev, slot_count, span)
    gate_acc = jnp.einsum("erw,efw->erf", rows, w_gate, preferred_element_type=jnp.float32)
    up_acc = jnp.einsum("erw,efw->erf", rows, w_up, preferred_element_type=jnp.float32)
    shared_gate_acc = contract_last(pieces[1], shared_gate)
    shared_up_acc = contract_last(pieces[1], shared_up)
    hidden_routed = (jax.nn.silu(gate_acc) * up_acc).astype(jnp.bfloat16)
    hidden_shared = (jax.nn.silu(shared_gate_acc) * shared_up_acc).astype(jnp.bfloat16)
    flat_hidden = hidden_routed.reshape(exp_dev * slot_count, width)
    pieces = (
        lax.all_gather(flat_hidden, "tensor", axis=1, tiled=True),
        lax.all_gather(hidden_shared, "tensor", axis=1, tiled=True),
    )
    span = pieces[0].shape[1]
    rows = pieces[0].reshape(exp_dev, slot_count, span)
    routed_out = jnp.einsum("erw,ewd->erd", rows, w_down, preferred_element_type=jnp.float32)
    shared_out = jnp.dot(pieces[1], shared_down, preferred_element_type=jnp.float32)
    returned = lax.all_to_all(
        routed_out.astype(jnp.bfloat16), "expert", split_axis=1, concat_axis=0, tiled=True
    )
    routed = jnp.einsum(
        "rsi,rsd->id", weigh, returned.astype(jnp.float32), precision=lax.Precision.HIGHEST
    )
    layer_out = (tokens.astype(jnp.float32) + shared_out + routed).astype(jnp.bfloat16)
    scored = layer_out[tok_rows - SCORE_E :].reshape(1, SCORE_E * out_width)
    collected = lax.all_gather(scored, ("expert", "tensor"), axis=0, tiled=True)
    full_rows = (
        collected.reshape(groups, lanes, SCORE_E, out_width)
        .transpose(0, 2, 1, 3)
        .reshape(groups * SCORE_E, lanes * out_width)
    )
    logits = contract_last(full_rows, vocab)
    exp_sums = jnp.sum(jnp.exp(logits), axis=1)
    offset = (lax.axis_index("expert") * lanes + lax.axis_index("tensor")) * vocab.shape[0]
    columns = offset + jnp.arange(vocab.shape[0], dtype=jnp.int32)
    target_part = jnp.sum(jnp.where(targets[:, None] == columns[None, :], logits, 0.0), axis=1)
    totals, target_logit = lax.psum((exp_sums, target_part), ("expert", "tensor"))
    loglik = target_logit - jnp.log(totals)
    return (layer_out, loglik)


def solution(mesh):
    placed = (
        P("expert", "tensor"),
        P("expert", None),
        P("expert", None),
        P("expert", "tensor", None),
        P("expert", "tensor", None),
        P("expert", None, "tensor"),
        P("tensor", None),
        P("tensor", None),
        P(None, "tensor"),
        P(("expert", "tensor"), None),
        P(),
    )
    return jax.shard_map(
        shards, mesh=mesh, in_specs=placed, out_specs=(P("expert", "tensor"), P()), check_vma=False
    )
```

profile of v0, /device:TPU:1, one launch (start us, length us, event | category | flops | bytes accessed | tf_op | source)
XLA Modules:
  0.0 622.9 jit_solution(7036797286087049021)
XLA Ops:
  7.2 0.0 copy-start
  7.2 0.0 all-gather.7.cloned.1.call-start
  7.2 0.9 copy.21
  8.1 0.3 convert_reduce_fusion
  8.4 0.0 copy-start.10
  8.4 0.2 reduce_window_sum.11
  8.6 2.4 select_reduce_fusion
  11.0 1.2 fusion
  12.2 0.0 copy-done.10
  12.2 0.3 convolution_convert_fusion.1
  12.6 0.0 copy-start.3
  12.6 29.1 %all_to_all.21 = bf16[16,64,160]{2,1,0:T(8,128)(2,1)S(1)} all-to-all(bf16[16,64,160]{2,1,0:T(8,128)(2,1)S(1)} %convolution_convert_fusion.1), channel_id=1, replica_groups=mesh['expert'=16,'tensor'=32] {'expert'}, dimensions={0} | all-to-all | bytes 655360 | tf_op jit(solution)/shard_map/all_to_all | solution.py:46
  41.7 0.9 copy.24
  42.6 0.0 all-gather.7.cloned.1.call-update
  42.6 0.0 copy-start.4
  42.6 0.0 all-gather.9.cloned.1.call-start
  42.7 110.4 %all-gather.7.cloned.1.call-done = bf16[1024,5120]{0,1:T(8,128)(2,1)} async-done(((bf16[1024,160]{0,1:T(8,128)(2,1)}), bf16[1024,5120]{0,1:T(8,128)(2,1)}) %all-gather.7.cloned.1.call-update) | async-done | bytes 10485776 | tf_op jit(solution)/shard_map/all_gather | solution.py:50
  153.1 0.0 copy-done.3
  153.1 6.1 fusion.11
  159.1 0.0 copy-done.4
  159.2 0.9 copy-done.1
  160.0 2.6 fusion.2
  162.7 0.0 all-gather.9.cloned.1.call-update
  162.7 0.2 all-gather.5.cloned.1.call-start
  162.9 0.5 all-gather.5.cloned.1.call-update
  163.5 0.1 copy.22
  163.6 0.0 copy-start.8
  163.6 2.7 convolution_bitcast_fusion
  166.3 76.0 %all-gather.9.cloned.1.call-done = bf16[1024,1536]{0,1:T(8,128)(2,1)} async-done(((bf16[1024,48]{0,1:T(8,128)(2,1)}), bf16[1024,1536]{0,1:T(8,128)(2,1)}) %all-gather.9.cloned.1.call-update) | async-done | bytes 3145744 | tf_op jit(solution)/shard_map/all_gather | solution.py:63
  242.3 2.6 fusion.1
  244.9 0.8 copy.25
  245.8 0.5 broadcast.28
  246.3 4.0 reduce.1
  250.3 0.0 copy-start.6
  250.3 1.5 reshape.84
  251.8 11.8 %all-to-all-start.1 = ((bf16[16,2,5120]{2,1,0:T(2,128)(2,1)}), bf16[16,2,5120]{2,1,0:T(2,128)(2,1)S(1)}, u32[]{:S(2)}, u32[]{:S(2)}) async-start(bf16[16,2,5120]{2,1,0:T(2,128)(2,1)} %reshape.84), calls=%async_computation.1 | async-start | bytes 655360 | tf_op jit(solution)/shard_map/all_to_all | solution.py:70
  263.6 60.0 %all-gather.5.cloned.1.call-done = bf16[128,5120]{0,1:T(8,128)(2,1)} async-done(((bf16[128,160]{0,1:T(8,128)(2,1)}), bf16[128,5120]{0,1:T(8,128)(2,1)}) %all-gather.5.cloned.1.call-update) | async-done | bytes 1310736 | tf_op jit(solution)/shard_map/all_gather | solution.py:51
  323.5 0.0 copy-done.6
  323.6 1.8 fusion.21
  325.3 0.0 copy-done.7
  325.3 0.0 copy-done.2
  325.3 0.4 fusion.5
  325.7 36.5 %all_gather.16 = bf16[128,1536]{0,1:T(8,128)(2,1)S(1)} all-gather(bf16[128,48]{0,1:T(8,128)(2,1)S(1)} %fusion.5), channel_id=1, replica_groups=mesh['expert'=16,'tensor'=32] {'tensor'}, dimensions={1}, use_global_device_ids=true | all-gather | bytes 405504 | tf_op jit(solution)/shard_map/all_gather | solution.py:64
  362.2 0.0 all-to-all-done.1
  362.2 0.9 reshape.85
  363.1 0.0 copy-start.9
  363.1 0.0 copy-start.11
  363.2 0.1 copy.32
  363.2 1.1 copy-done.5
  364.3 1.1 convolution_bitcast_fusion.1
  365.5 0.3 fusion.4
  365.8 0.0 copy-start.12
  365.8 0.1 slice.4
  365.9 0.1 copy.29
  366.0 0.1 reshape.76
  366.1 145.7 %all-gather = bf16[512,1,640]{2,1,0:T(2,128)(2,1)S(1)} all-gather(bf16[1,1,640]{2,1,0:T(2,128)(2,1)S(1)} %reshape.76), channel_id=1, replica_groups=mesh['expert'=16,'tensor'=32] {'expert','tensor'}, dimensions={0}, use_global_device_ids=true | all-gather | bytes 656640 | tf_op jit(solution)/shard_map/all_gather | solution.py:78
  511.8 4.0 reduce
  515.8 0.7 reshape.74
  516.5 0.2 copy.30
  516.7 0.0 copy-start.14
  516.7 1.7 reshape.75
  518.4 0.7 exponential_reduce_fusion
  519.1 96.8 %all-reduce = (f32[64]{0:T(128)S(1)}, f32[64]{0:T(128)S(1)}) all-reduce(f32[64]{0:T(128)S(1)} %get-tuple-element.3, f32[64]{0:T(128)S(1)} %get-tuple-element.2), channel_id=1, replica_groups=mesh['expert'=16,'tensor'=32] {'expert','tensor'}, use_global_device_ids=true, to_apply=%region_4.5 | all-reduce | flops 128 | bytes 1024 | tf_op jit(solution)/shard_map/psum | solution.py:89
  615.9 0.5 log_subtract_fusion
  (14 shorter events, 0.0 us)
Async XLA Ops:
  7.2 511.2 %copy-start = (bf16[128,5120]{1,0:T(8,128)(2,1)S(1)}, bf16[128,5120]{1,0:T(8,128)(2,1)}, u32[]{:S(2)}) copy-start(bf16[128,5120]{1,0:T(8,128)(2,1)} %param.20) | copy-start | bytes 3932164
  7.2 145.9 %all-gather.7.cloned.1.call-start = ((), (), s32[]{:S(2)}) async-start(), calls=%async_computation.3 | async-start | bytes 10813440 | tf_op jit(solution)/shard_map/all_gather | solution.py:50
  8.4 3.8 copy-start.10
  12.6 140.5 %copy-start.3 = (bf16[1,48,5120]{2,1,0:T(8,128)(2,1)S(1)}, bf16[1,48,5120]{2,1,0:T(8,128)(2,1)}, u32[]{:S(2)}) copy-start(bf16[1,48,5120]{2,1,0:T(8,128)(2,1)} %param.14) | copy-start | bytes 1474564
  42.6 116.5 %copy-start.4 = (bf16[1,48,5120]{2,1,0:T(8,128)(2,1)S(1)}, bf16[1,48,5120]{2,1,0:T(8,128)(2,1)}, u32[]{:S(2)}) copy-start(bf16[1,48,5120]{2,1,0:T(8,128)(2,1)} %param.15) | copy-start | bytes 1474564
  42.6 199.7 %all-gather.9.cloned.1.call-start = ((), (), s32[]{:S(2)}) async-start(), calls=%async_computation.4 | async-start | bytes 3244032 | tf_op jit(solution)/shard_map/all_gather | solution.py:63
  153.1 7.0 %copy-start.1 = (bf16[1024,5120]{0,1:T(8,128)(2,1)S(1)}, bf16[1024,5120]{0,1:T(8,128)(2,1)}, u32[]{:S(2)}) copy-start(bf16[1024,5120]{0,1:T(8,128)(2,1)} %all-gather.7.cloned.1.call-done) | copy-start | bytes 31457284
  160.0 3.4 copy-start.13
  162.7 160.8 %all-gather.5.cloned.1.call-start = ((), (), s32[]{:S(2)}) async-start(), calls=%async_computation.2 | async-start | bytes 1351680 | tf_op jit(solution)/shard_map/all_gather | solution.py:51
  163.6 78.8 %copy-start.8 = (bf16[1,1536,160]{1,2,0:T(8,128)(2,1)S(1)}, bf16[1,1536,160]{1,2,0:T(8,128)(2,1)}, u32[]{:S(2)}) copy-start(bf16[1,1536,160]{1,2,0:T(8,128)(2,1)} %param.16) | copy-start | bytes 1474564
  250.3 73.2 %copy-start.6 = (bf16[48,5120]{1,0:T(8,128)(2,1)S(1)}, bf16[48,5120]{1,0:T(8,128)(2,1)}, u32[]{:S(2)}) copy-start(bf16[48,5120]{1,0:T(8,128)(2,1)} %param.17) | copy-start | bytes 1474564
  251.8 73.5 %copy-start.7 = (bf16[48,5120]{1,0:T(8,128)(2,1)S(1)}, bf16[48,5120]{1,0:T(8,128)(2,1)}, u32[]{:S(2)}) copy-start(bf16[48,5120]{1,0:T(8,128)(2,1)} %param.18) | copy-start | bytes 1474564
  251.8 110.4 %all-to-all-start.1 = ((bf16[16,2,5120]{2,1,0:T(2,128)(2,1)}), bf16[16,2,5120]{2,1,0:T(2,128)(2,1)S(1)}, u32[]{:S(2)}, u32[]{:S(2)}) async-start(bf16[16,2,5120]{2,1,0:T(2,128)(2,1)} %reshape.84), calls=%async_computation.1 | async-start | bytes 655360 | tf_op jit(solution)/shard_map/all_to_all | solution.py:70
  323.6 1.8 copy-start.2
  363.1 1.2 copy-start.5
  363.1 2.4 copy-start.9
  363.1 2.4 copy-start.11
  365.8 150.0 %copy-start.12 = (bf16[128,160]{0,1:T(8,128)(2,1)}, bf16[128,160]{0,1:T(8,128)(2,1)S(1)}, u32[]{:S(2)}) copy-start(bf16[128,160]{0,1:T(8,128)(2,1)S(1)} %fusion.4) | copy-start | bytes 122884
  516.7 1.7 copy-start.14
Sparse Core Ops, SparseCore 0:
  42.7 110.3 all-gather.6
  162.8 79.4 all-gather.8
  245.5 78.0 all-gather.4
where the time goes:
time: 623 us
  blocking collectives  308 us (49%)
  waiting for transfers between devices  247 us (40%)
  matrix products  19.8 us (3%)
  between operations  14.1 us (2%)
  starting transfers between devices  12.1 us (2%)
  other arithmetic  11.4 us (2%)
  local copies, waits for them, and re-layouts  10.7 us (2%)
    all_gather x1, blocking collectives, shards(): collected = lax.all_gather(scored, ('expert', 'tensor'), axis=0, tiled=True)  146 us
    all_gather x1, waiting for transfers between devices, shards(): lax.all_gather(flat_rows, 'tensor', axis=1, tiled=True)  110 us
    psum x1, blocking collectives, shards(): lax.psum((exp_sums, target_part), ('expert', 'tensor'))  96.8 us
    all_gather x1, waiting for transfers between devices, shards(): lax.all_gather(flat_hidden, 'tensor', axis=1, tiled=True)  76 us
    all_gather x1, waiting for transfers between devices, shards(): lax.all_gather(tokens, 'tensor', axis=1, tiled=True)  60 us
    all_gather x1, blocking collectives, shards(): lax.all_gather(hidden_shared, 'tensor', axis=1, tiled=True)  36.5 us
    all_to_all x1, blocking collectives, shards(): lax.all_to_all(outgoing, 'expert', split_axis=0, concat_axis=1, tiled=True)  29.1 us
  transfers between devices with their start and end apart: 4, of which 3 were waited for; matrix products, arithmetic and copies ran while one was open for 2% of the time, Pallas kernels for 0%

commit v1 on v0

v1 whole, which is shorter than its diff:
```python
import jax
import jax.numpy as jnp
from jax import lax
from jax.experimental import pallas as pl
from jax.experimental.pallas import tpu as pltpu
from jax.sharding import Mesh
from jax.sharding import PartitionSpec as P

SCORE_E = 4
F32 = jnp.float32
BF16 = jnp.bfloat16
LINE = ("z", "core")
PLANE = ("x", "y")
VMEM_LIMIT = 48 << 20


def call(body, outs, args, scalars=0, scratch=(), flops=0):
    specs = [
        pl.BlockSpec(memory_space=pltpu.SMEM if n < scalars else pltpu.VMEM) for n in range(len(args))
    ]
    moved = sum(a.size * a.dtype.itemsize for a in args)
    moved += sum(o.size * o.dtype.itemsize for o in outs)
    return pl.pallas_call(
        body,
        out_shape=outs,
        in_specs=specs,
        out_specs=[pl.BlockSpec(memory_space=pltpu.VMEM) for _ in outs],
        scratch_shapes=list(scratch),
        cost_estimate=pl.CostEstimate(flops=flops, bytes_accessed=moved, transcendentals=0),
        compiler_params=pltpu.CompilerParams(vmem_limit_bytes=VMEM_LIMIT),
    )(*args)


def shape(dims, dtype=BF16):
    return jax.ShapeDtypeStruct(dims, dtype)


def nn(a, b):
    return lax.dot_general(a, b, (((1,), (0,)), ((), ())), preferred_element_type=F32)


def nt(a, b):
    return lax.dot_general(a, b, (((1,), (1,)), ((), ())), preferred_element_type=F32)


def iota(dims, axis):
    return lax.broadcasted_iota(jnp.int32, dims, axis)


def pair_low(a, b, half):
    lane = iota(a.shape, 1)
    return jnp.where(lane < half, a, pltpu.roll(b, half, 1))


def pair_high(a, b, half):
    lane = iota(a.shape, 1)
    return jnp.where(lane < half, pltpu.roll(a, half, 1), b)


def routing(routes_ref, gates_ref, experts):
    top, rows = routes_ref.shape
    expert = iota((experts, rows), 0)
    named = jnp.zeros((experts, rows), F32)
    gate = jnp.zeros((experts, rows), F32)
    for k in range(top):
        hit = expert == routes_ref[k : k + 1, :]
        named = named + jnp.where(hit, 1.0, 0.0)
        gate = gate + jnp.where(hit, gates_ref[k : k + 1, :], 0.0)
    before = jnp.where(iota((rows, rows), 0) < iota((rows, rows), 1), 1.0, 0.0).astype(BF16)
    earlier = nn(named.astype(BF16), before)
    return jnp.where(named > 0.0, earlier, -1.0).astype(jnp.int32), gate


def dispatch_body(routes_ref, gates_ref, tok_ref, out_ref, slot_ref, gate_ref):
    experts, half, lanes = out_ref.shape
    rows = tok_ref.shape[1]
    cap = lanes // 2
    slot, gate = routing(routes_ref, gates_ref, experts)
    slot_ref[...] = slot
    gate_ref[...] = gate
    tok = jnp.concatenate([tok_ref[:half, :], tok_ref[half:, :]], axis=1)
    place = iota((lanes, rows), 0)
    place = jnp.where(place < cap, place, place - cap)
    low = iota((lanes, rows), 0) < cap
    for e in range(experts):
        sel = jnp.where(slot[e : e + 1, :] == place, 1.0, 0.0)
        sel = jnp.concatenate([jnp.where(low, sel, 0.0), jnp.where(low, 0.0, sel)], axis=1)
        out_ref[e] = nt(tok, sel.astype(BF16)).astype(BF16)


def spread_body(in_ref, out_ref):
    lanes_x, groups, half, lanes = in_ref.shape
    cap = lanes // 2
    for x in range(lanes_x):
        for q in range(groups // 2):
            a = in_ref[x, 2 * q].astype(F32)
            b = in_ref[x, 2 * q + 1].astype(F32)
            cols = slice(q * lanes, (q + 1) * lanes)
            out_ref[2 * half * x : 2 * half * x + half, cols] = pair_low(a, b, cap).astype(BF16)
            out_ref[2 * half * x + half : 2 * half * (x + 1), cols] = pair_high(a, b, cap).astype(BF16)


def glu(gate, up):
    return (gate / (1.0 + jnp.exp(-gate)) * up).astype(BF16)


def hidden_body(rows_ref, *refs):
    *weights, out_ref, flat_ref = refs
    ny, block, _ = rows_ref.shape
    nx = len(weights) // 2
    width = block // nx
    for y in range(ny):
        for x in range(nx):
            at = (x * ny + y) * width
            flat_ref[at : at + width, :] = rows_ref[y, x * width : (x + 1) * width, :]
    units = weights[0].shape[0]
    rows = flat_ref[...]
    for x in range(nx):
        gate = nn(weights[2 * x][...], rows)
        up = nn(weights[2 * x + 1][...], rows)
        out_ref[x * units : (x + 1) * units, :] = glu(gate, up)


def shared_body(tok_ref, gate_ref, up_ref, out_ref):
    tok = tok_ref[...]
    out_ref[...] = glu(nn(gate_ref[...], tok), nn(up_ref[...], tok))


def down_body(x_ref, hidden_ref, *refs):
    *weights, out_ref, flat_ref = refs
    nx = len(weights)
    ny = hidden_ref.shape[0]
    units = hidden_ref.shape[1] // nx
    _, groups, half, lanes = out_ref.shape
    cap = lanes // 2
    own = [lax.rem(x_ref[0] + shift, nx) for shift in SHIFTS]
    for n in range(nx):
        for y in range(ny):
            at = pl.multiple_of((own[n] * ny + y) * units, units)
            flat_ref[pl.ds(at, units), :] = hidden_ref[y, n * units : (n + 1) * units, :]
    rows = flat_ref[...]
    for n in range(nx):
        out = nn(weights[n][...], rows)
        for q in range(groups // 2):
            cols = slice(q * lanes, (q + 1) * lanes)
            a, b = out[:half, cols], out[half:, cols]
            out_ref[own[n], 2 * q] = pair_low(a, b, cap).astype(BF16)
            out_ref[own[n], 2 * q + 1] = pair_high(a, b, cap).astype(BF16)


def combine_body(slot_ref, gate_ref, back_ref, tok_ref, hidden_ref, down_ref, out_ref, scored_ref):
    experts, half, lanes = back_ref.shape
    rows = tok_ref.shape[1]
    cap = lanes // 2
    place = iota((lanes, rows), 0)
    place = jnp.where(place < cap, place, place - cap)
    low = iota((lanes, rows), 0) < cap
    routed = jnp.zeros((half, 2 * rows), F32)
    for e in range(experts):
        mix = jnp.where(slot_ref[e : e + 1, :] == place, gate_ref[e : e + 1, :], 0.0)
        mix = jnp.concatenate([jnp.where(low, mix, 0.0), jnp.where(low, 0.0, mix)], axis=1)
        head = mix.astype(BF16)
        tail = (mix - head.astype(F32)).astype(BF16)
        routed = routed + nn(back_ref[e], head) + nn(back_ref[e], tail)
    shared = nn(down_ref[...], hidden_ref[...])
    routed = jnp.concatenate([routed[:, :rows], routed[:, rows:]], axis=0)
    out = (tok_ref[...].astype(F32) + shared + routed).astype(BF16)
    out_ref[...] = out
    take = iota((scored_ref.shape[0], rows), 1) == rows - SCORE_E + iota((scored_ref.shape[0], rows), 0)
    scored_ref[...] = nt(jnp.where(take, 1.0, 0.0).astype(BF16), out).astype(BF16)


def pack_body(rows_ref, out_ref):
    count, width = rows_ref.shape
    half = width // 2
    eye = jnp.where(iota((count, count), 0) == iota((count, count), 1), 1.0, 0.0).astype(BF16)
    flip = lax.dot_general(
        rows_ref[...], eye, (((0,), (0,)), ((), ())), preferred_element_type=F32
    )
    out_ref[...] = jnp.concatenate([flip[:half], flip[half:]], axis=1).astype(BF16)


def score_body(offset_ref, rows_ref, vocab_ref, targets_ref, out_ref, flat_ref):
    blocks, half, lanes = rows_ref.shape
    count = lanes // 2
    for b in range(blocks):
        both = rows_ref[b].astype(F32)
        flat_ref[2 * half * b : 2 * half * b + half, :] = rows_ref[b]
        flat_ref[2 * half * b + half : 2 * half * (b + 1), :] = pltpu.roll(both, count, 1).astype(BF16)
    logits = nn(vocab_ref[...], flat_ref[...])
    entry = iota(logits.shape, 0) + offset_ref[0]
    sums = jnp.sum(jnp.exp(logits), axis=0, keepdims=True)
    hits = jnp.sum(jnp.where(entry == targets_ref[0:1, :], logits, 0.0), axis=0, keepdims=True)
    lane = iota(sums.shape, 1)
    out_ref[...] = jnp.broadcast_to(jnp.where(lane < count, sums, pltpu.roll(hits, count, 1)), out_ref.shape)


SHIFTS = (0, 1, 3, 2)


def spread_all(value, axes, count):
    return lax.all_to_all(
        jnp.broadcast_to(value[None], (count, *value.shape)), axes, 0, 0, tiled=True
    )


def nearby(value, axis):
    count = lax.axis_size(axis)
    return [
        value
        if shift == 0
        else lax.ppermute(value, axis, [((i + shift) % count, i) for i in range(count)])
        for shift in SHIFTS
    ]


def shards(tokens, routes, gates, w_gate, w_up, w_down, shared_gate, shared_up, shared_down, vocab, targets):
    nx, ny = lax.axis_size("x"), lax.axis_size("y")
    nz, nc = lax.axis_size("z"), lax.axis_size("core")
    groups, lanes = nz * nc, nx * ny
    rows, width = tokens.shape
    half, cap = width // 2, rows // 2
    near = groups // nx
    units = w_gate.shape[1]
    tok = tokens.T
    x_at = lax.axis_index("x").astype(jnp.int32).reshape(1)

    gates_near = nearby(w_gate[0], "x")
    ups_near = nearby(w_up[0], "x")
    downs_near = nearby(w_down[0].T, "x")

    outgoing, slot, gate = call(
        dispatch_body,
        [
            shape((groups, half, 2 * cap)),
            shape((groups, rows), jnp.int32),
            shape((groups, rows), F32),
        ],
        [routes.T, gates.T, tok],
    )
    arrived = lax.all_to_all(outgoing, LINE, 0, 0, tiled=True)
    plane_tok = spread_all(tok, PLANE, lanes).reshape(lanes * width, rows)
    quarter = lax.all_to_all(arrived.reshape(nx, near, half, 2 * cap), "x", 0, 0, tiled=True)
    (spread,) = call(spread_body, [shape((nx * width, near * cap))], [quarter])
    gathered = spread_all(spread, "y", ny)
    (hidden,) = call(
        hidden_body,
        [shape((nx * units, near * cap))],
        [gathered, *[w for pair in zip(gates_near, ups_near) for w in pair]],
        scratch=[pltpu.VMEM((lanes * width, near * cap), BF16)],
    )
    (hidden_shared,) = call(shared_body, [shape((units, rows))], [plane_tok, shared_gate, shared_up])
    all_hidden = spread_all(hidden, "y", ny)
    all_shared = spread_all(hidden_shared, PLANE, lanes).reshape(lanes * units, rows)
    (returned,) = call(
        down_body,
        [shape((nx, near, half, 2 * cap))],
        [x_at, all_hidden, *downs_near],
        scalars=1,
        scratch=[pltpu.VMEM((lanes * units, near * cap), BF16)],
    )
    back = lax.all_to_all(returned, "x", 0, 0, tiled=True).reshape(groups, half, 2 * cap)
    back = lax.all_to_all(back, LINE, 0, 0, tiled=True)
    layer_out, scored = call(
        combine_body,
        [shape((width, rows)), shape((8, width))],
        [slot, gate, back, tok, all_shared, shared_down.T],
    )
    line_rows = spread_all(scored[:SCORE_E], LINE, groups).reshape(groups * SCORE_E, width)
    (packed,) = call(pack_body, [shape((half, 2 * groups * SCORE_E))], [line_rows])
    every = spread_all(packed, PLANE, lanes)
    offset = (
        (lax.axis_index("z") * nc + lax.axis_index("core")) * lanes
        + lax.axis_index("x") * ny
        + lax.axis_index("y")
    ) * vocab.shape[0]
    count = groups * SCORE_E
    (sums,) = call(
        score_body,
        [shape((8, 2 * count), F32)],
        [
            offset.astype(jnp.int32).reshape(1),
            every,
            vocab,
            jnp.concatenate([targets, targets]).reshape(1, 2 * count),
        ],
        scalars=1,
        scratch=[pltpu.VMEM((lanes * width, 2 * count), BF16)],
    )
    sums = jnp.sum(spread_all(sums[:1], PLANE, lanes), axis=0)
    sums = jnp.sum(spread_all(sums, LINE, groups), axis=0)[0]
    return layer_out.T, sums[count:] - jnp.log(sums[:count])


def solution(mesh):
    mesh = Mesh(mesh.devices.reshape(8, 2, 4, 8), ("z", "core", "x", "y"))
    placed = (
        P(LINE, PLANE),
        P(LINE, None),
        P(LINE, None),
        P(LINE, PLANE, None),
        P(LINE, PLANE, None),
        P(LINE, None, PLANE),
        P(PLANE, None),
        P(PLANE, None),
        P(None, PLANE),
        P((*LINE, *PLANE), None),
        P(),
    )
    return jax.shard_map(
        shards, mesh=mesh, in_specs=placed, out_specs=(P(LINE, PLANE), P()), check_vma=False
    )
```

time: 623 us -> 340 us (0.55)
  waiting for transfers between devices: 247 us -> 98.4 us
  blocking collectives: 308 us -> 171 us
  starting transfers between devices: 12.1 us -> 49.1 us
  matrix products: 19.8 us -> 0 us
  between operations: 14.1 us -> 0.91 us
  Pallas kernels: 0 us -> 10.8 us
  other arithmetic: 11.4 us -> 0.7 us
    all_gather x3 -> x0, waiting for transfers between devices: 246 us -> none  [the longest x1 110 us: shards(): lax.all_gather(flat_rows, 'tensor', axis=1, tiled=True)]
    all_gather x2 -> x0, blocking collectives: 182 us -> none  [the longest x1 146 us: shards(): collected = lax.all_gather(scored, ('expert', 'tensor'), axis=0, tiled=True)]
    all_to_all x1 -> x8, blocking collectives: 29.1 us -> 171 us  [the longest x4 107 us: spread_all(): lax.all_to_all(jnp.broadcast_to(value[None], (count, *value.shape)), axes...]
    psum x1 -> x0, blocking collectives: 96.8 us -> none  [shards(): lax.psum((exp_sums, target_part), ('expert', 'tensor'))]
    ppermute x0 -> x9, waiting for transfers between devices: none -> 62 us  [nearby(): lax.ppermute(value, axis, [((i + shift) % count, i) for i in range(count)])]
    all_to_all x1 -> x4, waiting for transfers between devices: 0.01 us -> 36.4 us  [spread_all(): lax.all_to_all(jnp.broadcast_to(value[None], (count, *value.shape)), axes...]
    ppermute x0 -> x9, starting transfers between devices: none -> 28.3 us  [nearby(): lax.ppermute(value, axis, [((i + shift) % count, i) for i in range(count)])]
    dot_general x11 -> x0, matrix products: 19.8 us -> none  [the longest x1 6.05 us: shards(): jnp.einsum('erw,efw->erf', rows, w_gate, preferred_element_type=jnp.float32)]
  transfers between devices with their start and end apart: 4 -> 13, of which waited for: 3 -> 10; matrix products, arithmetic and copies ran while one was open for 2% -> 0% of each run, Pallas kernels for 0% -> 2%
where the time goes in v1:
time: 340 us; the launch traced here: 338 us
  blocking collectives  171 us (50%)
  waiting for transfers between devices  98.4 us (29%)
  starting transfers between devices  49.1 us (14%)
  Pallas kernels  10.8 us (3%)
  local copies, waits for them, and re-layouts  7.38 us (2%)
    all_to_all x4, blocking collectives, spread_all(): lax.all_to_all(jnp.broadcast_to(value[None], (count, *value.shape)), axes...  107 us
    ppermute x9, waiting for transfers between devices, nearby(): lax.ppermute(value, axis, [((i + shift) % count, i) for i in range(count)])  62 us
    all_to_all x4, waiting for transfers between devices, spread_all(): lax.all_to_all(jnp.broadcast_to(value[None], (count, *value.shape)), axes...  36.4 us
    ppermute x9, starting transfers between devices, nearby(): lax.ppermute(value, axis, [((i + shift) % count, i) for i in range(count)])  28.3 us
    all_to_all x1, blocking collectives, shards(): arrived = lax.all_to_all(outgoing, LINE, 0, 0, tiled=True)  24.7 us
    all_to_all x4, starting transfers between devices, spread_all(): lax.all_to_all(jnp.broadcast_to(value[None], (count, *value.shape)), axes...  20.8 us
    all_to_all x1, blocking collectives, shards(): back = lax.all_to_all(back, LINE, 0, 0, tiled=True)  19.8 us
    all_to_all x1, blocking collectives, shards(): lax.all_to_all(arrived.reshape(nx, near, half, 2 * cap), 'x', 0, 0, tiled...  11.6 us
  transfers between devices with their start and end apart: 13, of which 10 were waited for; matrix products, arithmetic and copies ran while one was open for 0% of the time, Pallas kernels for 2%

profile of v1, /device:TPU:1, one launch (start us, length us, event | category | flops | bytes accessed | tf_op | source)
XLA Modules:
  0.0 338.2 jit_solution(18228906513541654599)
XLA Ops:
  0.6 0.0 copy-start.7
  0.6 0.8 copy-done.7
  1.4 0.7 copy-done.9
  2.1 0.7 copy-done.10
  2.8 0.6 shard_map.122
  3.4 24.7 %all_to_all.60 = bf16[16,80,128]{2,1,0:T(8,128)(2,1)S(1)} all-to-all(bf16[16,80,128]{2,1,0:T(8,128)(2,1)S(1)} %get-tuple-element.9), channel_id=1, replica_groups=mesh['z'=8,'core'=2,'x'=4,'y'=8] {'z','core'}, dimensions={0} | all-to-all | bytes 655360 | tf_op jit(solution)/shard_map/all_to_all | solution.py:241
  28.1 11.6 %all_to_all.61.in_ref = bf16[4,4,80,128]{3,2,1,0:T(8,128)(2,1)S(1)} all-to-all(bf16[4,4,80,128]{3,2,1,0:T(8,128)(2,1)S(1)} %bitcast.45), channel_id=1, replica_groups=mesh['z'=8,'core'=2,'x'=4,'y'=8] {'x'}, dimensions={0} | all-to-all | bytes 655360 | tf_op jit(solution)/shard_map/all_to_all | solution.py:243
  39.7 0.2 shard_map.123
  39.8 0.2 broadcast_in_dim.18
  40.0 0.0 copy-start.8
  40.0 67.9 %all_to_all.62.rows_ref = bf16[8,640,256]{2,1,0:T(8,128)(2,1)} all-to-all(bf16[8,640,256]{2,1,0:T(8,128)(2,1)S(1)} %broadcast_in_dim.18), channel_id=1, replica_groups=mesh['z'=8,'core'=2,'x'=4,'y'=8] {'y'}, dimensions={0} | all-to-all | bytes 5242880 | tf_op jit(solution)/shard_map/all_to_all | solution.py:202
  107.9 0.0 copy-done.8
  107.9 1.2 broadcast_in_dim.20
  109.1 4.1 %all-to-all-start.6 = ((bf16[32,160,128]{2,1,0:T(8,128)(2,1)}), bf16[32,160,128]{2,1,0:T(8,128)(2,1)S(1)}, u32[]{:S(2)}, u32[]{:S(2)}) async-start(bf16[32,160,128]{2,1,0:T(8,128)(2,1)} %broadcast_in_dim.20), calls=%async_computation.6 | async-start | bytes 2621440 | tf_op jit(solution)/shard_map/all_to_all | solution.py:202
  113.2 0.0 copy-done.2
  113.2 4.4 %collective-permute-start = (bf16[48,5120]{1,0:T(8,128)(2,1)S(1)}, bf16[48,5120]{1,0:T(8,128)(2,1)S(1)}, u32[]{:S(2)}, u32[]{:S(2)}) collective-permute-start(bf16[48,5120]{1,0:T(8,128)(2,1)S(1)} %bitcast.31), channel_id=1, source_target_pairs={{8,0},{16,8},{24,16},{0,24},{9,1},{17,9},{25,17},{1,25},{10,2},{18... | collective-permute-start | bytes 1474568 | tf_op jit(solution)/shard_map/ppermute | solution.py:212
  117.6 1.9 collective-permute-start.2
  119.6 0.0 copy-done.3
  119.6 4.6 %collective-permute-start.1 = (bf16[48,5120]{1,0:T(8,128)(2,1)S(1)}, bf16[48,5120]{1,0:T(8,128)(2,1)S(1)}, u32[]{:S(2)}, u32[]{:S(2)}) collective-permute-start(bf16[48,5120]{1,0:T(8,128)(2,1)S(1)} %bitcast.35), channel_id=1, source_target_pairs={{8,0},{16,8},{24,16},{0,24},{9,1},{17,9},{25,17},{1,25},{10,2},{18... | collective-permute-start | bytes 1474568 | tf_op jit(solution)/shard_map/ppermute | solution.py:212
  124.2 1.9 collective-permute-start.3
  126.1 3.1 collective-permute-start.4
  129.2 8.6 %collective-permute-done.refs_2_ = bf16[48,5120]{1,0:T(8,128)(2,1)S(1)} collective-permute-done((bf16[48,5120]{1,0:T(8,128)(2,1)S(1)}, bf16[48,5120]{1,0:T(8,128)(2,1)S(1)}, u32[]{:S(2)}, u32[]{:S(2)}) %collective-permute-start) | collective-permute-done | bytes 491552 | tf_op jit(solution)/shard_map/ppermute | solution.py:212
  137.8 2.5 collective-permute-start.5
  140.3 10.9 %collective-permute-done.1.refs_3_ = bf16[48,5120]{1,0:T(8,128)(2,1)S(1)} collective-permute-done((bf16[48,5120]{1,0:T(8,128)(2,1)S(1)}, bf16[48,5120]{1,0:T(8,128)(2,1)S(1)}, u32[]{:S(2)}, u32[]{:S(2)}) %collective-permute-start.1) | collective-permute-done | bytes 491552 | tf_op jit(solution)/shard_map/ppermute | solution.py:212
  151.2 0.0 collective-permute-done.2.refs_4_
  151.2 3.4 %collective-permute-done.3.refs_5_ = bf16[48,5120]{1,0:T(8,128)(2,1)S(1)} collective-permute-done((bf16[48,5120]{1,0:T(8,128)(2,1)S(1)}, bf16[48,5120]{1,0:T(8,128)(2,1)S(1)}, u32[]{:S(2)}, u32[]{:S(2)}) %collective-permute-start.3) | collective-permute-done | bytes 491552 | tf_op jit(solution)/shard_map/ppermute | solution.py:212
  154.6 8.3 %collective-permute-done.4.refs_6_ = bf16[48,5120]{1,0:T(8,128)(2,1)S(1)} collective-permute-done((bf16[48,5120]{1,0:T(8,128)(2,1)S(1)}, bf16[48,5120]{1,0:T(8,128)(2,1)S(1)}, u32[]{:S(2)}, u32[]{:S(2)}) %collective-permute-start.4) | collective-permute-done | bytes 491552 | tf_op jit(solution)/shard_map/ppermute | solution.py:212
  162.9 10.5 %collective-permute-done.5.refs_7_ = bf16[48,5120]{1,0:T(8,128)(2,1)S(1)} collective-permute-done((bf16[48,5120]{1,0:T(8,128)(2,1)S(1)}, bf16[48,5120]{1,0:T(8,128)(2,1)S(1)}, u32[]{:S(2)}, u32[]{:S(2)}) %collective-permute-start.5) | collective-permute-done | bytes 491552 | tf_op jit(solution)/shard_map/ppermute | solution.py:212
  173.5 5.4 %shard_map.124 = bf16[192,256]{1,0:T(8,128)(2,1)S(1)} custom-call(bf16[8,640,256]{2,1,0:T(8,128)(2,1)} %all_to_all.62.rows_ref, bf16[48,5120]{1,0:T(8,128)(2,1)S(1)} %bitcast.34, bf16[48,5120]{1,0:T(8,128)(2,1)S(1)} %bitcast.38, bf16[48,5120]{1,0:T(8,128)(2,1)S(1)} %collective-permute-done.refs_2_, bf16[48,5120]{1,0:T(8,128)(2,1)S(1)} %collective-permute-done.1.refs_3_, ...), custom_call_target="tpu_custom_call" | custom-call | bytes 6651904 | tf_op jit(solution)/shard_map/pallas_call | solution.py:23
  178.9 0.0 copy-start.4
  178.9 0.0 all-to-all-done.6
  178.9 0.9 broadcast_in_dim.19
  179.9 6.1 %all-to-all-start.3 = ((bf16[8,192,256]{2,1,0:T(8,128)(2,1)}), bf16[8,192,256]{2,1,0:T(8,128)(2,1)S(1)}, u32[]{:S(2)}, u32[]{:S(2)}) async-start(bf16[8,192,256]{2,1,0:T(8,128)(2,1)} %broadcast_in_dim.19), calls=%async_computation.3 | async-start | bytes 1572864 | tf_op jit(solution)/shard_map/all_to_all | solution.py:202
  186.0 0.0 copy-done.4
  186.0 0.0 copy-start.5
  186.0 1.0 copy-done.5
  187.0 0.5 shard_map.126
  187.6 19.6 %all-to-all-done.3.hidden_ref = bf16[8,192,256]{2,1,0:T(8,128)(2,1)S(1)} async-done(((bf16[8,192,256]{2,1,0:T(8,128)(2,1)}), bf16[8,192,256]{2,1,0:T(8,128)(2,1)S(1)}, u32[]{:S(2)}, u32[]{:S(2)}) %all-to-all-start.3) | async-done | bytes 786464 | tf_op jit(solution)/shard_map/all_to_all | solution.py:202
  207.2 0.8 broadcast_in_dim.21
  208.0 3.9 %all-to-all-start.7 = ((bf16[32,48,128]{2,1,0:T(8,128)(2,1)}), bf16[32,48,128]{2,1,0:T(8,128)(2,1)S(1)}, u32[]{:S(2)}, u32[]{:S(2)}) async-start(bf16[32,48,128]{2,1,0:T(8,128)(2,1)} %broadcast_in_dim.21), calls=%async_computation.7 | async-start | bytes 786432 | tf_op jit(solution)/shard_map/all_to_all | solution.py:202
  211.9 0.0 copy-done.1
  211.9 4.4 %collective-permute-start.6 = (bf16[160,1536]{1,0:T(8,128)(2,1)S(1)}, bf16[160,1536]{1,0:T(8,128)(2,1)S(1)}, u32[]{:S(2)}, u32[]{:S(2)}) collective-permute-start(bf16[160,1536]{1,0:T(8,128)(2,1)S(1)} %bitcast.27), channel_id=1, source_target_pairs={{8,0},{16,8},{24,16},{0,24},{9,1},{17,9},{25,17},{1,25},{10,2},{18... | collective-permute-start | bytes 1474568 | tf_op jit(solution)/shard_map/ppermute | solution.py:212
  216.3 1.9 collective-permute-start.7
  218.2 3.6 %collective-permute-start.8 = (bf16[160,1536]{1,0:T(8,128)(2,1)S(1)}, bf16[160,1536]{1,0:T(8,128)(2,1)}, u32[]{:S(2)}, u32[]{:S(2)}) collective-permute-start(bf16[160,1536]{1,0:T(8,128)(2,1)S(1)} %bitcast.29), channel_id=1, source_target_pairs={{16,0},{24,8},{0,16},{8,24},{17,1},{25,9},{1,17},{9,25},{18,2},{26... | collective-permute-start | bytes 1474568 | tf_op jit(solution)/shard_map/ppermute | solution.py:212
  221.8 7.4 %collective-permute-done.6.refs_1_ = bf16[160,1536]{1,0:T(8,128)(2,1)S(1)} collective-permute-done((bf16[160,1536]{1,0:T(8,128)(2,1)S(1)}, bf16[160,1536]{1,0:T(8,128)(2,1)S(1)}, u32[]{:S(2)}, u32[]{:S(2)}) %collective-permute-start.6) | collective-permute-done | bytes 491552 | tf_op jit(solution)/shard_map/ppermute | solution.py:212
  229.2 2.5 collective-permute-done.7.refs_2_
  231.6 10.4 %collective-permute-done.8.refs_3_ = bf16[160,1536]{1,0:T(8,128)(2,1)} collective-permute-done((bf16[160,1536]{1,0:T(8,128)(2,1)S(1)}, bf16[160,1536]{1,0:T(8,128)(2,1)}, u32[]{:S(2)}, u32[]{:S(2)}) %collective-permute-start.8) | collective-permute-done | bytes 491552 | tf_op jit(solution)/shard_map/ppermute | solution.py:212
  242.0 1.9 shard_map.125
  243.9 0.0 copy-start.6
  243.9 0.0 all-to-all-done.7
  243.9 8.4 %all_to_all.63 = bf16[4,4,80,128]{3,2,1,0:T(8,128)(2,1)S(1)} all-to-all(bf16[4,4,80,128]{3,2,1,0:T(8,128)(2,1)S(1)} %shard_map.125), channel_id=1, replica_groups=mesh['z'=8,'core'=2,'x'=4,'y'=8] {'x'}, dimensions={0} | all-to-all | bytes 655360 | tf_op jit(solution)/shard_map/all_to_all | solution.py:262
  252.3 19.8 %all_to_all.64.back_ref = bf16[16,80,128]{2,1,0:T(8,128)(2,1)S(1)} all-to-all(bf16[16,80,128]{2,1,0:T(8,128)(2,1)S(1)} %bitcast.46), channel_id=1, replica_groups=mesh['z'=8,'core'=2,'x'=4,'y'=8] {'z','core'}, dimensions={0} | all-to-all | bytes 655360 | tf_op jit(solution)/shard_map/all_to_all | solution.py:263
  272.1 0.0 copy-done.6
  272.1 1.3 shard_map.127
  273.4 10.3 %all_to_all.65 = bf16[16,4,160]{2,1,0:T(4,128)(2,1)S(1)} all-to-all(bf16[16,4,160]{2,1,0:T(4,128)(2,1)S(1)} %broadcast_in_dim.22), channel_id=1, replica_groups=mesh['z'=8,'core'=2,'x'=4,'y'=8] {'z','core'}, dimensions={0} | all-to-all | bytes 40960 | tf_op jit(solution)/shard_map/all_to_all | solution.py:202
  283.7 0.3 shard_map.128
  284.0 0.9 broadcast_in_dim.23
  284.9 6.7 %all-to-all-start.9 = ((bf16[32,80,128]{2,1,0:T(8,128)(2,1)}), bf16[32,80,128]{2,1,0:T(8,128)(2,1)S(1)}, u32[]{:S(2)}, u32[]{:S(2)}) async-start(bf16[32,80,128]{2,1,0:T(8,128)(2,1)} %broadcast_in_dim.23), calls=%async_computation.9 | async-start | bytes 1310720 | tf_op jit(solution)/shard_map/all_to_all | solution.py:202
  291.7 0.1 add_bitcast_fusion.targets_ref
  291.7 16.8 %all-to-all-done.9.rows_ref = bf16[32,80,128]{2,1,0:T(8,128)(2,1)S(1)} async-done(((bf16[32,80,128]{2,1,0:T(8,128)(2,1)}), bf16[32,80,128]{2,1,0:T(8,128)(2,1)S(1)}, u32[]{:S(2)}, u32[]{:S(2)}) %all-to-all-start.9) | async-done | bytes 655392 | tf_op jit(solution)/shard_map/all_to_all | solution.py:202
  308.5 0.7 shard_map.129
  309.2 16.5 %all_to_all.66 = f32[32,1,128]{2,1,0:T(1,128)S(1)} all-to-all(f32[32,1,128]{2,1,0:T(1,128)S(1)} %broadcast_in_dim.25), channel_id=1, replica_groups=mesh['z'=8,'core'=2,'x'=4,'y'=8] {'x','y'}, dimensions={0} | all-to-all | bytes 32768 | tf_op jit(solution)/shard_map/all_to_all | solution.py:202
  325.8 11.8 %all_to_all.67 = f32[16,1,128]{2,1,0:T(1,128)S(1)} all-to-all(f32[16,1,128]{2,1,0:T(1,128)S(1)} %broadcast_in_dim.26), channel_id=1, replica_groups=mesh['z'=8,'core'=2,'x'=4,'y'=8] {'z','core'}, dimensions={0} | all-to-all | bytes 16384 | tf_op jit(solution)/shard_map/all_to_all | solution.py:202
  337.6 0.6 subtract_bitcast_fusion
  (17 shorter events, 0.1 us)
Async XLA Ops:
  0.6 0.8 copy-start.7
  1.4 0.7 copy-start.9
  2.1 0.7 copy-start.10
  40.0 67.9 %copy-start.8 = (bf16[128,160]{0,1:T(8,128)(2,1)S(1)}, bf16[128,160]{0,1:T(8,128)(2,1)}, u32[]{:S(2)}) copy-start(bf16[128,160]{0,1:T(8,128)(2,1)} %param.11) | copy-start | bytes 122884
  109.1 4.1 %copy-start.2 = (bf16[1,48,5120]{2,1,0:T(8,128)(2,1)S(1)}, bf16[1,48,5120]{2,1,0:T(8,128)(2,1)}, u32[]{:S(2)}) copy-start(bf16[1,48,5120]{2,1,0:T(8,128)(2,1)} %param.14) | copy-start | bytes 1474564
  109.1 10.4 %copy-start.3 = (bf16[1,48,5120]{2,1,0:T(8,128)(2,1)S(1)}, bf16[1,48,5120]{2,1,0:T(8,128)(2,1)}, u32[]{:S(2)}) copy-start(bf16[1,48,5120]{2,1,0:T(8,128)(2,1)} %param.15) | copy-start | bytes 1474564
  109.1 69.8 %all-to-all-start.6 = ((bf16[32,160,128]{2,1,0:T(8,128)(2,1)}), bf16[32,160,128]{2,1,0:T(8,128)(2,1)S(1)}, u32[]{:S(2)}, u32[]{:S(2)}) async-start(bf16[32,160,128]{2,1,0:T(8,128)(2,1)} %broadcast_in_dim.20), calls=%async_computation.6 | async-start | bytes 2621440 | tf_op jit(solution)/shard_map/all_to_all | solution.py:202
  113.2 24.6 %collective-permute-start = (bf16[48,5120]{1,0:T(8,128)(2,1)S(1)}, bf16[48,5120]{1,0:T(8,128)(2,1)S(1)}, u32[]{:S(2)}, u32[]{:S(2)}) collective-permute-start(bf16[48,5120]{1,0:T(8,128)(2,1)S(1)} %bitcast.31), channel_id=1, source_target_pairs={{8,0},{16,8},{24,16},{0,24},{9,1},{17,9},{25,17},{1,25},{10,2},{18... | collective-permute-start | bytes 1474568 | tf_op jit(solution)/shard_map/ppermute | solution.py:212
  117.6 33.6 %collective-permute-start.2 = (bf16[48,5120]{1,0:T(8,128)(2,1)S(1)}, bf16[48,5120]{1,0:T(8,128)(2,1)S(1)}, u32[]{:S(2)}, u32[]{:S(2)}) collective-permute-start(bf16[48,5120]{1,0:T(8,128)(2,1)S(1)} %bitcast.32), channel_id=1, source_target_pairs={{24,0},{0,8},{8,16},{16,24},{25,1},{1,9},{9,17},{17,25},{26,2},{2,... | collective-permute-start | bytes 1474568 | tf_op jit(solution)/shard_map/ppermute | solution.py:212
  119.6 31.6 %collective-permute-start.1 = (bf16[48,5120]{1,0:T(8,128)(2,1)S(1)}, bf16[48,5120]{1,0:T(8,128)(2,1)S(1)}, u32[]{:S(2)}, u32[]{:S(2)}) collective-permute-start(bf16[48,5120]{1,0:T(8,128)(2,1)S(1)} %bitcast.35), channel_id=1, source_target_pairs={{8,0},{16,8},{24,16},{0,24},{9,1},{17,9},{25,17},{1,25},{10,2},{18... | collective-permute-start | bytes 1474568 | tf_op jit(solution)/shard_map/ppermute | solution.py:212
  124.2 30.5 %collective-permute-start.3 = (bf16[48,5120]{1,0:T(8,128)(2,1)S(1)}, bf16[48,5120]{1,0:T(8,128)(2,1)S(1)}, u32[]{:S(2)}, u32[]{:S(2)}) collective-permute-start(bf16[48,5120]{1,0:T(8,128)(2,1)S(1)} %bitcast.36), channel_id=1, source_target_pairs={{24,0},{0,8},{8,16},{16,24},{25,1},{1,9},{9,17},{17,25},{26,2},{2,... | collective-permute-start | bytes 1474568 | tf_op jit(solution)/shard_map/ppermute | solution.py:212
  126.1 36.9 %collective-permute-start.4 = (bf16[48,5120]{1,0:T(8,128)(2,1)S(1)}, bf16[48,5120]{1,0:T(8,128)(2,1)S(1)}, u32[]{:S(2)}, u32[]{:S(2)}) collective-permute-start(bf16[48,5120]{1,0:T(8,128)(2,1)S(1)} %bitcast.33), channel_id=1, source_target_pairs={{16,0},{24,8},{0,16},{8,24},{17,1},{25,9},{1,17},{9,25},{18,2},{26... | collective-permute-start | bytes 1474568 | tf_op jit(solution)/shard_map/ppermute | solution.py:212
  137.8 35.7 %collective-permute-start.5 = (bf16[48,5120]{1,0:T(8,128)(2,1)S(1)}, bf16[48,5120]{1,0:T(8,128)(2,1)S(1)}, u32[]{:S(2)}, u32[]{:S(2)}) collective-permute-start(bf16[48,5120]{1,0:T(8,128)(2,1)S(1)} %bitcast.37), channel_id=1, source_target_pairs={{16,0},{24,8},{0,16},{8,24},{17,1},{25,9},{1,17},{9,25},{18,2},{26... | collective-permute-start | bytes 1474568 | tf_op jit(solution)/shard_map/ppermute | solution.py:212
  178.9 7.1 %copy-start.4 = (bf16[48,5120]{1,0:T(8,128)(2,1)S(1)}, bf16[48,5120]{1,0:T(8,128)(2,1)}, u32[]{:S(2)}) copy-start(bf16[48,5120]{1,0:T(8,128)(2,1)} %gate_ref.1) | copy-start | bytes 1474564
  179.9 27.3 %all-to-all-start.3 = ((bf16[8,192,256]{2,1,0:T(8,128)(2,1)}), bf16[8,192,256]{2,1,0:T(8,128)(2,1)S(1)}, u32[]{:S(2)}, u32[]{:S(2)}) async-start(bf16[8,192,256]{2,1,0:T(8,128)(2,1)} %broadcast_in_dim.19), calls=%async_computation.3 | async-start | bytes 1572864 | tf_op jit(solution)/shard_map/all_to_all | solution.py:202
  186.0 1.0 copy-start.5
  187.0 24.8 %copy-start.1 = (bf16[1,1536,160]{1,2,0:T(8,128)(2,1)S(1)}, bf16[1,1536,160]{1,2,0:T(8,128)(2,1)}, u32[]{:S(2)}) copy-start(bf16[1,1536,160]{1,2,0:T(8,128)(2,1)} %param.16) | copy-start | bytes 1474564
  208.0 35.9 %all-to-all-start.7 = ((bf16[32,48,128]{2,1,0:T(8,128)(2,1)}), bf16[32,48,128]{2,1,0:T(8,128)(2,1)S(1)}, u32[]{:S(2)}, u32[]{:S(2)}) async-start(bf16[32,48,128]{2,1,0:T(8,128)(2,1)} %broadcast_in_dim.21), calls=%async_computation.7 | async-start | bytes 786432 | tf_op jit(solution)/shard_map/all_to_all | solution.py:202
  211.9 17.3 %collective-permute-start.6 = (bf16[160,1536]{1,0:T(8,128)(2,1)S(1)}, bf16[160,1536]{1,0:T(8,128)(2,1)S(1)}, u32[]{:S(2)}, u32[]{:S(2)}) collective-permute-start(bf16[160,1536]{1,0:T(8,128)(2,1)S(1)} %bitcast.27), channel_id=1, source_target_pairs={{8,0},{16,8},{24,16},{0,24},{9,1},{17,9},{25,17},{1,25},{10,2},{18... | collective-permute-start | bytes 1474568 | tf_op jit(solution)/shard_map/ppermute | solution.py:212
  216.3 15.4 %collective-permute-start.7 = (bf16[160,1536]{1,0:T(8,128)(2,1)S(1)}, bf16[160,1536]{1,0:T(8,128)(2,1)S(1)}, u32[]{:S(2)}, u32[]{:S(2)}) collective-permute-start(bf16[160,1536]{1,0:T(8,128)(2,1)S(1)} %bitcast.28), channel_id=1, source_target_pairs={{24,0},{0,8},{8,16},{16,24},{25,1},{1,9},{9,17},{17,25},{26,2},{2,... | collective-permute-start | bytes 1474568 | tf_op jit(solution)/shard_map/ppermute | solution.py:212
  218.2 23.8 %collective-permute-start.8 = (bf16[160,1536]{1,0:T(8,128)(2,1)S(1)}, bf16[160,1536]{1,0:T(8,128)(2,1)}, u32[]{:S(2)}, u32[]{:S(2)}) collective-permute-start(bf16[160,1536]{1,0:T(8,128)(2,1)S(1)} %bitcast.29), channel_id=1, source_target_pairs={{16,0},{24,8},{0,16},{8,24},{17,1},{25,9},{1,17},{9,25},{18,2},{26... | collective-permute-start | bytes 1474568 | tf_op jit(solution)/shard_map/ppermute | solution.py:212
  243.9 28.2 %copy-start.6 = (bf16[1536,160]{0,1:T(8,128)(2,1)S(1)}, bf16[1536,160]{0,1:T(8,128)(2,1)}, u32[]{:S(2)}) copy-start(bf16[1536,160]{0,1:T(8,128)(2,1)} %param.19) | copy-start | bytes 1474564
  273.3 18.3 %copy-start.11 = (s32[64]{0:T(128)S(1)}, s32[64]{0:T(128)}, u32[]{:S(2)}) copy-start(s32[64]{0:T(128)} %param.21) | copy-start | bytes 772
  273.3 35.2 %copy-start = (bf16[128,5120]{1,0:T(8,128)(2,1)S(1)}, bf16[128,5120]{1,0:T(8,128)(2,1)}, u32[]{:S(2)}) copy-start(bf16[128,5120]{1,0:T(8,128)(2,1)} %vocab_ref.1) | copy-start | bytes 3932164
  284.9 23.6 %all-to-all-start.9 = ((bf16[32,80,128]{2,1,0:T(8,128)(2,1)}), bf16[32,80,128]{2,1,0:T(8,128)(2,1)S(1)}, u32[]{:S(2)}, u32[]{:S(2)}) async-start(bf16[32,80,128]{2,1,0:T(8,128)(2,1)} %broadcast_in_dim.23), calls=%async_computation.9 | async-start | bytes 1310720 | tf_op jit(solution)/shard_map/all_to_all | solution.py:202

commit v2 on v1

--- a/solution.py
+++ b/solution.py
@@ -11,12 +11,12 @@
 BF16 = jnp.bfloat16
 LINE = ("z", "core")
 PLANE = ("x", "y")
-VMEM_LIMIT = 48 << 20
-
-
-def call(body, outs, args, scalars=0, scratch=(), flops=0):
+
+
+def call(body, outs, args, scalars=0, far=(), scratch=(), limit=16):
     specs = [
-        pl.BlockSpec(memory_space=pltpu.SMEM if n < scalars else pltpu.VMEM) for n in range(len(args))
+        pl.BlockSpec(memory_space=pltpu.SMEM if n < scalars else pltpu.HBM if n in far else pltpu.VMEM)
+        for n in range(len(args))
     ]
     moved = sum(a.size * a.dtype.itemsize for a in args)
     moved += sum(o.size * o.dtype.itemsize for o in outs)
@@ -26,9 +26,16 @@
         in_specs=specs,
         out_specs=[pl.BlockSpec(memory_space=pltpu.VMEM) for _ in outs],
         scratch_shapes=list(scratch),
-        cost_estimate=pl.CostEstimate(flops=flops, bytes_accessed=moved, transcendentals=0),
-        compiler_params=pltpu.CompilerParams(vmem_limit_bytes=VMEM_LIMIT),
+        cost_estimate=pl.CostEstimate(flops=0, bytes_accessed=moved, transcendentals=0),
+        compiler_params=pltpu.CompilerParams(vmem_limit_bytes=limit << 20),
     )(*args)
+
+
+def fetch(pairs, sems):
+    copies = [pltpu.make_async_copy(src, dst, sems.at[n]) for n, (src, dst) in enumerate(pairs)]
+    for copy in copies:
+        copy.start()
+    return copies
 
 
 def shape(dims, dtype=BF16):
@@ -89,50 +96,63 @@
 
 
 def spread_body(in_ref, out_ref):
-    lanes_x, groups, half, lanes = in_ref.shape
-    cap = lanes // 2
+    lanes_x, _, lanes = in_ref.shape
+    width = out_ref.shape[0] // lanes_x
+    half, cap = width // 2, lanes // 2
+    groups = (in_ref.shape[1] - width) // half
     for x in range(lanes_x):
+        top, mid, end = x * width, x * width + half, (x + 1) * width
         for q in range(groups // 2):
-            a = in_ref[x, 2 * q].astype(F32)
-            b = in_ref[x, 2 * q + 1].astype(F32)
+            a = in_ref[x, 2 * q * half : (2 * q + 1) * half, :].astype(F32)
+            b = in_ref[x, (2 * q + 1) * half : (2 * q + 2) * half, :].astype(F32)
             cols = slice(q * lanes, (q + 1) * lanes)
-            out_ref[2 * half * x : 2 * half * x + half, cols] = pair_low(a, b, cap).astype(BF16)
-            out_ref[2 * half * x + half : 2 * half * (x + 1), cols] = pair_high(a, b, cap).astype(BF16)
+            out_ref[top:mid, cols] = pair_low(a, b, cap).astype(BF16)
+            out_ref[mid:end, cols] = pair_high(a, b, cap).astype(BF16)
+        out_ref[top:end, groups * cap :] = in_ref[x, groups * half :, :]
 
 
 def glu(gate, up):
     return (gate / (1.0 + jnp.exp(-gate)) * up).astype(BF16)
 
 
-def hidden_body(rows_ref, *refs):
-    *weights, out_ref, flat_ref = refs
-    ny, block, _ = rows_ref.shape
-    nx = len(weights) // 2
-    width = block // nx
-    for y in range(ny):
-        for x in range(nx):
-            at = (x * ny + y) * width
-            flat_ref[at : at + width, :] = rows_ref[y, x * width : (x + 1) * width, :]
+def hidden_body(y_ref, *refs):
+    blocks = refs[: len(RING)]
+    out_ref, flat_ref, gates_ref, ups_ref, sems = refs[-5:]
+    weights = refs[len(RING) : -5]
+    nx = len(weights) // 2 - 1
     units = weights[0].shape[0]
-    rows = flat_ref[...]
-    for x in range(nx):
-        gate = nn(weights[2 * x][...], rows)
-        up = nn(weights[2 * x + 1][...], rows)
-        out_ref[x * units : (x + 1) * units, :] = glu(gate, up)
-
-
-def shared_body(tok_ref, gate_ref, up_ref, out_ref):
-    tok = tok_ref[...]
-    out_ref[...] = glu(nn(gate_ref[...], tok), nn(up_ref[...], tok))
+    width = blocks[0].shape[0] // nx
+    ny = flat_ref.shape[0] // (nx * width)
+    pairs = []
+    for n in range(nx + 1):
+        for at, into in enumerate((gates_ref, ups_ref)):
+            pairs.append((weights[2 * n + at], into.at[n * units : (n + 1) * units, :]))
+    for block, (shift, first) in zip(blocks, RING):
+        y = lax.rem(y_ref[0] + shift, ny)
+        for n in range(block.shape[0] // width):
+            at = pl.multiple_of(((first + n) * ny + y) * width, width)
+            pairs.append((block.at[n * width : (n + 1) * width, :], flat_ref.at[pl.ds(at, width), :]))
+    for copy in fetch(pairs, sems):
+        copy.wait()
+    cols = out_ref.shape[1]
+    top = nx * units
+    rows = flat_ref[:, :cols]
+    out_ref[:top, :] = glu(nn(gates_ref[:top, :], rows), nn(ups_ref[:top, :], rows))
+    toks = flat_ref[:, cols:]
+    own = glu(nn(gates_ref[top:, :], toks), nn(ups_ref[top:, :], toks))
+    fold = units // 2
+    out_ref[top : top + fold, :] = jnp.concatenate([own[:fold], own[fold:]], axis=1)
 
 
 def down_body(x_ref, hidden_ref, *refs):
-    *weights, out_ref, flat_ref = refs
+    *weights, out_ref, flat_ref, down_ref, sems = refs
     nx = len(weights)
+    copies = fetch([(weights[n], down_ref.at[n]) for n in range(nx)], sems)
     ny = hidden_ref.shape[0]
-    units = hidden_ref.shape[1] // nx
-    _, groups, half, lanes = out_ref.shape
-    cap = lanes // 2
+    units = flat_ref.shape[0] // (nx * ny)
+    width, lanes = weights[0].shape[0], out_ref.shape[2]
+    half, cap, fold = width // 2, lanes // 2, units // 2
+    groups = (out_ref.shape[1] - ny * units) // half
     own = [lax.rem(x_ref[0] + shift, nx) for shift in SHIFTS]
     for n in range(nx):
         for y in range(ny):
@@ -140,12 +160,18 @@
             flat_ref[pl.ds(at, units), :] = hidden_ref[y, n * units : (n + 1) * units, :]
     rows = flat_ref[...]
     for n in range(nx):
-        out = nn(weights[n][...], rows)
+        copies[n].wait()
+        out = nn(down_ref[n], rows)
         for q in range(groups // 2):
             cols = slice(q * lanes, (q + 1) * lanes)
             a, b = out[:half, cols], out[half:, cols]
-            out_ref[own[n], 2 * q] = pair_low(a, b, cap).astype(BF16)
-            out_ref[own[n], 2 * q + 1] = pair_high(a, b, cap).astype(BF16)
+            out_ref[own[n], 2 * q * half : (2 * q + 1) * half, :] = pair_low(a, b, cap).astype(BF16)
+            out_ref[own[n], (2 * q + 1) * half : (2 * q + 2) * half, :] = pair_high(a, b, cap).astype(BF16)
+        for y in range(ny):
+            at = groups * half + y * units
+            both = hidden_ref[y, nx * units : nx * units + fold, :]
+            out_ref[n, at : at + fold, :] = both[:, :lanes]
+            out_ref[n, at + fold : at + units, :] = both[:, lanes:]
 
 
 def combine_body(slot_ref, gate_ref, back_ref, tok_ref, hidden_ref, down_ref, out_ref, scored_ref):
@@ -162,7 +188,11 @@
         head = mix.astype(BF16)
         tail = (mix - head.astype(F32)).astype(BF16)
         routed = routed + nn(back_ref[e], head) + nn(back_ref[e], tail)
-    shared = nn(down_ref[...], hidden_ref[...])
+    depth = down_ref.shape[1] // hidden_ref.shape[0]
+    skip = hidden_ref.shape[1] - depth
+    shared = jnp.zeros((2 * half, rows), F32)
+    for x in range(hidden_ref.shape[0]):
+        shared = shared + nn(down_ref[:, x * depth : (x + 1) * depth], hidden_ref[x, skip:, :])
     routed = jnp.concatenate([routed[:, :rows], routed[:, rows:]], axis=0)
     out = (tok_ref[...].astype(F32) + shared + routed).astype(BF16)
     out_ref[...] = out
@@ -196,6 +226,7 @@
 
 
 SHIFTS = (0, 1, 3, 2)
+RING = ((0, 0), (7, 0), (1, 0), (6, 0), (2, 0), (5, 0), (3, 0), (4, 0), (4, 2))
 
 
 def spread_all(value, axes, count):
@@ -204,14 +235,24 @@
     )
 
 
-def nearby(value, axis):
+def from_shift(value, axis, shift):
     count = lax.axis_size(axis)
-    return [
-        value
-        if shift == 0
-        else lax.ppermute(value, axis, [((i + shift) % count, i) for i in range(count)])
-        for shift in SHIFTS
-    ]
+    return lax.ppermute(value, axis, [((i + shift) % count, i) for i in range(count)])
+
+
+def around(value, axis, *due):
+    count = lax.axis_size(axis)
+    left = right = value
+    got, kept = [value], []
+    for hop in range(3):
+        if hop and hop <= len(due):
+            left, right, *had = lax.optimization_barrier((left, right, *due[hop - 1]))
+            kept += had
+        left = from_shift(left, axis, count - 1)
+        right = from_shift(right, axis, 1)
+        got += [left, right]
+    part = value.shape[0] // 2
+    return [*got, from_shift(left[:part], axis, count - 1), from_shift(right[part:], axis, 1)], kept
 
 
 def shards(tokens, routes, gates, w_gate, w_up, w_down, shared_gate, shared_up, shared_down, vocab, targets):
@@ -224,10 +265,12 @@
     units = w_gate.shape[1]
     tok = tokens.T
     x_at = lax.axis_index("x").astype(jnp.int32).reshape(1)
-
-    gates_near = nearby(w_gate[0], "x")
-    ups_near = nearby(w_up[0], "x")
-    downs_near = nearby(w_down[0].T, "x")
+    y_at = lax.axis_index("y").astype(jnp.int32).reshape(1)
+
+    own_gate, own_up, own_down = w_gate[0], w_up[0], w_down[0].T
+    near_gate = [from_shift(own_gate, "x", shift) for shift in SHIFTS[1:]]
+    near_up = [from_shift(own_up, "x", shift) for shift in SHIFTS[1:]]
+    near_down = [from_shift(own_down, "x", shift) for shift in SHIFTS[1:]]
 
     outgoing, slot, gate = call(
         dispatch_body,
@@ -239,32 +282,48 @@
         [routes.T, gates.T, tok],
     )
     arrived = lax.all_to_all(outgoing, LINE, 0, 0, tiled=True)
-    plane_tok = spread_all(tok, PLANE, lanes).reshape(lanes * width, rows)
-    quarter = lax.all_to_all(arrived.reshape(nx, near, half, 2 * cap), "x", 0, 0, tiled=True)
-    (spread,) = call(spread_body, [shape((nx * width, near * cap))], [quarter])
-    gathered = spread_all(spread, "y", ny)
+    arrived, g1, g3, u1, u3 = lax.optimization_barrier((arrived, *near_gate[:2], *near_up[:2]))
+    leaving = jnp.concatenate(
+        [arrived.reshape(nx, near * half, 2 * cap), jnp.broadcast_to(tok[None], (nx, width, rows))], axis=1
+    )
+    quarter = lax.all_to_all(leaving, "x", 0, 0, tiled=True)
+    (spread,) = call(spread_body, [shape((nx * width, near * cap + rows))], [quarter])
+    blocks, (g2, u2, d1, d3) = around(spread, "y", (near_gate[2], near_up[2]), near_down[:2])
     (hidden,) = call(
         hidden_body,
-        [shape((nx * units, near * cap))],
-        [gathered, *[w for pair in zip(gates_near, ups_near) for w in pair]],
-        scratch=[pltpu.VMEM((lanes * width, near * cap), BF16)],
-    )
-    (hidden_shared,) = call(shared_body, [shape((units, rows))], [plane_tok, shared_gate, shared_up])
+        [shape((nx * units + units // 2 + 8, near * cap))],
+        [y_at, *blocks, own_gate, own_up, g1, u1, g3, u3, g2, u2, shared_gate, shared_up],
+        scalars=1,
+        far=range(1, 2 * nx + len(RING) + 3),
+        scratch=[
+            pltpu.VMEM((lanes * width, near * cap + rows), BF16),
+            pltpu.VMEM(((nx + 1) * units, lanes * width), BF16),
+            pltpu.VMEM(((nx + 1) * units, lanes * width), BF16),
+            pltpu.SemaphoreType.DMA((2 * nx + 2 + lanes,)),
+        ],
+        limit=60,
+    )
     all_hidden = spread_all(hidden, "y", ny)
-    all_shared = spread_all(hidden_shared, PLANE, lanes).reshape(lanes * units, rows)
     (returned,) = call(
         down_body,
-        [shape((nx, near, half, 2 * cap))],
-        [x_at, all_hidden, *downs_near],
+        [shape((nx, near * half + ny * units, 2 * cap))],
+        [x_at, all_hidden, own_down, d1, d3, near_down[2]],
         scalars=1,
-        scratch=[pltpu.VMEM((lanes * units, near * cap), BF16)],
-    )
-    back = lax.all_to_all(returned, "x", 0, 0, tiled=True).reshape(groups, half, 2 * cap)
+        far=range(2, 2 + nx),
+        scratch=[
+            pltpu.VMEM((lanes * units, near * cap), BF16),
+            pltpu.VMEM((nx, width, lanes * units), BF16),
+            pltpu.SemaphoreType.DMA((nx,)),
+        ],
+        limit=60,
+    )
+    mixed = lax.all_to_all(returned, "x", 0, 0, tiled=True)
+    back = mixed[:, : near * half].reshape(groups, half, 2 * cap)
     back = lax.all_to_all(back, LINE, 0, 0, tiled=True)
     layer_out, scored = call(
         combine_body,
         [shape((width, rows)), shape((8, width))],
-        [slot, gate, back, tok, all_shared, shared_down.T],
+        [slot, gate, back, tok, mixed, shared_down.T],
     )
     line_rows = spread_all(scored[:SCORE_E], LINE, groups).reshape(groups * SCORE_E, width)
     (packed,) = call(pack_body, [shape((half, 2 * groups * SCORE_E))], [line_rows])

time: 340 us -> 281 us (0.83)
  blocking collectives: 171 us -> 92.4 us
  starting transfers between devices: 49.1 us -> 84.3 us
  waiting for transfers between devices: 98.4 us -> 76.7 us
  Pallas kernels: 10.8 us -> 14.8 us
    all_to_all x4 -> x3, blocking collectives: 107 us -> 38.7 us  [spread_all(): lax.all_to_all(jnp.broadcast_to(value[None], (count, *value.shape)), axes...]
    all_to_all x3 -> x1, blocking collectives: 44.6 us -> 15.3 us  [shards(): mixed = lax.all_to_all(returned, 'x', 0, 0, tiled=True)]
    ppermute x9 -> x17, starting transfers between devices: 28.3 us -> 55.2 us  [from_shift(): lax.ppermute(value, axis, [((i + shift) % count, i) for i in range(count)])]
    all_to_all x1, blocking collectives: 19.8 us -> 38.4 us  [shards(): back = lax.all_to_all(back, LINE, 0, 0, tiled=True)]
    all_to_all x0 -> x2, starting transfers between devices: none -> 15.4 us  [the longest x1 12 us: shards(): arrived = lax.all_to_all(outgoing, LINE, 0, 0, tiled=True)]
    all_to_all x4 -> x2, waiting for transfers between devices: 36.4 us -> 22.1 us  [spread_all(): lax.all_to_all(jnp.broadcast_to(value[None], (count, *value.shape)), axes...]
    ppermute x9 -> x17, waiting for transfers between devices: 62 us -> 53.8 us  [from_shift(): lax.ppermute(value, axis, [((i + shift) % count, i) for i in range(count)])]
    all_to_all x4 -> x2, starting transfers between devices: 20.8 us -> 13.7 us  [spread_all(): lax.all_to_all(jnp.broadcast_to(value[None], (count, *value.shape)), axes...]
  transfers between devices with their start and end apart: 13 -> 21, of which waited for: 10 -> 15; matrix products, arithmetic and copies ran while one was open for 0% -> 1% of each run, Pallas kernels for 2% -> 0%
where the time goes in v2:
time: 281 us; the launch traced here: 279 us
  blocking collectives  92.4 us (33%)
  starting transfers between devices  84.3 us (30%)
  waiting for transfers between devices  76.7 us (27%)
  Pallas kernels  14.8 us (5%)
  local copies, waits for them, and re-layouts  8.54 us (3%)
    ppermute x17, starting transfers between devices, from_shift(): lax.ppermute(value, axis, [((i + shift) % count, i) for i in range(count)])  55.2 us
    ppermute x17, waiting for transfers between devices, from_shift(): lax.ppermute(value, axis, [((i + shift) % count, i) for i in range(count)])  53.8 us
    all_to_all x3, blocking collectives, spread_all(): lax.all_to_all(jnp.broadcast_to(value[None], (count, *value.shape)), axes...  38.7 us
    all_to_all x1, blocking collectives, shards(): back = lax.all_to_all(back, LINE, 0, 0, tiled=True)  38.4 us
    all_to_all x2, waiting for transfers between devices, spread_all(): lax.all_to_all(jnp.broadcast_to(value[None], (count, *value.shape)), axes...  22.1 us
    all_to_all x1, blocking collectives, shards(): mixed = lax.all_to_all(returned, 'x', 0, 0, tiled=True)  15.3 us
    pallas_call x7, Pallas kernels, call(): pl.pallas_call(body, out_shape=outs, in_specs=specs, out_specs=[pl.BlockS...  14.8 us
    all_to_all x2, starting transfers between devices, spread_all(): lax.all_to_all(jnp.broadcast_to(value[None], (count, *value.shape)), axes...  13.7 us
  transfers between devices with their start and end apart: 21, of which 15 were waited for; matrix products, arithmetic and copies ran while one was open for 1% of the time, Pallas kernels for 0%

profile of v2, /device:TPU:1, one launch (start us, length us, event | category | flops | bytes accessed | tf_op | source)
XLA Modules:
  0.0 279.3 jit_solution(3325593014818007059)
XLA Ops:
  0.6 0.0 copy-start.3
  0.6 0.8 copy-done.3
  1.4 0.7 copy-done.5
  2.1 0.7 copy-done.6
  2.8 1.3 shard_map.122
  4.1 12.0 %all-to-all-start = ((bf16[16,80,128]{2,1,0:T(8,128)(2,1)}), bf16[16,80,128]{2,1,0:T(8,128)(2,1)S(1)}, u32[]{:S(2)}, u32[]{:S(2)}) async-start(bf16[16,80,128]{2,1,0:T(8,128)(2,1)} %get-tuple-element.22), calls=%async_computation | async-start | bytes 655360 | tf_op jit(solution)/shard_map/all_to_all | solution.py:284
  16.1 4.4 %collective-permute-start = (bf16[48,5120]{1,0:T(8,128)(2,1)}, bf16[48,5120]{1,0:T(8,128)(2,1)S(1)}, u32[]{:S(2)}, u32[]{:S(2)}) collective-permute-start(bf16[48,5120]{1,0:T(8,128)(2,1)} %bitcast.32), channel_id=1, source_target_pairs={{8,0},{16,8},{24,16},{0,24},{9,1},{17,9},{25,17},{1,25},{10,2},{18... | collective-permute-start | bytes 1474568 | tf_op jit(solution)/shard_map/ppermute | solution.py:240
  20.5 1.9 collective-permute-start.1
  22.4 4.6 %collective-permute-start.2 = (bf16[48,5120]{1,0:T(8,128)(2,1)}, bf16[48,5120]{1,0:T(8,128)(2,1)S(1)}, u32[]{:S(2)}, u32[]{:S(2)}) collective-permute-start(bf16[48,5120]{1,0:T(8,128)(2,1)} %bitcast.36), channel_id=1, source_target_pairs={{8,0},{16,8},{24,16},{0,24},{9,1},{17,9},{25,17},{1,25},{10,2},{18... | collective-permute-start | bytes 1474568 | tf_op jit(solution)/shard_map/ppermute | solution.py:240
  27.0 1.9 collective-permute-start.3
  29.0 2.4 collective-permute-done.refs_11_
  31.4 4.9 %collective-permute-done.1.refs_13_ = bf16[48,5120]{1,0:T(8,128)(2,1)S(1)} collective-permute-done((bf16[48,5120]{1,0:T(8,128)(2,1)}, bf16[48,5120]{1,0:T(8,128)(2,1)S(1)}, u32[]{:S(2)}, u32[]{:S(2)}) %collective-permute-start.1) | collective-permute-done | bytes 491552 | tf_op jit(solution)/shard_map/ppermute | solution.py:240
  36.3 5.6 %collective-permute-done.2.refs_12_ = bf16[48,5120]{1,0:T(8,128)(2,1)S(1)} collective-permute-done((bf16[48,5120]{1,0:T(8,128)(2,1)}, bf16[48,5120]{1,0:T(8,128)(2,1)S(1)}, u32[]{:S(2)}, u32[]{:S(2)}) %collective-permute-start.2) | collective-permute-done | bytes 491552 | tf_op jit(solution)/shard_map/ppermute | solution.py:240
  41.9 4.9 %collective-permute-done.3.refs_14_ = bf16[48,5120]{1,0:T(8,128)(2,1)S(1)} collective-permute-done((bf16[48,5120]{1,0:T(8,128)(2,1)}, bf16[48,5120]{1,0:T(8,128)(2,1)S(1)}, u32[]{:S(2)}, u32[]{:S(2)}) %collective-permute-start.3) | collective-permute-done | bytes 491552 | tf_op jit(solution)/shard_map/ppermute | solution.py:240
  46.8 0.8 broadcast_in_dim.14
  47.6 0.8 pad_maximum_fusion
  48.5 3.5 %all-to-all-start.1 = ((bf16[4,480,128]{2,1,0:T(8,128)(2,1)}), bf16[4,480,128]{2,1,0:T(8,128)(2,1)S(1)}, u32[]{:S(2)}, u32[]{:S(2)}) async-start(bf16[4,480,128]{2,1,0:T(8,128)(2,1)} %pad_maximum_fusion), calls=%async_computation.1 | async-start | bytes 983040 | tf_op jit(solution)/shard_map/all_to_all | solution.py:289
  51.9 4.8 %collective-permute-start.6 = (bf16[48,5120]{1,0:T(8,128)(2,1)S(1)}, bf16[48,5120]{1,0:T(8,128)(2,1)S(1)}, u32[]{:S(2)}, u32[]{:S(2)}) collective-permute-start(bf16[48,5120]{1,0:T(8,128)(2,1)S(1)} %bitcast.35), channel_id=1, source_target_pairs={{16,0},{24,8},{0,16},{8,24},{17,1},{25,9},{1,17},{9,25},{18,2},{26... | collective-permute-start | bytes 1474568 | tf_op jit(solution)/shard_map/ppermute | solution.py:240
  56.8 2.0 collective-permute-start.7
  58.8 0.8 all-to-all-done.1.in_ref
  59.6 0.2 shard_map.123.refs_0_
  59.8 3.2 %collective-permute-start.4 = (bf16[640,384]{1,0:T(8,128)(2,1)S(1)}, bf16[640,384]{1,0:T(8,128)(2,1)S(1)}, u32[]{:S(2)}, u32[]{:S(2)}) collective-permute-start(bf16[640,384]{1,0:T(8,128)(2,1)S(1)} %shard_map.123.refs_0_), channel_id=1, source_target_pairs={{7,0},{0,1},{1,2},{2,3},{3,4},{4,5},{5,6},{6,7},{15,8},{8,9},{9,10... | collective-permute-start | bytes 1474568 | tf_op jit(solution)/shard_map/ppermute | solution.py:240
  63.0 3.8 %collective-permute-start.5 = (bf16[640,384]{1,0:T(8,128)(2,1)S(1)}, bf16[640,384]{1,0:T(8,128)(2,1)S(1)}, u32[]{:S(2)}, u32[]{:S(2)}) collective-permute-start(bf16[640,384]{1,0:T(8,128)(2,1)S(1)} %shard_map.123.refs_0_), channel_id=1, source_target_pairs={{1,0},{2,1},{3,2},{4,3},{5,4},{6,5},{7,6},{0,7},{9,8},{10,9},{11,1... | collective-permute-start | bytes 1474568 | tf_op jit(solution)/shard_map/ppermute | solution.py:240
  66.8 3.7 %collective-permute-start.10 = (bf16[160,1536]{1,0:T(8,128)(2,1)}, bf16[160,1536]{1,0:T(8,128)(2,1)S(1)}, u32[]{:S(2)}, u32[]{:S(2)}) collective-permute-start(bf16[160,1536]{1,0:T(8,128)(2,1)} %bitcast.40), channel_id=1, source_target_pairs={{8,0},{16,8},{24,16},{0,24},{9,1},{17,9},{25,17},{1,25},{10,2},{18... | collective-permute-start | bytes 1474568 | tf_op jit(solution)/shard_map/ppermute | solution.py:240
  70.6 2.0 collective-permute-start.11
  72.6 8.4 %collective-permute-done.7.refs_16_ = bf16[48,5120]{1,0:T(8,128)(2,1)} collective-permute-done((bf16[48,5120]{1,0:T(8,128)(2,1)S(1)}, bf16[48,5120]{1,0:T(8,128)(2,1)}, u32[]{:S(2)}, u32[]{:S(2)}) %collective-permute-start.7) | collective-permute-done | bytes 491552 | tf_op jit(solution)/shard_map/ppermute | solution.py:240
  81.1 3.2 %collective-permute-start.8 = (bf16[640,384]{1,0:T(8,128)(2,1)S(1)}, bf16[640,384]{1,0:T(8,128)(2,1)S(1)}, u32[]{:S(2)}, u32[]{:S(2)}) collective-permute-start(bf16[640,384]{1,0:T(8,128)(2,1)S(1)} %collective-permute-done.4.refs_1_), channel_id=1, source_target_pairs={{7,0},{0,1},{1,2},{2,3},{3,4},{4,5},{5,6},{6,7},{15,8},{8,9},{9,10... | collective-permute-start | bytes 1474568 | tf_op jit(solution)/shard_map/ppermute | solution.py:240
  84.3 3.8 %collective-permute-start.9 = (bf16[640,384]{1,0:T(8,128)(2,1)S(1)}, bf16[640,384]{1,0:T(8,128)(2,1)S(1)}, u32[]{:S(2)}, u32[]{:S(2)}) collective-permute-start(bf16[640,384]{1,0:T(8,128)(2,1)S(1)} %collective-permute-done.5.refs_2_), channel_id=1, source_target_pairs={{1,0},{2,1},{3,2},{4,3},{5,4},{6,5},{7,6},{0,7},{9,8},{10,9},{11,1... | collective-permute-start | bytes 1474568 | tf_op jit(solution)/shard_map/ppermute | solution.py:240
  88.1 2.6 collective-permute-done.10.refs_1_
  90.7 1.7 collective-permute-done.8.refs_3_
  92.4 1.8 collective-permute-done.9.refs_4_
  94.1 3.2 %collective-permute-start.12 = (bf16[640,384]{1,0:T(8,128)(2,1)S(1)}, bf16[640,384]{1,0:T(8,128)(2,1)S(1)}, u32[]{:S(2)}, u32[]{:S(2)}) collective-permute-start(bf16[640,384]{1,0:T(8,128)(2,1)S(1)} %collective-permute-done.8.refs_3_), channel_id=1, source_target_pairs={{7,0},{0,1},{1,2},{2,3},{3,4},{4,5},{5,6},{6,7},{15,8},{8,9},{9,10... | collective-permute-start | bytes 1474568 | tf_op jit(solution)/shard_map/ppermute | solution.py:240
  97.3 3.4 %collective-permute-start.13 = (bf16[640,384]{1,0:T(8,128)(2,1)S(1)}, bf16[640,384]{1,0:T(8,128)(2,1)S(1)}, u32[]{:S(2)}, u32[]{:S(2)}) collective-permute-start(bf16[640,384]{1,0:T(8,128)(2,1)S(1)} %collective-permute-done.9.refs_4_), channel_id=1, source_target_pairs={{1,0},{2,1},{3,2},{4,3},{5,4},{6,5},{7,6},{0,7},{9,8},{10,9},{11,1... | collective-permute-start | bytes 1474568 | tf_op jit(solution)/shard_map/ppermute | solution.py:240
  100.8 7.1 %collective-permute-done.12.refs_5_ = bf16[640,384]{1,0:T(8,128)(2,1)S(1)} collective-permute-done((bf16[640,384]{1,0:T(8,128)(2,1)S(1)}, bf16[640,384]{1,0:T(8,128)(2,1)S(1)}, u32[]{:S(2)}, u32[]{:S(2)}) %collective-permute-start.12) | collective-permute-done | bytes 491552 | tf_op jit(solution)/shard_map/ppermute | solution.py:240
  107.9 0.8 slice.30
  108.7 1.9 collective-permute-start.14
  110.6 0.8 slice.31
  111.4 4.6 %collective-permute-start.15 = (bf16[320,384]{1,0:T(8,128)(2,1)}, bf16[320,384]{1,0:T(8,128)(2,1)}, u32[]{:S(2)}, u32[]{:S(2)}) collective-permute-start(bf16[320,384]{1,0:T(8,128)(2,1)} %slice.31), channel_id=1, source_target_pairs={{1,0},{2,1},{3,2},{4,3},{5,4},{6,5},{7,6},{0,7},{9,8},{10,9},{11,1... | collective-permute-start | bytes 737288 | tf_op jit(solution)/shard_map/ppermute | solution.py:240
  116.0 4.0 %collective-permute-done.14.refs_7_ = bf16[320,384]{1,0:T(8,128)(2,1)} collective-permute-done((bf16[320,384]{1,0:T(8,128)(2,1)}, bf16[320,384]{1,0:T(8,128)(2,1)}, u32[]{:S(2)}, u32[]{:S(2)}) %collective-permute-start.14) | collective-permute-done | bytes 245792 | tf_op jit(solution)/shard_map/ppermute | solution.py:240
  119.9 2.0 collective-permute-done.15.refs_8_
  122.0 6.0 %shard_map.124 = bf16[224,256]{1,0:T(8,128)(2,1)} custom-call(s32[1]{0:T(128)} %bitcast.4.y_ref, bf16[640,384]{1,0:T(8,128)(2,1)} %copy-done, bf16[640,384]{1,0:T(8,128)(2,1)} %copy-done.17, bf16[640,384]{1,0:T(8,128)(2,1)} %copy-done.18, bf16[640,384]{1,0:T(8,128)(2,1)} %copy-done.19, bf16[640,384]{1,0:T(8,128)(2,1)} %copy-done.20, ...), custom_call_target="tpu_custom_call" | custom-call | bytes 8962052 | tf_op jit(solution)/shard_map/pallas_call | solution.py:23
  128.1 0.0 copy-start.21
  128.1 2.0 broadcast_in_dim.15
  130.0 7.5 %all-to-all-start.2 = ((bf16[8,224,256]{2,1,0:T(8,128)(2,1)}), bf16[8,224,256]{2,1,0:T(8,128)(2,1)S(1)}, u32[]{:S(2)}, u32[]{:S(2)}) async-start(bf16[8,224,256]{2,1,0:T(8,128)(2,1)} %broadcast_in_dim.15), calls=%async_computation.2 | async-start | bytes 1835008 | tf_op jit(solution)/shard_map/all_to_all | solution.py:233
  137.5 2.7 collective-permute-start.16
  140.2 8.4 %collective-permute-done.16.refs_3_ = bf16[160,1536]{1,0:T(8,128)(2,1)S(1)} collective-permute-done((bf16[160,1536]{1,0:T(8,128)(2,1)S(1)}, bf16[160,1536]{1,0:T(8,128)(2,1)S(1)}, u32[]{:S(2)}, u32[]{:S(2)}) %collective-permute-start.16) | collective-permute-done | bytes 491552 | tf_op jit(solution)/shard_map/ppermute | solution.py:240
  148.6 5.3 %all-to-all-done.2.hidden_ref = bf16[8,224,256]{2,1,0:T(8,128)(2,1)S(1)} async-done(((bf16[8,224,256]{2,1,0:T(8,128)(2,1)}), bf16[8,224,256]{2,1,0:T(8,128)(2,1)S(1)}, u32[]{:S(2)}, u32[]{:S(2)}) %all-to-all-start.2) | async-done | bytes 917536 | tf_op jit(solution)/shard_map/all_to_all | solution.py:233
  153.9 0.9 copy-done.7
  154.9 5.0 %shard_map.125 = bf16[4,704,128]{2,1,0:T(8,128)(2,1)} custom-call(s32[1]{0:T(128)} %bitcast.3.x_ref, bf16[8,224,256]{2,1,0:T(8,128)(2,1)} %copy-done.7, bf16[160,1536]{1,0:T(8,128)(2,1)} %bitcast.42, bf16[160,1536]{1,0:T(8,128)(2,1)} %copy-done.22, bf16[160,1536]{1,0:T(8,128)(2,1)} %copy-done.23, bf16[160,1536]{1,0:T(8,128)(2,1)} %copy-done.24), custom_call_target="tpu_custom_call" | custom-call | bytes 3604484 | tf_op jit(solution)/shard_map/pallas_call | solution.py:23
  159.9 0.0 copy-start.2
  159.9 0.0 copy-start.4
  159.9 15.3 %all_to_all.45.hidden_ref = bf16[4,704,128]{2,1,0:T(8,128)(2,1)S(1)} all-to-all(bf16[4,704,128]{2,1,0:T(8,128)(2,1)} %shard_map.125), channel_id=1, replica_groups=mesh['z'=8,'core'=2,'x'=4,'y'=8] {'x'}, dimensions={0} | all-to-all | bytes 1441792 | tf_op jit(solution)/shard_map/all_to_all | solution.py:320
  175.3 38.4 %all_to_all.46.back_ref = bf16[16,80,128]{2,1,0:T(8,128)(2,1)S(1)} all-to-all(bf16[16,80,128]{2,1,0:T(8,128)(2,1)S(1)} %bitcast.30), channel_id=1, replica_groups=mesh['z'=8,'core'=2,'x'=4,'y'=8] {'z','core'}, dimensions={0} | all-to-all | bytes 655360 | tf_op jit(solution)/shard_map/all_to_all | solution.py:322
  213.7 1.3 shard_map.126
  215.0 10.3 %all_to_all.47 = bf16[16,4,160]{2,1,0:T(4,128)(2,1)S(1)} all-to-all(bf16[16,4,160]{2,1,0:T(4,128)(2,1)S(1)} %broadcast_in_dim.16), channel_id=1, replica_groups=mesh['z'=8,'core'=2,'x'=4,'y'=8] {'z','core'}, dimensions={0} | all-to-all | bytes 40960 | tf_op jit(solution)/shard_map/all_to_all | solution.py:233
  225.3 0.3 shard_map.127
  225.6 0.9 broadcast_in_dim.17
  226.5 6.2 %all-to-all-start.6 = ((bf16[32,80,128]{2,1,0:T(8,128)(2,1)}), bf16[32,80,128]{2,1,0:T(8,128)(2,1)S(1)}, u32[]{:S(2)}, u32[]{:S(2)}) async-start(bf16[32,80,128]{2,1,0:T(8,128)(2,1)} %broadcast_in_dim.17), calls=%async_computation.6 | async-start | bytes 1310720 | tf_op jit(solution)/shard_map/all_to_all | solution.py:233
  232.7 0.1 add_bitcast_fusion.targets_ref
  232.8 16.8 %all-to-all-done.6.rows_ref = bf16[32,80,128]{2,1,0:T(8,128)(2,1)S(1)} async-done(((bf16[32,80,128]{2,1,0:T(8,128)(2,1)}), bf16[32,80,128]{2,1,0:T(8,128)(2,1)S(1)}, u32[]{:S(2)}, u32[]{:S(2)}) %all-to-all-start.6) | async-done | bytes 655392 | tf_op jit(solution)/shard_map/all_to_all | solution.py:233
  249.6 0.7 shard_map.128
  250.3 16.5 %all_to_all.48 = f32[32,1,128]{2,1,0:T(1,128)S(1)} all-to-all(f32[32,1,128]{2,1,0:T(1,128)S(1)} %broadcast_in_dim.19), channel_id=1, replica_groups=mesh['z'=8,'core'=2,'x'=4,'y'=8] {'x','y'}, dimensions={0} | all-to-all | bytes 32768 | tf_op jit(solution)/shard_map/all_to_all | solution.py:233
  266.8 11.8 %all_to_all.49 = f32[16,1,128]{2,1,0:T(1,128)S(1)} all-to-all(f32[16,1,128]{2,1,0:T(1,128)S(1)} %broadcast_in_dim.20), channel_id=1, replica_groups=mesh['z'=8,'core'=2,'x'=4,'y'=8] {'z','core'}, dimensions={0} | all-to-all | bytes 16384 | tf_op jit(solution)/shard_map/all_to_all | solution.py:233
  278.7 0.6 subtract_bitcast_fusion
  (59 shorter events, 0.2 us)
Async XLA Ops:
  0.6 0.8 copy-start.3
  1.4 0.7 copy-start.5
  2.1 0.7 copy-start.6
  4.1 47.8 %copy-start.10 = (bf16[1,48,5120]{2,1,0:T(8,128)(2,1)S(1)}, bf16[1,48,5120]{2,1,0:T(8,128)(2,1)}, u32[]{:S(2)}) copy-start(bf16[1,48,5120]{2,1,0:T(8,128)(2,1)} %param.14) | copy-start | bytes 1474564
  4.1 52.6 %copy-start.11 = (bf16[1,48,5120]{2,1,0:T(8,128)(2,1)S(1)}, bf16[1,48,5120]{2,1,0:T(8,128)(2,1)}, u32[]{:S(2)}) copy-start(bf16[1,48,5120]{2,1,0:T(8,128)(2,1)} %param.15) | copy-start | bytes 1474564
  4.1 42.7 %all-to-all-start = ((bf16[16,80,128]{2,1,0:T(8,128)(2,1)}), bf16[16,80,128]{2,1,0:T(8,128)(2,1)S(1)}, u32[]{:S(2)}, u32[]{:S(2)}) async-start(bf16[16,80,128]{2,1,0:T(8,128)(2,1)} %get-tuple-element.22), calls=%async_computation | async-start | bytes 655360 | tf_op jit(solution)/shard_map/all_to_all | solution.py:284
  16.1 15.3 %collective-permute-start = (bf16[48,5120]{1,0:T(8,128)(2,1)}, bf16[48,5120]{1,0:T(8,128)(2,1)S(1)}, u32[]{:S(2)}, u32[]{:S(2)}) collective-permute-start(bf16[48,5120]{1,0:T(8,128)(2,1)} %bitcast.32), channel_id=1, source_target_pairs={{8,0},{16,8},{24,16},{0,24},{9,1},{17,9},{25,17},{1,25},{10,2},{18... | collective-permute-start | bytes 1474568 | tf_op jit(solution)/shard_map/ppermute | solution.py:240
  20.5 15.8 %collective-permute-start.1 = (bf16[48,5120]{1,0:T(8,128)(2,1)}, bf16[48,5120]{1,0:T(8,128)(2,1)S(1)}, u32[]{:S(2)}, u32[]{:S(2)}) collective-permute-start(bf16[48,5120]{1,0:T(8,128)(2,1)} %bitcast.33), channel_id=1, source_target_pairs={{24,0},{0,8},{8,16},{16,24},{25,1},{1,9},{9,17},{17,25},{26,2},{2,... | collective-permute-start | bytes 1474568 | tf_op jit(solution)/shard_map/ppermute | solution.py:240
  22.4 19.5 %collective-permute-start.2 = (bf16[48,5120]{1,0:T(8,128)(2,1)}, bf16[48,5120]{1,0:T(8,128)(2,1)S(1)}, u32[]{:S(2)}, u32[]{:S(2)}) collective-permute-start(bf16[48,5120]{1,0:T(8,128)(2,1)} %bitcast.36), channel_id=1, source_target_pairs={{8,0},{16,8},{24,16},{0,24},{9,1},{17,9},{25,17},{1,25},{10,2},{18... | collective-permute-start | bytes 1474568 | tf_op jit(solution)/shard_map/ppermute | solution.py:240
  27.0 19.8 %collective-permute-start.3 = (bf16[48,5120]{1,0:T(8,128)(2,1)}, bf16[48,5120]{1,0:T(8,128)(2,1)S(1)}, u32[]{:S(2)}, u32[]{:S(2)}) collective-permute-start(bf16[48,5120]{1,0:T(8,128)(2,1)} %bitcast.37), channel_id=1, source_target_pairs={{24,0},{0,8},{8,16},{16,24},{25,1},{1,9},{9,17},{17,25},{26,2},{2,... | collective-permute-start | bytes 1474568 | tf_op jit(solution)/shard_map/ppermute | solution.py:240
  31.4 28.4 %copy-start.12 = (bf16[48,5120]{1,0:T(8,128)(2,1)}, bf16[48,5120]{1,0:T(8,128)(2,1)S(1)}, u32[]{:S(2)}) copy-start(bf16[48,5120]{1,0:T(8,128)(2,1)S(1)} %collective-permute-done.refs_11_) | copy-start | bytes 1474564
  36.3 23.5 %copy-start.13 = (bf16[48,5120]{1,0:T(8,128)(2,1)}, bf16[48,5120]{1,0:T(8,128)(2,1)S(1)}, u32[]{:S(2)}) copy-start(bf16[48,5120]{1,0:T(8,128)(2,1)S(1)} %collective-permute-done.1.refs_13_) | copy-start | bytes 1474564
  41.9 6.6 %copy-start.14 = (bf16[48,5120]{1,0:T(8,128)(2,1)}, bf16[48,5120]{1,0:T(8,128)(2,1)S(1)}, u32[]{:S(2)}) copy-start(bf16[48,5120]{1,0:T(8,128)(2,1)S(1)} %collective-permute-done.2.refs_12_) | copy-start | bytes 1474564
  46.8 1.7 copy-start.15
  48.5 11.1 %all-to-all-start.1 = ((bf16[4,480,128]{2,1,0:T(8,128)(2,1)}), bf16[4,480,128]{2,1,0:T(8,128)(2,1)S(1)}, u32[]{:S(2)}, u32[]{:S(2)}) async-start(bf16[4,480,128]{2,1,0:T(8,128)(2,1)} %pad_maximum_fusion), calls=%async_computation.1 | async-start | bytes 983040 | tf_op jit(solution)/shard_map/all_to_all | solution.py:289
  51.9 18.6 %collective-permute-start.6 = (bf16[48,5120]{1,0:T(8,128)(2,1)S(1)}, bf16[48,5120]{1,0:T(8,128)(2,1)S(1)}, u32[]{:S(2)}, u32[]{:S(2)}) collective-permute-start(bf16[48,5120]{1,0:T(8,128)(2,1)S(1)} %bitcast.35), channel_id=1, source_target_pairs={{16,0},{24,8},{0,16},{8,24},{17,1},{25,9},{1,17},{9,25},{18,2},{26... | collective-permute-start | bytes 1474568 | tf_op jit(solution)/shard_map/ppermute | solution.py:240
  56.8 24.3 %collective-permute-start.7 = (bf16[48,5120]{1,0:T(8,128)(2,1)S(1)}, bf16[48,5120]{1,0:T(8,128)(2,1)}, u32[]{:S(2)}, u32[]{:S(2)}) collective-permute-start(bf16[48,5120]{1,0:T(8,128)(2,1)S(1)} %bitcast.39), channel_id=1, source_target_pairs={{16,0},{24,8},{0,16},{8,24},{17,1},{25,9},{1,17},{9,25},{18,2},{26... | collective-permute-start | bytes 1474568 | tf_op jit(solution)/shard_map/ppermute | solution.py:240
  59.8 62.2 %copy-start = (bf16[640,384]{1,0:T(8,128)(2,1)}, bf16[640,384]{1,0:T(8,128)(2,1)S(1)}, u32[]{:S(2)}) copy-start(bf16[640,384]{1,0:T(8,128)(2,1)S(1)} %shard_map.123.refs_0_) | copy-start | bytes 1474564
  59.8 21.3 %collective-permute-start.4 = (bf16[640,384]{1,0:T(8,128)(2,1)S(1)}, bf16[640,384]{1,0:T(8,128)(2,1)S(1)}, u32[]{:S(2)}, u32[]{:S(2)}) collective-permute-start(bf16[640,384]{1,0:T(8,128)(2,1)S(1)} %shard_map.123.refs_0_), channel_id=1, source_target_pairs={{7,0},{0,1},{1,2},{2,3},{3,4},{4,5},{5,6},{6,7},{15,8},{8,9},{9,10... | collective-permute-start | bytes 1474568 | tf_op jit(solution)/shard_map/ppermute | solution.py:240
  63.0 18.1 %collective-permute-start.5 = (bf16[640,384]{1,0:T(8,128)(2,1)S(1)}, bf16[640,384]{1,0:T(8,128)(2,1)S(1)}, u32[]{:S(2)}, u32[]{:S(2)}) collective-permute-start(bf16[640,384]{1,0:T(8,128)(2,1)S(1)} %shard_map.123.refs_0_), channel_id=1, source_target_pairs={{1,0},{2,1},{3,2},{4,3},{5,4},{6,5},{7,6},{0,7},{9,8},{10,9},{11,1... | collective-permute-start | bytes 1474568 | tf_op jit(solution)/shard_map/ppermute | solution.py:240
  66.8 23.9 %collective-permute-start.10 = (bf16[160,1536]{1,0:T(8,128)(2,1)}, bf16[160,1536]{1,0:T(8,128)(2,1)S(1)}, u32[]{:S(2)}, u32[]{:S(2)}) collective-permute-start(bf16[160,1536]{1,0:T(8,128)(2,1)} %bitcast.40), channel_id=1, source_target_pairs={{8,0},{16,8},{24,16},{0,24},{9,1},{17,9},{25,17},{1,25},{10,2},{18... | collective-permute-start | bytes 1474568 | tf_op jit(solution)/shard_map/ppermute | solution.py:240
  70.6 23.6 %copy-start.16 = (bf16[48,5120]{1,0:T(8,128)(2,1)}, bf16[48,5120]{1,0:T(8,128)(2,1)S(1)}, u32[]{:S(2)}) copy-start(bf16[48,5120]{1,0:T(8,128)(2,1)S(1)} %collective-permute-done.6.refs_15_) | copy-start | bytes 1474564
  70.6 20.1 %collective-permute-start.11 = (bf16[160,1536]{1,0:T(8,128)(2,1)}, bf16[160,1536]{1,0:T(8,128)(2,1)S(1)}, u32[]{:S(2)}, u32[]{:S(2)}) collective-permute-start(bf16[160,1536]{1,0:T(8,128)(2,1)} %bitcast.41), channel_id=1, source_target_pairs={{24,0},{0,8},{8,16},{16,24},{25,1},{1,9},{9,17},{17,25},{26,2},{2,... | collective-permute-start | bytes 1474568 | tf_op jit(solution)/shard_map/ppermute | solution.py:240
  81.0 11.3 %copy-start.17 = (bf16[640,384]{1,0:T(8,128)(2,1)}, bf16[640,384]{1,0:T(8,128)(2,1)S(1)}, u32[]{:S(2)}) copy-start(bf16[640,384]{1,0:T(8,128)(2,1)S(1)} %collective-permute-done.4.refs_1_) | copy-start | bytes 1474564
  81.0 40.9 %copy-start.18 = (bf16[640,384]{1,0:T(8,128)(2,1)}, bf16[640,384]{1,0:T(8,128)(2,1)S(1)}, u32[]{:S(2)}) copy-start(bf16[640,384]{1,0:T(8,128)(2,1)S(1)} %collective-permute-done.5.refs_2_) | copy-start | bytes 1474564
  81.1 11.3 %collective-permute-start.8 = (bf16[640,384]{1,0:T(8,128)(2,1)S(1)}, bf16[640,384]{1,0:T(8,128)(2,1)S(1)}, u32[]{:S(2)}, u32[]{:S(2)}) collective-permute-start(bf16[640,384]{1,0:T(8,128)(2,1)S(1)} %collective-permute-done.4.refs_1_), channel_id=1, source_target_pairs={{7,0},{0,1},{1,2},{2,3},{3,4},{4,5},{5,6},{6,7},{15,8},{8,9},{9,10... | collective-permute-start | bytes 1474568 | tf_op jit(solution)/shard_map/ppermute | solution.py:240
  84.3 9.9 %collective-permute-start.9 = (bf16[640,384]{1,0:T(8,128)(2,1)S(1)}, bf16[640,384]{1,0:T(8,128)(2,1)S(1)}, u32[]{:S(2)}, u32[]{:S(2)}) collective-permute-start(bf16[640,384]{1,0:T(8,128)(2,1)S(1)} %collective-permute-done.5.refs_2_), channel_id=1, source_target_pairs={{1,0},{2,1},{3,2},{4,3},{5,4},{6,5},{7,6},{0,7},{9,8},{10,9},{11,1... | collective-permute-start | bytes 1474568 | tf_op jit(solution)/shard_map/ppermute | solution.py:240
  90.7 37.3 %copy-start.22 = (bf16[160,1536]{1,0:T(8,128)(2,1)}, bf16[160,1536]{1,0:T(8,128)(2,1)S(1)}, u32[]{:S(2)}) copy-start(bf16[160,1536]{1,0:T(8,128)(2,1)S(1)} %collective-permute-done.10.refs_1_) | copy-start | bytes 1474564
  90.7 1.7 copy-start.23
  92.4 29.6 %copy-start.19 = (bf16[640,384]{1,0:T(8,128)(2,1)}, bf16[640,384]{1,0:T(8,128)(2,1)S(1)}, u32[]{:S(2)}) copy-start(bf16[640,384]{1,0:T(8,128)(2,1)S(1)} %collective-permute-done.8.refs_3_) | copy-start | bytes 1474564
  94.1 27.8 %copy-start.20 = (bf16[640,384]{1,0:T(8,128)(2,1)}, bf16[640,384]{1,0:T(8,128)(2,1)S(1)}, u32[]{:S(2)}) copy-start(bf16[640,384]{1,0:T(8,128)(2,1)S(1)} %collective-permute-done.9.refs_4_) | copy-start | bytes 1474564
  94.1 13.8 %collective-permute-start.12 = (bf16[640,384]{1,0:T(8,128)(2,1)S(1)}, bf16[640,384]{1,0:T(8,128)(2,1)S(1)}, u32[]{:S(2)}, u32[]{:S(2)}) collective-permute-start(bf16[640,384]{1,0:T(8,128)(2,1)S(1)} %collective-permute-done.8.refs_3_), channel_id=1, source_target_pairs={{7,0},{0,1},{1,2},{2,3},{3,4},{4,5},{5,6},{6,7},{15,8},{8,9},{9,10... | collective-permute-start | bytes 1474568 | tf_op jit(solution)/shard_map/ppermute | solution.py:240
  97.3 13.2 %collective-permute-start.13 = (bf16[640,384]{1,0:T(8,128)(2,1)S(1)}, bf16[640,384]{1,0:T(8,128)(2,1)S(1)}, u32[]{:S(2)}, u32[]{:S(2)}) collective-permute-start(bf16[640,384]{1,0:T(8,128)(2,1)S(1)} %collective-permute-done.9.refs_4_), channel_id=1, source_target_pairs={{1,0},{2,1},{3,2},{4,3},{5,4},{6,5},{7,6},{0,7},{9,8},{10,9},{11,1... | collective-permute-start | bytes 1474568 | tf_op jit(solution)/shard_map/ppermute | solution.py:240
  107.9 14.1 %copy-start.8 = (bf16[640,384]{1,0:T(8,128)(2,1)}, bf16[640,384]{1,0:T(8,128)(2,1)S(1)}, u32[]{:S(2)}) copy-start(bf16[640,384]{1,0:T(8,128)(2,1)S(1)} %collective-permute-done.12.refs_5_) | copy-start | bytes 1474564
  108.7 11.3 %collective-permute-start.14 = (bf16[320,384]{1,0:T(8,128)(2,1)}, bf16[320,384]{1,0:T(8,128)(2,1)}, u32[]{:S(2)}, u32[]{:S(2)}) collective-permute-start(bf16[320,384]{1,0:T(8,128)(2,1)} %slice.30), channel_id=1, source_target_pairs={{7,0},{0,1},{1,2},{2,3},{3,4},{4,5},{5,6},{6,7},{15,8},{8,9},{9,10... | collective-permute-start | bytes 737288 | tf_op jit(solution)/shard_map/ppermute | solution.py:240
  110.6 11.4 %copy-start.9 = (bf16[640,384]{1,0:T(8,128)(2,1)}, bf16[640,384]{1,0:T(8,128)(2,1)S(1)}, u32[]{:S(2)}) copy-start(bf16[640,384]{1,0:T(8,128)(2,1)S(1)} %collective-permute-done.13.refs_6_) | copy-start | bytes 1474564
  111.4 10.6 %collective-permute-start.15 = (bf16[320,384]{1,0:T(8,128)(2,1)}, bf16[320,384]{1,0:T(8,128)(2,1)}, u32[]{:S(2)}, u32[]{:S(2)}) collective-permute-start(bf16[320,384]{1,0:T(8,128)(2,1)} %slice.31), channel_id=1, source_target_pairs={{1,0},{2,1},{3,2},{4,3},{5,4},{6,5},{7,6},{0,7},{9,8},{10,9},{11,1... | collective-permute-start | bytes 737288 | tf_op jit(solution)/shard_map/ppermute | solution.py:240
  128.1 9.5 %copy-start.21 = (bf16[1,1536,160]{1,2,0:T(8,128)(2,1)S(1)}, bf16[1,1536,160]{1,2,0:T(8,128)(2,1)}, u32[]{:S(2)}) copy-start(bf16[1,1536,160]{1,2,0:T(8,128)(2,1)} %param.16) | copy-start | bytes 1474564
  130.0 23.9 %all-to-all-start.2 = ((bf16[8,224,256]{2,1,0:T(8,128)(2,1)}), bf16[8,224,256]{2,1,0:T(8,128)(2,1)S(1)}, u32[]{:S(2)}, u32[]{:S(2)}) async-start(bf16[8,224,256]{2,1,0:T(8,128)(2,1)} %broadcast_in_dim.15), calls=%async_computation.2 | async-start | bytes 1835008 | tf_op jit(solution)/shard_map/all_to_all | solution.py:233
  137.5 11.1 %collective-permute-start.16 = (bf16[160,1536]{1,0:T(8,128)(2,1)S(1)}, bf16[160,1536]{1,0:T(8,128)(2,1)S(1)}, u32[]{:S(2)}, u32[]{:S(2)}) collective-permute-start(bf16[160,1536]{1,0:T(8,128)(2,1)S(1)} %bitcast.43), channel_id=1, source_target_pairs={{16,0},{24,8},{0,16},{8,24},{17,1},{25,9},{1,17},{9,25},{18,2},{26... | collective-permute-start | bytes 1474568 | tf_op jit(solution)/shard_map/ppermute | solution.py:240
  148.6 5.3 %copy-start.24 = (bf16[160,1536]{1,0:T(8,128)(2,1)}, bf16[160,1536]{1,0:T(8,128)(2,1)S(1)}, u32[]{:S(2)}) copy-start(bf16[160,1536]{1,0:T(8,128)(2,1)S(1)} %collective-permute-done.16.refs_3_) | copy-start | bytes 1474564
  153.9 1.0 copy-start.7
  159.9 53.8 %copy-start.2 = (bf16[1536,160]{0,1:T(8,128)(2,1)S(1)}, bf16[1536,160]{0,1:T(8,128)(2,1)}, u32[]{:S(2)}) copy-start(bf16[1536,160]{0,1:T(8,128)(2,1)} %param.19) | copy-start | bytes 1474564
  159.9 53.8 %copy-start.4 = (bf16[128,160]{0,1:T(8,128)(2,1)S(1)}, bf16[128,160]{0,1:T(8,128)(2,1)}, u32[]{:S(2)}) copy-start(bf16[128,160]{0,1:T(8,128)(2,1)} %param.11) | copy-start | bytes 122884
  215.0 17.7 %copy-start.25 = (s32[64]{0:T(128)S(1)}, s32[64]{0:T(128)}, u32[]{:S(2)}) copy-start(s32[64]{0:T(128)} %param.21) | copy-start | bytes 772
  215.0 34.6 %copy-start.1 = (bf16[128,5120]{1,0:T(8,128)(2,1)S(1)}, bf16[128,5120]{1,0:T(8,128)(2,1)}, u32[]{:S(2)}) copy-start(bf16[128,5120]{1,0:T(8,128)(2,1)} %vocab_ref.1) | copy-start | bytes 3932164
  226.5 23.1 %all-to-all-start.6 = ((bf16[32,80,128]{2,1,0:T(8,128)(2,1)}), bf16[32,80,128]{2,1,0:T(8,128)(2,1)S(1)}, u32[]{:S(2)}, u32[]{:S(2)}) async-start(bf16[32,80,128]{2,1,0:T(8,128)(2,1)} %broadcast_in_dim.17), calls=%async_computation.6 | async-start | bytes 1310720 | tf_op jit(solution)/shard_map/all_to_all | solution.py:233

commit v3 on v2

--- a/solution.py
+++ b/solution.py
@@ -78,7 +78,10 @@
     return jnp.where(named > 0.0, earlier, -1.0).astype(jnp.int32), gate
 
 
-def dispatch_body(routes_ref, gates_ref, tok_ref, out_ref, slot_ref, gate_ref):
+def dispatch_body(routes_far, gates_far, tok_far, out_ref, slot_ref, gate_ref, routes_ref, gates_ref, tok_ref, sems):
+    pairs = [(routes_far, routes_ref), (gates_far, gates_ref), (tok_far, tok_ref)]
+    for copy in fetch(pairs, sems):
+        copy.wait()
     experts, half, lanes = out_ref.shape
     rows = tok_ref.shape[1]
     cap = lanes // 2
@@ -146,11 +149,16 @@
 
 def down_body(x_ref, hidden_ref, *refs):
     *weights, out_ref, flat_ref, down_ref, sems = refs
-    nx = len(weights)
-    copies = fetch([(weights[n], down_ref.at[n]) for n in range(nx)], sems)
+    nx = out_ref.shape[0]
+    width = weights[0].shape[0]
+    copies, at = [], 0
+    for n, weight in enumerate(weights):
+        copies.append((weight, down_ref.at[at : at + weight.shape[0], :]))
+        at += weight.shape[0]
+    copies = fetch(copies, sems)
     ny = hidden_ref.shape[0]
     units = flat_ref.shape[0] // (nx * ny)
-    width, lanes = weights[0].shape[0], out_ref.shape[2]
+    lanes = out_ref.shape[2]
     half, cap, fold = width // 2, lanes // 2, units // 2
     groups = (out_ref.shape[1] - ny * units) // half
     own = [lax.rem(x_ref[0] + shift, nx) for shift in SHIFTS]
@@ -158,10 +166,11 @@
         for y in range(ny):
             at = pl.multiple_of((own[n] * ny + y) * units, units)
             flat_ref[pl.ds(at, units), :] = hidden_ref[y, n * units : (n + 1) * units, :]
-    rows = flat_ref[...]
+    for copy in copies:
+        copy.wait()
+    outs = nn(down_ref[...], flat_ref[...])
     for n in range(nx):
-        copies[n].wait()
-        out = nn(down_ref[n], rows)
+        out = outs[n * width : (n + 1) * width]
         for q in range(groups // 2):
             cols = slice(q * lanes, (q + 1) * lanes)
             a, b = out[:half, cols], out[half:, cols]
@@ -200,27 +209,33 @@
     scored_ref[...] = nt(jnp.where(take, 1.0, 0.0).astype(BF16), out).astype(BF16)
 
 
-def pack_body(rows_ref, out_ref):
-    count, width = rows_ref.shape
-    half = width // 2
+def pack_body(core_ref, rows_ref, out_ref):
+    count, width = rows_ref.shape[0] // 2, rows_ref.shape[1]
+    part = out_ref.shape[0]
     eye = jnp.where(iota((count, count), 0) == iota((count, count), 1), 1.0, 0.0).astype(BF16)
-    flip = lax.dot_general(
-        rows_ref[...], eye, (((0,), (0,)), ((), ())), preferred_element_type=F32
-    )
-    out_ref[...] = jnp.concatenate([flip[:half], flip[half:]], axis=1).astype(BF16)
-
-
-def score_body(offset_ref, rows_ref, vocab_ref, targets_ref, out_ref, flat_ref):
-    blocks, half, lanes = rows_ref.shape
-    count = lanes // 2
+    mine = rows_ref[pl.ds(pl.multiple_of(core_ref[0] * count, count), count), :]
+    flip = lax.dot_general(mine, eye, (((0,), (0,)), ((), ())), preferred_element_type=F32)
+    out_ref[...] = jnp.concatenate([flip[n : n + part] for n in range(0, width, part)], axis=1).astype(BF16)
+
+
+def score_body(at_ref, rows_ref, vocab_ref, other_ref, targets_ref, out_ref, flat_ref):
+    blocks, part, lanes = rows_ref.shape
+    parts = flat_ref.shape[0] // (blocks * part)
+    count = lanes // parts
     for b in range(blocks):
-        both = rows_ref[b].astype(F32)
-        flat_ref[2 * half * b : 2 * half * b + half, :] = rows_ref[b]
-        flat_ref[2 * half * b + half : 2 * half * (b + 1), :] = pltpu.roll(both, count, 1).astype(BF16)
-    logits = nn(vocab_ref[...], flat_ref[...])
-    entry = iota(logits.shape, 0) + offset_ref[0]
-    sums = jnp.sum(jnp.exp(logits), axis=0, keepdims=True)
-    hits = jnp.sum(jnp.where(entry == targets_ref[0:1, :], logits, 0.0), axis=0, keepdims=True)
+        block = rows_ref[b].astype(F32)
+        for n in range(parts):
+            at = (b * parts + n) * part
+            turned = block if n == 0 else pltpu.roll(block, lanes - n * count, 1)
+            flat_ref[at : at + part, :] = turned.astype(BF16)
+    target = targets_ref[pl.ds(at_ref[0], 1), :]
+    sums = jnp.zeros((1, lanes), F32)
+    hits = jnp.zeros((1, lanes), F32)
+    for n, block in enumerate((vocab_ref, other_ref)):
+        logits = nn(block[...], flat_ref[...])
+        entry = iota(logits.shape, 0) + at_ref[1 + n]
+        sums = sums + jnp.sum(jnp.exp(logits), axis=0, keepdims=True)
+        hits = hits + jnp.sum(jnp.where(entry == target, logits, 0.0), axis=0, keepdims=True)
     lane = iota(sums.shape, 1)
     out_ref[...] = jnp.broadcast_to(jnp.where(lane < count, sums, pltpu.roll(hits, count, 1)), out_ref.shape)
 
@@ -240,19 +255,19 @@
     return lax.ppermute(value, axis, [((i + shift) % count, i) for i in range(count)])
 
 
-def around(value, axis, *due):
+def around(value, axis, between):
     count = lax.axis_size(axis)
     left = right = value
-    got, kept = [value], []
+    got = [value]
     for hop in range(3):
-        if hop and hop <= len(due):
-            left, right, *had = lax.optimization_barrier((left, right, *due[hop - 1]))
-            kept += had
+        if hop:
+            left, right = between(hop, left, right)
         left = from_shift(left, axis, count - 1)
         right = from_shift(right, axis, 1)
         got += [left, right]
+    left, right = between(3, left, right)
     part = value.shape[0] // 2
-    return [*got, from_shift(left[:part], axis, count - 1), from_shift(right[part:], axis, 1)], kept
+    return [*got, from_shift(left[:part], axis, count - 1), from_shift(right[part:], axis, 1)]
 
 
 def shards(tokens, routes, gates, w_gate, w_up, w_down, shared_gate, shared_up, shared_down, vocab, targets):
@@ -267,10 +282,8 @@
     x_at = lax.axis_index("x").astype(jnp.int32).reshape(1)
     y_at = lax.axis_index("y").astype(jnp.int32).reshape(1)
 
-    own_gate, own_up, own_down = w_gate[0], w_up[0], w_down[0].T
-    near_gate = [from_shift(own_gate, "x", shift) for shift in SHIFTS[1:]]
-    near_up = [from_shift(own_up, "x", shift) for shift in SHIFTS[1:]]
-    near_down = [from_shift(own_down, "x", shift) for shift in SHIFTS[1:]]
+    own_gate, own_up = w_gate[0], w_up[0]
+    g1, g3, u1, u3 = [from_shift(own, "x", shift) for own in (own_gate, own_up) for shift in SHIFTS[1:3]]
 
     outgoing, slot, gate = call(
         dispatch_body,
@@ -280,15 +293,40 @@
             shape((groups, rows), F32),
         ],
         [routes.T, gates.T, tok],
+        far=range(3),
+        scratch=[
+            pltpu.VMEM(routes.T.shape, jnp.int32),
+            pltpu.VMEM(gates.T.shape, F32),
+            pltpu.VMEM(tok.shape, BF16),
+            pltpu.SemaphoreType.DMA((3,)),
+        ],
+        limit=60,
     )
     arrived = lax.all_to_all(outgoing, LINE, 0, 0, tiled=True)
-    arrived, g1, g3, u1, u3 = lax.optimization_barrier((arrived, *near_gate[:2], *near_up[:2]))
+    arrived, g1, u3 = lax.optimization_barrier((arrived, g1, u3))
     leaving = jnp.concatenate(
         [arrived.reshape(nx, near * half, 2 * cap), jnp.broadcast_to(tok[None], (nx, width, rows))], axis=1
     )
     quarter = lax.all_to_all(leaving, "x", 0, 0, tiled=True)
     (spread,) = call(spread_body, [shape((nx * width, near * cap + rows))], [quarter])
-    blocks, (g2, u2, d1, d3) = around(spread, "y", (near_gate[2], near_up[2]), near_down[:2])
+    held = {}
+
+    def between(hop, left, right):
+        if hop == 1:
+            left, right, held["g3"], held["u1"] = lax.optimization_barrier((left, right, g3, u1))
+        if hop == 2:
+            left, right, held["down"] = lax.optimization_barrier((left, right, w_down[0].T))
+            held["d1"] = from_shift(held["down"], "x", 1)
+            held["d3"] = from_shift(held["down"], "x", nx - 1)
+        if hop == 3:
+            left, right, held["g2"], held["u2"] = lax.optimization_barrier((left, right, held["g2"], held["u2"]))
+        return left, right
+
+    spread, g1, u3 = lax.optimization_barrier((spread, g1, u3))
+    held["g2"] = from_shift(g1, "x", 1)
+    held["u2"] = from_shift(u3, "x", nx - 1)
+    blocks = around(spread, "y", between)
+    g3, u1, g2, u2 = held["g3"], held["u1"], held["g2"], held["u2"]
     (hidden,) = call(
         hidden_body,
         [shape((nx * units + units // 2 + 8, near * cap))],
@@ -303,19 +341,21 @@
         ],
         limit=60,
     )
+    hidden, d1, d3 = lax.optimization_barrier((hidden, held["d1"], held["d3"]))
+    d2 = [from_shift(d1[:half], "x", 1), from_shift(d3[half:], "x", nx - 1)]
     all_hidden = spread_all(hidden, "y", ny)
     (returned,) = call(
         down_body,
         [shape((nx, near * half + ny * units, 2 * cap))],
-        [x_at, all_hidden, own_down, d1, d3, near_down[2]],
+        [x_at, all_hidden, held["down"], d1, d3, *d2],
         scalars=1,
-        far=range(2, 2 + nx),
+        far=range(2, 3 + nx),
         scratch=[
             pltpu.VMEM((lanes * units, near * cap), BF16),
-            pltpu.VMEM((nx, width, lanes * units), BF16),
-            pltpu.SemaphoreType.DMA((nx,)),
+            pltpu.VMEM((nx * width, lanes * units), BF16),
+            pltpu.SemaphoreType.DMA((nx + 1,)),
         ],
-        limit=60,
+        limit=40,
     )
     mixed = lax.all_to_all(returned, "x", 0, 0, tiled=True)
     back = mixed[:, : near * half].reshape(groups, half, 2 * cap)
@@ -326,29 +366,37 @@
         [slot, gate, back, tok, mixed, shared_down.T],
     )
     line_rows = spread_all(scored[:SCORE_E], LINE, groups).reshape(groups * SCORE_E, width)
-    (packed,) = call(pack_body, [shape((half, 2 * groups * SCORE_E))], [line_rows])
+    count = groups * SCORE_E // nc
+    core = lax.axis_index("core").astype(jnp.int32)
+    (packed,) = call(
+        pack_body,
+        [shape((width * count // (2 * cap), 2 * cap))],
+        [core.reshape(1), line_rows],
+        scalars=1,
+    )
     every = spread_all(packed, PLANE, lanes)
-    offset = (
-        (lax.axis_index("z") * nc + lax.axis_index("core")) * lanes
-        + lax.axis_index("x") * ny
-        + lax.axis_index("y")
-    ) * vocab.shape[0]
-    count = groups * SCORE_E
+    other_vocab = lax.ppermute(vocab, "core", [(0, 1), (1, 0)])
+    place = lax.axis_index("x") * ny + lax.axis_index("y")
+    first = [
+        (((lax.axis_index("z") * nc + c) * lanes + place) * vocab.shape[0]).astype(jnp.int32)
+        for c in (core, 1 - core)
+    ]
     (sums,) = call(
         score_body,
-        [shape((8, 2 * count), F32)],
+        [shape((8, 2 * cap), F32)],
         [
-            offset.astype(jnp.int32).reshape(1),
+            jnp.stack([core, *first]),
             every,
             vocab,
-            jnp.concatenate([targets, targets]).reshape(1, 2 * count),
+            other_vocab,
+            jnp.tile(targets.reshape(nc, count), (1, 2 * cap // count)),
         ],
         scalars=1,
-        scratch=[pltpu.VMEM((lanes * width, 2 * count), BF16)],
+        scratch=[pltpu.VMEM((lanes * width, 2 * cap), BF16)],
     )
     sums = jnp.sum(spread_all(sums[:1], PLANE, lanes), axis=0)
-    sums = jnp.sum(spread_all(sums, LINE, groups), axis=0)[0]
-    return layer_out.T, sums[count:] - jnp.log(sums[:count])
+    sums = jnp.sum(spread_all(sums, LINE, groups).reshape(nz, nc, 2 * cap), axis=0)
+    return layer_out.T, (sums[:, count : 2 * count] - jnp.log(sums[:, :count])).reshape(-1)
 
 
 def solution(mesh):

time: 281 us -> 238 us (0.85)
  blocking collectives: 92.4 us -> 53.1 us
  waiting for transfers between devices: 76.7 us -> 57.3 us
  starting transfers between devices: 84.3 us -> 101 us
    ppermute x17 -> x18, waiting for transfers between devices: 53.8 us -> 31.1 us  [from_shift(): lax.ppermute(value, axis, [((i + shift) % count, i) for i in range(count)])]
    all_to_all x1 -> x0, blocking collectives: 15.3 us -> none  [shards(): mixed = lax.all_to_all(returned, 'x', 0, 0, tiled=True)]
    all_to_all x1, blocking collectives: 38.4 us -> 25.8 us  [shards(): back = lax.all_to_all(back, LINE, 0, 0, tiled=True)]
    all_to_all x3 -> x2, blocking collectives: 38.7 us -> 27.4 us  [spread_all(): lax.all_to_all(jnp.broadcast_to(value[None], (count, *value.shape)), axes...]
    ppermute x0 -> x1, starting transfers between devices: none -> 9.12 us  [shards(): other_vocab = lax.ppermute(vocab, 'core', [(0, 1), (1, 0)])]
    ppermute x17 -> x18, starting transfers between devices: 55.2 us -> 60.1 us  [from_shift(): lax.ppermute(value, axis, [((i + shift) % count, i) for i in range(count)])]
    all_to_all x0 -> x1, starting transfers between devices: none -> 3.63 us  [shards(): mixed = lax.all_to_all(returned, 'x', 0, 0, tiled=True)]
    all_to_all x2 -> x3, waiting for transfers between devices: 22.1 us -> 25.1 us  [spread_all(): lax.all_to_all(jnp.broadcast_to(value[None], (count, *value.shape)), axes...]
  transfers between devices with their start and end apart: 21 -> 25, of which waited for: 15 -> 14; matrix products, arithmetic and copies ran while one was open for 1% -> 1% of each run, Pallas kernels for 0% -> 3%
where the time goes in v3:
time: 238 us; the launch traced here: 237 us
  starting transfers between devices  101 us (42%)
  waiting for transfers between devices  57.3 us (24%)
  blocking collectives  53.1 us (22%)
  Pallas kernels  14.8 us (6%)
  local copies, waits for them, and re-layouts  7.95 us (3%)
    ppermute x18, starting transfers between devices, from_shift(): lax.ppermute(value, axis, [((i + shift) % count, i) for i in range(count)])  60.1 us
    ppermute x18, waiting for transfers between devices, from_shift(): lax.ppermute(value, axis, [((i + shift) % count, i) for i in range(count)])  31.1 us
    all_to_all x2, blocking collectives, spread_all(): lax.all_to_all(jnp.broadcast_to(value[None], (count, *value.shape)), axes...  27.4 us
    all_to_all x1, blocking collectives, shards(): back = lax.all_to_all(back, LINE, 0, 0, tiled=True)  25.8 us
    all_to_all x3, waiting for transfers between devices, spread_all(): lax.all_to_all(jnp.broadcast_to(value[None], (count, *value.shape)), axes...  25.1 us
    pallas_call x7, Pallas kernels, call(): pl.pallas_call(body, out_shape=outs, in_specs=specs, out_specs=[pl.BlockS...  14.8 us
    all_to_all x3, starting transfers between devices, spread_all(): lax.all_to_all(jnp.broadcast_to(value[None], (count, *value.shape)), axes...  13 us
    all_to_all x1, starting transfers between devices, shards(): arrived = lax.all_to_all(outgoing, LINE, 0, 0, tiled=True)  12 us
  transfers between devices with their start and end apart: 25, of which 14 were waited for; matrix products, arithmetic and copies ran while one was open for 1% of the time, Pallas kernels for 3%

profile of v3, /device:TPU:1, one launch (start us, length us, event | category | flops | bytes accessed | tf_op | source)
XLA Modules:
  0.0 236.7 jit_solution(16772162924531666947)
XLA Ops:
  0.6 2.2 shard_map.122
  2.8 0.0 copy-start.9
  2.9 12.0 %all-to-all-start = ((bf16[16,80,128]{2,1,0:T(8,128)(2,1)}), bf16[16,80,128]{2,1,0:T(8,128)(2,1)S(1)}, u32[]{:S(2)}, u32[]{:S(2)}) async-start(bf16[16,80,128]{2,1,0:T(8,128)(2,1)} %get-tuple-element.29), calls=%async_computation | async-start | bytes 655360 | tf_op jit(solution)/shard_map/all_to_all | solution.py:305
  14.8 4.4 %collective-permute-start = (bf16[48,5120]{1,0:T(8,128)(2,1)}, bf16[48,5120]{1,0:T(8,128)(2,1)}, u32[]{:S(2)}, u32[]{:S(2)}) collective-permute-start(bf16[48,5120]{1,0:T(8,128)(2,1)} %bitcast.30), channel_id=1, source_target_pairs={{8,0},{16,8},{24,16},{0,24},{9,1},{17,9},{25,17},{1,25},{10,2},{18... | collective-permute-start | bytes 1474568 | tf_op jit(solution)/shard_map/ppermute | solution.py:255
  19.3 1.9 collective-permute-start.1
  21.2 8.9 %collective-permute-done.refs_11_ = bf16[48,5120]{1,0:T(8,128)(2,1)} collective-permute-done((bf16[48,5120]{1,0:T(8,128)(2,1)}, bf16[48,5120]{1,0:T(8,128)(2,1)}, u32[]{:S(2)}, u32[]{:S(2)}) %collective-permute-start) | collective-permute-done | bytes 491552 | tf_op jit(solution)/shard_map/ppermute | solution.py:255
  30.1 5.0 %collective-permute-done.1.refs_14_ = bf16[48,5120]{1,0:T(8,128)(2,1)} collective-permute-done((bf16[48,5120]{1,0:T(8,128)(2,1)}, bf16[48,5120]{1,0:T(8,128)(2,1)}, u32[]{:S(2)}, u32[]{:S(2)}) %collective-permute-start.1) | collective-permute-done | bytes 491552 | tf_op jit(solution)/shard_map/ppermute | solution.py:255
  35.1 0.8 broadcast_in_dim.14
  35.9 0.8 pad_maximum_fusion
  36.8 3.5 %all-to-all-start.1 = ((bf16[4,480,128]{2,1,0:T(8,128)(2,1)}), bf16[4,480,128]{2,1,0:T(8,128)(2,1)S(1)}, u32[]{:S(2)}, u32[]{:S(2)}) async-start(bf16[4,480,128]{2,1,0:T(8,128)(2,1)} %pad_maximum_fusion), calls=%async_computation.1 | async-start | bytes 983040 | tf_op jit(solution)/shard_map/all_to_all | solution.py:310
  40.2 3.3 %collective-permute-start.4 = (bf16[48,5120]{1,0:T(8,128)(2,1)S(1)}, bf16[48,5120]{1,0:T(8,128)(2,1)S(1)}, u32[]{:S(2)}, u32[]{:S(2)}) collective-permute-start(bf16[48,5120]{1,0:T(8,128)(2,1)S(1)} %bitcast.32), channel_id=1, source_target_pairs={{24,0},{0,8},{8,16},{16,24},{25,1},{1,9},{9,17},{17,25},{26,2},{2,... | collective-permute-start | bytes 1474568 | tf_op jit(solution)/shard_map/ppermute | solution.py:255
  43.6 3.2 %collective-permute-start.5 = (bf16[48,5120]{1,0:T(8,128)(2,1)S(1)}, bf16[48,5120]{1,0:T(8,128)(2,1)}, u32[]{:S(2)}, u32[]{:S(2)}) collective-permute-start(bf16[48,5120]{1,0:T(8,128)(2,1)S(1)} %bitcast.35), channel_id=1, source_target_pairs={{8,0},{16,8},{24,16},{0,24},{9,1},{17,9},{25,17},{1,25},{10,2},{18... | collective-permute-start | bytes 1474568 | tf_op jit(solution)/shard_map/ppermute | solution.py:255
  46.8 1.1 all-to-all-done.1.in_ref
  47.9 0.2 shard_map.123.refs_0_
  48.1 3.2 %collective-permute-start.2 = (bf16[640,384]{1,0:T(8,128)(2,1)S(1)}, bf16[640,384]{1,0:T(8,128)(2,1)S(1)}, u32[]{:S(2)}, u32[]{:S(2)}) collective-permute-start(bf16[640,384]{1,0:T(8,128)(2,1)S(1)} %shard_map.123.refs_0_), channel_id=1, source_target_pairs={{7,0},{0,1},{1,2},{2,3},{3,4},{4,5},{5,6},{6,7},{15,8},{8,9},{9,10... | collective-permute-start | bytes 1474568 | tf_op jit(solution)/shard_map/ppermute | solution.py:255
  51.3 3.8 %collective-permute-start.3 = (bf16[640,384]{1,0:T(8,128)(2,1)S(1)}, bf16[640,384]{1,0:T(8,128)(2,1)S(1)}, u32[]{:S(2)}, u32[]{:S(2)}) collective-permute-start(bf16[640,384]{1,0:T(8,128)(2,1)S(1)} %shard_map.123.refs_0_), channel_id=1, source_target_pairs={{1,0},{2,1},{3,2},{4,3},{5,4},{6,5},{7,6},{0,7},{9,8},{10,9},{11,1... | collective-permute-start | bytes 1474568 | tf_op jit(solution)/shard_map/ppermute | solution.py:255
  55.1 4.0 %collective-permute-done.4.refs_13_ = bf16[48,5120]{1,0:T(8,128)(2,1)S(1)} collective-permute-done((bf16[48,5120]{1,0:T(8,128)(2,1)S(1)}, bf16[48,5120]{1,0:T(8,128)(2,1)S(1)}, u32[]{:S(2)}, u32[]{:S(2)}) %collective-permute-start.4) | collective-permute-done | bytes 491552 | tf_op jit(solution)/shard_map/ppermute | solution.py:255
  59.1 1.5 collective-permute-done.2.refs_1_
  60.6 0.9 collective-permute-done.3.refs_2_
  61.5 3.2 %collective-permute-start.6 = (bf16[640,384]{1,0:T(8,128)(2,1)S(1)}, bf16[640,384]{1,0:T(8,128)(2,1)S(1)}, u32[]{:S(2)}, u32[]{:S(2)}) collective-permute-start(bf16[640,384]{1,0:T(8,128)(2,1)S(1)} %collective-permute-done.2.refs_1_), channel_id=1, source_target_pairs={{7,0},{0,1},{1,2},{2,3},{3,4},{4,5},{5,6},{6,7},{15,8},{8,9},{9,10... | collective-permute-start | bytes 1474568 | tf_op jit(solution)/shard_map/ppermute | solution.py:255
  64.7 4.0 %collective-permute-start.7 = (bf16[640,384]{1,0:T(8,128)(2,1)S(1)}, bf16[640,384]{1,0:T(8,128)(2,1)S(1)}, u32[]{:S(2)}, u32[]{:S(2)}) collective-permute-start(bf16[640,384]{1,0:T(8,128)(2,1)S(1)} %collective-permute-done.3.refs_2_), channel_id=1, source_target_pairs={{1,0},{2,1},{3,2},{4,3},{5,4},{6,5},{7,6},{0,7},{9,8},{10,9},{11,1... | collective-permute-start | bytes 1474568 | tf_op jit(solution)/shard_map/ppermute | solution.py:255
  68.7 4.4 %collective-permute-start.10 = (bf16[48,5120]{1,0:T(8,128)(2,1)}, bf16[48,5120]{1,0:T(8,128)(2,1)}, u32[]{:S(2)}, u32[]{:S(2)}) collective-permute-start(bf16[48,5120]{1,0:T(8,128)(2,1)} %collective-permute-done.refs_11_), channel_id=1, source_target_pairs={{8,0},{16,8},{24,16},{0,24},{9,1},{17,9},{25,17},{1,25},{10,2},{18... | collective-permute-start | bytes 1474568 | tf_op jit(solution)/shard_map/ppermute | solution.py:255
  73.1 1.9 collective-permute-start.11
  75.0 0.7 collective-permute-done.7.refs_4_
  75.7 4.3 %collective-permute-start.8 = (bf16[640,384]{1,0:T(8,128)(2,1)S(1)}, bf16[640,384]{1,0:T(8,128)(2,1)S(1)}, u32[]{:S(2)}, u32[]{:S(2)}) collective-permute-start(bf16[640,384]{1,0:T(8,128)(2,1)S(1)} %collective-permute-done.6.refs_3_), channel_id=1, source_target_pairs={{7,0},{0,1},{1,2},{2,3},{3,4},{4,5},{5,6},{6,7},{15,8},{8,9},{9,10... | collective-permute-start | bytes 1474568 | tf_op jit(solution)/shard_map/ppermute | solution.py:255
  80.0 2.2 collective-permute-start.9
  82.3 5.7 %collective-permute-start.14 = (bf16[160,1536]{1,0:T(8,128)(2,1)S(1)}, bf16[160,1536]{1,0:T(8,128)(2,1)S(1)}, u32[]{:S(2)}, u32[]{:S(2)}) collective-permute-start(bf16[160,1536]{1,0:T(8,128)(2,1)S(1)} %bitcast.22), channel_id=1, source_target_pairs={{8,0},{16,8},{24,16},{0,24},{9,1},{17,9},{25,17},{1,25},{10,2},{18... | collective-permute-start | bytes 1474568 | tf_op jit(solution)/shard_map/ppermute | solution.py:255
  87.9 1.9 collective-permute-start.15
  89.9 0.7 copy-done.16
  90.7 0.8 slice.27
  91.4 2.8 %collective-permute-start.12 = (bf16[320,384]{1,0:T(8,128)(2,1)}, bf16[320,384]{1,0:T(8,128)(2,1)S(1)}, u32[]{:S(2)}, u32[]{:S(2)}) collective-permute-start(bf16[320,384]{1,0:T(8,128)(2,1)} %slice.27), channel_id=1, source_target_pairs={{7,0},{0,1},{1,2},{2,3},{3,4},{4,5},{5,6},{6,7},{15,8},{8,9},{9,10... | collective-permute-start | bytes 737288 | tf_op jit(solution)/shard_map/ppermute | solution.py:255
  94.2 0.7 slice.28
  95.0 3.7 %collective-permute-start.13 = (bf16[320,384]{1,0:T(8,128)(2,1)}, bf16[320,384]{1,0:T(8,128)(2,1)S(1)}, u32[]{:S(2)}, u32[]{:S(2)}) collective-permute-start(bf16[320,384]{1,0:T(8,128)(2,1)} %slice.28), channel_id=1, source_target_pairs={{1,0},{2,1},{3,2},{4,3},{5,4},{6,5},{7,6},{0,7},{9,8},{10,9},{11,1... | collective-permute-start | bytes 737288 | tf_op jit(solution)/shard_map/ppermute | solution.py:255
  98.6 1.4 collective-permute-done.12.refs_7_
  100.1 2.3 collective-permute-done.13.refs_8_
  102.4 0.7 copy-done.18
  103.1 6.0 %shard_map.124 = bf16[224,256]{1,0:T(8,128)(2,1)} custom-call(s32[1]{0:T(128)} %bitcast.4.y_ref, bf16[640,384]{1,0:T(8,128)(2,1)} %copy-done, bf16[640,384]{1,0:T(8,128)(2,1)} %copy-done.12, bf16[640,384]{1,0:T(8,128)(2,1)} %copy-done.13, bf16[640,384]{1,0:T(8,128)(2,1)} %copy-done.14, bf16[640,384]{1,0:T(8,128)(2,1)} %copy-done.15, ...), custom_call_target="tpu_custom_call" | custom-call | bytes 8962052 | tf_op jit(solution)/shard_map/pallas_call | solution.py:23
  109.1 1.9 broadcast_in_dim.15
  111.0 5.8 %all-to-all-start.2 = ((bf16[8,224,256]{2,1,0:T(8,128)(2,1)}), bf16[8,224,256]{2,1,0:T(8,128)(2,1)S(1)}, u32[]{:S(2)}, u32[]{:S(2)}) async-start(bf16[8,224,256]{2,1,0:T(8,128)(2,1)} %broadcast_in_dim.15), calls=%async_computation.2 | async-start | bytes 1835008 | tf_op jit(solution)/shard_map/all_to_all | solution.py:248
  116.9 4.3 %collective-permute-start.16 = (bf16[80,1536]{1,0:T(8,128)(2,1)S(1)}, bf16[80,1536]{1,0:T(8,128)(2,1)S(1)}, u32[]{:S(2)}, u32[]{:S(2)}) collective-permute-start(bf16[80,1536]{1,0:T(8,128)(2,1)S(1)} %slice.29), channel_id=1, source_target_pairs={{8,0},{16,8},{24,16},{0,24},{9,1},{17,9},{25,17},{1,25},{10,2},{18... | collective-permute-start | bytes 737288 | tf_op jit(solution)/shard_map/ppermute | solution.py:255
  121.2 1.9 collective-permute-start.17
  123.1 1.2 collective-permute-done.16.refs_3_
  124.3 5.2 %collective-permute-done.17.refs_4_ = bf16[80,1536]{1,0:T(8,128)(2,1)S(1)} collective-permute-done((bf16[80,1536]{1,0:T(8,128)(2,1)S(1)}, bf16[80,1536]{1,0:T(8,128)(2,1)S(1)}, u32[]{:S(2)}, u32[]{:S(2)}) %collective-permute-start.17) | collective-permute-done | bytes 245792 | tf_op jit(solution)/shard_map/ppermute | solution.py:255
  129.5 7.5 %all-to-all-done.2.hidden_ref = bf16[8,224,256]{2,1,0:T(8,128)(2,1)S(1)} async-done(((bf16[8,224,256]{2,1,0:T(8,128)(2,1)}), bf16[8,224,256]{2,1,0:T(8,128)(2,1)S(1)}, u32[]{:S(2)}, u32[]{:S(2)}) %all-to-all-start.2) | async-done | bytes 917536 | tf_op jit(solution)/shard_map/all_to_all | solution.py:248
  137.0 3.3 %shard_map.125 = bf16[4,704,128]{2,1,0:T(8,128)(2,1)} custom-call(s32[1]{0:T(128)} %bitcast.3.x_ref, bf16[8,224,256]{2,1,0:T(8,128)(2,1)S(1)} %all-to-all-done.2.hidden_ref, bf16[160,1536]{1,0:T(8,128)(2,1)S(1)} %bitcast.24, bf16[160,1536]{1,0:T(8,128)(2,1)S(1)} %collective-permute-done.14.refs_1_, bf16[160,1536]{1,0:T(8,128)(2,1)S(1)} %collective-permute-done.15.refs_2_, ...), custom_call_target="tpu_custom_call" | custom-call | bytes 3604484 | tf_op jit(solution)/shard_map/pallas_call | solution.py:23
  140.3 3.6 %all-to-all-start.3 = ((bf16[4,704,128]{2,1,0:T(8,128)(2,1)}), bf16[4,704,128]{2,1,0:T(8,128)(2,1)S(1)}, u32[]{:S(2)}, u32[]{:S(2)}) async-start(bf16[4,704,128]{2,1,0:T(8,128)(2,1)} %shard_map.125), calls=%async_computation.3 | async-start | bytes 1441792 | tf_op jit(solution)/shard_map/all_to_all | solution.py:360
  144.0 9.1 %collective-permute-start.18 = (bf16[128,5120]{1,0:T(8,128)(2,1)S(1)}, bf16[128,5120]{1,0:T(8,128)(2,1)S(1)}, u32[]{:S(2)}, u32[]{:S(2)}) collective-permute-start(bf16[128,5120]{1,0:T(8,128)(2,1)S(1)} %copy-done.1), channel_id=1, source_target_pairs={{0,32},{32,0},{1,33},{33,1},{2,34},{34,2},{3,35},{35,3},{4,36},{36... | collective-permute-start | bytes 3932168 | tf_op jit(solution)/shard_map/ppermute | solution.py:378
  153.2 25.8 %all_to_all.45.back_ref = bf16[16,80,128]{2,1,0:T(8,128)(2,1)S(1)} all-to-all(bf16[16,80,128]{2,1,0:T(8,128)(2,1)S(1)} %bitcast.28), channel_id=1, replica_groups=mesh['z'=8,'core'=2,'x'=4,'y'=8] {'z','core'}, dimensions={0} | all-to-all | bytes 655360 | tf_op jit(solution)/shard_map/all_to_all | solution.py:362
  178.9 1.3 shard_map.126
  180.2 0.6 broadcast_in_dim.16
  180.8 3.3 %all-to-all-start.5 = ((bf16[16,4,160]{2,1,0:T(4,128)(2,1)}), bf16[16,4,160]{2,1,0:T(4,128)(2,1)S(1)}, u32[]{:S(2)}, u32[]{:S(2)}) async-start(bf16[16,4,160]{2,1,0:T(4,128)(2,1)} %broadcast_in_dim.16), calls=%async_computation.5 | async-start | bytes 65536 | tf_op jit(solution)/shard_map/all_to_all | solution.py:248
  184.2 7.0 %all-to-all-done.5 = bf16[16,4,160]{2,1,0:T(4,128)(2,1)S(1)} async-done(((bf16[16,4,160]{2,1,0:T(4,128)(2,1)}), bf16[16,4,160]{2,1,0:T(4,128)(2,1)S(1)}, u32[]{:S(2)}, u32[]{:S(2)}) %all-to-all-start.5) | async-done | bytes 20512 | tf_op jit(solution)/shard_map/all_to_all | solution.py:248
  191.2 0.3 shard_map.127
  191.5 0.8 broadcast_in_dim.17
  192.2 3.9 %all-to-all-start.6 = ((bf16[32,40,128]{2,1,0:T(8,128)(2,1)}), bf16[32,40,128]{2,1,0:T(8,128)(2,1)S(1)}, u32[]{:S(2)}, u32[]{:S(2)}) async-start(bf16[32,40,128]{2,1,0:T(8,128)(2,1)} %broadcast_in_dim.17), calls=%async_computation.6 | async-start | bytes 655360 | tf_op jit(solution)/shard_map/all_to_all | solution.py:248
  196.2 0.1 tile.10
  196.2 0.1 tile.12.targets_ref
  196.3 0.1 pad_add_fusion.at_ref
  196.4 10.6 %all-to-all-done.6.rows_ref = bf16[32,40,128]{2,1,0:T(8,128)(2,1)S(1)} async-done(((bf16[32,40,128]{2,1,0:T(8,128)(2,1)}), bf16[32,40,128]{2,1,0:T(8,128)(2,1)S(1)}, u32[]{:S(2)}, u32[]{:S(2)}) %all-to-all-start.6) | async-done | bytes 327712 | tf_op jit(solution)/shard_map/all_to_all | solution.py:248
  207.0 1.6 shard_map.128
  208.6 15.6 %all_to_all.46 = f32[32,1,128]{2,1,0:T(1,128)S(1)} all-to-all(f32[32,1,128]{2,1,0:T(1,128)S(1)} %broadcast_in_dim.19), channel_id=1, replica_groups=mesh['z'=8,'core'=2,'x'=4,'y'=8] {'x','y'}, dimensions={0} | all-to-all | bytes 32768 | tf_op jit(solution)/shard_map/all_to_all | solution.py:248
  224.2 11.8 %all_to_all.47 = f32[16,1,128]{2,1,0:T(1,128)S(1)} all-to-all(f32[16,1,128]{2,1,0:T(1,128)S(1)} %broadcast_in_dim.20), channel_id=1, replica_groups=mesh['z'=8,'core'=2,'x'=4,'y'=8] {'z','core'}, dimensions={0} | all-to-all | bytes 16384 | tf_op jit(solution)/shard_map/all_to_all | solution.py:248
  236.0 0.1 log_subtract_fusion
  236.1 0.6 reshape.48
  (59 shorter events, 0.3 us)
Async XLA Ops:
  2.8 37.4 %copy-start.9 = (bf16[1,48,5120]{2,1,0:T(8,128)(2,1)S(1)}, bf16[1,48,5120]{2,1,0:T(8,128)(2,1)}, u32[]{:S(2)}) copy-start(bf16[1,48,5120]{2,1,0:T(8,128)(2,1)} %param.14) | copy-start | bytes 1474564
  2.8 40.7 %copy-start.10 = (bf16[1,48,5120]{2,1,0:T(8,128)(2,1)S(1)}, bf16[1,48,5120]{2,1,0:T(8,128)(2,1)}, u32[]{:S(2)}) copy-start(bf16[1,48,5120]{2,1,0:T(8,128)(2,1)} %param.15) | copy-start | bytes 1474564
  2.9 32.3 %all-to-all-start = ((bf16[16,80,128]{2,1,0:T(8,128)(2,1)}), bf16[16,80,128]{2,1,0:T(8,128)(2,1)S(1)}, u32[]{:S(2)}, u32[]{:S(2)}) async-start(bf16[16,80,128]{2,1,0:T(8,128)(2,1)} %get-tuple-element.29), calls=%async_computation | async-start | bytes 655360 | tf_op jit(solution)/shard_map/all_to_all | solution.py:305
  14.8 15.3 %collective-permute-start = (bf16[48,5120]{1,0:T(8,128)(2,1)}, bf16[48,5120]{1,0:T(8,128)(2,1)}, u32[]{:S(2)}, u32[]{:S(2)}) collective-permute-start(bf16[48,5120]{1,0:T(8,128)(2,1)} %bitcast.30), channel_id=1, source_target_pairs={{8,0},{16,8},{24,16},{0,24},{9,1},{17,9},{25,17},{1,25},{10,2},{18... | collective-permute-start | bytes 1474568 | tf_op jit(solution)/shard_map/ppermute | solution.py:255
  19.3 15.9 %collective-permute-start.1 = (bf16[48,5120]{1,0:T(8,128)(2,1)}, bf16[48,5120]{1,0:T(8,128)(2,1)}, u32[]{:S(2)}, u32[]{:S(2)}) collective-permute-start(bf16[48,5120]{1,0:T(8,128)(2,1)} %bitcast.33), channel_id=1, source_target_pairs={{24,0},{0,8},{8,16},{16,24},{25,1},{1,9},{9,17},{17,25},{26,2},{2,... | collective-permute-start | bytes 1474568 | tf_op jit(solution)/shard_map/ppermute | solution.py:255
  35.9 46.3 %copy-start.3 = (bf16[1,1536,160]{1,2,0:T(8,128)(2,1)S(1)}, bf16[1,1536,160]{1,2,0:T(8,128)(2,1)}, u32[]{:S(2)}) copy-start(bf16[1,1536,160]{1,2,0:T(8,128)(2,1)} %param.16) | copy-start | bytes 1474564
  36.8 11.1 %all-to-all-start.1 = ((bf16[4,480,128]{2,1,0:T(8,128)(2,1)}), bf16[4,480,128]{2,1,0:T(8,128)(2,1)S(1)}, u32[]{:S(2)}, u32[]{:S(2)}) async-start(bf16[4,480,128]{2,1,0:T(8,128)(2,1)} %pad_maximum_fusion), calls=%async_computation.1 | async-start | bytes 983040 | tf_op jit(solution)/shard_map/all_to_all | solution.py:310
  40.2 18.9 %collective-permute-start.4 = (bf16[48,5120]{1,0:T(8,128)(2,1)S(1)}, bf16[48,5120]{1,0:T(8,128)(2,1)S(1)}, u32[]{:S(2)}, u32[]{:S(2)}) collective-permute-start(bf16[48,5120]{1,0:T(8,128)(2,1)S(1)} %bitcast.32), channel_id=1, source_target_pairs={{24,0},{0,8},{8,16},{16,24},{25,1},{1,9},{9,17},{17,25},{26,2},{2,... | collective-permute-start | bytes 1474568 | tf_op jit(solution)/shard_map/ppermute | solution.py:255
  43.6 15.5 %collective-permute-start.5 = (bf16[48,5120]{1,0:T(8,128)(2,1)S(1)}, bf16[48,5120]{1,0:T(8,128)(2,1)}, u32[]{:S(2)}, u32[]{:S(2)}) collective-permute-start(bf16[48,5120]{1,0:T(8,128)(2,1)S(1)} %bitcast.35), channel_id=1, source_target_pairs={{8,0},{16,8},{24,16},{0,24},{9,1},{17,9},{25,17},{1,25},{10,2},{18... | collective-permute-start | bytes 1474568 | tf_op jit(solution)/shard_map/ppermute | solution.py:255
  48.1 54.3 %copy-start = (bf16[640,384]{1,0:T(8,128)(2,1)}, bf16[640,384]{1,0:T(8,128)(2,1)S(1)}, u32[]{:S(2)}) copy-start(bf16[640,384]{1,0:T(8,128)(2,1)S(1)} %shard_map.123.refs_0_) | copy-start | bytes 1474564
  48.1 12.5 %collective-permute-start.2 = (bf16[640,384]{1,0:T(8,128)(2,1)S(1)}, bf16[640,384]{1,0:T(8,128)(2,1)S(1)}, u32[]{:S(2)}, u32[]{:S(2)}) collective-permute-start(bf16[640,384]{1,0:T(8,128)(2,1)S(1)} %shard_map.123.refs_0_), channel_id=1, source_target_pairs={{7,0},{0,1},{1,2},{2,3},{3,4},{4,5},{5,6},{6,7},{15,8},{8,9},{9,10... | collective-permute-start | bytes 1474568 | tf_op jit(solution)/shard_map/ppermute | solution.py:255
  51.3 10.2 %collective-permute-start.3 = (bf16[640,384]{1,0:T(8,128)(2,1)S(1)}, bf16[640,384]{1,0:T(8,128)(2,1)S(1)}, u32[]{:S(2)}, u32[]{:S(2)}) collective-permute-start(bf16[640,384]{1,0:T(8,128)(2,1)S(1)} %shard_map.123.refs_0_), channel_id=1, source_target_pairs={{1,0},{2,1},{3,2},{4,3},{5,4},{6,5},{7,6},{0,7},{9,8},{10,9},{11,1... | collective-permute-start | bytes 1474568 | tf_op jit(solution)/shard_map/ppermute | solution.py:255
  59.1 16.6 %copy-start.11 = (bf16[48,5120]{1,0:T(8,128)(2,1)}, bf16[48,5120]{1,0:T(8,128)(2,1)S(1)}, u32[]{:S(2)}) copy-start(bf16[48,5120]{1,0:T(8,128)(2,1)S(1)} %collective-permute-done.4.refs_13_) | copy-start | bytes 1474564
  60.6 19.5 %copy-start.12 = (bf16[640,384]{1,0:T(8,128)(2,1)}, bf16[640,384]{1,0:T(8,128)(2,1)S(1)}, u32[]{:S(2)}) copy-start(bf16[640,384]{1,0:T(8,128)(2,1)S(1)} %collective-permute-done.2.refs_1_) | copy-start | bytes 1474564
  61.5 28.4 %copy-start.13 = (bf16[640,384]{1,0:T(8,128)(2,1)}, bf16[640,384]{1,0:T(8,128)(2,1)S(1)}, u32[]{:S(2)}) copy-start(bf16[640,384]{1,0:T(8,128)(2,1)S(1)} %collective-permute-done.3.refs_2_) | copy-start | bytes 1474564
  61.5 13.5 %collective-permute-start.6 = (bf16[640,384]{1,0:T(8,128)(2,1)S(1)}, bf16[640,384]{1,0:T(8,128)(2,1)S(1)}, u32[]{:S(2)}, u32[]{:S(2)}) collective-permute-start(bf16[640,384]{1,0:T(8,128)(2,1)S(1)} %collective-permute-done.2.refs_1_), channel_id=1, source_target_pairs={{7,0},{0,1},{1,2},{2,3},{3,4},{4,5},{5,6},{6,7},{15,8},{8,9},{9,10... | collective-permute-start | bytes 1474568 | tf_op jit(solution)/shard_map/ppermute | solution.py:255
  64.7 11.0 %collective-permute-start.7 = (bf16[640,384]{1,0:T(8,128)(2,1)S(1)}, bf16[640,384]{1,0:T(8,128)(2,1)S(1)}, u32[]{:S(2)}, u32[]{:S(2)}) collective-permute-start(bf16[640,384]{1,0:T(8,128)(2,1)S(1)} %collective-permute-done.3.refs_2_), channel_id=1, source_target_pairs={{1,0},{2,1},{3,2},{4,3},{5,4},{6,5},{7,6},{0,7},{9,8},{10,9},{11,1... | collective-permute-start | bytes 1474568 | tf_op jit(solution)/shard_map/ppermute | solution.py:255
  68.7 19.2 %collective-permute-start.10 = (bf16[48,5120]{1,0:T(8,128)(2,1)}, bf16[48,5120]{1,0:T(8,128)(2,1)}, u32[]{:S(2)}, u32[]{:S(2)}) collective-permute-start(bf16[48,5120]{1,0:T(8,128)(2,1)} %collective-permute-done.refs_11_), channel_id=1, source_target_pairs={{8,0},{16,8},{24,16},{0,24},{9,1},{17,9},{25,17},{1,25},{10,2},{18... | collective-permute-start | bytes 1474568 | tf_op jit(solution)/shard_map/ppermute | solution.py:255
  73.1 16.8 %collective-permute-start.11 = (bf16[48,5120]{1,0:T(8,128)(2,1)}, bf16[48,5120]{1,0:T(8,128)(2,1)S(1)}, u32[]{:S(2)}, u32[]{:S(2)}) collective-permute-start(bf16[48,5120]{1,0:T(8,128)(2,1)} %collective-permute-done.1.refs_14_), channel_id=1, source_target_pairs={{24,0},{0,8},{8,16},{16,24},{25,1},{1,9},{9,17},{17,25},{26,2},{2,... | collective-permute-start | bytes 1474568 | tf_op jit(solution)/shard_map/ppermute | solution.py:255
  75.0 14.9 %copy-start.14 = (bf16[640,384]{1,0:T(8,128)(2,1)}, bf16[640,384]{1,0:T(8,128)(2,1)S(1)}, u32[]{:S(2)}) copy-start(bf16[640,384]{1,0:T(8,128)(2,1)S(1)} %collective-permute-done.6.refs_3_) | copy-start | bytes 1474564
  75.7 14.2 %copy-start.15 = (bf16[640,384]{1,0:T(8,128)(2,1)}, bf16[640,384]{1,0:T(8,128)(2,1)S(1)}, u32[]{:S(2)}) copy-start(bf16[640,384]{1,0:T(8,128)(2,1)S(1)} %collective-permute-done.7.refs_4_) | copy-start | bytes 1474564
  75.7 14.1 %collective-permute-start.8 = (bf16[640,384]{1,0:T(8,128)(2,1)S(1)}, bf16[640,384]{1,0:T(8,128)(2,1)S(1)}, u32[]{:S(2)}, u32[]{:S(2)}) collective-permute-start(bf16[640,384]{1,0:T(8,128)(2,1)S(1)} %collective-permute-done.6.refs_3_), channel_id=1, source_target_pairs={{7,0},{0,1},{1,2},{2,3},{3,4},{4,5},{5,6},{6,7},{15,8},{8,9},{9,10... | collective-permute-start | bytes 1474568 | tf_op jit(solution)/shard_map/ppermute | solution.py:255
  80.0 10.6 %collective-permute-start.9 = (bf16[640,384]{1,0:T(8,128)(2,1)S(1)}, bf16[640,384]{1,0:T(8,128)(2,1)S(1)}, u32[]{:S(2)}, u32[]{:S(2)}) collective-permute-start(bf16[640,384]{1,0:T(8,128)(2,1)S(1)} %collective-permute-done.7.refs_4_), channel_id=1, source_target_pairs={{1,0},{2,1},{3,2},{4,3},{5,4},{6,5},{7,6},{0,7},{9,8},{10,9},{11,1... | collective-permute-start | bytes 1474568 | tf_op jit(solution)/shard_map/ppermute | solution.py:255
  82.3 26.9 %collective-permute-start.14 = (bf16[160,1536]{1,0:T(8,128)(2,1)S(1)}, bf16[160,1536]{1,0:T(8,128)(2,1)S(1)}, u32[]{:S(2)}, u32[]{:S(2)}) collective-permute-start(bf16[160,1536]{1,0:T(8,128)(2,1)S(1)} %bitcast.22), channel_id=1, source_target_pairs={{8,0},{16,8},{24,16},{0,24},{9,1},{17,9},{25,17},{1,25},{10,2},{18... | collective-permute-start | bytes 1474568 | tf_op jit(solution)/shard_map/ppermute | solution.py:255
  87.9 21.2 %collective-permute-start.15 = (bf16[160,1536]{1,0:T(8,128)(2,1)S(1)}, bf16[160,1536]{1,0:T(8,128)(2,1)S(1)}, u32[]{:S(2)}, u32[]{:S(2)}) collective-permute-start(bf16[160,1536]{1,0:T(8,128)(2,1)S(1)} %bitcast.23), channel_id=1, source_target_pairs={{24,0},{0,8},{8,16},{16,24},{25,1},{1,9},{9,17},{17,25},{26,2},{2,... | collective-permute-start | bytes 1474568 | tf_op jit(solution)/shard_map/ppermute | solution.py:255
  89.9 0.8 copy-start.16
  90.6 11.8 %copy-start.7 = (bf16[640,384]{1,0:T(8,128)(2,1)}, bf16[640,384]{1,0:T(8,128)(2,1)S(1)}, u32[]{:S(2)}) copy-start(bf16[640,384]{1,0:T(8,128)(2,1)S(1)} %collective-permute-done.8.refs_5_) | copy-start | bytes 1474564
  90.7 11.7 %copy-start.8 = (bf16[640,384]{1,0:T(8,128)(2,1)}, bf16[640,384]{1,0:T(8,128)(2,1)S(1)}, u32[]{:S(2)}) copy-start(bf16[640,384]{1,0:T(8,128)(2,1)S(1)} %collective-permute-done.9.refs_6_) | copy-start | bytes 1474564
  91.4 8.6 %collective-permute-start.12 = (bf16[320,384]{1,0:T(8,128)(2,1)}, bf16[320,384]{1,0:T(8,128)(2,1)S(1)}, u32[]{:S(2)}, u32[]{:S(2)}) collective-permute-start(bf16[320,384]{1,0:T(8,128)(2,1)} %slice.27), channel_id=1, source_target_pairs={{7,0},{0,1},{1,2},{2,3},{3,4},{4,5},{5,6},{6,7},{15,8},{8,9},{9,10... | collective-permute-start | bytes 737288 | tf_op jit(solution)/shard_map/ppermute | solution.py:255
  95.0 7.4 %collective-permute-start.13 = (bf16[320,384]{1,0:T(8,128)(2,1)}, bf16[320,384]{1,0:T(8,128)(2,1)S(1)}, u32[]{:S(2)}, u32[]{:S(2)}) collective-permute-start(bf16[320,384]{1,0:T(8,128)(2,1)} %slice.28), channel_id=1, source_target_pairs={{1,0},{2,1},{3,2},{4,3},{5,4},{6,5},{7,6},{0,7},{9,8},{10,9},{11,1... | collective-permute-start | bytes 737288 | tf_op jit(solution)/shard_map/ppermute | solution.py:255
  100.1 2.3 copy-start.17
  102.4 0.7 copy-start.18
  111.0 25.9 %all-to-all-start.2 = ((bf16[8,224,256]{2,1,0:T(8,128)(2,1)}), bf16[8,224,256]{2,1,0:T(8,128)(2,1)S(1)}, u32[]{:S(2)}, u32[]{:S(2)}) async-start(bf16[8,224,256]{2,1,0:T(8,128)(2,1)} %broadcast_in_dim.15), calls=%async_computation.2 | async-start | bytes 1835008 | tf_op jit(solution)/shard_map/all_to_all | solution.py:248
  116.9 7.4 %collective-permute-start.16 = (bf16[80,1536]{1,0:T(8,128)(2,1)S(1)}, bf16[80,1536]{1,0:T(8,128)(2,1)S(1)}, u32[]{:S(2)}, u32[]{:S(2)}) collective-permute-start(bf16[80,1536]{1,0:T(8,128)(2,1)S(1)} %slice.29), channel_id=1, source_target_pairs={{8,0},{16,8},{24,16},{0,24},{9,1},{17,9},{25,17},{1,25},{10,2},{18... | collective-permute-start | bytes 737288 | tf_op jit(solution)/shard_map/ppermute | solution.py:255
  121.2 8.3 %collective-permute-start.17 = (bf16[80,1536]{1,0:T(8,128)(2,1)S(1)}, bf16[80,1536]{1,0:T(8,128)(2,1)S(1)}, u32[]{:S(2)}, u32[]{:S(2)}) collective-permute-start(bf16[80,1536]{1,0:T(8,128)(2,1)S(1)} %slice.30), channel_id=1, source_target_pairs={{24,0},{0,8},{8,16},{16,24},{25,1},{1,9},{9,17},{17,25},{26,2},{2,... | collective-permute-start | bytes 737288 | tf_op jit(solution)/shard_map/ppermute | solution.py:255
  140.3 3.7 %copy-start.1 = (bf16[128,5120]{1,0:T(8,128)(2,1)S(1)}, bf16[128,5120]{1,0:T(8,128)(2,1)}, u32[]{:S(2)}) copy-start(bf16[128,5120]{1,0:T(8,128)(2,1)} %vocab_ref.1) | copy-start | bytes 3932164
  140.3 38.6 %copy-start.4 = (bf16[128,160]{0,1:T(8,128)(2,1)S(1)}, bf16[128,160]{0,1:T(8,128)(2,1)}, u32[]{:S(2)}) copy-start(bf16[128,160]{0,1:T(8,128)(2,1)} %param.11) | copy-start | bytes 122884
  140.3 38.6 %copy-start.5 = (s32[16,128]{1,0:T(8,128)S(1)}, s32[16,128]{1,0:T(8,128)}, u32[]{:S(2)}) copy-start(s32[16,128]{1,0:T(8,128)} %get-tuple-element.27.slot_ref) | copy-start | bytes 24580
  140.3 38.6 %copy-start.6 = (f32[16,128]{1,0:T(8,128)S(1)}, f32[16,128]{1,0:T(8,128)}, u32[]{:S(2)}) copy-start(f32[16,128]{1,0:T(8,128)} %get-tuple-element.28.gate_ref) | copy-start | bytes 24580
  140.3 12.8 %all-to-all-start.3 = ((bf16[4,704,128]{2,1,0:T(8,128)(2,1)}), bf16[4,704,128]{2,1,0:T(8,128)(2,1)S(1)}, u32[]{:S(2)}, u32[]{:S(2)}) async-start(bf16[4,704,128]{2,1,0:T(8,128)(2,1)} %shard_map.125), calls=%async_computation.3 | async-start | bytes 1441792 | tf_op jit(solution)/shard_map/all_to_all | solution.py:360
  144.0 52.4 %collective-permute-start.18 = (bf16[128,5120]{1,0:T(8,128)(2,1)S(1)}, bf16[128,5120]{1,0:T(8,128)(2,1)S(1)}, u32[]{:S(2)}, u32[]{:S(2)}) collective-permute-start(bf16[128,5120]{1,0:T(8,128)(2,1)S(1)} %copy-done.1), channel_id=1, source_target_pairs={{0,32},{32,0},{1,33},{33,1},{2,34},{34,2},{3,35},{35,3},{4,36},{36... | collective-permute-start | bytes 3932168 | tf_op jit(solution)/shard_map/ppermute | solution.py:378
  153.1 25.8 %copy-start.2 = (bf16[1536,160]{0,1:T(8,128)(2,1)S(1)}, bf16[1536,160]{0,1:T(8,128)(2,1)}, u32[]{:S(2)}) copy-start(bf16[1536,160]{0,1:T(8,128)(2,1)} %param.19) | copy-start | bytes 1474564
  178.9 17.2 %copy-start.19 = (s32[64]{0:T(128)S(1)}, s32[64]{0:T(128)}, u32[]{:S(2)}) copy-start(s32[64]{0:T(128)} %param.21) | copy-start | bytes 772
  180.8 10.3 %all-to-all-start.5 = ((bf16[16,4,160]{2,1,0:T(4,128)(2,1)}), bf16[16,4,160]{2,1,0:T(4,128)(2,1)S(1)}, u32[]{:S(2)}, u32[]{:S(2)}) async-start(bf16[16,4,160]{2,1,0:T(4,128)(2,1)} %broadcast_in_dim.16), calls=%async_computation.5 | async-start | bytes 65536 | tf_op jit(solution)/shard_map/all_to_all | solution.py:248
  192.2 14.7 %all-to-all-start.6 = ((bf16[32,40,128]{2,1,0:T(8,128)(2,1)}), bf16[32,40,128]{2,1,0:T(8,128)(2,1)S(1)}, u32[]{:S(2)}, u32[]{:S(2)}) async-start(bf16[32,40,128]{2,1,0:T(8,128)(2,1)} %broadcast_in_dim.17), calls=%async_computation.6 | async-start | bytes 655360 | tf_op jit(solution)/shard_map/all_to_all | solution.py:248

commit v4 on v3

--- a/solution.py
+++ b/solution.py
@@ -98,11 +98,12 @@
         out_ref[e] = nt(tok, sel.astype(BF16)).astype(BF16)
 
 
-def spread_body(in_ref, out_ref):
+def spread_body(x_ref, in_ref, *refs):
+    *tokens, out_ref = refs
     lanes_x, _, lanes = in_ref.shape
     width = out_ref.shape[0] // lanes_x
     half, cap = width // 2, lanes // 2
-    groups = (in_ref.shape[1] - width) // half
+    groups = in_ref.shape[1] // half
     for x in range(lanes_x):
         top, mid, end = x * width, x * width + half, (x + 1) * width
         for q in range(groups // 2):
@@ -111,7 +112,9 @@
             cols = slice(q * lanes, (q + 1) * lanes)
             out_ref[top:mid, cols] = pair_low(a, b, cap).astype(BF16)
             out_ref[mid:end, cols] = pair_high(a, b, cap).astype(BF16)
-        out_ref[top:end, groups * cap :] = in_ref[x, groups * half :, :]
+    for tok, shift in zip(tokens, SHIFTS):
+        at = pl.multiple_of(lax.rem(x_ref[0] + shift, lanes_x) * width, width)
+        out_ref[pl.ds(at, width), groups * cap :] = tok[...]
 
 
 def glu(gate, up):
@@ -120,31 +123,34 @@
 
 def hidden_body(y_ref, *refs):
     blocks = refs[: len(RING)]
-    out_ref, flat_ref, gates_ref, ups_ref, sems = refs[-5:]
-    weights = refs[len(RING) : -5]
+    out_ref, flat_ref, weight_ref, sems = refs[-4:]
+    weights = refs[len(RING) : -4]
     nx = len(weights) // 2 - 1
     units = weights[0].shape[0]
     width = blocks[0].shape[0] // nx
     ny = flat_ref.shape[0] // (nx * width)
+    top = nx * units
     pairs = []
-    for n in range(nx + 1):
-        for at, into in enumerate((gates_ref, ups_ref)):
-            pairs.append((weights[2 * n + at], into.at[n * units : (n + 1) * units, :]))
-    for block, (shift, first) in zip(blocks, RING):
+    for n, weight in enumerate(weights):
+        at = n // 2 * units + (n % 2) * top if n < 2 * nx else n * units
+        pairs.append((weight, weight_ref.at[at : at + units, :]))
+    for block, shift in zip(blocks, RING):
         y = lax.rem(y_ref[0] + shift, ny)
-        for n in range(block.shape[0] // width):
-            at = pl.multiple_of(((first + n) * ny + y) * width, width)
+        for n in range(nx):
+            at = pl.multiple_of((n * ny + y) * width, width)
             pairs.append((block.at[n * width : (n + 1) * width, :], flat_ref.at[pl.ds(at, width), :]))
     for copy in fetch(pairs, sems):
         copy.wait()
-    cols = out_ref.shape[1]
-    top = nx * units
-    rows = flat_ref[:, :cols]
-    out_ref[:top, :] = glu(nn(gates_ref[:top, :], rows), nn(ups_ref[:top, :], rows))
-    toks = flat_ref[:, cols:]
-    own = glu(nn(gates_ref[top:, :], toks), nn(ups_ref[top:, :], toks))
+    cols = out_ref.shape[2]
+    both = nn(weight_ref[: 2 * top, :], flat_ref[:, :cols])
+    routed = glu(both[:top], both[top:])
+    both = nn(weight_ref[2 * top :, :], flat_ref[:, cols:])
+    own = glu(both[:units], both[units:])
     fold = units // 2
-    out_ref[top : top + fold, :] = jnp.concatenate([own[:fold], own[fold:]], axis=1)
+    folded = jnp.concatenate([own[:fold], own[fold:]], axis=1)
+    for y in range(ny):
+        out_ref[y, :top, :] = routed
+        out_ref[y, top : top + fold, :] = folded
 
 
 def down_body(x_ref, hidden_ref, *refs):
@@ -205,17 +211,21 @@
     routed = jnp.concatenate([routed[:, :rows], routed[:, rows:]], axis=0)
     out = (tok_ref[...].astype(F32) + shared + routed).astype(BF16)
     out_ref[...] = out
-    take = iota((scored_ref.shape[0], rows), 1) == rows - SCORE_E + iota((scored_ref.shape[0], rows), 0)
-    scored_ref[...] = nt(jnp.where(take, 1.0, 0.0).astype(BF16), out).astype(BF16)
+    take = iota((2 * SCORE_E, rows), 1) == rows - SCORE_E + iota((2 * SCORE_E, rows), 0)
+    scored = nt(jnp.where(take, 1.0, 0.0).astype(BF16), out).astype(BF16)
+    for g in range(scored_ref.shape[0]):
+        scored_ref[g] = scored[:SCORE_E]
 
 
 def pack_body(core_ref, rows_ref, out_ref):
     count, width = rows_ref.shape[0] // 2, rows_ref.shape[1]
-    part = out_ref.shape[0]
+    part = out_ref.shape[1]
     eye = jnp.where(iota((count, count), 0) == iota((count, count), 1), 1.0, 0.0).astype(BF16)
     mine = rows_ref[pl.ds(pl.multiple_of(core_ref[0] * count, count), count), :]
     flip = lax.dot_general(mine, eye, (((0,), (0,)), ((), ())), preferred_element_type=F32)
-    out_ref[...] = jnp.concatenate([flip[n : n + part] for n in range(0, width, part)], axis=1).astype(BF16)
+    packed = jnp.concatenate([flip[n : n + part] for n in range(0, width, part)], axis=1).astype(BF16)
+    for n in range(out_ref.shape[0]):
+        out_ref[n] = packed
 
 
 def score_body(at_ref, rows_ref, vocab_ref, other_ref, targets_ref, out_ref, flat_ref):
@@ -241,7 +251,11 @@
 
 
 SHIFTS = (0, 1, 3, 2)
-RING = ((0, 0), (7, 0), (1, 0), (6, 0), (2, 0), (5, 0), (3, 0), (4, 0), (4, 2))
+RING = (0, 7, 1, 6, 2, 5, 3, 4)
+
+
+def exchange(value, axes):
+    return lax.all_to_all(value, axes, 0, 0, tiled=True)
 
 
 def spread_all(value, axes, count):
@@ -266,8 +280,7 @@
         right = from_shift(right, axis, 1)
         got += [left, right]
     left, right = between(3, left, right)
-    part = value.shape[0] // 2
-    return [*got, from_shift(left[:part], axis, count - 1), from_shift(right[part:], axis, 1)]
+    return [*got, from_shift(left, axis, count - 1)]
 
 
 def shards(tokens, routes, gates, w_gate, w_up, w_down, shared_gate, shared_up, shared_down, vocab, targets):
@@ -281,9 +294,6 @@
     tok = tokens.T
     x_at = lax.axis_index("x").astype(jnp.int32).reshape(1)
     y_at = lax.axis_index("y").astype(jnp.int32).reshape(1)
-
-    own_gate, own_up = w_gate[0], w_up[0]
-    g1, g3, u1, u3 = [from_shift(own, "x", shift) for own in (own_gate, own_up) for shift in SHIFTS[1:3]]
 
     outgoing, slot, gate = call(
         dispatch_body,
@@ -302,52 +312,62 @@
         ],
         limit=60,
     )
-    arrived = lax.all_to_all(outgoing, LINE, 0, 0, tiled=True)
-    arrived, g1, u3 = lax.optimization_barrier((arrived, g1, u3))
-    leaving = jnp.concatenate(
-        [arrived.reshape(nx, near * half, 2 * cap), jnp.broadcast_to(tok[None], (nx, width, rows))], axis=1
-    )
-    quarter = lax.all_to_all(leaving, "x", 0, 0, tiled=True)
-    (spread,) = call(spread_body, [shape((nx * width, near * cap + rows))], [quarter])
-    held = {}
+    arrived = exchange(outgoing, LINE)
+    arrived, t1, t3, t2 = lax.optimization_barrier((arrived, *[from_shift(tok, "x", shift) for shift in SHIFTS[1:]]))
+    quarter = exchange(arrived.reshape(nx, near * half, 2 * cap), "x")
+    (spread,) = call(
+        spread_body,
+        [shape((nx * width, near * cap + rows))],
+        [x_at, quarter, tok, t1, t3, t2],
+        scalars=1,
+    )
+    spread, own_gate, own_up = lax.optimization_barrier((spread, w_gate[0], w_up[0]))
+    after = {"own_gate": own_gate, "own_up": own_up}
+    after["g1"] = from_shift(own_gate, "x", 1)
+    after["u3"] = from_shift(own_up, "x", nx - 1)
 
     def between(hop, left, right):
         if hop == 1:
-            left, right, held["g3"], held["u1"] = lax.optimization_barrier((left, right, g3, u1))
+            left, right, after["g1"], after["u3"] = lax.optimization_barrier((left, right, after["g1"], after["u3"]))
+            after["g2"] = from_shift(after["g1"], "x", 1)
+            after["u2"] = from_shift(after["u3"], "x", nx - 1)
         if hop == 2:
-            left, right, held["down"] = lax.optimization_barrier((left, right, w_down[0].T))
-            held["d1"] = from_shift(held["down"], "x", 1)
-            held["d3"] = from_shift(held["down"], "x", nx - 1)
+            names = ("g2", "u2", "own_gate", "own_up")
+            left, right, *due = lax.optimization_barrier((left, right, *[after[n] for n in names]))
+            after.update(zip(names, due))
+            after["g3"] = from_shift(after["own_gate"], "x", nx - 1)
+            after["u1"] = from_shift(after["own_up"], "x", 1)
         if hop == 3:
-            left, right, held["g2"], held["u2"] = lax.optimization_barrier((left, right, held["g2"], held["u2"]))
+            names = ("g3", "u1", "down")
+            after["down"] = w_down[0].T
+            left, right, *due = lax.optimization_barrier((left, right, *[after[n] for n in names]))
+            after.update(zip(names, due))
+            after["d1"] = from_shift(after["down"], "x", 1)
+            after["d3"] = from_shift(after["down"], "x", nx - 1)
         return left, right
 
-    spread, g1, u3 = lax.optimization_barrier((spread, g1, u3))
-    held["g2"] = from_shift(g1, "x", 1)
-    held["u2"] = from_shift(u3, "x", nx - 1)
     blocks = around(spread, "y", between)
-    g3, u1, g2, u2 = held["g3"], held["u1"], held["g2"], held["u2"]
+    near_weights = [after[n] for n in ("own_gate", "own_up", "g1", "u1", "g3", "u3", "g2", "u2")]
     (hidden,) = call(
         hidden_body,
-        [shape((nx * units + units // 2 + 8, near * cap))],
-        [y_at, *blocks, own_gate, own_up, g1, u1, g3, u3, g2, u2, shared_gate, shared_up],
+        [shape((ny, nx * units + units // 2 + 8, near * cap))],
+        [y_at, *blocks, *near_weights, shared_gate, shared_up],
         scalars=1,
-        far=range(1, 2 * nx + len(RING) + 3),
+        far=(*range(1, len(RING)), *range(len(RING) + 1, len(RING) + 2 * nx + 3)),
         scratch=[
             pltpu.VMEM((lanes * width, near * cap + rows), BF16),
-            pltpu.VMEM(((nx + 1) * units, lanes * width), BF16),
-            pltpu.VMEM(((nx + 1) * units, lanes * width), BF16),
+            pltpu.VMEM((2 * (nx + 1) * units, lanes * width), BF16),
             pltpu.SemaphoreType.DMA((2 * nx + 2 + lanes,)),
         ],
-        limit=60,
-    )
-    hidden, d1, d3 = lax.optimization_barrier((hidden, held["d1"], held["d3"]))
+        limit=56,
+    )
+    hidden, d1, d3 = lax.optimization_barrier((hidden, after["d1"], after["d3"]))
     d2 = [from_shift(d1[:half], "x", 1), from_shift(d3[half:], "x", nx - 1)]
-    all_hidden = spread_all(hidden, "y", ny)
+    all_hidden = exchange(hidden, "y")
     (returned,) = call(
         down_body,
         [shape((nx, near * half + ny * units, 2 * cap))],
-        [x_at, all_hidden, held["down"], d1, d3, *d2],
+        [x_at, all_hidden, after["down"], d1, d3, *d2],
         scalars=1,
         far=range(2, 3 + nx),
         scratch=[
@@ -362,19 +382,19 @@
     back = lax.all_to_all(back, LINE, 0, 0, tiled=True)
     layer_out, scored = call(
         combine_body,
-        [shape((width, rows)), shape((8, width))],
+        [shape((width, rows)), shape((groups, SCORE_E, width))],
         [slot, gate, back, tok, mixed, shared_down.T],
     )
-    line_rows = spread_all(scored[:SCORE_E], LINE, groups).reshape(groups * SCORE_E, width)
+    line_rows = exchange(scored, LINE).reshape(groups * SCORE_E, width)
     count = groups * SCORE_E // nc
     core = lax.axis_index("core").astype(jnp.int32)
     (packed,) = call(
         pack_body,
-        [shape((width * count // (2 * cap), 2 * cap))],
+        [shape((lanes, width * count // (2 * cap), 2 * cap))],
         [core.reshape(1), line_rows],
         scalars=1,
     )
-    every = spread_all(packed, PLANE, lanes)
+    every = exchange(packed, PLANE)
     other_vocab = lax.ppermute(vocab, "core", [(0, 1), (1, 0)])
     place = lax.axis_index("x") * ny + lax.axis_index("y")
     first = [

time: 238 us -> 250 us (1.050)
  starting transfers between devices: 101 us -> 113 us
  local copies, waits for them, and re-layouts: 7.95 us -> 1.81 us
  waiting for transfers between devices: 57.3 us -> 61 us
    all_to_all x5, starting transfers between devices: 28.5 us -> 32.8 us  [exchange(): return lax.all_to_all(value, axes, 0, 0, tiled=True)]
    ppermute x1, starting transfers between devices: 9.12 us -> 12.7 us  [shards(): other_vocab = lax.ppermute(vocab, 'core', [(0, 1), (1, 0)])]
    broadcast_in_dim x6 -> x3, local copies, waits for them, and re-layouts: 3.3 us -> 0.03 us  [spread_all(): jnp.broadcast_to(value[None], (count, *value.shape))]
    ppermute x18 -> x20, waiting for transfers between devices: 31.1 us -> 34.3 us  [from_shift(): lax.ppermute(value, axis, [((i + shift) % count, i) for i in range(count)])]
    ppermute x18 -> x20, starting transfers between devices: 60.1 us -> 62.8 us  [from_shift(): lax.ppermute(value, axis, [((i + shift) % count, i) for i in range(count)])]
  transfers between devices with their start and end apart: 25 -> 27, of which waited for: 14 -> 19; matrix products, arithmetic and copies ran while one was open for 1% -> 0% of each run, Pallas kernels for 3% -> 4%
where the time goes in v4:
time: 250 us; the launch traced here: 248 us
  starting transfers between devices  113 us (45%)
  waiting for transfers between devices  61 us (24%)
  blocking collectives  54.5 us (22%)
  Pallas kernels  16.9 us (7%)
    ppermute x20, starting transfers between devices, from_shift(): lax.ppermute(value, axis, [((i + shift) % count, i) for i in range(count)])  62.8 us
    ppermute x20, waiting for transfers between devices, from_shift(): lax.ppermute(value, axis, [((i + shift) % count, i) for i in range(count)])  34.3 us
    all_to_all x5, starting transfers between devices, exchange(): return lax.all_to_all(value, axes, 0, 0, tiled=True)  32.8 us
    all_to_all x2, blocking collectives, spread_all(): lax.all_to_all(jnp.broadcast_to(value[None], (count, *value.shape)), axes...  27.8 us
    all_to_all x1, blocking collectives, shards(): back = lax.all_to_all(back, LINE, 0, 0, tiled=True)  26.7 us
    all_to_all x5, waiting for transfers between devices, exchange(): return lax.all_to_all(value, axes, 0, 0, tiled=True)  26.7 us
    pallas_call x7, Pallas kernels, call(): pl.pallas_call(body, out_shape=outs, in_specs=specs, out_specs=[pl.BlockS...  16.9 us
    ppermute x1, starting transfers between devices, shards(): other_vocab = lax.ppermute(vocab, 'core', [(0, 1), (1, 0)])  12.7 us
  transfers between devices with their start and end apart: 27, of which 19 were waited for; matrix products, arithmetic and copies ran while one was open for 0% of the time, Pallas kernels for 4%

profile of v4, /device:TPU:1, one launch (start us, length us, event | category | flops | bytes accessed | tf_op | source)
XLA Modules:
  0.0 248.4 jit_solution(14203997861150374125)
XLA Ops:
  0.6 0.0 copy-start.4
  0.6 0.0 copy-start.7
  0.7 2.3 shard_map.122
  3.0 11.8 %all-to-all-start = ((bf16[16,80,128]{2,1,0:T(8,128)(2,1)}), bf16[16,80,128]{2,1,0:T(8,128)(2,1)}, u32[]{:S(2)}, u32[]{:S(2)}) async-start(bf16[16,80,128]{2,1,0:T(8,128)(2,1)} %get-tuple-element.33), calls=%async_computation | async-start | bytes 655360 | tf_op jit(solution)/shard_map/all_to_all | solution.py:258
  14.8 4.4 %collective-permute-start = (bf16[160,128]{1,0:T(8,128)(2,1)}, bf16[160,128]{1,0:T(8,128)(2,1)S(1)}, u32[]{:S(2)}, u32[]{:S(2)}) collective-permute-start(bf16[160,128]{1,0:T(8,128)(2,1)} %bitcast.26), channel_id=1, source_target_pairs={{8,0},{16,8},{24,16},{0,24},{9,1},{17,9},{25,17},{1,25},{10,2},{18... | collective-permute-start | bytes 122888 | tf_op jit(solution)/shard_map/ppermute | solution.py:269
  19.2 1.9 collective-permute-start.1
  21.1 3.6 %collective-permute-start.2 = (bf16[160,128]{1,0:T(8,128)(2,1)}, bf16[160,128]{1,0:T(8,128)(2,1)S(1)}, u32[]{:S(2)}, u32[]{:S(2)}) collective-permute-start(bf16[160,128]{1,0:T(8,128)(2,1)} %bitcast.28), channel_id=1, source_target_pairs={{16,0},{24,8},{0,16},{8,24},{17,1},{25,9},{1,17},{9,25},{18,2},{26... | collective-permute-start | bytes 122888 | tf_op jit(solution)/shard_map/ppermute | solution.py:269
  24.8 1.0 collective-permute-done.1.refs_2_
  25.8 1.8 collective-permute-done.2.refs_3_
  27.6 0.4 all-to-all-done
  28.0 4.0 %all-to-all-start.1 = ((bf16[4,320,128]{2,1,0:T(8,128)(2,1)}), bf16[4,320,128]{2,1,0:T(8,128)(2,1)S(1)}, u32[]{:S(2)}, u32[]{:S(2)}) async-start(bf16[4,320,128]{2,1,0:T(8,128)(2,1)} %bitcast.5), calls=%async_computation.1 | async-start | bytes 655360 | tf_op jit(solution)/shard_map/all_to_all | solution.py:258
  32.0 5.9 %all-to-all-done.1.in_ref = bf16[4,320,128]{2,1,0:T(8,128)(2,1)S(1)} async-done(((bf16[4,320,128]{2,1,0:T(8,128)(2,1)}), bf16[4,320,128]{2,1,0:T(8,128)(2,1)S(1)}, u32[]{:S(2)}, u32[]{:S(2)}) %all-to-all-start.1) | async-done | bytes 327712 | tf_op jit(solution)/shard_map/all_to_all | solution.py:258
  37.9 0.2 shard_map.123.refs_0_
  38.1 3.2 %collective-permute-start.3 = (bf16[640,384]{1,0:T(8,128)(2,1)S(1)}, bf16[640,384]{1,0:T(8,128)(2,1)S(1)}, u32[]{:S(2)}, u32[]{:S(2)}) collective-permute-start(bf16[640,384]{1,0:T(8,128)(2,1)S(1)} %shard_map.123.refs_0_), channel_id=1, source_target_pairs={{7,0},{0,1},{1,2},{2,3},{3,4},{4,5},{5,6},{6,7},{15,8},{8,9},{9,10... | collective-permute-start | bytes 1474568 | tf_op jit(solution)/shard_map/ppermute | solution.py:269
  41.3 3.8 %collective-permute-start.4 = (bf16[640,384]{1,0:T(8,128)(2,1)S(1)}, bf16[640,384]{1,0:T(8,128)(2,1)S(1)}, u32[]{:S(2)}, u32[]{:S(2)}) collective-permute-start(bf16[640,384]{1,0:T(8,128)(2,1)S(1)} %shard_map.123.refs_0_), channel_id=1, source_target_pairs={{1,0},{2,1},{3,2},{4,3},{5,4},{6,5},{7,6},{0,7},{9,8},{10,9},{11,1... | collective-permute-start | bytes 1474568 | tf_op jit(solution)/shard_map/ppermute | solution.py:269
  45.1 2.9 %collective-permute-start.5 = (bf16[48,5120]{1,0:T(8,128)(2,1)S(1)}, bf16[48,5120]{1,0:T(8,128)(2,1)S(1)}, u32[]{:S(2)}, u32[]{:S(2)}) collective-permute-start(bf16[48,5120]{1,0:T(8,128)(2,1)S(1)} %bitcast.33), channel_id=1, source_target_pairs={{8,0},{16,8},{24,16},{0,24},{9,1},{17,9},{25,17},{1,25},{10,2},{18... | collective-permute-start | bytes 1474568 | tf_op jit(solution)/shard_map/ppermute | solution.py:269
  48.0 2.4 collective-permute-start.6
  50.4 1.4 collective-permute-done.3.refs_1_
  51.9 0.9 collective-permute-done.4.refs_2_
  52.8 3.8 %collective-permute-done.5.refs_10_ = bf16[48,5120]{1,0:T(8,128)(2,1)S(1)} collective-permute-done((bf16[48,5120]{1,0:T(8,128)(2,1)S(1)}, bf16[48,5120]{1,0:T(8,128)(2,1)S(1)}, u32[]{:S(2)}, u32[]{:S(2)}) %collective-permute-start.5) | collective-permute-done | bytes 491552 | tf_op jit(solution)/shard_map/ppermute | solution.py:269
  56.6 4.0 %collective-permute-done.6.refs_13_ = bf16[48,5120]{1,0:T(8,128)(2,1)S(1)} collective-permute-done((bf16[48,5120]{1,0:T(8,128)(2,1)S(1)}, bf16[48,5120]{1,0:T(8,128)(2,1)S(1)}, u32[]{:S(2)}, u32[]{:S(2)}) %collective-permute-start.6) | collective-permute-done | bytes 491552 | tf_op jit(solution)/shard_map/ppermute | solution.py:269
  60.6 1.9 collective-permute-start.7
  62.5 4.6 %collective-permute-start.8 = (bf16[640,384]{1,0:T(8,128)(2,1)S(1)}, bf16[640,384]{1,0:T(8,128)(2,1)S(1)}, u32[]{:S(2)}, u32[]{:S(2)}) collective-permute-start(bf16[640,384]{1,0:T(8,128)(2,1)S(1)} %collective-permute-done.4.refs_2_), channel_id=1, source_target_pairs={{1,0},{2,1},{3,2},{4,3},{5,4},{6,5},{7,6},{0,7},{9,8},{10,9},{11,1... | collective-permute-start | bytes 1474568 | tf_op jit(solution)/shard_map/ppermute | solution.py:269
  67.1 1.9 collective-permute-start.9
  69.0 3.4 %collective-permute-start.10 = (bf16[48,5120]{1,0:T(8,128)(2,1)S(1)}, bf16[48,5120]{1,0:T(8,128)(2,1)S(1)}, u32[]{:S(2)}, u32[]{:S(2)}) collective-permute-start(bf16[48,5120]{1,0:T(8,128)(2,1)S(1)} %collective-permute-done.6.refs_13_), channel_id=1, source_target_pairs={{24,0},{0,8},{8,16},{16,24},{25,1},{1,9},{9,17},{17,25},{26,2},{2,... | collective-permute-start | bytes 1474568 | tf_op jit(solution)/shard_map/ppermute | solution.py:269
  72.4 0.7 collective-permute-done.8.refs_4_
  73.1 3.9 %collective-permute-done.9.refs_14_ = bf16[48,5120]{1,0:T(8,128)(2,1)S(1)} collective-permute-done((bf16[48,5120]{1,0:T(8,128)(2,1)S(1)}, bf16[48,5120]{1,0:T(8,128)(2,1)S(1)}, u32[]{:S(2)}, u32[]{:S(2)}) %collective-permute-start.9) | collective-permute-done | bytes 491552 | tf_op jit(solution)/shard_map/ppermute | solution.py:269
  76.9 2.8 %collective-permute-done.10.refs_15_ = bf16[48,5120]{1,0:T(8,128)(2,1)S(1)} collective-permute-done((bf16[48,5120]{1,0:T(8,128)(2,1)S(1)}, bf16[48,5120]{1,0:T(8,128)(2,1)S(1)}, u32[]{:S(2)}, u32[]{:S(2)}) %collective-permute-start.10) | collective-permute-done | bytes 491552 | tf_op jit(solution)/shard_map/ppermute | solution.py:269
  79.8 1.9 collective-permute-start.11
  81.7 4.6 %collective-permute-start.12 = (bf16[640,384]{1,0:T(8,128)(2,1)S(1)}, bf16[640,384]{1,0:T(8,128)(2,1)S(1)}, u32[]{:S(2)}, u32[]{:S(2)}) collective-permute-start(bf16[640,384]{1,0:T(8,128)(2,1)S(1)} %collective-permute-done.8.refs_4_), channel_id=1, source_target_pairs={{1,0},{2,1},{3,2},{4,3},{5,4},{6,5},{7,6},{0,7},{9,8},{10,9},{11,1... | collective-permute-start | bytes 1474568 | tf_op jit(solution)/shard_map/ppermute | solution.py:269
  86.3 2.4 collective-permute-start.13
  88.7 4.0 %collective-permute-start.14 = (bf16[48,5120]{1,0:T(8,128)(2,1)S(1)}, bf16[48,5120]{1,0:T(8,128)(2,1)S(1)}, u32[]{:S(2)}, u32[]{:S(2)}) collective-permute-start(bf16[48,5120]{1,0:T(8,128)(2,1)S(1)} %bitcast.37), channel_id=1, source_target_pairs={{8,0},{16,8},{24,16},{0,24},{9,1},{17,9},{25,17},{1,25},{10,2},{18... | collective-permute-start | bytes 1474568 | tf_op jit(solution)/shard_map/ppermute | solution.py:269
  92.8 4.6 %collective-permute-done.13.refs_12_ = bf16[48,5120]{1,0:T(8,128)(2,1)S(1)} collective-permute-done((bf16[48,5120]{1,0:T(8,128)(2,1)S(1)}, bf16[48,5120]{1,0:T(8,128)(2,1)S(1)}, u32[]{:S(2)}, u32[]{:S(2)}) %collective-permute-start.13) | collective-permute-done | bytes 491552 | tf_op jit(solution)/shard_map/ppermute | solution.py:269
  97.4 1.2 collective-permute-done.14.refs_11_
  98.6 1.9 collective-permute-start.15
  100.5 5.0 %collective-permute-start.16 = (bf16[160,1536]{1,0:T(8,128)(2,1)S(1)}, bf16[160,1536]{1,0:T(8,128)(2,1)S(1)}, u32[]{:S(2)}, u32[]{:S(2)}) collective-permute-start(bf16[160,1536]{1,0:T(8,128)(2,1)S(1)} %bitcast.22), channel_id=1, source_target_pairs={{8,0},{16,8},{24,16},{0,24},{9,1},{17,9},{25,17},{1,25},{10,2},{18... | collective-permute-start | bytes 1474568 | tf_op jit(solution)/shard_map/ppermute | solution.py:269
  105.6 1.9 collective-permute-start.17
  107.5 2.0 collective-permute-done.15.refs_7_
  109.5 0.8 copy-done.20
  110.4 7.2 %shard_map.124 = bf16[8,224,256]{2,1,0:T(8,128)(2,1)} custom-call(s32[1]{0:T(128)} %bitcast.4.y_ref, bf16[640,384]{1,0:T(8,128)(2,1)} %copy-done, bf16[640,384]{1,0:T(8,128)(2,1)} %copy-done.9, bf16[640,384]{1,0:T(8,128)(2,1)} %copy-done.10, bf16[640,384]{1,0:T(8,128)(2,1)} %copy-done.13, bf16[640,384]{1,0:T(8,128)(2,1)} %copy-done.14, ...), custom_call_target="tpu_custom_call" | custom-call | bytes 9764868 | tf_op jit(solution)/shard_map/pallas_call | solution.py:23
  117.6 6.0 %all-to-all-start.2 = ((bf16[8,224,256]{2,1,0:T(8,128)(2,1)}), bf16[8,224,256]{2,1,0:T(8,128)(2,1)S(1)}, u32[]{:S(2)}, u32[]{:S(2)}) async-start(bf16[8,224,256]{2,1,0:T(8,128)(2,1)} %shard_map.124), calls=%async_computation.2 | async-start | bytes 1835008 | tf_op jit(solution)/shard_map/all_to_all | solution.py:258
  123.6 5.0 %collective-permute-start.18 = (bf16[80,1536]{1,0:T(8,128)(2,1)S(1)}, bf16[80,1536]{1,0:T(8,128)(2,1)S(1)}, u32[]{:S(2)}, u32[]{:S(2)}) collective-permute-start(bf16[80,1536]{1,0:T(8,128)(2,1)S(1)} %slice.18), channel_id=1, source_target_pairs={{8,0},{16,8},{24,16},{0,24},{9,1},{17,9},{25,17},{1,25},{10,2},{18... | collective-permute-start | bytes 737288 | tf_op jit(solution)/shard_map/ppermute | solution.py:269
  128.7 1.9 collective-permute-start.19
  130.6 1.2 collective-permute-done.18.refs_3_
  131.8 5.1 %collective-permute-done.19.refs_4_ = bf16[80,1536]{1,0:T(8,128)(2,1)S(1)} collective-permute-done((bf16[80,1536]{1,0:T(8,128)(2,1)S(1)}, bf16[80,1536]{1,0:T(8,128)(2,1)S(1)}, u32[]{:S(2)}, u32[]{:S(2)}) %collective-permute-start.19) | collective-permute-done | bytes 245792 | tf_op jit(solution)/shard_map/ppermute | solution.py:269
  136.8 3.3 %all-to-all-done.2.hidden_ref = bf16[8,224,256]{2,1,0:T(8,128)(2,1)S(1)} async-done(((bf16[8,224,256]{2,1,0:T(8,128)(2,1)}), bf16[8,224,256]{2,1,0:T(8,128)(2,1)S(1)}, u32[]{:S(2)}, u32[]{:S(2)}) %all-to-all-start.2) | async-done | bytes 917536 | tf_op jit(solution)/shard_map/all_to_all | solution.py:258
  140.1 3.3 %shard_map.125 = bf16[4,704,128]{2,1,0:T(8,128)(2,1)} custom-call(s32[1]{0:T(128)} %bitcast.3.x_ref, bf16[8,224,256]{2,1,0:T(8,128)(2,1)S(1)} %all-to-all-done.2.hidden_ref, bf16[160,1536]{1,0:T(8,128)(2,1)S(1)} %bitcast.24, bf16[160,1536]{1,0:T(8,128)(2,1)S(1)} %collective-permute-done.16.refs_1_, bf16[160,1536]{1,0:T(8,128)(2,1)S(1)} %collective-permute-done.17.refs_2_, ...), custom_call_target="tpu_custom_call" | custom-call | bytes 3604484 | tf_op jit(solution)/shard_map/pallas_call | solution.py:23
  143.5 4.6 %all-to-all-start.3 = ((bf16[4,704,128]{2,1,0:T(8,128)(2,1)}), bf16[4,704,128]{2,1,0:T(8,128)(2,1)S(1)}, u32[]{:S(2)}, u32[]{:S(2)}) async-start(bf16[4,704,128]{2,1,0:T(8,128)(2,1)} %shard_map.125), calls=%async_computation.3 | async-start | bytes 1441792 | tf_op jit(solution)/shard_map/all_to_all | solution.py:380
  148.1 12.7 %collective-permute-start.20 = (bf16[128,5120]{1,0:T(8,128)(2,1)S(1)}, bf16[128,5120]{1,0:T(8,128)(2,1)S(1)}, u32[]{:S(2)}, u32[]{:S(2)}) collective-permute-start(bf16[128,5120]{1,0:T(8,128)(2,1)S(1)} %copy-done.1), channel_id=1, source_target_pairs={{0,32},{32,0},{1,33},{33,1},{2,34},{34,2},{3,35},{35,3},{4,36},{36... | collective-permute-start | bytes 3932168 | tf_op jit(solution)/shard_map/ppermute | solution.py:398
  160.8 26.7 %all_to_all.45.back_ref = bf16[16,80,128]{2,1,0:T(8,128)(2,1)S(1)} all-to-all(bf16[16,80,128]{2,1,0:T(8,128)(2,1)S(1)} %bitcast.31), channel_id=1, replica_groups=mesh['z'=8,'core'=2,'x'=4,'y'=8] {'z','core'}, dimensions={0} | all-to-all | bytes 655360 | tf_op jit(solution)/shard_map/all_to_all | solution.py:382
  187.6 1.4 shard_map.126
  189.0 3.4 %all-to-all-start.5 = ((bf16[16,4,160]{2,1,0:T(4,128)(2,1)}), bf16[16,4,160]{2,1,0:T(4,128)(2,1)S(1)}, u32[]{:S(2)}, u32[]{:S(2)}) async-start(bf16[16,4,160]{2,1,0:T(4,128)(2,1)} %get-tuple-element.59), calls=%async_computation.5 | async-start | bytes 65536 | tf_op jit(solution)/shard_map/all_to_all | solution.py:258
  192.4 6.9 %all-to-all-done.5 = bf16[16,4,160]{2,1,0:T(4,128)(2,1)S(1)} async-done(((bf16[16,4,160]{2,1,0:T(4,128)(2,1)}), bf16[16,4,160]{2,1,0:T(4,128)(2,1)S(1)}, u32[]{:S(2)}, u32[]{:S(2)}) %all-to-all-start.5) | async-done | bytes 20512 | tf_op jit(solution)/shard_map/all_to_all | solution.py:258
  199.4 1.0 shard_map.127
  200.4 7.5 %all-to-all-start.6 = ((bf16[32,40,128]{2,1,0:T(8,128)(2,1)}), bf16[32,40,128]{2,1,0:T(8,128)(2,1)S(1)}, u32[]{:S(2)}, u32[]{:S(2)}) async-start(bf16[32,40,128]{2,1,0:T(8,128)(2,1)} %shard_map.127), calls=%async_computation.6 | async-start | bytes 655360 | tf_op jit(solution)/shard_map/all_to_all | solution.py:258
  207.9 0.1 tile.10
  208.0 0.1 tile.12.targets_ref
  208.1 0.1 pad_add_fusion.at_ref
  208.2 10.2 %all-to-all-done.6.rows_ref = bf16[32,40,128]{2,1,0:T(8,128)(2,1)S(1)} async-done(((bf16[32,40,128]{2,1,0:T(8,128)(2,1)}), bf16[32,40,128]{2,1,0:T(8,128)(2,1)S(1)}, u32[]{:S(2)}, u32[]{:S(2)}) %all-to-all-start.6) | async-done | bytes 327712 | tf_op jit(solution)/shard_map/all_to_all | solution.py:258
  218.3 1.6 shard_map.128
  219.9 16.0 %all_to_all.46 = f32[32,1,128]{2,1,0:T(1,128)S(1)} all-to-all(f32[32,1,128]{2,1,0:T(1,128)S(1)} %broadcast_in_dim.7), channel_id=1, replica_groups=mesh['z'=8,'core'=2,'x'=4,'y'=8] {'x','y'}, dimensions={0} | all-to-all | bytes 32768 | tf_op jit(solution)/shard_map/all_to_all | solution.py:262
  235.9 11.8 %all_to_all.47 = f32[16,1,128]{2,1,0:T(1,128)S(1)} all-to-all(f32[16,1,128]{2,1,0:T(1,128)S(1)} %broadcast_in_dim.16), channel_id=1, replica_groups=mesh['z'=8,'core'=2,'x'=4,'y'=8] {'z','core'}, dimensions={0} | all-to-all | bytes 16384 | tf_op jit(solution)/shard_map/all_to_all | solution.py:262
  247.8 0.1 log_subtract_fusion
  247.8 0.6 reshape.44
  (59 shorter events, 0.3 us)
Async XLA Ops:
  0.6 37.3 %copy-start.4 = (bf16[128,160]{0,1:T(8,128)(2,1)S(1)}, bf16[128,160]{0,1:T(8,128)(2,1)}, u32[]{:S(2)}) copy-start(bf16[128,160]{0,1:T(8,128)(2,1)} %param.11) | copy-start | bytes 122884
  0.6 44.5 %copy-start.7 = (bf16[1,48,5120]{2,1,0:T(8,128)(2,1)S(1)}, bf16[1,48,5120]{2,1,0:T(8,128)(2,1)}, u32[]{:S(2)}) copy-start(bf16[1,48,5120]{2,1,0:T(8,128)(2,1)} %param.14) | copy-start | bytes 1474564
  0.7 47.4 %copy-start.8 = (bf16[1,48,5120]{2,1,0:T(8,128)(2,1)S(1)}, bf16[1,48,5120]{2,1,0:T(8,128)(2,1)}, u32[]{:S(2)}) copy-start(bf16[1,48,5120]{2,1,0:T(8,128)(2,1)} %param.15) | copy-start | bytes 1474564
  0.7 99.8 %copy-start.3 = (bf16[1,1536,160]{1,2,0:T(8,128)(2,1)S(1)}, bf16[1,1536,160]{1,2,0:T(8,128)(2,1)}, u32[]{:S(2)}) copy-start(bf16[1,1536,160]{1,2,0:T(8,128)(2,1)} %param.16) | copy-start | bytes 1474564
  3.0 25.0 %all-to-all-start = ((bf16[16,80,128]{2,1,0:T(8,128)(2,1)}), bf16[16,80,128]{2,1,0:T(8,128)(2,1)}, u32[]{:S(2)}, u32[]{:S(2)}) async-start(bf16[16,80,128]{2,1,0:T(8,128)(2,1)} %get-tuple-element.33), calls=%async_computation | async-start | bytes 655360 | tf_op jit(solution)/shard_map/all_to_all | solution.py:258
  14.8 10.0 %collective-permute-start = (bf16[160,128]{1,0:T(8,128)(2,1)}, bf16[160,128]{1,0:T(8,128)(2,1)S(1)}, u32[]{:S(2)}, u32[]{:S(2)}) collective-permute-start(bf16[160,128]{1,0:T(8,128)(2,1)} %bitcast.26), channel_id=1, source_target_pairs={{8,0},{16,8},{24,16},{0,24},{9,1},{17,9},{25,17},{1,25},{10,2},{18... | collective-permute-start | bytes 122888 | tf_op jit(solution)/shard_map/ppermute | solution.py:269
  19.2 6.6 %collective-permute-start.1 = (bf16[160,128]{1,0:T(8,128)(2,1)}, bf16[160,128]{1,0:T(8,128)(2,1)S(1)}, u32[]{:S(2)}, u32[]{:S(2)}) collective-permute-start(bf16[160,128]{1,0:T(8,128)(2,1)} %bitcast.27), channel_id=1, source_target_pairs={{24,0},{0,8},{8,16},{16,24},{25,1},{1,9},{9,17},{17,25},{26,2},{2,... | collective-permute-start | bytes 122888 | tf_op jit(solution)/shard_map/ppermute | solution.py:269
  21.1 6.5 %collective-permute-start.2 = (bf16[160,128]{1,0:T(8,128)(2,1)}, bf16[160,128]{1,0:T(8,128)(2,1)S(1)}, u32[]{:S(2)}, u32[]{:S(2)}) collective-permute-start(bf16[160,128]{1,0:T(8,128)(2,1)} %bitcast.28), channel_id=1, source_target_pairs={{16,0},{24,8},{0,16},{8,24},{17,1},{25,9},{1,17},{9,25},{18,2},{26... | collective-permute-start | bytes 122888 | tf_op jit(solution)/shard_map/ppermute | solution.py:269
  28.0 9.9 %all-to-all-start.1 = ((bf16[4,320,128]{2,1,0:T(8,128)(2,1)}), bf16[4,320,128]{2,1,0:T(8,128)(2,1)S(1)}, u32[]{:S(2)}, u32[]{:S(2)}) async-start(bf16[4,320,128]{2,1,0:T(8,128)(2,1)} %bitcast.5), calls=%async_computation.1 | async-start | bytes 655360 | tf_op jit(solution)/shard_map/all_to_all | solution.py:258
  38.1 71.5 %copy-start = (bf16[640,384]{1,0:T(8,128)(2,1)}, bf16[640,384]{1,0:T(8,128)(2,1)S(1)}, u32[]{:S(2)}) copy-start(bf16[640,384]{1,0:T(8,128)(2,1)S(1)} %shard_map.123.refs_0_) | copy-start | bytes 1474564
  38.1 13.8 %collective-permute-start.3 = (bf16[640,384]{1,0:T(8,128)(2,1)S(1)}, bf16[640,384]{1,0:T(8,128)(2,1)S(1)}, u32[]{:S(2)}, u32[]{:S(2)}) collective-permute-start(bf16[640,384]{1,0:T(8,128)(2,1)S(1)} %shard_map.123.refs_0_), channel_id=1, source_target_pairs={{7,0},{0,1},{1,2},{2,3},{3,4},{4,5},{5,6},{6,7},{15,8},{8,9},{9,10... | collective-permute-start | bytes 1474568 | tf_op jit(solution)/shard_map/ppermute | solution.py:269
  41.3 11.5 %collective-permute-start.4 = (bf16[640,384]{1,0:T(8,128)(2,1)S(1)}, bf16[640,384]{1,0:T(8,128)(2,1)S(1)}, u32[]{:S(2)}, u32[]{:S(2)}) collective-permute-start(bf16[640,384]{1,0:T(8,128)(2,1)S(1)} %shard_map.123.refs_0_), channel_id=1, source_target_pairs={{1,0},{2,1},{3,2},{4,3},{5,4},{6,5},{7,6},{0,7},{9,8},{10,9},{11,1... | collective-permute-start | bytes 1474568 | tf_op jit(solution)/shard_map/ppermute | solution.py:269
  45.1 11.5 %collective-permute-start.5 = (bf16[48,5120]{1,0:T(8,128)(2,1)S(1)}, bf16[48,5120]{1,0:T(8,128)(2,1)S(1)}, u32[]{:S(2)}, u32[]{:S(2)}) collective-permute-start(bf16[48,5120]{1,0:T(8,128)(2,1)S(1)} %bitcast.33), channel_id=1, source_target_pairs={{8,0},{16,8},{24,16},{0,24},{9,1},{17,9},{25,17},{1,25},{10,2},{18... | collective-permute-start | bytes 1474568 | tf_op jit(solution)/shard_map/ppermute | solution.py:269
  48.0 12.5 %collective-permute-start.6 = (bf16[48,5120]{1,0:T(8,128)(2,1)S(1)}, bf16[48,5120]{1,0:T(8,128)(2,1)S(1)}, u32[]{:S(2)}, u32[]{:S(2)}) collective-permute-start(bf16[48,5120]{1,0:T(8,128)(2,1)S(1)} %bitcast.36), channel_id=1, source_target_pairs={{24,0},{0,8},{8,16},{16,24},{25,1},{1,9},{9,17},{17,25},{26,2},{2,... | collective-permute-start | bytes 1474568 | tf_op jit(solution)/shard_map/ppermute | solution.py:269
  51.9 46.7 %copy-start.9 = (bf16[640,384]{1,0:T(8,128)(2,1)}, bf16[640,384]{1,0:T(8,128)(2,1)S(1)}, u32[]{:S(2)}) copy-start(bf16[640,384]{1,0:T(8,128)(2,1)S(1)} %collective-permute-done.3.refs_1_) | copy-start | bytes 1474564
  52.8 47.7 %copy-start.10 = (bf16[640,384]{1,0:T(8,128)(2,1)}, bf16[640,384]{1,0:T(8,128)(2,1)S(1)}, u32[]{:S(2)}) copy-start(bf16[640,384]{1,0:T(8,128)(2,1)S(1)} %collective-permute-done.4.refs_2_) | copy-start | bytes 1474564
  56.6 48.9 %copy-start.11 = (bf16[48,5120]{1,0:T(8,128)(2,1)}, bf16[48,5120]{1,0:T(8,128)(2,1)S(1)}, u32[]{:S(2)}) copy-start(bf16[48,5120]{1,0:T(8,128)(2,1)S(1)} %collective-permute-done.5.refs_10_) | copy-start | bytes 1474564
  60.6 45.0 %copy-start.12 = (bf16[48,5120]{1,0:T(8,128)(2,1)}, bf16[48,5120]{1,0:T(8,128)(2,1)S(1)}, u32[]{:S(2)}) copy-start(bf16[48,5120]{1,0:T(8,128)(2,1)S(1)} %collective-permute-done.6.refs_13_) | copy-start | bytes 1474564
  60.6 11.8 %collective-permute-start.7 = (bf16[640,384]{1,0:T(8,128)(2,1)S(1)}, bf16[640,384]{1,0:T(8,128)(2,1)S(1)}, u32[]{:S(2)}, u32[]{:S(2)}) collective-permute-start(bf16[640,384]{1,0:T(8,128)(2,1)S(1)} %collective-permute-done.3.refs_1_), channel_id=1, source_target_pairs={{7,0},{0,1},{1,2},{2,3},{3,4},{4,5},{5,6},{6,7},{15,8},{8,9},{9,10... | collective-permute-start | bytes 1474568 | tf_op jit(solution)/shard_map/ppermute | solution.py:269
  62.5 10.6 %collective-permute-start.8 = (bf16[640,384]{1,0:T(8,128)(2,1)S(1)}, bf16[640,384]{1,0:T(8,128)(2,1)S(1)}, u32[]{:S(2)}, u32[]{:S(2)}) collective-permute-start(bf16[640,384]{1,0:T(8,128)(2,1)S(1)} %collective-permute-done.4.refs_2_), channel_id=1, source_target_pairs={{1,0},{2,1},{3,2},{4,3},{5,4},{6,5},{7,6},{0,7},{9,8},{10,9},{11,1... | collective-permute-start | bytes 1474568 | tf_op jit(solution)/shard_map/ppermute | solution.py:269
  67.1 9.9 %collective-permute-start.9 = (bf16[48,5120]{1,0:T(8,128)(2,1)S(1)}, bf16[48,5120]{1,0:T(8,128)(2,1)S(1)}, u32[]{:S(2)}, u32[]{:S(2)}) collective-permute-start(bf16[48,5120]{1,0:T(8,128)(2,1)S(1)} %collective-permute-done.5.refs_10_), channel_id=1, source_target_pairs={{8,0},{16,8},{24,16},{0,24},{9,1},{17,9},{25,17},{1,25},{10,2},{18... | collective-permute-start | bytes 1474568 | tf_op jit(solution)/shard_map/ppermute | solution.py:269
  69.0 10.8 %collective-permute-start.10 = (bf16[48,5120]{1,0:T(8,128)(2,1)S(1)}, bf16[48,5120]{1,0:T(8,128)(2,1)S(1)}, u32[]{:S(2)}, u32[]{:S(2)}) collective-permute-start(bf16[48,5120]{1,0:T(8,128)(2,1)S(1)} %collective-permute-done.6.refs_13_), channel_id=1, source_target_pairs={{24,0},{0,8},{8,16},{16,24},{25,1},{1,9},{9,17},{17,25},{26,2},{2,... | collective-permute-start | bytes 1474568 | tf_op jit(solution)/shard_map/ppermute | solution.py:269
  72.4 33.2 %copy-start.13 = (bf16[640,384]{1,0:T(8,128)(2,1)}, bf16[640,384]{1,0:T(8,128)(2,1)S(1)}, u32[]{:S(2)}) copy-start(bf16[640,384]{1,0:T(8,128)(2,1)S(1)} %collective-permute-done.7.refs_3_) | copy-start | bytes 1474564
  73.1 32.5 %copy-start.14 = (bf16[640,384]{1,0:T(8,128)(2,1)}, bf16[640,384]{1,0:T(8,128)(2,1)S(1)}, u32[]{:S(2)}) copy-start(bf16[640,384]{1,0:T(8,128)(2,1)S(1)} %collective-permute-done.8.refs_4_) | copy-start | bytes 1474564
  76.9 28.6 %copy-start.15 = (bf16[48,5120]{1,0:T(8,128)(2,1)}, bf16[48,5120]{1,0:T(8,128)(2,1)S(1)}, u32[]{:S(2)}) copy-start(bf16[48,5120]{1,0:T(8,128)(2,1)S(1)} %collective-permute-done.9.refs_14_) | copy-start | bytes 1474564
  79.8 25.8 %copy-start.16 = (bf16[48,5120]{1,0:T(8,128)(2,1)}, bf16[48,5120]{1,0:T(8,128)(2,1)S(1)}, u32[]{:S(2)}) copy-start(bf16[48,5120]{1,0:T(8,128)(2,1)S(1)} %collective-permute-done.10.refs_15_) | copy-start | bytes 1474564
  79.8 13.0 %collective-permute-start.11 = (bf16[640,384]{1,0:T(8,128)(2,1)S(1)}, bf16[640,384]{1,0:T(8,128)(2,1)}, u32[]{:S(2)}, u32[]{:S(2)}) collective-permute-start(bf16[640,384]{1,0:T(8,128)(2,1)S(1)} %collective-permute-done.7.refs_3_), channel_id=1, source_target_pairs={{7,0},{0,1},{1,2},{2,3},{3,4},{4,5},{5,6},{6,7},{15,8},{8,9},{9,10... | collective-permute-start | bytes 1474568 | tf_op jit(solution)/shard_map/ppermute | solution.py:269
  81.7 11.1 %collective-permute-start.12 = (bf16[640,384]{1,0:T(8,128)(2,1)S(1)}, bf16[640,384]{1,0:T(8,128)(2,1)S(1)}, u32[]{:S(2)}, u32[]{:S(2)}) collective-permute-start(bf16[640,384]{1,0:T(8,128)(2,1)S(1)} %collective-permute-done.8.refs_4_), channel_id=1, source_target_pairs={{1,0},{2,1},{3,2},{4,3},{5,4},{6,5},{7,6},{0,7},{9,8},{10,9},{11,1... | collective-permute-start | bytes 1474568 | tf_op jit(solution)/shard_map/ppermute | solution.py:269
  86.3 11.1 %collective-permute-start.13 = (bf16[48,5120]{1,0:T(8,128)(2,1)S(1)}, bf16[48,5120]{1,0:T(8,128)(2,1)S(1)}, u32[]{:S(2)}, u32[]{:S(2)}) collective-permute-start(bf16[48,5120]{1,0:T(8,128)(2,1)S(1)} %bitcast.34), channel_id=1, source_target_pairs={{24,0},{0,8},{8,16},{16,24},{25,1},{1,9},{9,17},{17,25},{26,2},{2,... | collective-permute-start | bytes 1474568 | tf_op jit(solution)/shard_map/ppermute | solution.py:269
  88.7 9.8 %collective-permute-start.14 = (bf16[48,5120]{1,0:T(8,128)(2,1)S(1)}, bf16[48,5120]{1,0:T(8,128)(2,1)S(1)}, u32[]{:S(2)}, u32[]{:S(2)}) collective-permute-start(bf16[48,5120]{1,0:T(8,128)(2,1)S(1)} %bitcast.37), channel_id=1, source_target_pairs={{8,0},{16,8},{24,16},{0,24},{9,1},{17,9},{25,17},{1,25},{10,2},{18... | collective-permute-start | bytes 1474568 | tf_op jit(solution)/shard_map/ppermute | solution.py:269
  92.8 12.8 %copy-start.17 = (bf16[640,384]{1,0:T(8,128)(2,1)}, bf16[640,384]{1,0:T(8,128)(2,1)S(1)}, u32[]{:S(2)}) copy-start(bf16[640,384]{1,0:T(8,128)(2,1)S(1)} %collective-permute-done.12.refs_6_) | copy-start | bytes 1474564
  97.4 8.2 %copy-start.18 = (bf16[48,5120]{1,0:T(8,128)(2,1)}, bf16[48,5120]{1,0:T(8,128)(2,1)S(1)}, u32[]{:S(2)}) copy-start(bf16[48,5120]{1,0:T(8,128)(2,1)S(1)} %collective-permute-done.13.refs_12_) | copy-start | bytes 1474564
  98.6 7.1 %copy-start.19 = (bf16[48,5120]{1,0:T(8,128)(2,1)}, bf16[48,5120]{1,0:T(8,128)(2,1)S(1)}, u32[]{:S(2)}) copy-start(bf16[48,5120]{1,0:T(8,128)(2,1)S(1)} %collective-permute-done.14.refs_11_) | copy-start | bytes 1474564
  98.6 11.0 %collective-permute-start.15 = (bf16[640,384]{1,0:T(8,128)(2,1)}, bf16[640,384]{1,0:T(8,128)(2,1)S(1)}, u32[]{:S(2)}, u32[]{:S(2)}) collective-permute-start(bf16[640,384]{1,0:T(8,128)(2,1)} %collective-permute-done.11.refs_5_), channel_id=1, source_target_pairs={{7,0},{0,1},{1,2},{2,3},{3,4},{4,5},{5,6},{6,7},{15,8},{8,9},{9,10... | collective-permute-start | bytes 1474568 | tf_op jit(solution)/shard_map/ppermute | solution.py:269
  100.5 17.1 %collective-permute-start.16 = (bf16[160,1536]{1,0:T(8,128)(2,1)S(1)}, bf16[160,1536]{1,0:T(8,128)(2,1)S(1)}, u32[]{:S(2)}, u32[]{:S(2)}) collective-permute-start(bf16[160,1536]{1,0:T(8,128)(2,1)S(1)} %bitcast.22), channel_id=1, source_target_pairs={{8,0},{16,8},{24,16},{0,24},{9,1},{17,9},{25,17},{1,25},{10,2},{18... | collective-permute-start | bytes 1474568 | tf_op jit(solution)/shard_map/ppermute | solution.py:269
  105.6 11.9 %collective-permute-start.17 = (bf16[160,1536]{1,0:T(8,128)(2,1)S(1)}, bf16[160,1536]{1,0:T(8,128)(2,1)S(1)}, u32[]{:S(2)}, u32[]{:S(2)}) collective-permute-start(bf16[160,1536]{1,0:T(8,128)(2,1)S(1)} %bitcast.23), channel_id=1, source_target_pairs={{24,0},{0,8},{8,16},{16,24},{25,1},{1,9},{9,17},{17,25},{26,2},{2,... | collective-permute-start | bytes 1474568 | tf_op jit(solution)/shard_map/ppermute | solution.py:269
  109.5 0.8 copy-start.20
  117.6 22.5 %all-to-all-start.2 = ((bf16[8,224,256]{2,1,0:T(8,128)(2,1)}), bf16[8,224,256]{2,1,0:T(8,128)(2,1)S(1)}, u32[]{:S(2)}, u32[]{:S(2)}) async-start(bf16[8,224,256]{2,1,0:T(8,128)(2,1)} %shard_map.124), calls=%async_computation.2 | async-start | bytes 1835008 | tf_op jit(solution)/shard_map/all_to_all | solution.py:258
  123.6 8.1 %collective-permute-start.18 = (bf16[80,1536]{1,0:T(8,128)(2,1)S(1)}, bf16[80,1536]{1,0:T(8,128)(2,1)S(1)}, u32[]{:S(2)}, u32[]{:S(2)}) collective-permute-start(bf16[80,1536]{1,0:T(8,128)(2,1)S(1)} %slice.18), channel_id=1, source_target_pairs={{8,0},{16,8},{24,16},{0,24},{9,1},{17,9},{25,17},{1,25},{10,2},{18... | collective-permute-start | bytes 737288 | tf_op jit(solution)/shard_map/ppermute | solution.py:269
  128.7 8.2 %collective-permute-start.19 = (bf16[80,1536]{1,0:T(8,128)(2,1)S(1)}, bf16[80,1536]{1,0:T(8,128)(2,1)S(1)}, u32[]{:S(2)}, u32[]{:S(2)}) collective-permute-start(bf16[80,1536]{1,0:T(8,128)(2,1)S(1)} %slice.19), channel_id=1, source_target_pairs={{24,0},{0,8},{8,16},{16,24},{25,1},{1,9},{9,17},{17,25},{26,2},{2,... | collective-permute-start | bytes 737288 | tf_op jit(solution)/shard_map/ppermute | solution.py:269
  143.4 4.6 %copy-start.1 = (bf16[128,5120]{1,0:T(8,128)(2,1)S(1)}, bf16[128,5120]{1,0:T(8,128)(2,1)}, u32[]{:S(2)}) copy-start(bf16[128,5120]{1,0:T(8,128)(2,1)} %vocab_ref.1) | copy-start | bytes 3932164
  143.4 44.1 %copy-start.5 = (s32[16,128]{1,0:T(8,128)S(1)}, s32[16,128]{1,0:T(8,128)}, u32[]{:S(2)}) copy-start(s32[16,128]{1,0:T(8,128)} %get-tuple-element.31.slot_ref) | copy-start | bytes 24580
  143.5 44.1 %copy-start.6 = (f32[16,128]{1,0:T(8,128)S(1)}, f32[16,128]{1,0:T(8,128)}, u32[]{:S(2)}) copy-start(f32[16,128]{1,0:T(8,128)} %get-tuple-element.32.gate_ref) | copy-start | bytes 24580
  143.5 17.3 %all-to-all-start.3 = ((bf16[4,704,128]{2,1,0:T(8,128)(2,1)}), bf16[4,704,128]{2,1,0:T(8,128)(2,1)S(1)}, u32[]{:S(2)}, u32[]{:S(2)}) async-start(bf16[4,704,128]{2,1,0:T(8,128)(2,1)} %shard_map.125), calls=%async_computation.3 | async-start | bytes 1441792 | tf_op jit(solution)/shard_map/all_to_all | solution.py:380
  148.1 60.1 %collective-permute-start.20 = (bf16[128,5120]{1,0:T(8,128)(2,1)S(1)}, bf16[128,5120]{1,0:T(8,128)(2,1)S(1)}, u32[]{:S(2)}, u32[]{:S(2)}) collective-permute-start(bf16[128,5120]{1,0:T(8,128)(2,1)S(1)} %copy-done.1), channel_id=1, source_target_pairs={{0,32},{32,0},{1,33},{33,1},{2,34},{34,2},{3,35},{35,3},{4,36},{36... | collective-permute-start | bytes 3932168 | tf_op jit(solution)/shard_map/ppermute | solution.py:398
  160.8 26.8 %copy-start.2 = (bf16[1536,160]{0,1:T(8,128)(2,1)S(1)}, bf16[1536,160]{0,1:T(8,128)(2,1)}, u32[]{:S(2)}) copy-start(bf16[1536,160]{0,1:T(8,128)(2,1)} %param.19) | copy-start | bytes 1474564
  187.6 20.3 %copy-start.21 = (s32[64]{0:T(128)S(1)}, s32[64]{0:T(128)}, u32[]{:S(2)}) copy-start(s32[64]{0:T(128)} %param.21) | copy-start | bytes 772
  189.0 10.3 %all-to-all-start.5 = ((bf16[16,4,160]{2,1,0:T(4,128)(2,1)}), bf16[16,4,160]{2,1,0:T(4,128)(2,1)S(1)}, u32[]{:S(2)}, u32[]{:S(2)}) async-start(bf16[16,4,160]{2,1,0:T(4,128)(2,1)} %get-tuple-element.59), calls=%async_computation.5 | async-start | bytes 65536 | tf_op jit(solution)/shard_map/all_to_all | solution.py:258
  200.4 18.0 %all-to-all-start.6 = ((bf16[32,40,128]{2,1,0:T(8,128)(2,1)}), bf16[32,40,128]{2,1,0:T(8,128)(2,1)S(1)}, u32[]{:S(2)}, u32[]{:S(2)}) async-start(bf16[32,40,128]{2,1,0:T(8,128)(2,1)} %shard_map.127), calls=%async_computation.6 | async-start | bytes 655360 | tf_op jit(solution)/shard_map/all_to_all | solution.py:258

commit v5 on v4

--- a/solution.py
+++ b/solution.py
@@ -322,26 +322,26 @@
         scalars=1,
     )
     spread, own_gate, own_up = lax.optimization_barrier((spread, w_gate[0], w_up[0]))
-    after = {"own_gate": own_gate, "own_up": own_up}
+    after = {"own_gate": own_gate, "own_up": own_up, "down": w_down[0].T}
     after["g1"] = from_shift(own_gate, "x", 1)
     after["u3"] = from_shift(own_up, "x", nx - 1)
 
+    def tie(left, right, *names):
+        left, right, *due = lax.optimization_barrier((left, right, *[after[n] for n in names]))
+        after.update(zip(names, due))
+        return left, right
+
     def between(hop, left, right):
         if hop == 1:
-            left, right, after["g1"], after["u3"] = lax.optimization_barrier((left, right, after["g1"], after["u3"]))
+            left, right = tie(left, right, "own_gate", "own_up")
+            after["g3"] = from_shift(after["own_gate"], "x", nx - 1)
+            after["u1"] = from_shift(after["own_up"], "x", 1)
+        if hop == 2:
+            left, right = tie(left, right, "g1", "u3")
             after["g2"] = from_shift(after["g1"], "x", 1)
             after["u2"] = from_shift(after["u3"], "x", nx - 1)
-        if hop == 2:
-            names = ("g2", "u2", "own_gate", "own_up")
-            left, right, *due = lax.optimization_barrier((left, right, *[after[n] for n in names]))
-            after.update(zip(names, due))
-            after["g3"] = from_shift(after["own_gate"], "x", nx - 1)
-            after["u1"] = from_shift(after["own_up"], "x", 1)
         if hop == 3:
-            names = ("g3", "u1", "down")
-            after["down"] = w_down[0].T
-            left, right, *due = lax.optimization_barrier((left, right, *[after[n] for n in names]))
-            after.update(zip(names, due))
+            left, right = tie(left, right, "g3", "u1", "down")
             after["d1"] = from_shift(after["down"], "x", 1)
             after["d3"] = from_shift(after["down"], "x", nx - 1)
         return left, right

time: 250 us -> 227 us (0.908)
  starting transfers between devices: 113 us -> 101 us
  waiting for transfers between devices: 61 us -> 54.3 us
  blocking collectives: 54.5 us -> 51.5 us
    ppermute x20, waiting for transfers between devices: 34.3 us -> 16.3 us  [from_shift(): lax.ppermute(value, axis, [((i + shift) % count, i) for i in range(count)])]
    all_to_all x5, waiting for transfers between devices: 26.7 us -> 36.3 us  [exchange(): return lax.all_to_all(value, axes, 0, 0, tiled=True)]
    ppermute x1, starting transfers between devices: 12.7 us -> 6.28 us  [shards(): other_vocab = lax.ppermute(vocab, 'core', [(0, 1), (1, 0)])]
    all_to_all x5, starting transfers between devices: 32.8 us -> 29.6 us  [exchange(): return lax.all_to_all(value, axes, 0, 0, tiled=True)]
    all_to_all x1, blocking collectives: 26.7 us -> 24.1 us  [shards(): back = lax.all_to_all(back, LINE, 0, 0, tiled=True)]
  transfers between devices with their start and end apart: 27 -> 27, of which waited for: 19 -> 15; matrix products, arithmetic and copies ran while one was open for 0% -> 0% of each run, Pallas kernels for 4% -> 4%
where the time goes in v5:
time: 227 us; the launch traced here: 226 us
  starting transfers between devices  101 us (44%)
  waiting for transfers between devices  54.3 us (24%)
  blocking collectives  51.5 us (23%)
  Pallas kernels  16.9 us (7%)
    ppermute x20, starting transfers between devices, from_shift(): lax.ppermute(value, axis, [((i + shift) % count, i) for i in range(count)])  61.4 us
    all_to_all x5, waiting for transfers between devices, exchange(): return lax.all_to_all(value, axes, 0, 0, tiled=True)  36.3 us
    all_to_all x5, starting transfers between devices, exchange(): return lax.all_to_all(value, axes, 0, 0, tiled=True)  29.6 us
    all_to_all x2, blocking collectives, spread_all(): lax.all_to_all(jnp.broadcast_to(value[None], (count, *value.shape)), axes...  27.4 us
    all_to_all x1, blocking collectives, shards(): back = lax.all_to_all(back, LINE, 0, 0, tiled=True)  24.1 us
    pallas_call x7, Pallas kernels, call(): pl.pallas_call(body, out_shape=outs, in_specs=specs, out_specs=[pl.BlockS...  16.9 us
    ppermute x20, waiting for transfers between devices, from_shift(): lax.ppermute(value, axis, [((i + shift) % count, i) for i in range(count)])  16.3 us
    ppermute x1, starting transfers between devices, shards(): other_vocab = lax.ppermute(vocab, 'core', [(0, 1), (1, 0)])  6.28 us
  transfers between devices with their start and end apart: 27, of which 15 were waited for; matrix products, arithmetic and copies ran while one was open for 0% of the time, Pallas kernels for 4%

profile of v5, /device:TPU:1, one launch (start us, length us, event | category | flops | bytes accessed | tf_op | source)
XLA Modules:
  0.0 225.8 jit_solution(6002892515063059599)
XLA Ops:
  0.6 0.0 copy-start.4
  0.6 0.0 copy-start.7
  0.7 0.0 copy-start.8
  0.7 2.3 %shard_map.122 = (bf16[16,80,128]{2,1,0:T(8,128)(2,1)}, s32[16,128]{1,0:T(8,128)}, f32[16,128]{1,0:T(8,128)}) custom-call(s32[6,128]{1,0:T(8,128)} %bitcast.40, f32[6,128]{1,0:T(8,128)} %bitcast.41, bf16[160,128]{1,0:T(8,128)(2,1)} %bitcast.25), custom_call_target="tpu_custom_call" | custom-call | bytes 391168 | tf_op jit(solution)/shard_map/pallas_call | solution.py:23
  3.0 11.8 %all-to-all-start = ((bf16[16,80,128]{2,1,0:T(8,128)(2,1)}), bf16[16,80,128]{2,1,0:T(8,128)(2,1)}, u32[]{:S(2)}, u32[]{:S(2)}) async-start(bf16[16,80,128]{2,1,0:T(8,128)(2,1)} %get-tuple-element.31), calls=%async_computation | async-start | bytes 655360 | tf_op jit(solution)/shard_map/all_to_all | solution.py:258
  14.8 4.4 %collective-permute-start = (bf16[160,128]{1,0:T(8,128)(2,1)}, bf16[160,128]{1,0:T(8,128)(2,1)S(1)}, u32[]{:S(2)}, u32[]{:S(2)}) collective-permute-start(bf16[160,128]{1,0:T(8,128)(2,1)} %bitcast.26), channel_id=1, source_target_pairs={{8,0},{16,8},{24,16},{0,24},{9,1},{17,9},{25,17},{1,25},{10,2},{18... | collective-permute-start | bytes 122888 | tf_op jit(solution)/shard_map/ppermute | solution.py:269
  19.2 1.9 collective-permute-start.1
  21.1 3.6 %collective-permute-start.2 = (bf16[160,128]{1,0:T(8,128)(2,1)}, bf16[160,128]{1,0:T(8,128)(2,1)S(1)}, u32[]{:S(2)}, u32[]{:S(2)}) collective-permute-start(bf16[160,128]{1,0:T(8,128)(2,1)} %bitcast.28), channel_id=1, source_target_pairs={{16,0},{24,8},{0,16},{8,24},{17,1},{25,9},{1,17},{9,25},{18,2},{26... | collective-permute-start | bytes 122888 | tf_op jit(solution)/shard_map/ppermute | solution.py:269
  24.8 0.0 collective-permute-done.refs_1_
  24.8 1.0 collective-permute-done.1.refs_2_
  25.8 1.8 collective-permute-done.2.refs_3_
  27.6 0.4 all-to-all-done
  28.0 4.0 %all-to-all-start.1 = ((bf16[4,320,128]{2,1,0:T(8,128)(2,1)}), bf16[4,320,128]{2,1,0:T(8,128)(2,1)S(1)}, u32[]{:S(2)}, u32[]{:S(2)}) async-start(bf16[4,320,128]{2,1,0:T(8,128)(2,1)} %bitcast.5), calls=%async_computation.1 | async-start | bytes 655360 | tf_op jit(solution)/shard_map/all_to_all | solution.py:258
  32.0 5.9 %all-to-all-done.1.in_ref = bf16[4,320,128]{2,1,0:T(8,128)(2,1)S(1)} async-done(((bf16[4,320,128]{2,1,0:T(8,128)(2,1)}), bf16[4,320,128]{2,1,0:T(8,128)(2,1)S(1)}, u32[]{:S(2)}, u32[]{:S(2)}) %all-to-all-start.1) | async-done | bytes 327712 | tf_op jit(solution)/shard_map/all_to_all | solution.py:258
  37.9 0.2 shard_map.123.refs_0_
  38.1 3.2 %collective-permute-start.3 = (bf16[640,384]{1,0:T(8,128)(2,1)S(1)}, bf16[640,384]{1,0:T(8,128)(2,1)S(1)}, u32[]{:S(2)}, u32[]{:S(2)}) collective-permute-start(bf16[640,384]{1,0:T(8,128)(2,1)S(1)} %shard_map.123.refs_0_), channel_id=1, source_target_pairs={{7,0},{0,1},{1,2},{2,3},{3,4},{4,5},{5,6},{6,7},{15,8},{8,9},{9,10... | collective-permute-start | bytes 1474568 | tf_op jit(solution)/shard_map/ppermute | solution.py:269
  41.3 3.8 %collective-permute-start.4 = (bf16[640,384]{1,0:T(8,128)(2,1)S(1)}, bf16[640,384]{1,0:T(8,128)(2,1)S(1)}, u32[]{:S(2)}, u32[]{:S(2)}) collective-permute-start(bf16[640,384]{1,0:T(8,128)(2,1)S(1)} %shard_map.123.refs_0_), channel_id=1, source_target_pairs={{1,0},{2,1},{3,2},{4,3},{5,4},{6,5},{7,6},{0,7},{9,8},{10,9},{11,1... | collective-permute-start | bytes 1474568 | tf_op jit(solution)/shard_map/ppermute | solution.py:269
  45.1 2.9 %collective-permute-start.7 = (bf16[48,5120]{1,0:T(8,128)(2,1)S(1)}, bf16[48,5120]{1,0:T(8,128)(2,1)}, u32[]{:S(2)}, u32[]{:S(2)}) collective-permute-start(bf16[48,5120]{1,0:T(8,128)(2,1)S(1)} %bitcast.33), channel_id=1, source_target_pairs={{8,0},{16,8},{24,16},{0,24},{9,1},{17,9},{25,17},{1,25},{10,2},{18... | collective-permute-start | bytes 1474568 | tf_op jit(solution)/shard_map/ppermute | solution.py:269
  48.0 2.4 %collective-permute-start.8 = (bf16[48,5120]{1,0:T(8,128)(2,1)S(1)}, bf16[48,5120]{1,0:T(8,128)(2,1)}, u32[]{:S(2)}, u32[]{:S(2)}) collective-permute-start(bf16[48,5120]{1,0:T(8,128)(2,1)S(1)} %bitcast.36), channel_id=1, source_target_pairs={{24,0},{0,8},{8,16},{16,24},{25,1},{1,9},{9,17},{17,25},{26,2},{2,... | collective-permute-start | bytes 1474568 | tf_op jit(solution)/shard_map/ppermute | solution.py:269
  50.4 1.4 collective-permute-done.3.refs_1_
  51.9 0.9 collective-permute-done.4.refs_2_
  52.8 3.3 %collective-permute-start.5 = (bf16[640,384]{1,0:T(8,128)(2,1)S(1)}, bf16[640,384]{1,0:T(8,128)(2,1)S(1)}, u32[]{:S(2)}, u32[]{:S(2)}) collective-permute-start(bf16[640,384]{1,0:T(8,128)(2,1)S(1)} %collective-permute-done.3.refs_1_), channel_id=1, source_target_pairs={{7,0},{0,1},{1,2},{2,3},{3,4},{4,5},{5,6},{6,7},{15,8},{8,9},{9,10... | collective-permute-start | bytes 1474568 | tf_op jit(solution)/shard_map/ppermute | solution.py:269
  56.1 3.9 %collective-permute-start.6 = (bf16[640,384]{1,0:T(8,128)(2,1)S(1)}, bf16[640,384]{1,0:T(8,128)(2,1)S(1)}, u32[]{:S(2)}, u32[]{:S(2)}) collective-permute-start(bf16[640,384]{1,0:T(8,128)(2,1)S(1)} %collective-permute-done.4.refs_2_), channel_id=1, source_target_pairs={{1,0},{2,1},{3,2},{4,3},{5,4},{6,5},{7,6},{0,7},{9,8},{10,9},{11,1... | collective-permute-start | bytes 1474568 | tf_op jit(solution)/shard_map/ppermute | solution.py:269
  60.0 2.2 collective-permute-start.11
  62.3 4.3 %collective-permute-start.12 = (bf16[48,5120]{1,0:T(8,128)(2,1)S(1)}, bf16[48,5120]{1,0:T(8,128)(2,1)S(1)}, u32[]{:S(2)}, u32[]{:S(2)}) collective-permute-start(bf16[48,5120]{1,0:T(8,128)(2,1)S(1)} %bitcast.37), channel_id=1, source_target_pairs={{8,0},{16,8},{24,16},{0,24},{9,1},{17,9},{25,17},{1,25},{10,2},{18... | collective-permute-start | bytes 1474568 | tf_op jit(solution)/shard_map/ppermute | solution.py:269
  66.6 1.7 collective-permute-done.6.refs_4_
  68.2 3.8 %collective-permute-start.9 = (bf16[640,384]{1,0:T(8,128)(2,1)S(1)}, bf16[640,384]{1,0:T(8,128)(2,1)}, u32[]{:S(2)}, u32[]{:S(2)}) collective-permute-start(bf16[640,384]{1,0:T(8,128)(2,1)S(1)} %collective-permute-done.5.refs_3_), channel_id=1, source_target_pairs={{7,0},{0,1},{1,2},{2,3},{3,4},{4,5},{5,6},{6,7},{15,8},{8,9},{9,10... | collective-permute-start | bytes 1474568 | tf_op jit(solution)/shard_map/ppermute | solution.py:269
  72.0 2.7 %collective-permute-start.10 = (bf16[640,384]{1,0:T(8,128)(2,1)S(1)}, bf16[640,384]{1,0:T(8,128)(2,1)S(1)}, u32[]{:S(2)}, u32[]{:S(2)}) collective-permute-start(bf16[640,384]{1,0:T(8,128)(2,1)S(1)} %collective-permute-done.6.refs_4_), channel_id=1, source_target_pairs={{1,0},{2,1},{3,2},{4,3},{5,4},{6,5},{7,6},{0,7},{9,8},{10,9},{11,1... | collective-permute-start | bytes 1474568 | tf_op jit(solution)/shard_map/ppermute | solution.py:269
  74.7 3.1 %collective-permute-start.14 = (bf16[48,5120]{1,0:T(8,128)(2,1)}, bf16[48,5120]{1,0:T(8,128)(2,1)}, u32[]{:S(2)}, u32[]{:S(2)}) collective-permute-start(bf16[48,5120]{1,0:T(8,128)(2,1)} %collective-permute-done.7.refs_10_), channel_id=1, source_target_pairs={{8,0},{16,8},{24,16},{0,24},{9,1},{17,9},{25,17},{1,25},{10,2},{18... | collective-permute-start | bytes 1474568 | tf_op jit(solution)/shard_map/ppermute | solution.py:269
  77.9 2.2 collective-permute-start.15
  80.1 1.9 collective-permute-done.10.refs_6_
  82.0 3.1 %collective-permute-start.13 = (bf16[640,384]{1,0:T(8,128)(2,1)}, bf16[640,384]{1,0:T(8,128)(2,1)}, u32[]{:S(2)}, u32[]{:S(2)}) collective-permute-start(bf16[640,384]{1,0:T(8,128)(2,1)} %collective-permute-done.9.refs_5_), channel_id=1, source_target_pairs={{7,0},{0,1},{1,2},{2,3},{3,4},{4,5},{5,6},{6,7},{15,8},{8,9},{9,10... | collective-permute-start | bytes 1474568 | tf_op jit(solution)/shard_map/ppermute | solution.py:269
  85.2 3.3 %collective-permute-start.16 = (bf16[160,1536]{1,0:T(8,128)(2,1)S(1)}, bf16[160,1536]{1,0:T(8,128)(2,1)S(1)}, u32[]{:S(2)}, u32[]{:S(2)}) collective-permute-start(bf16[160,1536]{1,0:T(8,128)(2,1)S(1)} %bitcast.22), channel_id=1, source_target_pairs={{8,0},{16,8},{24,16},{0,24},{9,1},{17,9},{25,17},{1,25},{10,2},{18... | collective-permute-start | bytes 1474568 | tf_op jit(solution)/shard_map/ppermute | solution.py:269
  88.6 1.9 collective-permute-start.17
  90.6 2.8 %collective-permute-done.13.refs_7_ = bf16[640,384]{1,0:T(8,128)(2,1)} collective-permute-done((bf16[640,384]{1,0:T(8,128)(2,1)}, bf16[640,384]{1,0:T(8,128)(2,1)}, u32[]{:S(2)}, u32[]{:S(2)}) %collective-permute-start.13) | collective-permute-done | bytes 491552 | tf_op jit(solution)/shard_map/ppermute | solution.py:269
  93.3 7.2 %shard_map.124 = bf16[8,224,256]{2,1,0:T(8,128)(2,1)} custom-call(s32[1]{0:T(128)} %bitcast.4.y_ref, bf16[640,384]{1,0:T(8,128)(2,1)} %copy-done, bf16[640,384]{1,0:T(8,128)(2,1)} %copy-done.9, bf16[640,384]{1,0:T(8,128)(2,1)} %copy-done.10, bf16[640,384]{1,0:T(8,128)(2,1)} %copy-done.11, bf16[640,384]{1,0:T(8,128)(2,1)} %copy-done.12, ...), custom_call_target="tpu_custom_call" | custom-call | bytes 9764868 | tf_op jit(solution)/shard_map/pallas_call | solution.py:23
  100.5 6.5 %all-to-all-start.2 = ((bf16[8,224,256]{2,1,0:T(8,128)(2,1)}), bf16[8,224,256]{2,1,0:T(8,128)(2,1)S(1)}, u32[]{:S(2)}, u32[]{:S(2)}) async-start(bf16[8,224,256]{2,1,0:T(8,128)(2,1)} %shard_map.124), calls=%async_computation.2 | async-start | bytes 1835008 | tf_op jit(solution)/shard_map/all_to_all | solution.py:258
  107.0 1.9 collective-permute-start.18
  109.0 3.4 %collective-permute-start.19 = (bf16[80,1536]{1,0:T(8,128)(2,1)S(1)}, bf16[80,1536]{1,0:T(8,128)(2,1)S(1)}, u32[]{:S(2)}, u32[]{:S(2)}) collective-permute-start(bf16[80,1536]{1,0:T(8,128)(2,1)S(1)} %slice.19), channel_id=1, source_target_pairs={{24,0},{0,8},{8,16},{16,24},{25,1},{1,9},{9,17},{17,25},{26,2},{2,... | collective-permute-start | bytes 737288 | tf_op jit(solution)/shard_map/ppermute | solution.py:269
  112.3 1.6 collective-permute-done.18.refs_3_
  113.9 3.2 %collective-permute-done.19.refs_4_ = bf16[80,1536]{1,0:T(8,128)(2,1)S(1)} collective-permute-done((bf16[80,1536]{1,0:T(8,128)(2,1)S(1)}, bf16[80,1536]{1,0:T(8,128)(2,1)S(1)}, u32[]{:S(2)}, u32[]{:S(2)}) %collective-permute-start.19) | collective-permute-done | bytes 245792 | tf_op jit(solution)/shard_map/ppermute | solution.py:269
  117.1 12.4 %all-to-all-done.2.hidden_ref = bf16[8,224,256]{2,1,0:T(8,128)(2,1)S(1)} async-done(((bf16[8,224,256]{2,1,0:T(8,128)(2,1)}), bf16[8,224,256]{2,1,0:T(8,128)(2,1)S(1)}, u32[]{:S(2)}, u32[]{:S(2)}) %all-to-all-start.2) | async-done | bytes 917536 | tf_op jit(solution)/shard_map/all_to_all | solution.py:258
  129.5 3.3 %shard_map.125 = bf16[4,704,128]{2,1,0:T(8,128)(2,1)} custom-call(s32[1]{0:T(128)} %bitcast.3.x_ref, bf16[8,224,256]{2,1,0:T(8,128)(2,1)S(1)} %all-to-all-done.2.hidden_ref, bf16[160,1536]{1,0:T(8,128)(2,1)S(1)} %bitcast.24, bf16[160,1536]{1,0:T(8,128)(2,1)S(1)} %collective-permute-done.16.refs_1_, bf16[160,1536]{1,0:T(8,128)(2,1)S(1)} %collective-permute-done.17.refs_2_, ...), custom_call_target="tpu_custom_call" | custom-call | bytes 3604484 | tf_op jit(solution)/shard_map/pallas_call | solution.py:23
  132.8 0.0 copy-start.1
  132.9 0.0 copy-start.5
  132.9 3.6 %all-to-all-start.3 = ((bf16[4,704,128]{2,1,0:T(8,128)(2,1)}), bf16[4,704,128]{2,1,0:T(8,128)(2,1)S(1)}, u32[]{:S(2)}, u32[]{:S(2)}) async-start(bf16[4,704,128]{2,1,0:T(8,128)(2,1)} %shard_map.125), calls=%async_computation.3 | async-start | bytes 1441792 | tf_op jit(solution)/shard_map/all_to_all | solution.py:380
  136.5 6.3 %collective-permute-start.20 = (bf16[128,5120]{1,0:T(8,128)(2,1)S(1)}, bf16[128,5120]{1,0:T(8,128)(2,1)S(1)}, u32[]{:S(2)}, u32[]{:S(2)}) collective-permute-start(bf16[128,5120]{1,0:T(8,128)(2,1)S(1)} %copy-done.1), channel_id=1, source_target_pairs={{0,32},{32,0},{1,33},{33,1},{2,34},{34,2},{3,35},{35,3},{4,36},{36... | collective-permute-start | bytes 3932168 | tf_op jit(solution)/shard_map/ppermute | solution.py:398
  142.8 1.7 all-to-all-done.3.hidden_ref
  144.5 24.1 %all_to_all.45.back_ref = bf16[16,80,128]{2,1,0:T(8,128)(2,1)S(1)} all-to-all(bf16[16,80,128]{2,1,0:T(8,128)(2,1)S(1)} %bitcast.31), channel_id=1, replica_groups=mesh['z'=8,'core'=2,'x'=4,'y'=8] {'z','core'}, dimensions={0} | all-to-all | bytes 655360 | tf_op jit(solution)/shard_map/all_to_all | solution.py:382
  168.6 0.0 copy-start.17
  168.6 1.4 shard_map.126
  170.0 3.3 %all-to-all-start.5 = ((bf16[16,4,160]{2,1,0:T(4,128)(2,1)}), bf16[16,4,160]{2,1,0:T(4,128)(2,1)S(1)}, u32[]{:S(2)}, u32[]{:S(2)}) async-start(bf16[16,4,160]{2,1,0:T(4,128)(2,1)} %get-tuple-element.55), calls=%async_computation.5 | async-start | bytes 65536 | tf_op jit(solution)/shard_map/all_to_all | solution.py:258
  173.4 7.0 %all-to-all-done.5 = bf16[16,4,160]{2,1,0:T(4,128)(2,1)S(1)} async-done(((bf16[16,4,160]{2,1,0:T(4,128)(2,1)}), bf16[16,4,160]{2,1,0:T(4,128)(2,1)S(1)}, u32[]{:S(2)}, u32[]{:S(2)}) %all-to-all-start.5) | async-done | bytes 20512 | tf_op jit(solution)/shard_map/all_to_all | solution.py:258
  180.4 1.0 shard_map.127
  181.4 3.9 %all-to-all-start.6 = ((bf16[32,40,128]{2,1,0:T(8,128)(2,1)}), bf16[32,40,128]{2,1,0:T(8,128)(2,1)S(1)}, u32[]{:S(2)}, u32[]{:S(2)}) async-start(bf16[32,40,128]{2,1,0:T(8,128)(2,1)} %shard_map.127), calls=%async_computation.6 | async-start | bytes 655360 | tf_op jit(solution)/shard_map/all_to_all | solution.py:258
  185.3 0.1 tile.10
  185.4 0.1 tile.12.targets_ref
  185.5 0.1 pad_add_fusion.at_ref
  185.5 10.6 %all-to-all-done.6.rows_ref = bf16[32,40,128]{2,1,0:T(8,128)(2,1)S(1)} async-done(((bf16[32,40,128]{2,1,0:T(8,128)(2,1)}), bf16[32,40,128]{2,1,0:T(8,128)(2,1)S(1)}, u32[]{:S(2)}, u32[]{:S(2)}) %all-to-all-start.6) | async-done | bytes 327712 | tf_op jit(solution)/shard_map/all_to_all | solution.py:258
  196.1 1.6 shard_map.128
  197.7 15.6 %all_to_all.46 = f32[32,1,128]{2,1,0:T(1,128)S(1)} all-to-all(f32[32,1,128]{2,1,0:T(1,128)S(1)} %broadcast_in_dim.7), channel_id=1, replica_groups=mesh['z'=8,'core'=2,'x'=4,'y'=8] {'x','y'}, dimensions={0} | all-to-all | bytes 32768 | tf_op jit(solution)/shard_map/all_to_all | solution.py:262
  213.3 11.8 %all_to_all.47 = f32[16,1,128]{2,1,0:T(1,128)S(1)} all-to-all(f32[16,1,128]{2,1,0:T(1,128)S(1)} %broadcast_in_dim.16), channel_id=1, replica_groups=mesh['z'=8,'core'=2,'x'=4,'y'=8] {'z','core'}, dimensions={0} | all-to-all | bytes 16384 | tf_op jit(solution)/shard_map/all_to_all | solution.py:262
  225.1 0.1 log_subtract_fusion
  225.2 0.6 reshape.44
  (51 shorter events, 0.2 us)
Async XLA Ops:
  0.6 37.3 %copy-start.4 = (bf16[128,160]{0,1:T(8,128)(2,1)S(1)}, bf16[128,160]{0,1:T(8,128)(2,1)}, u32[]{:S(2)}) copy-start(bf16[128,160]{0,1:T(8,128)(2,1)} %param.11) | copy-start | bytes 122884
  0.6 44.5 %copy-start.7 = (bf16[1,48,5120]{2,1,0:T(8,128)(2,1)S(1)}, bf16[1,48,5120]{2,1,0:T(8,128)(2,1)}, u32[]{:S(2)}) copy-start(bf16[1,48,5120]{2,1,0:T(8,128)(2,1)} %param.14) | copy-start | bytes 1474564
  0.7 47.4 %copy-start.8 = (bf16[1,48,5120]{2,1,0:T(8,128)(2,1)S(1)}, bf16[1,48,5120]{2,1,0:T(8,128)(2,1)}, u32[]{:S(2)}) copy-start(bf16[1,48,5120]{2,1,0:T(8,128)(2,1)} %param.15) | copy-start | bytes 1474564
  0.7 84.5 %copy-start.3 = (bf16[1,1536,160]{1,2,0:T(8,128)(2,1)S(1)}, bf16[1,1536,160]{1,2,0:T(8,128)(2,1)}, u32[]{:S(2)}) copy-start(bf16[1,1536,160]{1,2,0:T(8,128)(2,1)} %param.16) | copy-start | bytes 1474564
  3.0 25.0 %all-to-all-start = ((bf16[16,80,128]{2,1,0:T(8,128)(2,1)}), bf16[16,80,128]{2,1,0:T(8,128)(2,1)}, u32[]{:S(2)}, u32[]{:S(2)}) async-start(bf16[16,80,128]{2,1,0:T(8,128)(2,1)} %get-tuple-element.31), calls=%async_computation | async-start | bytes 655360 | tf_op jit(solution)/shard_map/all_to_all | solution.py:258
  14.8 10.0 %collective-permute-start = (bf16[160,128]{1,0:T(8,128)(2,1)}, bf16[160,128]{1,0:T(8,128)(2,1)S(1)}, u32[]{:S(2)}, u32[]{:S(2)}) collective-permute-start(bf16[160,128]{1,0:T(8,128)(2,1)} %bitcast.26), channel_id=1, source_target_pairs={{8,0},{16,8},{24,16},{0,24},{9,1},{17,9},{25,17},{1,25},{10,2},{18... | collective-permute-start | bytes 122888 | tf_op jit(solution)/shard_map/ppermute | solution.py:269
  19.2 6.6 %collective-permute-start.1 = (bf16[160,128]{1,0:T(8,128)(2,1)}, bf16[160,128]{1,0:T(8,128)(2,1)S(1)}, u32[]{:S(2)}, u32[]{:S(2)}) collective-permute-start(bf16[160,128]{1,0:T(8,128)(2,1)} %bitcast.27), channel_id=1, source_target_pairs={{24,0},{0,8},{8,16},{16,24},{25,1},{1,9},{9,17},{17,25},{26,2},{2,... | collective-permute-start | bytes 122888 | tf_op jit(solution)/shard_map/ppermute | solution.py:269
  21.1 6.5 %collective-permute-start.2 = (bf16[160,128]{1,0:T(8,128)(2,1)}, bf16[160,128]{1,0:T(8,128)(2,1)S(1)}, u32[]{:S(2)}, u32[]{:S(2)}) collective-permute-start(bf16[160,128]{1,0:T(8,128)(2,1)} %bitcast.28), channel_id=1, source_target_pairs={{16,0},{24,8},{0,16},{8,24},{17,1},{25,9},{1,17},{9,25},{18,2},{26... | collective-permute-start | bytes 122888 | tf_op jit(solution)/shard_map/ppermute | solution.py:269
  28.0 9.9 %all-to-all-start.1 = ((bf16[4,320,128]{2,1,0:T(8,128)(2,1)}), bf16[4,320,128]{2,1,0:T(8,128)(2,1)S(1)}, u32[]{:S(2)}, u32[]{:S(2)}) async-start(bf16[4,320,128]{2,1,0:T(8,128)(2,1)} %bitcast.5), calls=%async_computation.1 | async-start | bytes 655360 | tf_op jit(solution)/shard_map/all_to_all | solution.py:258
  38.1 55.2 %copy-start = (bf16[640,384]{1,0:T(8,128)(2,1)}, bf16[640,384]{1,0:T(8,128)(2,1)S(1)}, u32[]{:S(2)}) copy-start(bf16[640,384]{1,0:T(8,128)(2,1)S(1)} %shard_map.123.refs_0_) | copy-start | bytes 1474564
  38.1 13.8 %collective-permute-start.3 = (bf16[640,384]{1,0:T(8,128)(2,1)S(1)}, bf16[640,384]{1,0:T(8,128)(2,1)S(1)}, u32[]{:S(2)}, u32[]{:S(2)}) collective-permute-start(bf16[640,384]{1,0:T(8,128)(2,1)S(1)} %shard_map.123.refs_0_), channel_id=1, source_target_pairs={{7,0},{0,1},{1,2},{2,3},{3,4},{4,5},{5,6},{6,7},{15,8},{8,9},{9,10... | collective-permute-start | bytes 1474568 | tf_op jit(solution)/shard_map/ppermute | solution.py:269
  41.3 11.5 %collective-permute-start.4 = (bf16[640,384]{1,0:T(8,128)(2,1)S(1)}, bf16[640,384]{1,0:T(8,128)(2,1)S(1)}, u32[]{:S(2)}, u32[]{:S(2)}) collective-permute-start(bf16[640,384]{1,0:T(8,128)(2,1)S(1)} %shard_map.123.refs_0_), channel_id=1, source_target_pairs={{1,0},{2,1},{3,2},{4,3},{5,4},{6,5},{7,6},{0,7},{9,8},{10,9},{11,1... | collective-permute-start | bytes 1474568 | tf_op jit(solution)/shard_map/ppermute | solution.py:269
  45.1 17.1 %collective-permute-start.7 = (bf16[48,5120]{1,0:T(8,128)(2,1)S(1)}, bf16[48,5120]{1,0:T(8,128)(2,1)}, u32[]{:S(2)}, u32[]{:S(2)}) collective-permute-start(bf16[48,5120]{1,0:T(8,128)(2,1)S(1)} %bitcast.33), channel_id=1, source_target_pairs={{8,0},{16,8},{24,16},{0,24},{9,1},{17,9},{25,17},{1,25},{10,2},{18... | collective-permute-start | bytes 1474568 | tf_op jit(solution)/shard_map/ppermute | solution.py:269
  48.0 18.5 %collective-permute-start.8 = (bf16[48,5120]{1,0:T(8,128)(2,1)S(1)}, bf16[48,5120]{1,0:T(8,128)(2,1)}, u32[]{:S(2)}, u32[]{:S(2)}) collective-permute-start(bf16[48,5120]{1,0:T(8,128)(2,1)S(1)} %bitcast.36), channel_id=1, source_target_pairs={{24,0},{0,8},{8,16},{16,24},{25,1},{1,9},{9,17},{17,25},{26,2},{2,... | collective-permute-start | bytes 1474568 | tf_op jit(solution)/shard_map/ppermute | solution.py:269
  51.9 30.2 %copy-start.9 = (bf16[640,384]{1,0:T(8,128)(2,1)}, bf16[640,384]{1,0:T(8,128)(2,1)S(1)}, u32[]{:S(2)}) copy-start(bf16[640,384]{1,0:T(8,128)(2,1)S(1)} %collective-permute-done.3.refs_1_) | copy-start | bytes 1474564
  52.8 32.4 %copy-start.10 = (bf16[640,384]{1,0:T(8,128)(2,1)}, bf16[640,384]{1,0:T(8,128)(2,1)S(1)}, u32[]{:S(2)}) copy-start(bf16[640,384]{1,0:T(8,128)(2,1)S(1)} %collective-permute-done.4.refs_2_) | copy-start | bytes 1474564
  52.8 13.8 %collective-permute-start.5 = (bf16[640,384]{1,0:T(8,128)(2,1)S(1)}, bf16[640,384]{1,0:T(8,128)(2,1)S(1)}, u32[]{:S(2)}, u32[]{:S(2)}) collective-permute-start(bf16[640,384]{1,0:T(8,128)(2,1)S(1)} %collective-permute-done.3.refs_1_), channel_id=1, source_target_pairs={{7,0},{0,1},{1,2},{2,3},{3,4},{4,5},{5,6},{6,7},{15,8},{8,9},{9,10... | collective-permute-start | bytes 1474568 | tf_op jit(solution)/shard_map/ppermute | solution.py:269
  56.1 12.1 %collective-permute-start.6 = (bf16[640,384]{1,0:T(8,128)(2,1)S(1)}, bf16[640,384]{1,0:T(8,128)(2,1)S(1)}, u32[]{:S(2)}, u32[]{:S(2)}) collective-permute-start(bf16[640,384]{1,0:T(8,128)(2,1)S(1)} %collective-permute-done.4.refs_2_), channel_id=1, source_target_pairs={{1,0},{2,1},{3,2},{4,3},{5,4},{6,5},{7,6},{0,7},{9,8},{10,9},{11,1... | collective-permute-start | bytes 1474568 | tf_op jit(solution)/shard_map/ppermute | solution.py:269
  60.0 17.9 %collective-permute-start.11 = (bf16[48,5120]{1,0:T(8,128)(2,1)S(1)}, bf16[48,5120]{1,0:T(8,128)(2,1)S(1)}, u32[]{:S(2)}, u32[]{:S(2)}) collective-permute-start(bf16[48,5120]{1,0:T(8,128)(2,1)S(1)} %bitcast.34), channel_id=1, source_target_pairs={{24,0},{0,8},{8,16},{16,24},{25,1},{1,9},{9,17},{17,25},{26,2},{2,... | collective-permute-start | bytes 1474568 | tf_op jit(solution)/shard_map/ppermute | solution.py:269
  62.3 17.8 %collective-permute-start.12 = (bf16[48,5120]{1,0:T(8,128)(2,1)S(1)}, bf16[48,5120]{1,0:T(8,128)(2,1)S(1)}, u32[]{:S(2)}, u32[]{:S(2)}) collective-permute-start(bf16[48,5120]{1,0:T(8,128)(2,1)S(1)} %bitcast.37), channel_id=1, source_target_pairs={{8,0},{16,8},{24,16},{0,24},{9,1},{17,9},{25,17},{1,25},{10,2},{18... | collective-permute-start | bytes 1474568 | tf_op jit(solution)/shard_map/ppermute | solution.py:269
  66.6 22.0 %copy-start.11 = (bf16[640,384]{1,0:T(8,128)(2,1)}, bf16[640,384]{1,0:T(8,128)(2,1)S(1)}, u32[]{:S(2)}) copy-start(bf16[640,384]{1,0:T(8,128)(2,1)S(1)} %collective-permute-done.5.refs_3_) | copy-start | bytes 1474564
  68.2 20.3 %copy-start.12 = (bf16[640,384]{1,0:T(8,128)(2,1)}, bf16[640,384]{1,0:T(8,128)(2,1)S(1)}, u32[]{:S(2)}) copy-start(bf16[640,384]{1,0:T(8,128)(2,1)S(1)} %collective-permute-done.6.refs_4_) | copy-start | bytes 1474564
  68.2 11.8 %collective-permute-start.9 = (bf16[640,384]{1,0:T(8,128)(2,1)S(1)}, bf16[640,384]{1,0:T(8,128)(2,1)}, u32[]{:S(2)}, u32[]{:S(2)}) collective-permute-start(bf16[640,384]{1,0:T(8,128)(2,1)S(1)} %collective-permute-done.5.refs_3_), channel_id=1, source_target_pairs={{7,0},{0,1},{1,2},{2,3},{3,4},{4,5},{5,6},{6,7},{15,8},{8,9},{9,10... | collective-permute-start | bytes 1474568 | tf_op jit(solution)/shard_map/ppermute | solution.py:269
  72.0 10.0 %collective-permute-start.10 = (bf16[640,384]{1,0:T(8,128)(2,1)S(1)}, bf16[640,384]{1,0:T(8,128)(2,1)S(1)}, u32[]{:S(2)}, u32[]{:S(2)}) collective-permute-start(bf16[640,384]{1,0:T(8,128)(2,1)S(1)} %collective-permute-done.6.refs_4_), channel_id=1, source_target_pairs={{1,0},{2,1},{3,2},{4,3},{5,4},{6,5},{7,6},{0,7},{9,8},{10,9},{11,1... | collective-permute-start | bytes 1474568 | tf_op jit(solution)/shard_map/ppermute | solution.py:269
  74.7 15.8 %collective-permute-start.14 = (bf16[48,5120]{1,0:T(8,128)(2,1)}, bf16[48,5120]{1,0:T(8,128)(2,1)}, u32[]{:S(2)}, u32[]{:S(2)}) collective-permute-start(bf16[48,5120]{1,0:T(8,128)(2,1)} %collective-permute-done.7.refs_10_), channel_id=1, source_target_pairs={{8,0},{16,8},{24,16},{0,24},{9,1},{17,9},{25,17},{1,25},{10,2},{18... | collective-permute-start | bytes 1474568 | tf_op jit(solution)/shard_map/ppermute | solution.py:269
  77.9 10.7 %copy-start.13 = (bf16[48,5120]{1,0:T(8,128)(2,1)}, bf16[48,5120]{1,0:T(8,128)(2,1)S(1)}, u32[]{:S(2)}) copy-start(bf16[48,5120]{1,0:T(8,128)(2,1)S(1)} %collective-permute-done.11.refs_12_) | copy-start | bytes 1474564
  77.9 12.6 %collective-permute-start.15 = (bf16[48,5120]{1,0:T(8,128)(2,1)}, bf16[48,5120]{1,0:T(8,128)(2,1)S(1)}, u32[]{:S(2)}, u32[]{:S(2)}) collective-permute-start(bf16[48,5120]{1,0:T(8,128)(2,1)} %collective-permute-done.8.refs_13_), channel_id=1, source_target_pairs={{24,0},{0,8},{8,16},{16,24},{25,1},{1,9},{9,17},{17,25},{26,2},{2,... | collective-permute-start | bytes 1474568 | tf_op jit(solution)/shard_map/ppermute | solution.py:269
  80.1 8.5 %copy-start.14 = (bf16[48,5120]{1,0:T(8,128)(2,1)}, bf16[48,5120]{1,0:T(8,128)(2,1)S(1)}, u32[]{:S(2)}) copy-start(bf16[48,5120]{1,0:T(8,128)(2,1)S(1)} %collective-permute-done.12.refs_11_) | copy-start | bytes 1474564
  82.0 6.5 %copy-start.15 = (bf16[640,384]{1,0:T(8,128)(2,1)}, bf16[640,384]{1,0:T(8,128)(2,1)S(1)}, u32[]{:S(2)}) copy-start(bf16[640,384]{1,0:T(8,128)(2,1)S(1)} %collective-permute-done.10.refs_6_) | copy-start | bytes 1474564
  82.0 11.3 %collective-permute-start.13 = (bf16[640,384]{1,0:T(8,128)(2,1)}, bf16[640,384]{1,0:T(8,128)(2,1)}, u32[]{:S(2)}, u32[]{:S(2)}) collective-permute-start(bf16[640,384]{1,0:T(8,128)(2,1)} %collective-permute-done.9.refs_5_), channel_id=1, source_target_pairs={{7,0},{0,1},{1,2},{2,3},{3,4},{4,5},{5,6},{6,7},{15,8},{8,9},{9,10... | collective-permute-start | bytes 1474568 | tf_op jit(solution)/shard_map/ppermute | solution.py:269
  85.2 15.3 %collective-permute-start.16 = (bf16[160,1536]{1,0:T(8,128)(2,1)S(1)}, bf16[160,1536]{1,0:T(8,128)(2,1)S(1)}, u32[]{:S(2)}, u32[]{:S(2)}) collective-permute-start(bf16[160,1536]{1,0:T(8,128)(2,1)S(1)} %bitcast.22), channel_id=1, source_target_pairs={{8,0},{16,8},{24,16},{0,24},{9,1},{17,9},{25,17},{1,25},{10,2},{18... | collective-permute-start | bytes 1474568 | tf_op jit(solution)/shard_map/ppermute | solution.py:269
  88.6 11.9 %collective-permute-start.17 = (bf16[160,1536]{1,0:T(8,128)(2,1)S(1)}, bf16[160,1536]{1,0:T(8,128)(2,1)S(1)}, u32[]{:S(2)}, u32[]{:S(2)}) collective-permute-start(bf16[160,1536]{1,0:T(8,128)(2,1)S(1)} %bitcast.23), channel_id=1, source_target_pairs={{24,0},{0,8},{8,16},{16,24},{25,1},{1,9},{9,17},{17,25},{26,2},{2,... | collective-permute-start | bytes 1474568 | tf_op jit(solution)/shard_map/ppermute | solution.py:269
  90.5 2.8 %copy-start.16 = (bf16[48,5120]{1,0:T(8,128)(2,1)}, bf16[48,5120]{1,0:T(8,128)(2,1)S(1)}, u32[]{:S(2)}) copy-start(bf16[48,5120]{1,0:T(8,128)(2,1)S(1)} %collective-permute-done.15.refs_15_) | copy-start | bytes 1474564
  100.5 29.0 %all-to-all-start.2 = ((bf16[8,224,256]{2,1,0:T(8,128)(2,1)}), bf16[8,224,256]{2,1,0:T(8,128)(2,1)S(1)}, u32[]{:S(2)}, u32[]{:S(2)}) async-start(bf16[8,224,256]{2,1,0:T(8,128)(2,1)} %shard_map.124), calls=%async_computation.2 | async-start | bytes 1835008 | tf_op jit(solution)/shard_map/all_to_all | solution.py:258
  107.0 6.9 %collective-permute-start.18 = (bf16[80,1536]{1,0:T(8,128)(2,1)S(1)}, bf16[80,1536]{1,0:T(8,128)(2,1)S(1)}, u32[]{:S(2)}, u32[]{:S(2)}) collective-permute-start(bf16[80,1536]{1,0:T(8,128)(2,1)S(1)} %slice.18), channel_id=1, source_target_pairs={{8,0},{16,8},{24,16},{0,24},{9,1},{17,9},{25,17},{1,25},{10,2},{18... | collective-permute-start | bytes 737288 | tf_op jit(solution)/shard_map/ppermute | solution.py:269
  109.0 8.2 %collective-permute-start.19 = (bf16[80,1536]{1,0:T(8,128)(2,1)S(1)}, bf16[80,1536]{1,0:T(8,128)(2,1)S(1)}, u32[]{:S(2)}, u32[]{:S(2)}) collective-permute-start(bf16[80,1536]{1,0:T(8,128)(2,1)S(1)} %slice.19), channel_id=1, source_target_pairs={{24,0},{0,8},{8,16},{16,24},{25,1},{1,9},{9,17},{17,25},{26,2},{2,... | collective-permute-start | bytes 737288 | tf_op jit(solution)/shard_map/ppermute | solution.py:269
  132.8 3.7 %copy-start.1 = (bf16[128,5120]{1,0:T(8,128)(2,1)S(1)}, bf16[128,5120]{1,0:T(8,128)(2,1)}, u32[]{:S(2)}) copy-start(bf16[128,5120]{1,0:T(8,128)(2,1)} %vocab_ref.1) | copy-start | bytes 3932164
  132.9 35.7 %copy-start.5 = (s32[16,128]{1,0:T(8,128)S(1)}, s32[16,128]{1,0:T(8,128)}, u32[]{:S(2)}) copy-start(s32[16,128]{1,0:T(8,128)} %get-tuple-element.29.slot_ref) | copy-start | bytes 24580
  132.9 35.7 %copy-start.6 = (f32[16,128]{1,0:T(8,128)S(1)}, f32[16,128]{1,0:T(8,128)}, u32[]{:S(2)}) copy-start(f32[16,128]{1,0:T(8,128)} %get-tuple-element.30.gate_ref) | copy-start | bytes 24580
  132.9 11.6 %all-to-all-start.3 = ((bf16[4,704,128]{2,1,0:T(8,128)(2,1)}), bf16[4,704,128]{2,1,0:T(8,128)(2,1)S(1)}, u32[]{:S(2)}, u32[]{:S(2)}) async-start(bf16[4,704,128]{2,1,0:T(8,128)(2,1)} %shard_map.125), calls=%async_computation.3 | async-start | bytes 1441792 | tf_op jit(solution)/shard_map/all_to_all | solution.py:380
  136.5 49.0 %collective-permute-start.20 = (bf16[128,5120]{1,0:T(8,128)(2,1)S(1)}, bf16[128,5120]{1,0:T(8,128)(2,1)S(1)}, u32[]{:S(2)}, u32[]{:S(2)}) collective-permute-start(bf16[128,5120]{1,0:T(8,128)(2,1)S(1)} %copy-done.1), channel_id=1, source_target_pairs={{0,32},{32,0},{1,33},{33,1},{2,34},{34,2},{3,35},{35,3},{4,36},{36... | collective-permute-start | bytes 3932168 | tf_op jit(solution)/shard_map/ppermute | solution.py:398
  144.5 24.1 %copy-start.2 = (bf16[1536,160]{0,1:T(8,128)(2,1)S(1)}, bf16[1536,160]{0,1:T(8,128)(2,1)}, u32[]{:S(2)}) copy-start(bf16[1536,160]{0,1:T(8,128)(2,1)} %param.19) | copy-start | bytes 1474564
  168.6 16.7 %copy-start.17 = (s32[64]{0:T(128)S(1)}, s32[64]{0:T(128)}, u32[]{:S(2)}) copy-start(s32[64]{0:T(128)} %param.21) | copy-start | bytes 772
  170.0 10.3 %all-to-all-start.5 = ((bf16[16,4,160]{2,1,0:T(4,128)(2,1)}), bf16[16,4,160]{2,1,0:T(4,128)(2,1)S(1)}, u32[]{:S(2)}, u32[]{:S(2)}) async-start(bf16[16,4,160]{2,1,0:T(4,128)(2,1)} %get-tuple-element.55), calls=%async_computation.5 | async-start | bytes 65536 | tf_op jit(solution)/shard_map/all_to_all | solution.py:258
  181.4 14.7 %all-to-all-start.6 = ((bf16[32,40,128]{2,1,0:T(8,128)(2,1)}), bf16[32,40,128]{2,1,0:T(8,128)(2,1)S(1)}, u32[]{:S(2)}, u32[]{:S(2)}) async-start(bf16[32,40,128]{2,1,0:T(8,128)(2,1)} %shard_map.127), calls=%async_computation.6 | async-start | bytes 655360 | tf_op jit(solution)/shard_map/all_to_all | solution.py:258

commit v6 on v5

--- a/solution.py
+++ b/solution.py
@@ -13,7 +13,7 @@
 PLANE = ("x", "y")
 
 
-def call(body, outs, args, scalars=0, far=(), scratch=(), limit=16):
+def call(body, outs, args, scalars=0, far=(), scratch=(), limit=16, out_space=pltpu.VMEM):
     specs = [
         pl.BlockSpec(memory_space=pltpu.SMEM if n < scalars else pltpu.HBM if n in far else pltpu.VMEM)
         for n in range(len(args))
@@ -24,7 +24,7 @@
         body,
         out_shape=outs,
         in_specs=specs,
-        out_specs=[pl.BlockSpec(memory_space=pltpu.VMEM) for _ in outs],
+        out_specs=[pl.BlockSpec(memory_space=out_space) for _ in outs],
         scratch_shapes=list(scratch),
         cost_estimate=pl.CostEstimate(flops=0, bytes_accessed=moved, transcendentals=0),
         compiler_params=pltpu.CompilerParams(vmem_limit_bytes=limit << 20),
@@ -98,23 +98,24 @@
         out_ref[e] = nt(tok, sel.astype(BF16)).astype(BF16)
 
 
-def spread_body(x_ref, in_ref, *refs):
-    *tokens, out_ref = refs
+def spread_body(in_ref, out_ref):
     lanes_x, _, lanes = in_ref.shape
     width = out_ref.shape[0] // lanes_x
     half, cap = width // 2, lanes // 2
-    groups = in_ref.shape[1] // half
     for x in range(lanes_x):
         top, mid, end = x * width, x * width + half, (x + 1) * width
-        for q in range(groups // 2):
+        for q in range(out_ref.shape[1] // lanes):
             a = in_ref[x, 2 * q * half : (2 * q + 1) * half, :].astype(F32)
             b = in_ref[x, (2 * q + 1) * half : (2 * q + 2) * half, :].astype(F32)
             cols = slice(q * lanes, (q + 1) * lanes)
             out_ref[top:mid, cols] = pair_low(a, b, cap).astype(BF16)
             out_ref[mid:end, cols] = pair_high(a, b, cap).astype(BF16)
-    for tok, shift in zip(tokens, SHIFTS):
-        at = pl.multiple_of(lax.rem(x_ref[0] + shift, lanes_x) * width, width)
-        out_ref[pl.ds(at, width), groups * cap :] = tok[...]
+
+
+def stack_body(gate_ref, up_ref, out_ref, sems):
+    units = gate_ref.shape[0]
+    for copy in fetch([(gate_ref, out_ref.at[:units, :]), (up_ref, out_ref.at[units:, :])], sems):
+        copy.wait()
 
 
 def glu(gate, up):
@@ -122,30 +123,36 @@
 
 
 def hidden_body(y_ref, *refs):
+    out_ref, flat_ref, weight_ref, tok_ref, sems = refs[-5:]
     blocks = refs[: len(RING)]
-    out_ref, flat_ref, weight_ref, sems = refs[-4:]
-    weights = refs[len(RING) : -4]
-    nx = len(weights) // 2 - 1
-    units = weights[0].shape[0]
+    *stacked, shared_gate, shared_up, tok_far = refs[len(RING) : -5]
+    nx = len(stacked)
+    units = shared_gate.shape[0]
     width = blocks[0].shape[0] // nx
     ny = flat_ref.shape[0] // (nx * width)
     top = nx * units
-    pairs = []
-    for n, weight in enumerate(weights):
-        at = n // 2 * units + (n % 2) * top if n < 2 * nx else n * units
-        pairs.append((weight, weight_ref.at[at : at + units, :]))
+    pairs = [
+        (shared_gate, weight_ref.at[2 * top : 2 * top + units, :]),
+        (shared_up, weight_ref.at[2 * top + units :, :]),
+        (tok_far, tok_ref),
+    ]
+    for n, block in enumerate(stacked):
+        pairs.append((block.at[:units, :], weight_ref.at[n * units : (n + 1) * units, :]))
+        pairs.append((block.at[units:, :], weight_ref.at[top + n * units : top + (n + 1) * units, :]))
     for block, shift in zip(blocks, RING):
         y = lax.rem(y_ref[0] + shift, ny)
         for n in range(nx):
             at = pl.multiple_of((n * ny + y) * width, width)
             pairs.append((block.at[n * width : (n + 1) * width, :], flat_ref.at[pl.ds(at, width), :]))
-    for copy in fetch(pairs, sems):
+    copies = fetch(pairs, sems)
+    for copy in copies[:3]:
         copy.wait()
-    cols = out_ref.shape[2]
-    both = nn(weight_ref[: 2 * top, :], flat_ref[:, :cols])
+    both = nn(weight_ref[2 * top :, :], tok_ref[...])
+    own = glu(both[:units], both[units:])
+    for copy in copies[3:]:
+        copy.wait()
+    both = nn(weight_ref[: 2 * top, :], flat_ref[...])
     routed = glu(both[:top], both[top:])
-    both = nn(weight_ref[2 * top :, :], flat_ref[:, cols:])
-    own = glu(both[:units], both[units:])
     fold = units // 2
     folded = jnp.concatenate([own[:fold], own[fold:]], axis=1)
     for y in range(ny):
@@ -313,18 +320,24 @@
         limit=60,
     )
     arrived = exchange(outgoing, LINE)
-    arrived, t1, t3, t2 = lax.optimization_barrier((arrived, *[from_shift(tok, "x", shift) for shift in SHIFTS[1:]]))
+    plane_tok = lax.all_gather(tok, PLANE, axis=0, tiled=True)
+    (stacked,) = call(
+        stack_body,
+        [shape((2 * units, lanes * width))],
+        [w_gate[0], w_up[0]],
+        far=range(2),
+        scratch=[pltpu.SemaphoreType.DMA((2,))],
+        out_space=pltpu.HBM,
+    )
+    arrived, stacked = lax.optimization_barrier((arrived, stacked))
     quarter = exchange(arrived.reshape(nx, near * half, 2 * cap), "x")
-    (spread,) = call(
-        spread_body,
-        [shape((nx * width, near * cap + rows))],
-        [x_at, quarter, tok, t1, t3, t2],
-        scalars=1,
-    )
-    spread, own_gate, own_up = lax.optimization_barrier((spread, w_gate[0], w_up[0]))
-    after = {"own_gate": own_gate, "own_up": own_up, "down": w_down[0].T}
-    after["g1"] = from_shift(own_gate, "x", 1)
-    after["u3"] = from_shift(own_up, "x", nx - 1)
+    (spread,) = call(spread_body, [shape((nx * width, near * cap))], [quarter])
+    own_down = w_down[0].T
+    d1, d3 = from_shift(own_down, "x", 1), from_shift(own_down, "x", nx - 1)
+    spread, stacked, d1, d3 = lax.optimization_barrier((spread, stacked, d1, d3))
+    after = {"own": stacked}
+    after["g1"] = from_shift(stacked, "x", 1)
+    after["g3"] = from_shift(stacked, "x", nx - 1)
 
     def tie(left, right, *names):
         left, right, *due = lax.optimization_barrier((left, right, *[after[n] for n in names]))
@@ -332,48 +345,40 @@
         return left, right
 
     def between(hop, left, right):
-        if hop == 1:
-            left, right = tie(left, right, "own_gate", "own_up")
-            after["g3"] = from_shift(after["own_gate"], "x", nx - 1)
-            after["u1"] = from_shift(after["own_up"], "x", 1)
         if hop == 2:
-            left, right = tie(left, right, "g1", "u3")
+            left, right = tie(left, right, "g1", "g3")
             after["g2"] = from_shift(after["g1"], "x", 1)
-            after["u2"] = from_shift(after["u3"], "x", nx - 1)
-        if hop == 3:
-            left, right = tie(left, right, "g3", "u1", "down")
-            after["d1"] = from_shift(after["down"], "x", 1)
-            after["d3"] = from_shift(after["down"], "x", nx - 1)
         return left, right
 
     blocks = around(spread, "y", between)
-    near_weights = [after[n] for n in ("own_gate", "own_up", "g1", "u1", "g3", "u3", "g2", "u2")]
+    near_weights = [after[n] for n in ("own", "g1", "g3", "g2")]
     (hidden,) = call(
         hidden_body,
         [shape((ny, nx * units + units // 2 + 8, near * cap))],
-        [y_at, *blocks, *near_weights, shared_gate, shared_up],
+        [y_at, *blocks, *near_weights, shared_gate, shared_up, plane_tok],
         scalars=1,
-        far=(*range(1, len(RING)), *range(len(RING) + 1, len(RING) + 2 * nx + 3)),
+        far=range(1, len(RING) + nx + 4),
         scratch=[
-            pltpu.VMEM((lanes * width, near * cap + rows), BF16),
+            pltpu.VMEM((lanes * width, near * cap), BF16),
             pltpu.VMEM((2 * (nx + 1) * units, lanes * width), BF16),
-            pltpu.SemaphoreType.DMA((2 * nx + 2 + lanes,)),
+            pltpu.VMEM((lanes * width, rows), BF16),
+            pltpu.SemaphoreType.DMA((3 + 2 * nx + lanes,)),
         ],
         limit=56,
     )
-    hidden, d1, d3 = lax.optimization_barrier((hidden, after["d1"], after["d3"]))
-    d2 = [from_shift(d1[:half], "x", 1), from_shift(d3[half:], "x", nx - 1)]
+    hidden, d3 = lax.optimization_barrier((hidden, d3))
+    d2 = from_shift(d3, "x", nx - 1)
     all_hidden = exchange(hidden, "y")
     (returned,) = call(
         down_body,
         [shape((nx, near * half + ny * units, 2 * cap))],
-        [x_at, all_hidden, after["down"], d1, d3, *d2],
+        [x_at, all_hidden, own_down, d1, d3, d2],
         scalars=1,
-        far=range(2, 3 + nx),
+        far=range(2, 2 + nx),
         scratch=[
             pltpu.VMEM((lanes * units, near * cap), BF16),
             pltpu.VMEM((nx * width, lanes * units), BF16),
-            pltpu.SemaphoreType.DMA((nx + 1,)),
+            pltpu.SemaphoreType.DMA((nx,)),
         ],
         limit=40,
     )

time: 227 us -> 244 us (1.075)
  starting transfers between devices: 101 us -> 78.4 us
  waiting for transfers between devices: 54.3 us -> 70.3 us
  between operations: 1.2 us -> 14.4 us
  blocking collectives: 51.5 us -> 59.9 us
  local copies, waits for them, and re-layouts: 0.97 us -> 3.95 us
    ppermute x20 -> x13, waiting for transfers between devices: 16.3 us -> 35.9 us  [from_shift(): lax.ppermute(value, axis, [((i + shift) % count, i) for i in range(count)])]
    ppermute x20 -> x13, starting transfers between devices: 61.4 us -> 42.6 us  [from_shift(): lax.ppermute(value, axis, [((i + shift) % count, i) for i in range(count)])]
    all_to_all x0 -> x1, blocking collectives: none -> 11.6 us  [exchange(): return lax.all_to_all(value, axes, 0, 0, tiled=True)]
    all_to_all x5 -> x4, waiting for transfers between devices: 36.3 us -> 30 us  [exchange(): return lax.all_to_all(value, axes, 0, 0, tiled=True)]
    all_to_all x5 -> x4, starting transfers between devices: 29.6 us -> 25 us  [exchange(): return lax.all_to_all(value, axes, 0, 0, tiled=True)]
    all_to_all x1, blocking collectives: 24.1 us -> 20.9 us  [shards(): back = lax.all_to_all(back, LINE, 0, 0, tiled=True)]
    unnamed x36 -> x32, local copies, waits for them, and re-layouts: 0.09 us -> 3.1 us
    pallas_call x7 -> x8, Pallas kernels: 16.9 us -> 16 us  [call(): pl.pallas_call(body, out_shape=outs, in_specs=specs, out_specs=[pl.BlockS...]
  transfers between devices with their start and end apart: 27 -> 20, of which waited for: 15 -> 11; matrix products, arithmetic and copies ran while one was open for 0% -> 0% of each run, Pallas kernels for 4% -> 1%
where the time goes in v6:
time: 244 us; the launch traced here: 243 us
  starting transfers between devices  78.4 us (32%)
  waiting for transfers between devices  70.3 us (29%)
  blocking collectives  59.9 us (25%)
  Pallas kernels  16 us (7%)
  between operations  14.4 us (6%)
  local copies, waits for them, and re-layouts  3.95 us (2%)
    ppermute x13, starting transfers between devices, from_shift(): lax.ppermute(value, axis, [((i + shift) % count, i) for i in range(count)])  42.6 us
    ppermute x13, waiting for transfers between devices, from_shift(): lax.ppermute(value, axis, [((i + shift) % count, i) for i in range(count)])  35.9 us
    all_to_all x4, waiting for transfers between devices, exchange(): return lax.all_to_all(value, axes, 0, 0, tiled=True)  30 us
    all_to_all x2, blocking collectives, spread_all(): lax.all_to_all(jnp.broadcast_to(value[None], (count, *value.shape)), axes...  27.4 us
    all_to_all x4, starting transfers between devices, exchange(): return lax.all_to_all(value, axes, 0, 0, tiled=True)  25 us
    all_to_all x1, blocking collectives, shards(): back = lax.all_to_all(back, LINE, 0, 0, tiled=True)  20.9 us
    pallas_call x8, Pallas kernels, call(): pl.pallas_call(body, out_shape=outs, in_specs=specs, out_specs=[pl.BlockS...  16 us
    all_to_all x1, blocking collectives, exchange(): return lax.all_to_all(value, axes, 0, 0, tiled=True)  11.6 us
  transfers between devices with their start and end apart: 20, of which 11 were waited for; matrix products, arithmetic and copies ran while one was open for 0% of the time, Pallas kernels for 1%

profile of v6, /device:TPU:1, one launch (start us, length us, event | category | flops | bytes accessed | tf_op | source)
XLA Modules:
  0.0 243.1 jit_solution(10447395351749594302)
XLA Ops:
  7.2 2.2 shard_map.122
  9.4 11.8 %all-to-all-start = ((bf16[16,80,128]{2,1,0:T(8,128)(2,1)}), bf16[16,80,128]{2,1,0:T(8,128)(2,1)S(1)}, u32[]{:S(2)}, u32[]{:S(2)}) async-start(bf16[16,80,128]{2,1,0:T(8,128)(2,1)} %get-tuple-element.21), calls=%async_computation | async-start | bytes 655360 | tf_op jit(solution)/shard_map/all_to_all | solution.py:265
  21.2 0.0 all-gather.2.cloned.1.call-start
  21.3 0.7 all-gather.2.cloned.1.call-update
  21.9 4.4 %collective-permute-start = (bf16[160,1536]{1,0:T(8,128)(2,1)}, bf16[160,1536]{1,0:T(8,128)(2,1)S(1)}, u32[]{:S(2)}, u32[]{:S(2)}) collective-permute-start(bf16[160,1536]{1,0:T(8,128)(2,1)} %bitcast.24), channel_id=1, source_target_pairs={{8,0},{16,8},{24,16},{0,24},{9,1},{17,9},{25,17},{1,25},{10,2},{18... | collective-permute-start | bytes 1474568 | tf_op jit(solution)/shard_map/ppermute | solution.py:276
  26.4 1.9 collective-permute-start.1
  28.3 0.0 copy-start.4
  28.3 1.0 copy-done.4
  29.3 1.0 copy-done.5
  30.4 0.6 shard_map.123.refs_8_
  31.0 3.3 %all-to-all-done = bf16[16,80,128]{2,1,0:T(8,128)(2,1)S(1)} async-done(((bf16[16,80,128]{2,1,0:T(8,128)(2,1)}), bf16[16,80,128]{2,1,0:T(8,128)(2,1)S(1)}, u32[]{:S(2)}, u32[]{:S(2)}) %all-to-all-start) | async-done | bytes 327712 | tf_op jit(solution)/shard_map/all_to_all | solution.py:265
  34.3 11.6 %all_to_all.45.in_ref = bf16[4,320,128]{2,1,0:T(8,128)(2,1)S(1)} all-to-all(bf16[4,320,128]{2,1,0:T(8,128)(2,1)S(1)} %bitcast.30), channel_id=1, replica_groups=mesh['z'=8,'core'=2,'x'=4,'y'=8] {'x'}, dimensions={0} | all-to-all | bytes 655360 | tf_op jit(solution)/shard_map/all_to_all | solution.py:265
  45.9 0.2 shard_map.124.refs_0_
  46.0 0.0 collective-permute-done.refs_1_
  46.1 0.0 collective-permute-done.1.refs_2_
  46.1 2.8 %collective-permute-start.6 = (bf16[96,5120]{1,0:T(8,128)(2,1)S(1)}, bf16[96,5120]{1,0:T(8,128)(2,1)S(1)}, u32[]{:S(2)}, u32[]{:S(2)}) collective-permute-start(bf16[96,5120]{1,0:T(8,128)(2,1)S(1)} %shard_map.123.refs_8_), channel_id=1, source_target_pairs={{8,0},{16,8},{24,16},{0,24},{9,1},{17,9},{25,17},{1,25},{10,2},{18... | collective-permute-start | bytes 2949128 | tf_op jit(solution)/shard_map/ppermute | solution.py:276
  48.9 2.5 %collective-permute-start.7 = (bf16[96,5120]{1,0:T(8,128)(2,1)S(1)}, bf16[96,5120]{1,0:T(8,128)(2,1)S(1)}, u32[]{:S(2)}, u32[]{:S(2)}) collective-permute-start(bf16[96,5120]{1,0:T(8,128)(2,1)S(1)} %shard_map.123.refs_8_), channel_id=1, source_target_pairs={{24,0},{0,8},{8,16},{16,24},{25,1},{1,9},{9,17},{17,25},{26,2},{2,... | collective-permute-start | bytes 2949128 | tf_op jit(solution)/shard_map/ppermute | solution.py:276
  51.4 3.2 %collective-permute-start.2 = (bf16[640,256]{1,0:T(8,128)(2,1)S(1)}, bf16[640,256]{1,0:T(8,128)(2,1)S(1)}, u32[]{:S(2)}, u32[]{:S(2)}) collective-permute-start(bf16[640,256]{1,0:T(8,128)(2,1)S(1)} %shard_map.124.refs_0_), channel_id=1, source_target_pairs={{7,0},{0,1},{1,2},{2,3},{3,4},{4,5},{5,6},{6,7},{15,8},{8,9},{9,10... | collective-permute-start | bytes 983048 | tf_op jit(solution)/shard_map/ppermute | solution.py:276
  54.6 4.0 %collective-permute-start.3 = (bf16[640,256]{1,0:T(8,128)(2,1)S(1)}, bf16[640,256]{1,0:T(8,128)(2,1)S(1)}, u32[]{:S(2)}, u32[]{:S(2)}) collective-permute-start(bf16[640,256]{1,0:T(8,128)(2,1)S(1)} %shard_map.124.refs_0_), channel_id=1, source_target_pairs={{1,0},{2,1},{3,2},{4,3},{5,4},{6,5},{7,6},{0,7},{9,8},{10,9},{11,1... | collective-permute-start | bytes 983048 | tf_op jit(solution)/shard_map/ppermute | solution.py:276
  58.6 5.1 %collective-permute-done.2.refs_1_ = bf16[640,256]{1,0:T(8,128)(2,1)S(1)} collective-permute-done((bf16[640,256]{1,0:T(8,128)(2,1)S(1)}, bf16[640,256]{1,0:T(8,128)(2,1)S(1)}, u32[]{:S(2)}, u32[]{:S(2)}) %collective-permute-start.2) | collective-permute-done | bytes 327712 | tf_op jit(solution)/shard_map/ppermute | solution.py:276
  63.7 1.9 collective-permute-start.4
  65.6 0.0 collective-permute-done.3.refs_2_
  65.6 4.6 %collective-permute-start.5 = (bf16[640,256]{1,0:T(8,128)(2,1)S(1)}, bf16[640,256]{1,0:T(8,128)(2,1)}, u32[]{:S(2)}, u32[]{:S(2)}) collective-permute-start(bf16[640,256]{1,0:T(8,128)(2,1)S(1)} %collective-permute-done.3.refs_2_), channel_id=1, source_target_pairs={{1,0},{2,1},{3,2},{4,3},{5,4},{6,5},{7,6},{0,7},{9,8},{10,9},{11,1... | collective-permute-start | bytes 983048 | tf_op jit(solution)/shard_map/ppermute | solution.py:276
  70.2 3.6 %collective-permute-done.4.refs_3_ = bf16[640,256]{1,0:T(8,128)(2,1)S(1)} collective-permute-done((bf16[640,256]{1,0:T(8,128)(2,1)S(1)}, bf16[640,256]{1,0:T(8,128)(2,1)S(1)}, u32[]{:S(2)}, u32[]{:S(2)}) %collective-permute-start.4) | collective-permute-done | bytes 327712 | tf_op jit(solution)/shard_map/ppermute | solution.py:276
  73.8 0.9 collective-permute-done.5.refs_4_
  74.7 0.0 collective-permute-done.6.refs_9_
  74.7 0.0 collective-permute-done.7.refs_10_
  74.7 1.0 copy-done.11
  75.7 5.1 %collective-permute-start.11 = (bf16[96,5120]{1,0:T(8,128)(2,1)S(1)}, bf16[96,5120]{1,0:T(8,128)(2,1)}, u32[]{:S(2)}, u32[]{:S(2)}) collective-permute-start(bf16[96,5120]{1,0:T(8,128)(2,1)S(1)} %collective-permute-done.6.refs_9_), channel_id=1, source_target_pairs={{8,0},{16,8},{24,16},{0,24},{9,1},{17,9},{25,17},{1,25},{10,2},{18... | collective-permute-start | bytes 2949128 | tf_op jit(solution)/shard_map/ppermute | solution.py:276
  80.8 2.7 %collective-permute-start.8 = (bf16[640,256]{1,0:T(8,128)(2,1)S(1)}, bf16[640,256]{1,0:T(8,128)(2,1)}, u32[]{:S(2)}, u32[]{:S(2)}) collective-permute-start(bf16[640,256]{1,0:T(8,128)(2,1)S(1)} %collective-permute-done.4.refs_3_), channel_id=1, source_target_pairs={{7,0},{0,1},{1,2},{2,3},{3,4},{4,5},{5,6},{6,7},{15,8},{8,9},{9,10... | collective-permute-start | bytes 983048 | tf_op jit(solution)/shard_map/ppermute | solution.py:276
  83.5 4.7 %collective-permute-start.9 = (bf16[640,256]{1,0:T(8,128)(2,1)}, bf16[640,256]{1,0:T(8,128)(2,1)}, u32[]{:S(2)}, u32[]{:S(2)}) collective-permute-start(bf16[640,256]{1,0:T(8,128)(2,1)} %collective-permute-done.5.refs_4_), channel_id=1, source_target_pairs={{1,0},{2,1},{3,2},{4,3},{5,4},{6,5},{7,6},{0,7},{9,8},{10,9},{11,1... | collective-permute-start | bytes 983048 | tf_op jit(solution)/shard_map/ppermute | solution.py:276
  88.2 5.3 %collective-permute-done.8.refs_5_ = bf16[640,256]{1,0:T(8,128)(2,1)} collective-permute-done((bf16[640,256]{1,0:T(8,128)(2,1)S(1)}, bf16[640,256]{1,0:T(8,128)(2,1)}, u32[]{:S(2)}, u32[]{:S(2)}) %collective-permute-start.8) | collective-permute-done | bytes 327712 | tf_op jit(solution)/shard_map/ppermute | solution.py:276
  93.4 1.9 collective-permute-start.10
  95.4 10.0 %collective-permute-done.10.refs_7_ = bf16[640,256]{1,0:T(8,128)(2,1)} collective-permute-done((bf16[640,256]{1,0:T(8,128)(2,1)}, bf16[640,256]{1,0:T(8,128)(2,1)}, u32[]{:S(2)}, u32[]{:S(2)}) %collective-permute-start.10) | collective-permute-done | bytes 327712 | tf_op jit(solution)/shard_map/ppermute | solution.py:276
  105.4 6.0 %shard_map.125 = bf16[8,224,256]{2,1,0:T(8,128)(2,1)} custom-call(s32[1]{0:T(128)} %bitcast.4.y_ref, bf16[640,256]{1,0:T(8,128)(2,1)} %copy-done.1, bf16[640,256]{1,0:T(8,128)(2,1)} %copy-done.12, bf16[640,256]{1,0:T(8,128)(2,1)} %copy-done.13, bf16[640,256]{1,0:T(8,128)(2,1)} %copy-done.14, bf16[640,256]{1,0:T(8,128)(2,1)} %collective-permute-done.5.refs_4_, ...), custom_call_target="tpu_custom_call" | custom-call | bytes 9764868 | tf_op jit(solution)/shard_map/pallas_call | solution.py:23
  111.4 0.0 copy-start.6
  111.4 5.9 %all-to-all-start.2 = ((bf16[8,224,256]{2,1,0:T(8,128)(2,1)}), bf16[8,224,256]{2,1,0:T(8,128)(2,1)S(1)}, u32[]{:S(2)}, u32[]{:S(2)}) async-start(bf16[8,224,256]{2,1,0:T(8,128)(2,1)} %shard_map.125), calls=%async_computation.2 | async-start | bytes 1835008 | tf_op jit(solution)/shard_map/all_to_all | solution.py:265
  117.3 3.0 %collective-permute-start.12 = (bf16[160,1536]{1,0:T(8,128)(2,1)S(1)}, bf16[160,1536]{1,0:T(8,128)(2,1)S(1)}, u32[]{:S(2)}, u32[]{:S(2)}) collective-permute-start(bf16[160,1536]{1,0:T(8,128)(2,1)S(1)} %collective-permute-done.1.refs_2_), channel_id=1, source_target_pairs={{24,0},{0,8},{8,16},{16,24},{25,1},{1,9},{9,17},{17,25},{26,2},{2,... | collective-permute-start | bytes 1474568 | tf_op jit(solution)/shard_map/ppermute | solution.py:276
  120.3 11.0 %collective-permute-done.12.refs_3_ = bf16[160,1536]{1,0:T(8,128)(2,1)S(1)} collective-permute-done((bf16[160,1536]{1,0:T(8,128)(2,1)S(1)}, bf16[160,1536]{1,0:T(8,128)(2,1)S(1)}, u32[]{:S(2)}, u32[]{:S(2)}) %collective-permute-start.12) | collective-permute-done | bytes 491552 | tf_op jit(solution)/shard_map/ppermute | solution.py:276
  131.4 9.2 %all-to-all-done.2.hidden_ref = bf16[8,224,256]{2,1,0:T(8,128)(2,1)S(1)} async-done(((bf16[8,224,256]{2,1,0:T(8,128)(2,1)}), bf16[8,224,256]{2,1,0:T(8,128)(2,1)S(1)}, u32[]{:S(2)}, u32[]{:S(2)}) %all-to-all-start.2) | async-done | bytes 917536 | tf_op jit(solution)/shard_map/all_to_all | solution.py:265
  140.5 3.0 %shard_map.126 = bf16[4,704,128]{2,1,0:T(8,128)(2,1)} custom-call(s32[1]{0:T(128)} %bitcast.3.x_ref, bf16[8,224,256]{2,1,0:T(8,128)(2,1)S(1)} %all-to-all-done.2.hidden_ref, bf16[160,1536]{1,0:T(8,128)(2,1)S(1)} %bitcast.26, bf16[160,1536]{1,0:T(8,128)(2,1)S(1)} %collective-permute-done.refs_1_, bf16[160,1536]{1,0:T(8,128)(2,1)S(1)} %collective-permute-done.1.refs_2_, ...), custom_call_target="tpu_custom_call" | custom-call | bytes 3604484 | tf_op jit(solution)/shard_map/pallas_call | solution.py:23
  143.5 0.0 copy-start.2
  143.5 0.0 copy-start.7
  143.5 0.0 copy-start.8
  143.6 6.0 %all-to-all-start.3 = ((bf16[4,704,128]{2,1,0:T(8,128)(2,1)}), bf16[4,704,128]{2,1,0:T(8,128)(2,1)S(1)}, u32[]{:S(2)}, u32[]{:S(2)}) async-start(bf16[4,704,128]{2,1,0:T(8,128)(2,1)} %shard_map.126), calls=%async_computation.3 | async-start | bytes 1441792 | tf_op jit(solution)/shard_map/all_to_all | solution.py:385
  149.6 4.8 %collective-permute-start.13 = (bf16[128,5120]{1,0:T(8,128)(2,1)S(1)}, bf16[128,5120]{1,0:T(8,128)(2,1)S(1)}, u32[]{:S(2)}, u32[]{:S(2)}) collective-permute-start(bf16[128,5120]{1,0:T(8,128)(2,1)S(1)} %copy-done.2), channel_id=1, source_target_pairs={{0,32},{32,0},{1,33},{33,1},{2,34},{34,2},{3,35},{35,3},{4,36},{36... | collective-permute-start | bytes 3932168 | tf_op jit(solution)/shard_map/ppermute | solution.py:403
  154.3 3.7 %all-to-all-done.3.hidden_ref = bf16[4,704,128]{2,1,0:T(8,128)(2,1)S(1)} async-done(((bf16[4,704,128]{2,1,0:T(8,128)(2,1)}), bf16[4,704,128]{2,1,0:T(8,128)(2,1)S(1)}, u32[]{:S(2)}, u32[]{:S(2)}) %all-to-all-start.3) | async-done | bytes 720928 | tf_op jit(solution)/shard_map/all_to_all | solution.py:385
  158.1 20.9 %all_to_all.46.back_ref = bf16[16,80,128]{2,1,0:T(8,128)(2,1)S(1)} all-to-all(bf16[16,80,128]{2,1,0:T(8,128)(2,1)S(1)} %bitcast.31), channel_id=1, replica_groups=mesh['z'=8,'core'=2,'x'=4,'y'=8] {'z','core'}, dimensions={0} | all-to-all | bytes 655360 | tf_op jit(solution)/shard_map/all_to_all | solution.py:387
  179.0 0.0 copy-start.15
  179.0 1.4 shard_map.127
  180.4 3.4 %all-to-all-start.5 = ((bf16[16,4,160]{2,1,0:T(4,128)(2,1)}), bf16[16,4,160]{2,1,0:T(4,128)(2,1)S(1)}, u32[]{:S(2)}, u32[]{:S(2)}) async-start(bf16[16,4,160]{2,1,0:T(4,128)(2,1)} %get-tuple-element.35), calls=%async_computation.5 | async-start | bytes 65536 | tf_op jit(solution)/shard_map/all_to_all | solution.py:265
  183.8 6.9 %all-to-all-done.5 = bf16[16,4,160]{2,1,0:T(4,128)(2,1)S(1)} async-done(((bf16[16,4,160]{2,1,0:T(4,128)(2,1)}), bf16[16,4,160]{2,1,0:T(4,128)(2,1)S(1)}, u32[]{:S(2)}, u32[]{:S(2)}) %all-to-all-start.5) | async-done | bytes 20512 | tf_op jit(solution)/shard_map/all_to_all | solution.py:265
  190.8 1.0 shard_map.128
  191.8 3.9 %all-to-all-start.6 = ((bf16[32,40,128]{2,1,0:T(8,128)(2,1)}), bf16[32,40,128]{2,1,0:T(8,128)(2,1)S(1)}, u32[]{:S(2)}, u32[]{:S(2)}) async-start(bf16[32,40,128]{2,1,0:T(8,128)(2,1)} %shard_map.128), calls=%async_computation.6 | async-start | bytes 655360 | tf_op jit(solution)/shard_map/all_to_all | solution.py:265
  195.7 0.1 tile.10
  195.8 0.1 tile.12.targets_ref
  195.9 0.1 pad_add_fusion.at_ref
  196.0 0.0 collective-permute-done.13.other_ref
  196.0 10.6 %all-to-all-done.6.rows_ref = bf16[32,40,128]{2,1,0:T(8,128)(2,1)S(1)} async-done(((bf16[32,40,128]{2,1,0:T(8,128)(2,1)}), bf16[32,40,128]{2,1,0:T(8,128)(2,1)S(1)}, u32[]{:S(2)}, u32[]{:S(2)}) %all-to-all-start.6) | async-done | bytes 327712 | tf_op jit(solution)/shard_map/all_to_all | solution.py:265
  206.6 1.6 shard_map.129
  208.2 15.6 %all_to_all.47 = f32[32,1,128]{2,1,0:T(1,128)S(1)} all-to-all(f32[32,1,128]{2,1,0:T(1,128)S(1)} %broadcast_in_dim.7), channel_id=1, replica_groups=mesh['z'=8,'core'=2,'x'=4,'y'=8] {'x','y'}, dimensions={0} | all-to-all | bytes 32768 | tf_op jit(solution)/shard_map/all_to_all | solution.py:269
  223.8 11.8 %all_to_all.48 = f32[16,1,128]{2,1,0:T(1,128)S(1)} all-to-all(f32[16,1,128]{2,1,0:T(1,128)S(1)} %broadcast_in_dim.16), channel_id=1, replica_groups=mesh['z'=8,'core'=2,'x'=4,'y'=8] {'z','core'}, dimensions={0} | all-to-all | bytes 16384 | tf_op jit(solution)/shard_map/all_to_all | solution.py:269
  235.6 0.1 log_subtract_fusion
  235.7 0.6 reshape.44
  (34 shorter events, 0.2 us)
Async XLA Ops:
  9.4 24.9 %all-to-all-start = ((bf16[16,80,128]{2,1,0:T(8,128)(2,1)}), bf16[16,80,128]{2,1,0:T(8,128)(2,1)S(1)}, u32[]{:S(2)}, u32[]{:S(2)}) async-start(bf16[16,80,128]{2,1,0:T(8,128)(2,1)} %get-tuple-element.21), calls=%async_computation | async-start | bytes 655360 | tf_op jit(solution)/shard_map/all_to_all | solution.py:265
  21.2 84.1 %all-gather.2.cloned.1.call-start = ((), (), s32[]{:S(2)}) async-start(), calls=%async_computation.9 | async-start | bytes 1351680 | tf_op jit(solution)/shard_map/all_gather | solution.py:323
  21.9 24.1 %collective-permute-start = (bf16[160,1536]{1,0:T(8,128)(2,1)}, bf16[160,1536]{1,0:T(8,128)(2,1)S(1)}, u32[]{:S(2)}, u32[]{:S(2)}) collective-permute-start(bf16[160,1536]{1,0:T(8,128)(2,1)} %bitcast.24), channel_id=1, source_target_pairs={{8,0},{16,8},{24,16},{0,24},{9,1},{17,9},{25,17},{1,25},{10,2},{18... | collective-permute-start | bytes 1474568 | tf_op jit(solution)/shard_map/ppermute | solution.py:276
  26.4 19.7 %collective-permute-start.1 = (bf16[160,1536]{1,0:T(8,128)(2,1)}, bf16[160,1536]{1,0:T(8,128)(2,1)S(1)}, u32[]{:S(2)}, u32[]{:S(2)}) collective-permute-start(bf16[160,1536]{1,0:T(8,128)(2,1)} %bitcast.25), channel_id=1, source_target_pairs={{24,0},{0,8},{8,16},{16,24},{25,1},{1,9},{9,17},{17,25},{26,2},{2,... | collective-permute-start | bytes 1474568 | tf_op jit(solution)/shard_map/ppermute | solution.py:276
  28.3 1.0 copy-start.4
  29.3 1.0 copy-start.5
  31.0 74.4 %copy-start = (bf16[96,5120]{1,0:T(8,128)(2,1)}, bf16[96,5120]{1,0:T(8,128)(2,1)S(1)}, u32[]{:S(2)}) copy-start(bf16[96,5120]{1,0:T(8,128)(2,1)S(1)} %shard_map.123.refs_8_) | copy-start | bytes 2949124
  46.0 59.3 %copy-start.1 = (bf16[640,256]{1,0:T(8,128)(2,1)}, bf16[640,256]{1,0:T(8,128)(2,1)S(1)}, u32[]{:S(2)}) copy-start(bf16[640,256]{1,0:T(8,128)(2,1)S(1)} %shard_map.124.refs_0_) | copy-start | bytes 983044
  46.1 28.6 %collective-permute-start.6 = (bf16[96,5120]{1,0:T(8,128)(2,1)S(1)}, bf16[96,5120]{1,0:T(8,128)(2,1)S(1)}, u32[]{:S(2)}, u32[]{:S(2)}) collective-permute-start(bf16[96,5120]{1,0:T(8,128)(2,1)S(1)} %shard_map.123.refs_8_), channel_id=1, source_target_pairs={{8,0},{16,8},{24,16},{0,24},{9,1},{17,9},{25,17},{1,25},{10,2},{18... | collective-permute-start | bytes 2949128 | tf_op jit(solution)/shard_map/ppermute | solution.py:276
  48.9 25.9 %collective-permute-start.7 = (bf16[96,5120]{1,0:T(8,128)(2,1)S(1)}, bf16[96,5120]{1,0:T(8,128)(2,1)S(1)}, u32[]{:S(2)}, u32[]{:S(2)}) collective-permute-start(bf16[96,5120]{1,0:T(8,128)(2,1)S(1)} %shard_map.123.refs_8_), channel_id=1, source_target_pairs={{24,0},{0,8},{8,16},{16,24},{25,1},{1,9},{9,17},{17,25},{26,2},{2,... | collective-permute-start | bytes 2949128 | tf_op jit(solution)/shard_map/ppermute | solution.py:276
  51.4 12.3 %collective-permute-start.2 = (bf16[640,256]{1,0:T(8,128)(2,1)S(1)}, bf16[640,256]{1,0:T(8,128)(2,1)S(1)}, u32[]{:S(2)}, u32[]{:S(2)}) collective-permute-start(bf16[640,256]{1,0:T(8,128)(2,1)S(1)} %shard_map.124.refs_0_), channel_id=1, source_target_pairs={{7,0},{0,1},{1,2},{2,3},{3,4},{4,5},{5,6},{6,7},{15,8},{8,9},{9,10... | collective-permute-start | bytes 983048 | tf_op jit(solution)/shard_map/ppermute | solution.py:276
  54.6 11.0 %collective-permute-start.3 = (bf16[640,256]{1,0:T(8,128)(2,1)S(1)}, bf16[640,256]{1,0:T(8,128)(2,1)S(1)}, u32[]{:S(2)}, u32[]{:S(2)}) collective-permute-start(bf16[640,256]{1,0:T(8,128)(2,1)S(1)} %shard_map.124.refs_0_), channel_id=1, source_target_pairs={{1,0},{2,1},{3,2},{4,3},{5,4},{6,5},{7,6},{0,7},{9,8},{10,9},{11,1... | collective-permute-start | bytes 983048 | tf_op jit(solution)/shard_map/ppermute | solution.py:276
  63.7 17.1 %copy-start.12 = (bf16[640,256]{1,0:T(8,128)(2,1)}, bf16[640,256]{1,0:T(8,128)(2,1)S(1)}, u32[]{:S(2)}) copy-start(bf16[640,256]{1,0:T(8,128)(2,1)S(1)} %collective-permute-done.2.refs_1_) | copy-start | bytes 983044
  63.7 10.1 %collective-permute-start.4 = (bf16[640,256]{1,0:T(8,128)(2,1)S(1)}, bf16[640,256]{1,0:T(8,128)(2,1)S(1)}, u32[]{:S(2)}, u32[]{:S(2)}) collective-permute-start(bf16[640,256]{1,0:T(8,128)(2,1)S(1)} %collective-permute-done.2.refs_1_), channel_id=1, source_target_pairs={{7,0},{0,1},{1,2},{2,3},{3,4},{4,5},{5,6},{6,7},{15,8},{8,9},{9,10... | collective-permute-start | bytes 983048 | tf_op jit(solution)/shard_map/ppermute | solution.py:276
  65.6 17.8 %copy-start.13 = (bf16[640,256]{1,0:T(8,128)(2,1)}, bf16[640,256]{1,0:T(8,128)(2,1)S(1)}, u32[]{:S(2)}) copy-start(bf16[640,256]{1,0:T(8,128)(2,1)S(1)} %collective-permute-done.3.refs_2_) | copy-start | bytes 983044
  65.6 9.1 %collective-permute-start.5 = (bf16[640,256]{1,0:T(8,128)(2,1)S(1)}, bf16[640,256]{1,0:T(8,128)(2,1)}, u32[]{:S(2)}, u32[]{:S(2)}) collective-permute-start(bf16[640,256]{1,0:T(8,128)(2,1)S(1)} %collective-permute-done.3.refs_2_), channel_id=1, source_target_pairs={{1,0},{2,1},{3,2},{4,3},{5,4},{6,5},{7,6},{0,7},{9,8},{10,9},{11,1... | collective-permute-start | bytes 983048 | tf_op jit(solution)/shard_map/ppermute | solution.py:276
  73.8 14.4 %copy-start.14 = (bf16[640,256]{1,0:T(8,128)(2,1)}, bf16[640,256]{1,0:T(8,128)(2,1)S(1)}, u32[]{:S(2)}) copy-start(bf16[640,256]{1,0:T(8,128)(2,1)S(1)} %collective-permute-done.4.refs_3_) | copy-start | bytes 983044
  74.7 30.7 %copy-start.10 = (bf16[96,5120]{1,0:T(8,128)(2,1)}, bf16[96,5120]{1,0:T(8,128)(2,1)S(1)}, u32[]{:S(2)}) copy-start(bf16[96,5120]{1,0:T(8,128)(2,1)S(1)} %collective-permute-done.6.refs_9_) | copy-start | bytes 2949124
  74.7 1.0 copy-start.11
  75.7 29.7 %collective-permute-start.11 = (bf16[96,5120]{1,0:T(8,128)(2,1)S(1)}, bf16[96,5120]{1,0:T(8,128)(2,1)}, u32[]{:S(2)}, u32[]{:S(2)}) collective-permute-start(bf16[96,5120]{1,0:T(8,128)(2,1)S(1)} %collective-permute-done.6.refs_9_), channel_id=1, source_target_pairs={{8,0},{16,8},{24,16},{0,24},{9,1},{17,9},{25,17},{1,25},{10,2},{18... | collective-permute-start | bytes 2949128 | tf_op jit(solution)/shard_map/ppermute | solution.py:276
  80.8 12.7 %collective-permute-start.8 = (bf16[640,256]{1,0:T(8,128)(2,1)S(1)}, bf16[640,256]{1,0:T(8,128)(2,1)}, u32[]{:S(2)}, u32[]{:S(2)}) collective-permute-start(bf16[640,256]{1,0:T(8,128)(2,1)S(1)} %collective-permute-done.4.refs_3_), channel_id=1, source_target_pairs={{7,0},{0,1},{1,2},{2,3},{3,4},{4,5},{5,6},{6,7},{15,8},{8,9},{9,10... | collective-permute-start | bytes 983048 | tf_op jit(solution)/shard_map/ppermute | solution.py:276
  83.5 11.9 %collective-permute-start.9 = (bf16[640,256]{1,0:T(8,128)(2,1)}, bf16[640,256]{1,0:T(8,128)(2,1)}, u32[]{:S(2)}, u32[]{:S(2)}) collective-permute-start(bf16[640,256]{1,0:T(8,128)(2,1)} %collective-permute-done.5.refs_4_), channel_id=1, source_target_pairs={{1,0},{2,1},{3,2},{4,3},{5,4},{6,5},{7,6},{0,7},{9,8},{10,9},{11,1... | collective-permute-start | bytes 983048 | tf_op jit(solution)/shard_map/ppermute | solution.py:276
  93.4 11.9 %collective-permute-start.10 = (bf16[640,256]{1,0:T(8,128)(2,1)}, bf16[640,256]{1,0:T(8,128)(2,1)}, u32[]{:S(2)}, u32[]{:S(2)}) collective-permute-start(bf16[640,256]{1,0:T(8,128)(2,1)} %collective-permute-done.8.refs_5_), channel_id=1, source_target_pairs={{7,0},{0,1},{1,2},{2,3},{3,4},{4,5},{5,6},{6,7},{15,8},{8,9},{9,10... | collective-permute-start | bytes 983048 | tf_op jit(solution)/shard_map/ppermute | solution.py:276
  111.4 29.1 %copy-start.6 = (bf16[1,1536,160]{1,2,0:T(8,128)(2,1)S(1)}, bf16[1,1536,160]{1,2,0:T(8,128)(2,1)}, u32[]{:S(2)}) copy-start(bf16[1,1536,160]{1,2,0:T(8,128)(2,1)} %param.16) | copy-start | bytes 1474564
  111.4 29.1 %all-to-all-start.2 = ((bf16[8,224,256]{2,1,0:T(8,128)(2,1)}), bf16[8,224,256]{2,1,0:T(8,128)(2,1)S(1)}, u32[]{:S(2)}, u32[]{:S(2)}) async-start(bf16[8,224,256]{2,1,0:T(8,128)(2,1)} %shard_map.125), calls=%async_computation.2 | async-start | bytes 1835008 | tf_op jit(solution)/shard_map/all_to_all | solution.py:265
  117.3 14.1 %collective-permute-start.12 = (bf16[160,1536]{1,0:T(8,128)(2,1)S(1)}, bf16[160,1536]{1,0:T(8,128)(2,1)S(1)}, u32[]{:S(2)}, u32[]{:S(2)}) collective-permute-start(bf16[160,1536]{1,0:T(8,128)(2,1)S(1)} %collective-permute-done.1.refs_2_), channel_id=1, source_target_pairs={{24,0},{0,8},{8,16},{16,24},{25,1},{1,9},{9,17},{17,25},{26,2},{2,... | collective-permute-start | bytes 1474568 | tf_op jit(solution)/shard_map/ppermute | solution.py:276
  143.5 6.0 %copy-start.2 = (bf16[128,5120]{1,0:T(8,128)(2,1)S(1)}, bf16[128,5120]{1,0:T(8,128)(2,1)}, u32[]{:S(2)}) copy-start(bf16[128,5120]{1,0:T(8,128)(2,1)} %vocab_ref.1) | copy-start | bytes 3932164
  143.5 35.5 %copy-start.7 = (bf16[128,160]{0,1:T(8,128)(2,1)S(1)}, bf16[128,160]{0,1:T(8,128)(2,1)}, u32[]{:S(2)}) copy-start(bf16[128,160]{0,1:T(8,128)(2,1)} %param.11) | copy-start | bytes 122884
  143.5 35.5 %copy-start.8 = (s32[16,128]{1,0:T(8,128)S(1)}, s32[16,128]{1,0:T(8,128)}, u32[]{:S(2)}) copy-start(s32[16,128]{1,0:T(8,128)} %get-tuple-element.19.slot_ref) | copy-start | bytes 24580
  143.6 35.5 %copy-start.9 = (f32[16,128]{1,0:T(8,128)S(1)}, f32[16,128]{1,0:T(8,128)}, u32[]{:S(2)}) copy-start(f32[16,128]{1,0:T(8,128)} %get-tuple-element.20.gate_ref) | copy-start | bytes 24580
  143.6 14.5 %all-to-all-start.3 = ((bf16[4,704,128]{2,1,0:T(8,128)(2,1)}), bf16[4,704,128]{2,1,0:T(8,128)(2,1)S(1)}, u32[]{:S(2)}, u32[]{:S(2)}) async-start(bf16[4,704,128]{2,1,0:T(8,128)(2,1)} %shard_map.126), calls=%async_computation.3 | async-start | bytes 1441792 | tf_op jit(solution)/shard_map/all_to_all | solution.py:385
  149.6 46.4 %collective-permute-start.13 = (bf16[128,5120]{1,0:T(8,128)(2,1)S(1)}, bf16[128,5120]{1,0:T(8,128)(2,1)S(1)}, u32[]{:S(2)}, u32[]{:S(2)}) collective-permute-start(bf16[128,5120]{1,0:T(8,128)(2,1)S(1)} %copy-done.2), channel_id=1, source_target_pairs={{0,32},{32,0},{1,33},{33,1},{2,34},{34,2},{3,35},{35,3},{4,36},{36... | collective-permute-start | bytes 3932168 | tf_op jit(solution)/shard_map/ppermute | solution.py:403
  158.0 21.0 %copy-start.3 = (bf16[1536,160]{0,1:T(8,128)(2,1)S(1)}, bf16[1536,160]{0,1:T(8,128)(2,1)}, u32[]{:S(2)}) copy-start(bf16[1536,160]{0,1:T(8,128)(2,1)} %param.19) | copy-start | bytes 1474564
  179.0 16.7 %copy-start.15 = (s32[64]{0:T(128)S(1)}, s32[64]{0:T(128)}, u32[]{:S(2)}) copy-start(s32[64]{0:T(128)} %param.21) | copy-start | bytes 772
  180.4 10.3 %all-to-all-start.5 = ((bf16[16,4,160]{2,1,0:T(4,128)(2,1)}), bf16[16,4,160]{2,1,0:T(4,128)(2,1)S(1)}, u32[]{:S(2)}, u32[]{:S(2)}) async-start(bf16[16,4,160]{2,1,0:T(4,128)(2,1)} %get-tuple-element.35), calls=%async_computation.5 | async-start | bytes 65536 | tf_op jit(solution)/shard_map/all_to_all | solution.py:265
  191.8 14.7 %all-to-all-start.6 = ((bf16[32,40,128]{2,1,0:T(8,128)(2,1)}), bf16[32,40,128]{2,1,0:T(8,128)(2,1)S(1)}, u32[]{:S(2)}, u32[]{:S(2)}) async-start(bf16[32,40,128]{2,1,0:T(8,128)(2,1)} %shard_map.128), calls=%async_computation.6 | async-start | bytes 655360 | tf_op jit(solution)/shard_map/all_to_all | solution.py:265
Sparse Core Ops, SparseCore 0:
  25.2 79.9 all-gather.1

commit v7 on v5

--- a/solution.py
+++ b/solution.py
@@ -7,10 +7,12 @@
 from jax.sharding import PartitionSpec as P
 
 SCORE_E = 4
+EIGHT = 8
 F32 = jnp.float32
 BF16 = jnp.bfloat16
 LINE = ("z", "core")
 PLANE = ("x", "y")
+BOTH = ("z", "core", "x")
 
 
 def call(body, outs, args, scalars=0, far=(), scratch=(), limit=16):
@@ -54,14 +56,32 @@
     return lax.broadcasted_iota(jnp.int32, dims, axis)
 
 
-def pair_low(a, b, half):
-    lane = iota(a.shape, 1)
-    return jnp.where(lane < half, a, pltpu.roll(b, half, 1))
-
-
-def pair_high(a, b, half):
-    lane = iota(a.shape, 1)
-    return jnp.where(lane < half, pltpu.roll(a, half, 1), b)
+class Fold:
+    def __init__(self, width, lanes, near):
+        self.width, self.lanes, self.near = width, lanes, near
+        self.rest = width - lanes
+        self.parts = lanes // self.rest
+        self.per = near // self.parts
+        self.lines = near + EIGHT
+
+    def to_lines(self, rows, axis):
+        dims = (rows // self.near * EIGHT, rows)
+        dims = dims if axis == 0 else dims[::-1]
+        line, row = iota(dims, axis), iota(dims, 1 - axis)
+        same = lax.div(line, EIGHT) == lax.div(row, self.near)
+        hit = same & (lax.rem(line, EIGHT) == lax.rem(row, self.per))
+        return hit
+
+    def part_of(self, row):
+        return lax.div(lax.rem(row, self.near), self.per)
+
+
+def bf(mask):
+    return jnp.where(mask, 1.0, 0.0).astype(BF16)
+
+
+def tn(a, b):
+    return lax.dot_general(a, b, (((0,), (0,)), ((), ())), preferred_element_type=F32)
 
 
 def routing(routes_ref, gates_ref, experts):
@@ -82,39 +102,56 @@
     pairs = [(routes_far, routes_ref), (gates_far, gates_ref), (tok_far, tok_ref)]
     for copy in fetch(pairs, sems):
         copy.wait()
-    experts, half, lanes = out_ref.shape
-    rows = tok_ref.shape[1]
-    cap = lanes // 2
+    experts = slot_ref.shape[0]
+    width, rows = tok_ref.shape
+    lanes = out_ref.shape[2]
+    near = out_ref.shape[1] - EIGHT
+    fold = Fold(width, lanes, near)
+    cap = out_ref.shape[0] // experts * near
     slot, gate = routing(routes_ref, gates_ref, experts)
     slot_ref[...] = slot
     gate_ref[...] = gate
-    tok = jnp.concatenate([tok_ref[:half, :], tok_ref[half:, :]], axis=1)
-    place = iota((lanes, rows), 0)
-    place = jnp.where(place < cap, place, place - cap)
-    low = iota((lanes, rows), 0) < cap
-    for e in range(experts):
-        sel = jnp.where(slot[e : e + 1, :] == place, 1.0, 0.0)
-        sel = jnp.concatenate([jnp.where(low, sel, 0.0), jnp.where(low, 0.0, sel)], axis=1)
-        out_ref[e] = nt(tok, sel.astype(BF16)).astype(BF16)
+    tok = tok_ref[...]
+    tok = jnp.concatenate([tok[:lanes]] + [tok[lanes:]] * fold.parts, axis=0)
+    place = iota((cap, rows), 0)
+    several = 2 * lanes // cap
+    lines = bf(fold.to_lines(several * cap, 0))
+    dims = (several * cap, lanes)
+    own_part = fold.part_of(iota(dims, 0)) == lax.div(iota(dims, 1), fold.rest)
+    for first in range(0, experts, several):
+        sel = jnp.concatenate([bf(slot[e : e + 1, :] == place) for e in range(first, first + several)], axis=0)
+        out = nt(sel, tok)
+        rest = nn(lines, jnp.where(own_part, out[:, lanes:], 0.0).astype(BF16))
+        for n in range(several * cap // near):
+            piece = first * cap // near + n
+            out_ref[piece, :near, :] = out[n * near : (n + 1) * near, :lanes].astype(BF16)
+            out_ref[piece, near:, :] = rest[n * EIGHT : (n + 1) * EIGHT, :].astype(BF16)
 
 
 def spread_body(x_ref, in_ref, *refs):
     *tokens, out_ref = refs
-    lanes_x, _, lanes = in_ref.shape
-    width = out_ref.shape[0] // lanes_x
-    half, cap = width // 2, lanes // 2
-    groups = in_ref.shape[1] // half
-    for x in range(lanes_x):
-        top, mid, end = x * width, x * width + half, (x + 1) * width
-        for q in range(groups // 2):
-            a = in_ref[x, 2 * q * half : (2 * q + 1) * half, :].astype(F32)
-            b = in_ref[x, (2 * q + 1) * half : (2 * q + 2) * half, :].astype(F32)
-            cols = slice(q * lanes, (q + 1) * lanes)
-            out_ref[top:mid, cols] = pair_low(a, b, cap).astype(BF16)
-            out_ref[mid:end, cols] = pair_high(a, b, cap).astype(BF16)
+    nx = len(tokens)
+    width, rows = tokens[0].shape
+    lanes = in_ref.shape[2]
+    near = in_ref.shape[1] - EIGHT
+    groups = in_ref.shape[0] // nx
+    fold = Fold(width, lanes, near)
+    count = groups * near
+    eye = bf(iota((count, count), 0) == iota((count, count), 1))
+    lines = fold.to_lines(count, 0)
+    part = fold.part_of(iota(lines.shape, 1))
+    takes = [bf(lines & (part == q)) for q in range(fold.parts)]
+    for x in range(nx):
+        full = jnp.concatenate([in_ref[g * nx + x, :near, :] for g in range(groups)], axis=0)
+        rest = jnp.concatenate([in_ref[g * nx + x, near:, :].astype(F32) for g in range(groups)], axis=0).astype(BF16)
+        out_ref[x * width : x * width + lanes, :count] = tn(full, eye).astype(BF16)
+        tail = jnp.zeros((fold.rest, count), F32)
+        for q, take in enumerate(takes):
+            tail = tail + tn(rest, take)[q * fold.rest : (q + 1) * fold.rest]
+        out_ref[x * width + lanes : (x + 1) * width, :count] = tail.astype(BF16)
     for tok, shift in zip(tokens, SHIFTS):
-        at = pl.multiple_of(lax.rem(x_ref[0] + shift, lanes_x) * width, width)
-        out_ref[pl.ds(at, width), groups * cap :] = tok[...]
+        at = pl.multiple_of(lax.rem(x_ref[0] + shift, nx) * width, width)
+        out_ref[pl.ds(at, width), count:] = tok[...]
 
 
 def glu(gate, up):
@@ -154,65 +191,95 @@
 
 
 def down_body(x_ref, hidden_ref, *refs):
-    *weights, out_ref, flat_ref, down_ref, sems = refs
-    nx = out_ref.shape[0]
+    *weights, out_ref, shared_ref, flat_ref, down_ref, sems = refs
+    nx = len(weights)
     width = weights[0].shape[0]
-    copies, at = [], 0
+    lanes = out_ref.shape[2]
+    near = out_ref.shape[1] - EIGHT
+    fold = Fold(width, lanes, near)
+    pairs = []
     for n, weight in enumerate(weights):
-        copies.append((weight, down_ref.at[at : at + weight.shape[0], :]))
-        at += weight.shape[0]
-    copies = fetch(copies, sems)
+        pairs.append((weight.at[:lanes, :], down_ref.at[n, :lanes, :]))
+        for q in range(fold.parts):
+            at = lanes + q * fold.rest
+            pairs.append((weight.at[lanes:, :], down_ref.at[n, at : at + fold.rest, :]))
+    copies = fetch(pairs, sems)
     ny = hidden_ref.shape[0]
     units = flat_ref.shape[0] // (nx * ny)
-    lanes = out_ref.shape[2]
-    half, cap, fold = width // 2, lanes // 2, units // 2
-    groups = (out_ref.shape[1] - ny * units) // half
+    count = flat_ref.shape[1]
     own = [lax.rem(x_ref[0] + shift, nx) for shift in SHIFTS]
-    for n in range(nx):
-        for y in range(ny):
+    half = units // 2
+    for y in range(ny):
+        for n in range(nx):
             at = pl.multiple_of((own[n] * ny + y) * units, units)
             flat_ref[pl.ds(at, units), :] = hidden_ref[y, n * units : (n + 1) * units, :]
+        both = hidden_ref[y, nx * units : nx * units + half, :]
+        shared_ref[y * units : y * units + half, :] = both[:, :lanes]
+        shared_ref[y * units + half : (y + 1) * units, :] = both[:, lanes:]
+    eye = bf(iota((count, count), 0) == iota((count, count), 1))
+    lines = bf(fold.to_lines(count, 0))
+    dims = (lanes, count)
+    own_part = lax.div(iota(dims, 0), fold.rest) == fold.part_of(iota(dims, 1))
     for copy in copies:
         copy.wait()
-    outs = nn(down_ref[...], flat_ref[...])
     for n in range(nx):
-        out = outs[n * width : (n + 1) * width]
-        for q in range(groups // 2):
-            cols = slice(q * lanes, (q + 1) * lanes)
-            a, b = out[:half, cols], out[half:, cols]
-            out_ref[own[n], 2 * q * half : (2 * q + 1) * half, :] = pair_low(a, b, cap).astype(BF16)
-            out_ref[own[n], (2 * q + 1) * half : (2 * q + 2) * half, :] = pair_high(a, b, cap).astype(BF16)
-        for y in range(ny):
-            at = groups * half + y * units
-            both = hidden_ref[y, nx * units : nx * units + fold, :]
-            out_ref[n, at : at + fold, :] = both[:, :lanes]
-            out_ref[n, at + fold : at + units, :] = both[:, lanes:]
-
-
-def combine_body(slot_ref, gate_ref, back_ref, tok_ref, hidden_ref, down_ref, out_ref, scored_ref):
-    experts, half, lanes = back_ref.shape
-    rows = tok_ref.shape[1]
-    cap = lanes // 2
-    place = iota((lanes, rows), 0)
-    place = jnp.where(place < cap, place, place - cap)
-    low = iota((lanes, rows), 0) < cap
-    routed = jnp.zeros((half, 2 * rows), F32)
-    for e in range(experts):
-        mix = jnp.where(slot_ref[e : e + 1, :] == place, gate_ref[e : e + 1, :], 0.0)
-        mix = jnp.concatenate([jnp.where(low, mix, 0.0), jnp.where(low, 0.0, mix)], axis=1)
-        head = mix.astype(BF16)
-        tail = (mix - head.astype(F32)).astype(BF16)
-        routed = routed + nn(back_ref[e], head) + nn(back_ref[e], tail)
-    depth = down_ref.shape[1] // hidden_ref.shape[0]
-    skip = hidden_ref.shape[1] - depth
-    shared = jnp.zeros((2 * half, rows), F32)
-    for x in range(hidden_ref.shape[0]):
-        shared = shared + nn(down_ref[:, x * depth : (x + 1) * depth], hidden_ref[x, skip:, :])
-    routed = jnp.concatenate([routed[:, :rows], routed[:, rows:]], axis=0)
+        out = nn(down_ref[n], flat_ref[...])
+        full = nt(eye, out[:lanes].astype(BF16)).astype(BF16)
+        rest = nt(lines, jnp.where(own_part, out[lanes:], 0.0).astype(BF16))
+        for g in range(count // near):
+            out_ref[g * nx + own[n], :near, :] = full[g * near : (g + 1) * near, :]
+            out_ref[g * nx + own[n], near:, :] = rest[g * EIGHT : (g + 1) * EIGHT, :].astype(BF16)
+
+
+def combine_body(x_ref, slot_ref, gate_ref, back_ref, tok_ref, down_ref, *refs):
+    *hidden, out_ref, scored_ref = refs
+    experts, rows = slot_ref.shape
+    width = tok_ref.shape[0]
+    lanes = back_ref.shape[2]
+    near = back_ref.shape[1] - EIGHT
+    fold = Fold(width, lanes, near)
+    pieces = back_ref.shape[0] // experts
+    cap = pieces * near
+    several = 2 * lanes // cap
+
+    def mix(first, target):
+        weigh = [
+            jnp.where(slot_ref[e : e + 1, :] == target, gate_ref[e : e + 1, :], 0.0)
+            for e in range(first, first + several)
+        ]
+        weigh = jnp.concatenate(weigh, axis=0)
+        head = weigh.astype(BF16)
+        return [head, (weigh - head.astype(F32)).astype(BF16)]
+
+    place = iota((cap, rows), 0)
+    line = iota((pieces * EIGHT, rows), 0)
+    line, piece = lax.rem(line, EIGHT), lax.div(line, EIGHT)
+    full = jnp.zeros((lanes, rows), F32)
+    rest = jnp.zeros((fold.rest, rows), F32)
+    for first in range(0, experts, several):
+        span = range(first * pieces, (first + several) * pieces)
+        block = jnp.concatenate([back_ref[n, :near, :] for n in span], axis=0)
+        got = tn(block, jnp.concatenate(mix(first, place), axis=1))
+        full = full + got[:, :rows] + got[:, rows:]
+        block = jnp.concatenate([back_ref[n, near:, :].astype(F32) for n in span], axis=0).astype(BF16)
+        terms = []
+        for q in range(fold.parts):
+            target = jnp.where(line < fold.per, piece * near + q * fold.per + line, -2)
+            terms += mix(first, target)
+        got = tn(block, jnp.concatenate(terms, axis=1))
+        for q in range(fold.parts):
+            part = got[q * fold.rest : (q + 1) * fold.rest]
+            rest = rest + part[:, 2 * q * rows : (2 * q + 1) * rows] + part[:, (2 * q + 1) * rows : (2 * q + 2) * rows]
+    routed = jnp.concatenate([full, rest], axis=0)
+    shared = jnp.zeros((width, rows), F32)
+    for shift, units in zip(SHIFTS, hidden):
+        depth = units.shape[0]
+        at = pl.multiple_of(lax.rem(x_ref[0] + shift, len(hidden)) * depth, lanes)
+        shared = shared + nn(down_ref[:, pl.ds(at, depth)], units[...])
     out = (tok_ref[...].astype(F32) + shared + routed).astype(BF16)
     out_ref[...] = out
-    take = iota((2 * SCORE_E, rows), 1) == rows - SCORE_E + iota((2 * SCORE_E, rows), 0)
-    scored = nt(jnp.where(take, 1.0, 0.0).astype(BF16), out).astype(BF16)
+    take = iota((EIGHT, rows), 1) == rows - SCORE_E + iota((EIGHT, rows), 0)
+    scored = nt(bf(take), out).astype(BF16)
     for g in range(scored_ref.shape[0]):
         scored_ref[g] = scored[:SCORE_E]
 
@@ -288,8 +355,10 @@
     nz, nc = lax.axis_size("z"), lax.axis_size("core")
     groups, lanes = nz * nc, nx * ny
     rows, width = tokens.shape
-    half, cap = width // 2, rows // 2
-    near = groups // nx
+    cap = rows // 2
+    near = cap // nx
+    count = groups * near
+    lines = near + EIGHT
     units = w_gate.shape[1]
     tok = tokens.T
     x_at = lax.axis_index("x").astype(jnp.int32).reshape(1)
@@ -298,7 +367,7 @@
     outgoing, slot, gate = call(
         dispatch_body,
         [
-            shape((groups, half, 2 * cap)),
+            shape((groups * nx, lines, rows)),
             shape((groups, rows), jnp.int32),
             shape((groups, rows), F32),
         ],
@@ -312,13 +381,12 @@
         ],
         limit=60,
     )
-    arrived = exchange(outgoing, LINE)
+    arrived = exchange(outgoing, BOTH)
     arrived, t1, t3, t2 = lax.optimization_barrier((arrived, *[from_shift(tok, "x", shift) for shift in SHIFTS[1:]]))
-    quarter = exchange(arrived.reshape(nx, near * half, 2 * cap), "x")
     (spread,) = call(
         spread_body,
-        [shape((nx * width, near * cap + rows))],
-        [x_at, quarter, tok, t1, t3, t2],
+        [shape((nx * width, count + rows))],
+        [x_at, arrived, tok, t1, t3, t2],
         scalars=1,
     )
     spread, own_gate, own_up = lax.optimization_barrier((spread, w_gate[0], w_up[0]))
@@ -350,40 +418,40 @@
     near_weights = [after[n] for n in ("own_gate", "own_up", "g1", "u1", "g3", "u3", "g2", "u2")]
     (hidden,) = call(
         hidden_body,
-        [shape((ny, nx * units + units // 2 + 8, near * cap))],
+        [shape((ny, nx * units + units // 2 + EIGHT, count))],
         [y_at, *blocks, *near_weights, shared_gate, shared_up],
         scalars=1,
         far=(*range(1, len(RING)), *range(len(RING) + 1, len(RING) + 2 * nx + 3)),
         scratch=[
-            pltpu.VMEM((lanes * width, near * cap + rows), BF16),
+            pltpu.VMEM((lanes * width, count + rows), BF16),
             pltpu.VMEM((2 * (nx + 1) * units, lanes * width), BF16),
             pltpu.SemaphoreType.DMA((2 * nx + 2 + lanes,)),
         ],
         limit=56,
     )
     hidden, d1, d3 = lax.optimization_barrier((hidden, after["d1"], after["d3"]))
-    d2 = [from_shift(d1[:half], "x", 1), from_shift(d3[half:], "x", nx - 1)]
+    d2 = from_shift(d3, "x", nx - 1)
     all_hidden = exchange(hidden, "y")
-    (returned,) = call(
+    returned, own_shared = call(
         down_body,
-        [shape((nx, near * half + ny * units, 2 * cap))],
-        [x_at, all_hidden, after["down"], d1, d3, *d2],
+        [shape((groups * nx, lines, rows)), shape((ny * units, rows))],
+        [x_at, all_hidden, after["down"], d1, d3, d2],
         scalars=1,
-        far=range(2, 3 + nx),
+        far=range(2, 2 + nx),
         scratch=[
-            pltpu.VMEM((lanes * units, near * cap), BF16),
-            pltpu.VMEM((nx * width, lanes * units), BF16),
-            pltpu.SemaphoreType.DMA((nx + 1,)),
+            pltpu.VMEM((lanes * units, count), BF16),
+            pltpu.VMEM((nx, 2 * rows, lanes * units), BF16),
+            pltpu.SemaphoreType.DMA((nx * (1 + rows // (width - rows)),)),
         ],
         limit=40,
     )
-    mixed = lax.all_to_all(returned, "x", 0, 0, tiled=True)
-    back = mixed[:, : near * half].reshape(groups, half, 2 * cap)
-    back = lax.all_to_all(back, LINE, 0, 0, tiled=True)
+    near_shared = [own_shared, *[from_shift(own_shared, "x", shift) for shift in SHIFTS[1:]]]
+    back = exchange(returned, BOTH)
     layer_out, scored = call(
         combine_body,
         [shape((width, rows)), shape((groups, SCORE_E, width))],
-        [slot, gate, back, tok, mixed, shared_down.T],
+        [x_at, slot, gate, back, tok, shared_down.T, *near_shared],
+        scalars=1,
     )
     line_rows = exchange(scored, LINE).reshape(groups * SCORE_E, width)
     count = groups * SCORE_E // nc

time: 227 us -> 230 us (1.013)
  blocking collectives: 51.5 us -> 27.8 us
  starting transfers between devices: 101 us -> 120 us
  local copies, waits for them, and re-layouts: 0.97 us -> 7.03 us
  Pallas kernels: 16.9 us -> 19.9 us
    all_to_all x1 -> x0, blocking collectives: 24.1 us -> none  [shards(): back = lax.all_to_all(back, LINE, 0, 0, tiled=True)]
    all_to_all x5, starting transfers between devices: 29.6 us -> 43.8 us  [exchange(): return lax.all_to_all(value, axes, 0, 0, tiled=True)]
    ppermute x20 -> x22, starting transfers between devices: 61.4 us -> 73.4 us  [from_shift(): lax.ppermute(value, axis, [((i + shift) % count, i) for i in range(count)])]
    ppermute x20 -> x22, waiting for transfers between devices: 16.3 us -> 24.8 us  [from_shift(): lax.ppermute(value, axis, [((i + shift) % count, i) for i in range(count)])]
    all_to_all x5, waiting for transfers between devices: 36.3 us -> 28.6 us  [exchange(): return lax.all_to_all(value, axes, 0, 0, tiled=True)]
    unnamed x36 -> x42, local copies, waits for them, and re-layouts: 0.09 us -> 6.21 us
    ppermute x1, starting transfers between devices: 6.28 us -> 2.36 us  [shards(): other_vocab = lax.ppermute(vocab, 'core', [(0, 1), (1, 0)])]
    all_to_all x1 -> x0, starting transfers between devices: 3.63 us -> none  [shards(): mixed = lax.all_to_all(returned, 'x', 0, 0, tiled=True)]
  transfers between devices with their start and end apart: 27 -> 28, of which waited for: 15 -> 16; matrix products, arithmetic and copies ran while one was open for 0% -> 0% of each run, Pallas kernels for 4% -> 4%
where the time goes in v7:
time: 230 us; the launch traced here: 229 us
  starting transfers between devices  120 us (52%)
  waiting for transfers between devices  53.4 us (23%)
  blocking collectives  27.8 us (12%)
  Pallas kernels  19.9 us (9%)
  local copies, waits for them, and re-layouts  7.03 us (3%)
    ppermute x22, starting transfers between devices, from_shift(): lax.ppermute(value, axis, [((i + shift) % count, i) for i in range(count)])  73.4 us
    all_to_all x5, starting transfers between devices, exchange(): return lax.all_to_all(value, axes, 0, 0, tiled=True)  43.8 us
    all_to_all x5, waiting for transfers between devices, exchange(): return lax.all_to_all(value, axes, 0, 0, tiled=True)  28.6 us
    all_to_all x2, blocking collectives, spread_all(): lax.all_to_all(jnp.broadcast_to(value[None], (count, *value.shape)), axes...  27.8 us
    ppermute x22, waiting for transfers between devices, from_shift(): lax.ppermute(value, axis, [((i + shift) % count, i) for i in range(count)])  24.8 us
    pallas_call x7, Pallas kernels, call(): pl.pallas_call(body, out_shape=outs, in_specs=specs, out_specs=[pl.BlockS...  19.9 us
    unnamed x42, local copies, waits for them, and re-layouts  6.21 us
  transfers between devices with their start and end apart: 28, of which 16 were waited for; matrix products, arithmetic and copies ran while one was open for 0% of the time, Pallas kernels for 4%

profile of v7, /device:TPU:1, one launch (start us, length us, event | category | flops | bytes accessed | tf_op | source)
XLA Modules:
  0.0 229.0 jit_solution(3555537714517137623)
XLA Ops:
  0.6 2.6 %shard_map.122 = (bf16[64,24,128]{2,1,0:T(8,128)(2,1)}, s32[16,128]{1,0:T(8,128)}, f32[16,128]{1,0:T(8,128)}) custom-call(s32[6,128]{1,0:T(8,128)} %bitcast.37, f32[6,128]{1,0:T(8,128)} %bitcast.38, bf16[160,128]{1,0:T(8,128)(2,1)} %bitcast.23), custom_call_target="tpu_custom_call" | custom-call | bytes 456704 | tf_op jit(solution)/shard_map/pallas_call | solution.py:25
  3.3 14.8 %all-to-all-start = ((bf16[64,24,128]{2,1,0:T(8,128)(2,1)}), bf16[64,24,128]{2,1,0:T(8,128)(2,1)S(1)}, u32[]{:S(2)}, u32[]{:S(2)}) async-start(bf16[64,24,128]{2,1,0:T(8,128)(2,1)} %get-tuple-element.33), calls=%async_computation | async-start | bytes 786432 | tf_op jit(solution)/shard_map/all_to_all | solution.py:325
  18.1 4.5 %collective-permute-start = (bf16[160,128]{1,0:T(8,128)(2,1)}, bf16[160,128]{1,0:T(8,128)(2,1)S(1)}, u32[]{:S(2)}, u32[]{:S(2)}) collective-permute-start(bf16[160,128]{1,0:T(8,128)(2,1)} %bitcast.24), channel_id=1, source_target_pairs={{8,0},{16,8},{24,16},{0,24},{9,1},{17,9},{25,17},{1,25},{10,2},{18... | collective-permute-start | bytes 122888 | tf_op jit(solution)/shard_map/ppermute | solution.py:336
  22.6 1.9 collective-permute-start.1
  24.6 3.7 %collective-permute-start.2 = (bf16[160,128]{1,0:T(8,128)(2,1)}, bf16[160,128]{1,0:T(8,128)(2,1)S(1)}, u32[]{:S(2)}, u32[]{:S(2)}) collective-permute-start(bf16[160,128]{1,0:T(8,128)(2,1)} %bitcast.26), channel_id=1, source_target_pairs={{16,0},{24,8},{0,16},{8,24},{17,1},{25,9},{1,17},{9,25},{18,2},{26... | collective-permute-start | bytes 122888 | tf_op jit(solution)/shard_map/ppermute | solution.py:336
  28.2 1.1 collective-permute-done.1.refs_2_
  29.4 2.2 collective-permute-done.2.refs_3_
  31.6 1.2 all-to-all-done.in_ref
  32.8 0.8 copy-done.9
  33.5 0.5 shard_map.123.refs_0_
  34.1 3.2 %collective-permute-start.3 = (bf16[640,384]{1,0:T(8,128)(2,1)S(1)}, bf16[640,384]{1,0:T(8,128)(2,1)S(1)}, u32[]{:S(2)}, u32[]{:S(2)}) collective-permute-start(bf16[640,384]{1,0:T(8,128)(2,1)S(1)} %shard_map.123.refs_0_), channel_id=1, source_target_pairs={{7,0},{0,1},{1,2},{2,3},{3,4},{4,5},{5,6},{6,7},{15,8},{8,9},{9,10... | collective-permute-start | bytes 1474568 | tf_op jit(solution)/shard_map/ppermute | solution.py:336
  37.3 3.8 %collective-permute-start.4 = (bf16[640,384]{1,0:T(8,128)(2,1)S(1)}, bf16[640,384]{1,0:T(8,128)(2,1)S(1)}, u32[]{:S(2)}, u32[]{:S(2)}) collective-permute-start(bf16[640,384]{1,0:T(8,128)(2,1)S(1)} %shard_map.123.refs_0_), channel_id=1, source_target_pairs={{1,0},{2,1},{3,2},{4,3},{5,4},{6,5},{7,6},{0,7},{9,8},{10,9},{11,1... | collective-permute-start | bytes 1474568 | tf_op jit(solution)/shard_map/ppermute | solution.py:336
  41.1 3.8 %collective-permute-start.7 = (bf16[48,5120]{1,0:T(8,128)(2,1)}, bf16[48,5120]{1,0:T(8,128)(2,1)}, u32[]{:S(2)}, u32[]{:S(2)}) collective-permute-start(bf16[48,5120]{1,0:T(8,128)(2,1)} %bitcast.29), channel_id=1, source_target_pairs={{8,0},{16,8},{24,16},{0,24},{9,1},{17,9},{25,17},{1,25},{10,2},{18... | collective-permute-start | bytes 1474568 | tf_op jit(solution)/shard_map/ppermute | solution.py:336
  45.0 1.9 collective-permute-start.8
  46.9 2.0 collective-permute-done.3.refs_1_
  48.9 1.0 collective-permute-done.4.refs_2_
  49.9 3.2 %collective-permute-start.5 = (bf16[640,384]{1,0:T(8,128)(2,1)S(1)}, bf16[640,384]{1,0:T(8,128)(2,1)S(1)}, u32[]{:S(2)}, u32[]{:S(2)}) collective-permute-start(bf16[640,384]{1,0:T(8,128)(2,1)S(1)} %collective-permute-done.3.refs_1_), channel_id=1, source_target_pairs={{7,0},{0,1},{1,2},{2,3},{3,4},{4,5},{5,6},{6,7},{15,8},{8,9},{9,10... | collective-permute-start | bytes 1474568 | tf_op jit(solution)/shard_map/ppermute | solution.py:336
  53.1 3.9 %collective-permute-start.6 = (bf16[640,384]{1,0:T(8,128)(2,1)S(1)}, bf16[640,384]{1,0:T(8,128)(2,1)S(1)}, u32[]{:S(2)}, u32[]{:S(2)}) collective-permute-start(bf16[640,384]{1,0:T(8,128)(2,1)S(1)} %collective-permute-done.4.refs_2_), channel_id=1, source_target_pairs={{1,0},{2,1},{3,2},{4,3},{5,4},{6,5},{7,6},{0,7},{9,8},{10,9},{11,1... | collective-permute-start | bytes 1474568 | tf_op jit(solution)/shard_map/ppermute | solution.py:336
  57.0 2.3 collective-permute-start.11
  59.3 4.3 %collective-permute-start.12 = (bf16[48,5120]{1,0:T(8,128)(2,1)}, bf16[48,5120]{1,0:T(8,128)(2,1)S(1)}, u32[]{:S(2)}, u32[]{:S(2)}) collective-permute-start(bf16[48,5120]{1,0:T(8,128)(2,1)} %bitcast.33), channel_id=1, source_target_pairs={{8,0},{16,8},{24,16},{0,24},{9,1},{17,9},{25,17},{1,25},{10,2},{18... | collective-permute-start | bytes 1474568 | tf_op jit(solution)/shard_map/ppermute | solution.py:336
  63.6 0.2 collective-permute-done.5.refs_3_
  63.8 2.3 %collective-permute-done.6.refs_4_ = bf16[640,384]{1,0:T(8,128)(2,1)S(1)} collective-permute-done((bf16[640,384]{1,0:T(8,128)(2,1)S(1)}, bf16[640,384]{1,0:T(8,128)(2,1)S(1)}, u32[]{:S(2)}, u32[]{:S(2)}) %collective-permute-start.6) | collective-permute-done | bytes 491552 | tf_op jit(solution)/shard_map/ppermute | solution.py:336
  66.2 3.8 %collective-permute-start.9 = (bf16[640,384]{1,0:T(8,128)(2,1)S(1)}, bf16[640,384]{1,0:T(8,128)(2,1)}, u32[]{:S(2)}, u32[]{:S(2)}) collective-permute-start(bf16[640,384]{1,0:T(8,128)(2,1)S(1)} %collective-permute-done.5.refs_3_), channel_id=1, source_target_pairs={{7,0},{0,1},{1,2},{2,3},{3,4},{4,5},{5,6},{6,7},{15,8},{8,9},{9,10... | collective-permute-start | bytes 1474568 | tf_op jit(solution)/shard_map/ppermute | solution.py:336
  70.0 2.7 %collective-permute-start.10 = (bf16[640,384]{1,0:T(8,128)(2,1)S(1)}, bf16[640,384]{1,0:T(8,128)(2,1)S(1)}, u32[]{:S(2)}, u32[]{:S(2)}) collective-permute-start(bf16[640,384]{1,0:T(8,128)(2,1)S(1)} %collective-permute-done.6.refs_4_), channel_id=1, source_target_pairs={{1,0},{2,1},{3,2},{4,3},{5,4},{6,5},{7,6},{0,7},{9,8},{10,9},{11,1... | collective-permute-start | bytes 1474568 | tf_op jit(solution)/shard_map/ppermute | solution.py:336
  72.7 5.3 %collective-permute-start.14 = (bf16[48,5120]{1,0:T(8,128)(2,1)}, bf16[48,5120]{1,0:T(8,128)(2,1)}, u32[]{:S(2)}, u32[]{:S(2)}) collective-permute-start(bf16[48,5120]{1,0:T(8,128)(2,1)} %collective-permute-done.7.refs_10_), channel_id=1, source_target_pairs={{8,0},{16,8},{24,16},{0,24},{9,1},{17,9},{25,17},{1,25},{10,2},{18... | collective-permute-start | bytes 1474568 | tf_op jit(solution)/shard_map/ppermute | solution.py:336
  78.0 1.9 collective-permute-start.15
  79.9 0.5 collective-permute-done.10.refs_6_
  80.4 2.9 %collective-permute-start.13 = (bf16[640,384]{1,0:T(8,128)(2,1)}, bf16[640,384]{1,0:T(8,128)(2,1)}, u32[]{:S(2)}, u32[]{:S(2)}) collective-permute-start(bf16[640,384]{1,0:T(8,128)(2,1)} %collective-permute-done.9.refs_5_), channel_id=1, source_target_pairs={{7,0},{0,1},{1,2},{2,3},{3,4},{4,5},{5,6},{6,7},{15,8},{8,9},{9,10... | collective-permute-start | bytes 1474568 | tf_op jit(solution)/shard_map/ppermute | solution.py:336
  83.3 6.3 %collective-permute-start.16 = (bf16[160,1536]{1,0:T(8,128)(2,1)S(1)}, bf16[160,1536]{1,0:T(8,128)(2,1)S(1)}, u32[]{:S(2)}, u32[]{:S(2)}) collective-permute-start(bf16[160,1536]{1,0:T(8,128)(2,1)S(1)} %bitcast.19), channel_id=1, source_target_pairs={{8,0},{16,8},{24,16},{0,24},{9,1},{17,9},{25,17},{1,25},{10,2},{18... | collective-permute-start | bytes 1474568 | tf_op jit(solution)/shard_map/ppermute | solution.py:336
  89.7 1.9 collective-permute-start.17
  91.6 0.2 collective-permute-done.13.refs_7_
  91.8 7.2 %shard_map.124 = bf16[8,224,256]{2,1,0:T(8,128)(2,1)} custom-call(s32[1]{0:T(128)} %bitcast.4.y_ref, bf16[640,384]{1,0:T(8,128)(2,1)} %copy-done, bf16[640,384]{1,0:T(8,128)(2,1)} %copy-done.13, bf16[640,384]{1,0:T(8,128)(2,1)} %copy-done.14, bf16[640,384]{1,0:T(8,128)(2,1)} %copy-done.15, bf16[640,384]{1,0:T(8,128)(2,1)} %copy-done.16, ...), custom_call_target="tpu_custom_call" | custom-call | bytes 9764868 | tf_op jit(solution)/shard_map/pallas_call | solution.py:25
  99.0 1.5 collective-permute-done.17.refs_2_
  100.5 0.8 copy-done.3
  101.2 6.3 %all-to-all-start.1 = ((bf16[8,224,256]{2,1,0:T(8,128)(2,1)}), bf16[8,224,256]{2,1,0:T(8,128)(2,1)S(1)}, u32[]{:S(2)}, u32[]{:S(2)}) async-start(bf16[8,224,256]{2,1,0:T(8,128)(2,1)} %shard_map.124), calls=%async_computation.1 | async-start | bytes 1835008 | tf_op jit(solution)/shard_map/all_to_all | solution.py:325
  107.6 2.1 collective-permute-start.18
  109.6 9.9 %collective-permute-done.18.refs_3_ = bf16[160,1536]{1,0:T(8,128)(2,1)S(1)} collective-permute-done((bf16[160,1536]{1,0:T(8,128)(2,1)}, bf16[160,1536]{1,0:T(8,128)(2,1)S(1)}, u32[]{:S(2)}, u32[]{:S(2)}) %collective-permute-start.18) | collective-permute-done | bytes 491552 | tf_op jit(solution)/shard_map/ppermute | solution.py:336
  119.6 0.8 copy-done.5
  120.3 9.9 %all-to-all-done.1.hidden_ref = bf16[8,224,256]{2,1,0:T(8,128)(2,1)S(1)} async-done(((bf16[8,224,256]{2,1,0:T(8,128)(2,1)}), bf16[8,224,256]{2,1,0:T(8,128)(2,1)S(1)}, u32[]{:S(2)}, u32[]{:S(2)}) %all-to-all-start.1) | async-done | bytes 917536 | tf_op jit(solution)/shard_map/all_to_all | solution.py:325
  130.2 1.0 copy-done.4
  131.3 1.0 copy-done.6
  132.3 5.6 %shard_map.125 = (bf16[64,24,128]{2,1,0:T(8,128)(2,1)S(1)}, bf16[384,128]{1,0:T(8,128)(2,1)S(1)}) custom-call(s32[1]{0:T(128)} %bitcast.x_ref, bf16[8,224,256]{2,1,0:T(8,128)(2,1)S(1)} %all-to-all-done.1.hidden_ref, bf16[160,1536]{1,0:T(8,128)(2,1)S(1)} %bitcast.21, bf16[160,1536]{1,0:T(8,128)(2,1)S(1)} %collective-permute-done.16.refs_1_, ...), custom_call_target="tpu_custom_call" | custom-call | bytes 3375108 | tf_op jit(solution)/shard_map/pallas_call | solution.py:25
  137.9 0.7 copy-done.8
  138.6 10.4 %all-to-all-start.2 = ((bf16[64,24,128]{2,1,0:T(8,128)(2,1)}), bf16[64,24,128]{2,1,0:T(8,128)(2,1)S(1)}, u32[]{:S(2)}, u32[]{:S(2)}) async-start(bf16[64,24,128]{2,1,0:T(8,128)(2,1)} %copy-done.8), calls=%async_computation.2 | async-start | bytes 786432 | tf_op jit(solution)/shard_map/all_to_all | solution.py:325
  149.0 2.4 %collective-permute-start.22 = (bf16[128,5120]{1,0:T(8,128)(2,1)S(1)}, bf16[128,5120]{1,0:T(8,128)(2,1)S(1)}, u32[]{:S(2)}, u32[]{:S(2)}) collective-permute-start(bf16[128,5120]{1,0:T(8,128)(2,1)S(1)} %copy-done.1), channel_id=1, source_target_pairs={{0,32},{32,0},{1,33},{33,1},{2,34},{34,2},{3,35},{35,3},{4,36},{36... | collective-permute-start | bytes 3932168 | tf_op jit(solution)/shard_map/ppermute | solution.py:466
  151.4 4.4 %collective-permute-start.19 = (bf16[384,128]{1,0:T(8,128)(2,1)S(1)}, bf16[384,128]{1,0:T(8,128)(2,1)S(1)}, u32[]{:S(2)}, u32[]{:S(2)}) collective-permute-start(bf16[384,128]{1,0:T(8,128)(2,1)S(1)} %get-tuple-element.57.refs_0_), channel_id=1, source_target_pairs={{8,0},{16,8},{24,16},{0,24},{9,1},{17,9},{25,17},{1,25},{10,2},{18... | collective-permute-start | bytes 294920 | tf_op jit(solution)/shard_map/ppermute | solution.py:336
  155.8 1.9 collective-permute-start.20
  157.7 3.7 %collective-permute-start.21 = (bf16[384,128]{1,0:T(8,128)(2,1)S(1)}, bf16[384,128]{1,0:T(8,128)(2,1)S(1)}, u32[]{:S(2)}, u32[]{:S(2)}) collective-permute-start(bf16[384,128]{1,0:T(8,128)(2,1)S(1)} %get-tuple-element.57.refs_0_), channel_id=1, source_target_pairs={{16,0},{24,8},{0,16},{8,24},{17,1},{25,9},{1,17},{9,25},{18,2},{26... | collective-permute-start | bytes 294920 | tf_op jit(solution)/shard_map/ppermute | solution.py:336
  161.4 2.1 collective-permute-done.20.refs_2_
  163.5 1.8 collective-permute-done.21.refs_3_
  165.3 1.0 copy-done.7
  166.3 1.4 shard_map.126
  167.7 7.8 %all-to-all-start.3 = ((bf16[16,4,160]{2,1,0:T(4,128)(2,1)}), bf16[16,4,160]{2,1,0:T(4,128)(2,1)S(1)}, u32[]{:S(2)}, u32[]{:S(2)}) async-start(bf16[16,4,160]{2,1,0:T(4,128)(2,1)} %get-tuple-element.59), calls=%async_computation.3 | async-start | bytes 65536 | tf_op jit(solution)/shard_map/all_to_all | solution.py:325
  175.6 7.4 %all-to-all-done.3 = bf16[16,4,160]{2,1,0:T(4,128)(2,1)S(1)} async-done(((bf16[16,4,160]{2,1,0:T(4,128)(2,1)}), bf16[16,4,160]{2,1,0:T(4,128)(2,1)S(1)}, u32[]{:S(2)}, u32[]{:S(2)}) %all-to-all-start.3) | async-done | bytes 20512 | tf_op jit(solution)/shard_map/all_to_all | solution.py:325
  183.0 1.0 shard_map.127
  184.0 4.5 %all-to-all-start.4 = ((bf16[32,40,128]{2,1,0:T(8,128)(2,1)}), bf16[32,40,128]{2,1,0:T(8,128)(2,1)S(1)}, u32[]{:S(2)}, u32[]{:S(2)}) async-start(bf16[32,40,128]{2,1,0:T(8,128)(2,1)} %shard_map.127), calls=%async_computation.4 | async-start | bytes 655360 | tf_op jit(solution)/shard_map/all_to_all | solution.py:325
  188.5 0.1 tile.10
  188.6 0.1 tile.12.targets_ref
  188.7 0.1 pad_add_fusion.at_ref
  188.7 10.2 %all-to-all-done.4.rows_ref = bf16[32,40,128]{2,1,0:T(8,128)(2,1)S(1)} async-done(((bf16[32,40,128]{2,1,0:T(8,128)(2,1)}), bf16[32,40,128]{2,1,0:T(8,128)(2,1)S(1)}, u32[]{:S(2)}, u32[]{:S(2)}) %all-to-all-start.4) | async-done | bytes 327712 | tf_op jit(solution)/shard_map/all_to_all | solution.py:325
  198.9 1.6 shard_map.128
  200.5 16.0 %all_to_all.35 = f32[32,1,128]{2,1,0:T(1,128)S(1)} all-to-all(f32[32,1,128]{2,1,0:T(1,128)S(1)} %broadcast_in_dim.7), channel_id=1, replica_groups=mesh['z'=8,'core'=2,'x'=4,'y'=8] {'x','y'}, dimensions={0} | all-to-all | bytes 32768 | tf_op jit(solution)/shard_map/all_to_all | solution.py:329
  216.5 11.8 %all_to_all.36 = f32[16,1,128]{2,1,0:T(1,128)S(1)} all-to-all(f32[16,1,128]{2,1,0:T(1,128)S(1)} %broadcast_in_dim.16), channel_id=1, replica_groups=mesh['z'=8,'core'=2,'x'=4,'y'=8] {'z','core'}, dimensions={0} | all-to-all | bytes 16384 | tf_op jit(solution)/shard_map/all_to_all | solution.py:329
  228.4 0.6 reshape.36
  (55 shorter events, 0.3 us)
Async XLA Ops:
  0.6 82.7 %copy-start.2 = (bf16[1,1536,160]{1,2,0:T(8,128)(2,1)S(1)}, bf16[1,1536,160]{1,2,0:T(8,128)(2,1)}, u32[]{:S(2)}) copy-start(bf16[1,1536,160]{1,2,0:T(8,128)(2,1)} %param.16) | copy-start | bytes 1474564
  3.3 29.5 %all-to-all-start = ((bf16[64,24,128]{2,1,0:T(8,128)(2,1)}), bf16[64,24,128]{2,1,0:T(8,128)(2,1)S(1)}, u32[]{:S(2)}, u32[]{:S(2)}) async-start(bf16[64,24,128]{2,1,0:T(8,128)(2,1)} %get-tuple-element.33), calls=%async_computation | async-start | bytes 786432 | tf_op jit(solution)/shard_map/all_to_all | solution.py:325
  18.1 10.1 %collective-permute-start = (bf16[160,128]{1,0:T(8,128)(2,1)}, bf16[160,128]{1,0:T(8,128)(2,1)S(1)}, u32[]{:S(2)}, u32[]{:S(2)}) collective-permute-start(bf16[160,128]{1,0:T(8,128)(2,1)} %bitcast.24), channel_id=1, source_target_pairs={{8,0},{16,8},{24,16},{0,24},{9,1},{17,9},{25,17},{1,25},{10,2},{18... | collective-permute-start | bytes 122888 | tf_op jit(solution)/shard_map/ppermute | solution.py:336
  22.6 6.8 %collective-permute-start.1 = (bf16[160,128]{1,0:T(8,128)(2,1)}, bf16[160,128]{1,0:T(8,128)(2,1)S(1)}, u32[]{:S(2)}, u32[]{:S(2)}) collective-permute-start(bf16[160,128]{1,0:T(8,128)(2,1)} %bitcast.25), channel_id=1, source_target_pairs={{24,0},{0,8},{8,16},{16,24},{25,1},{1,9},{9,17},{17,25},{26,2},{2,... | collective-permute-start | bytes 122888 | tf_op jit(solution)/shard_map/ppermute | solution.py:336
  24.6 7.0 %collective-permute-start.2 = (bf16[160,128]{1,0:T(8,128)(2,1)}, bf16[160,128]{1,0:T(8,128)(2,1)S(1)}, u32[]{:S(2)}, u32[]{:S(2)}) collective-permute-start(bf16[160,128]{1,0:T(8,128)(2,1)} %bitcast.26), channel_id=1, source_target_pairs={{16,0},{24,8},{0,16},{8,24},{17,1},{25,9},{1,17},{9,25},{18,2},{26... | collective-permute-start | bytes 122888 | tf_op jit(solution)/shard_map/ppermute | solution.py:336
  32.8 0.8 copy-start.9
  34.1 57.7 %copy-start = (bf16[640,384]{1,0:T(8,128)(2,1)}, bf16[640,384]{1,0:T(8,128)(2,1)S(1)}, u32[]{:S(2)}) copy-start(bf16[640,384]{1,0:T(8,128)(2,1)S(1)} %shard_map.123.refs_0_) | copy-start | bytes 1474564
  34.1 14.8 %collective-permute-start.3 = (bf16[640,384]{1,0:T(8,128)(2,1)S(1)}, bf16[640,384]{1,0:T(8,128)(2,1)S(1)}, u32[]{:S(2)}, u32[]{:S(2)}) collective-permute-start(bf16[640,384]{1,0:T(8,128)(2,1)S(1)} %shard_map.123.refs_0_), channel_id=1, source_target_pairs={{7,0},{0,1},{1,2},{2,3},{3,4},{4,5},{5,6},{6,7},{15,8},{8,9},{9,10... | collective-permute-start | bytes 1474568 | tf_op jit(solution)/shard_map/ppermute | solution.py:336
  37.3 12.6 %collective-permute-start.4 = (bf16[640,384]{1,0:T(8,128)(2,1)S(1)}, bf16[640,384]{1,0:T(8,128)(2,1)S(1)}, u32[]{:S(2)}, u32[]{:S(2)}) collective-permute-start(bf16[640,384]{1,0:T(8,128)(2,1)S(1)} %shard_map.123.refs_0_), channel_id=1, source_target_pairs={{1,0},{2,1},{3,2},{4,3},{5,4},{6,5},{7,6},{0,7},{9,8},{10,9},{11,1... | collective-permute-start | bytes 1474568 | tf_op jit(solution)/shard_map/ppermute | solution.py:336
  41.1 18.2 %collective-permute-start.7 = (bf16[48,5120]{1,0:T(8,128)(2,1)}, bf16[48,5120]{1,0:T(8,128)(2,1)}, u32[]{:S(2)}, u32[]{:S(2)}) collective-permute-start(bf16[48,5120]{1,0:T(8,128)(2,1)} %bitcast.29), channel_id=1, source_target_pairs={{8,0},{16,8},{24,16},{0,24},{9,1},{17,9},{25,17},{1,25},{10,2},{18... | collective-permute-start | bytes 1474568 | tf_op jit(solution)/shard_map/ppermute | solution.py:336
  45.0 18.6 %collective-permute-start.8 = (bf16[48,5120]{1,0:T(8,128)(2,1)}, bf16[48,5120]{1,0:T(8,128)(2,1)}, u32[]{:S(2)}, u32[]{:S(2)}) collective-permute-start(bf16[48,5120]{1,0:T(8,128)(2,1)} %bitcast.32), channel_id=1, source_target_pairs={{24,0},{0,8},{8,16},{16,24},{25,1},{1,9},{9,17},{17,25},{26,2},{2,... | collective-permute-start | bytes 1474568 | tf_op jit(solution)/shard_map/ppermute | solution.py:336
  48.9 42.9 %copy-start.13 = (bf16[640,384]{1,0:T(8,128)(2,1)}, bf16[640,384]{1,0:T(8,128)(2,1)S(1)}, u32[]{:S(2)}) copy-start(bf16[640,384]{1,0:T(8,128)(2,1)S(1)} %collective-permute-done.3.refs_1_) | copy-start | bytes 1474564
  49.9 41.9 %copy-start.14 = (bf16[640,384]{1,0:T(8,128)(2,1)}, bf16[640,384]{1,0:T(8,128)(2,1)S(1)}, u32[]{:S(2)}) copy-start(bf16[640,384]{1,0:T(8,128)(2,1)S(1)} %collective-permute-done.4.refs_2_) | copy-start | bytes 1474564
  49.9 13.9 %collective-permute-start.5 = (bf16[640,384]{1,0:T(8,128)(2,1)S(1)}, bf16[640,384]{1,0:T(8,128)(2,1)S(1)}, u32[]{:S(2)}, u32[]{:S(2)}) collective-permute-start(bf16[640,384]{1,0:T(8,128)(2,1)S(1)} %collective-permute-done.3.refs_1_), channel_id=1, source_target_pairs={{7,0},{0,1},{1,2},{2,3},{3,4},{4,5},{5,6},{6,7},{15,8},{8,9},{9,10... | collective-permute-start | bytes 1474568 | tf_op jit(solution)/shard_map/ppermute | solution.py:336
  53.1 13.1 %collective-permute-start.6 = (bf16[640,384]{1,0:T(8,128)(2,1)S(1)}, bf16[640,384]{1,0:T(8,128)(2,1)S(1)}, u32[]{:S(2)}, u32[]{:S(2)}) collective-permute-start(bf16[640,384]{1,0:T(8,128)(2,1)S(1)} %collective-permute-done.4.refs_2_), channel_id=1, source_target_pairs={{1,0},{2,1},{3,2},{4,3},{5,4},{6,5},{7,6},{0,7},{9,8},{10,9},{11,1... | collective-permute-start | bytes 1474568 | tf_op jit(solution)/shard_map/ppermute | solution.py:336
  57.0 20.9 %collective-permute-start.11 = (bf16[48,5120]{1,0:T(8,128)(2,1)}, bf16[48,5120]{1,0:T(8,128)(2,1)S(1)}, u32[]{:S(2)}, u32[]{:S(2)}) collective-permute-start(bf16[48,5120]{1,0:T(8,128)(2,1)} %bitcast.30), channel_id=1, source_target_pairs={{24,0},{0,8},{8,16},{16,24},{25,1},{1,9},{9,17},{17,25},{26,2},{2,... | collective-permute-start | bytes 1474568 | tf_op jit(solution)/shard_map/ppermute | solution.py:336
  59.3 20.6 %collective-permute-start.12 = (bf16[48,5120]{1,0:T(8,128)(2,1)}, bf16[48,5120]{1,0:T(8,128)(2,1)S(1)}, u32[]{:S(2)}, u32[]{:S(2)}) collective-permute-start(bf16[48,5120]{1,0:T(8,128)(2,1)} %bitcast.33), channel_id=1, source_target_pairs={{8,0},{16,8},{24,16},{0,24},{9,1},{17,9},{25,17},{1,25},{10,2},{18... | collective-permute-start | bytes 1474568 | tf_op jit(solution)/shard_map/ppermute | solution.py:336
  63.8 19.5 %copy-start.15 = (bf16[640,384]{1,0:T(8,128)(2,1)}, bf16[640,384]{1,0:T(8,128)(2,1)S(1)}, u32[]{:S(2)}) copy-start(bf16[640,384]{1,0:T(8,128)(2,1)S(1)} %collective-permute-done.5.refs_3_) | copy-start | bytes 1474564
  66.2 14.2 %copy-start.16 = (bf16[640,384]{1,0:T(8,128)(2,1)}, bf16[640,384]{1,0:T(8,128)(2,1)S(1)}, u32[]{:S(2)}) copy-start(bf16[640,384]{1,0:T(8,128)(2,1)S(1)} %collective-permute-done.6.refs_4_) | copy-start | bytes 1474564
  66.2 13.8 %collective-permute-start.9 = (bf16[640,384]{1,0:T(8,128)(2,1)S(1)}, bf16[640,384]{1,0:T(8,128)(2,1)}, u32[]{:S(2)}, u32[]{:S(2)}) collective-permute-start(bf16[640,384]{1,0:T(8,128)(2,1)S(1)} %collective-permute-done.5.refs_3_), channel_id=1, source_target_pairs={{7,0},{0,1},{1,2},{2,3},{3,4},{4,5},{5,6},{6,7},{15,8},{8,9},{9,10... | collective-permute-start | bytes 1474568 | tf_op jit(solution)/shard_map/ppermute | solution.py:336
  70.0 10.4 %collective-permute-start.10 = (bf16[640,384]{1,0:T(8,128)(2,1)S(1)}, bf16[640,384]{1,0:T(8,128)(2,1)S(1)}, u32[]{:S(2)}, u32[]{:S(2)}) collective-permute-start(bf16[640,384]{1,0:T(8,128)(2,1)S(1)} %collective-permute-done.6.refs_4_), channel_id=1, source_target_pairs={{1,0},{2,1},{3,2},{4,3},{5,4},{6,5},{7,6},{0,7},{9,8},{10,9},{11,1... | collective-permute-start | bytes 1474568 | tf_op jit(solution)/shard_map/ppermute | solution.py:336
  72.7 18.9 %collective-permute-start.14 = (bf16[48,5120]{1,0:T(8,128)(2,1)}, bf16[48,5120]{1,0:T(8,128)(2,1)}, u32[]{:S(2)}, u32[]{:S(2)}) collective-permute-start(bf16[48,5120]{1,0:T(8,128)(2,1)} %collective-permute-done.7.refs_10_), channel_id=1, source_target_pairs={{8,0},{16,8},{24,16},{0,24},{9,1},{17,9},{25,17},{1,25},{10,2},{18... | collective-permute-start | bytes 1474568 | tf_op jit(solution)/shard_map/ppermute | solution.py:336
  78.0 11.7 %copy-start.17 = (bf16[48,5120]{1,0:T(8,128)(2,1)}, bf16[48,5120]{1,0:T(8,128)(2,1)S(1)}, u32[]{:S(2)}) copy-start(bf16[48,5120]{1,0:T(8,128)(2,1)S(1)} %collective-permute-done.11.refs_12_) | copy-start | bytes 1474564
  78.0 13.6 %collective-permute-start.15 = (bf16[48,5120]{1,0:T(8,128)(2,1)}, bf16[48,5120]{1,0:T(8,128)(2,1)}, u32[]{:S(2)}, u32[]{:S(2)}) collective-permute-start(bf16[48,5120]{1,0:T(8,128)(2,1)} %collective-permute-done.8.refs_13_), channel_id=1, source_target_pairs={{24,0},{0,8},{8,16},{16,24},{25,1},{1,9},{9,17},{17,25},{26,2},{2,... | collective-permute-start | bytes 1474568 | tf_op jit(solution)/shard_map/ppermute | solution.py:336
  79.9 9.7 %copy-start.18 = (bf16[48,5120]{1,0:T(8,128)(2,1)}, bf16[48,5120]{1,0:T(8,128)(2,1)S(1)}, u32[]{:S(2)}) copy-start(bf16[48,5120]{1,0:T(8,128)(2,1)S(1)} %collective-permute-done.12.refs_11_) | copy-start | bytes 1474564
  80.4 9.3 %copy-start.19 = (bf16[640,384]{1,0:T(8,128)(2,1)}, bf16[640,384]{1,0:T(8,128)(2,1)S(1)}, u32[]{:S(2)}) copy-start(bf16[640,384]{1,0:T(8,128)(2,1)S(1)} %collective-permute-done.10.refs_6_) | copy-start | bytes 1474564
  80.4 11.4 %collective-permute-start.13 = (bf16[640,384]{1,0:T(8,128)(2,1)}, bf16[640,384]{1,0:T(8,128)(2,1)}, u32[]{:S(2)}, u32[]{:S(2)}) collective-permute-start(bf16[640,384]{1,0:T(8,128)(2,1)} %collective-permute-done.9.refs_5_), channel_id=1, source_target_pairs={{7,0},{0,1},{1,2},{2,3},{3,4},{4,5},{5,6},{6,7},{15,8},{8,9},{9,10... | collective-permute-start | bytes 1474568 | tf_op jit(solution)/shard_map/ppermute | solution.py:336
  83.3 15.7 %collective-permute-start.16 = (bf16[160,1536]{1,0:T(8,128)(2,1)S(1)}, bf16[160,1536]{1,0:T(8,128)(2,1)S(1)}, u32[]{:S(2)}, u32[]{:S(2)}) collective-permute-start(bf16[160,1536]{1,0:T(8,128)(2,1)S(1)} %bitcast.19), channel_id=1, source_target_pairs={{8,0},{16,8},{24,16},{0,24},{9,1},{17,9},{25,17},{1,25},{10,2},{18... | collective-permute-start | bytes 1474568 | tf_op jit(solution)/shard_map/ppermute | solution.py:336
  89.7 10.8 %collective-permute-start.17 = (bf16[160,1536]{1,0:T(8,128)(2,1)S(1)}, bf16[160,1536]{1,0:T(8,128)(2,1)S(1)}, u32[]{:S(2)}, u32[]{:S(2)}) collective-permute-start(bf16[160,1536]{1,0:T(8,128)(2,1)S(1)} %bitcast.20), channel_id=1, source_target_pairs={{24,0},{0,8},{8,16},{16,24},{25,1},{1,9},{9,17},{17,25},{26,2},{2,... | collective-permute-start | bytes 1474568 | tf_op jit(solution)/shard_map/ppermute | solution.py:336
  100.5 0.8 copy-start.3
  100.5 64.8 %copy-start.10 = (bf16[128,160]{0,1:T(8,128)(2,1)S(1)}, bf16[128,160]{0,1:T(8,128)(2,1)}, u32[]{:S(2)}) copy-start(bf16[128,160]{0,1:T(8,128)(2,1)} %param.11) | copy-start | bytes 122884
  100.5 64.8 %copy-start.11 = (s32[16,128]{1,0:T(8,128)S(1)}, s32[16,128]{1,0:T(8,128)}, u32[]{:S(2)}) copy-start(s32[16,128]{1,0:T(8,128)} %get-tuple-element.31.slot_ref) | copy-start | bytes 24580
  100.5 64.8 %copy-start.12 = (f32[16,128]{1,0:T(8,128)S(1)}, f32[16,128]{1,0:T(8,128)}, u32[]{:S(2)}) copy-start(f32[16,128]{1,0:T(8,128)} %get-tuple-element.32.gate_ref) | copy-start | bytes 24580
  101.2 29.0 %all-to-all-start.1 = ((bf16[8,224,256]{2,1,0:T(8,128)(2,1)}), bf16[8,224,256]{2,1,0:T(8,128)(2,1)S(1)}, u32[]{:S(2)}, u32[]{:S(2)}) async-start(bf16[8,224,256]{2,1,0:T(8,128)(2,1)} %shard_map.124), calls=%async_computation.1 | async-start | bytes 1835008 | tf_op jit(solution)/shard_map/all_to_all | solution.py:325
  107.6 41.4 %copy-start.1 = (bf16[128,5120]{1,0:T(8,128)(2,1)S(1)}, bf16[128,5120]{1,0:T(8,128)(2,1)}, u32[]{:S(2)}) copy-start(bf16[128,5120]{1,0:T(8,128)(2,1)} %vocab_ref.1) | copy-start | bytes 3932164
  107.6 12.0 %collective-permute-start.18 = (bf16[160,1536]{1,0:T(8,128)(2,1)}, bf16[160,1536]{1,0:T(8,128)(2,1)S(1)}, u32[]{:S(2)}, u32[]{:S(2)}) collective-permute-start(bf16[160,1536]{1,0:T(8,128)(2,1)} %copy-done.3), channel_id=1, source_target_pairs={{24,0},{0,8},{8,16},{16,24},{25,1},{1,9},{9,17},{17,25},{26,2},{2,... | collective-permute-start | bytes 1474568 | tf_op jit(solution)/shard_map/ppermute | solution.py:336
  119.6 0.8 copy-start.5
  130.2 1.0 copy-start.4
  131.2 1.0 copy-start.6
  137.9 0.7 copy-start.8
  138.6 26.7 %all-to-all-start.2 = ((bf16[64,24,128]{2,1,0:T(8,128)(2,1)}), bf16[64,24,128]{2,1,0:T(8,128)(2,1)S(1)}, u32[]{:S(2)}, u32[]{:S(2)}) async-start(bf16[64,24,128]{2,1,0:T(8,128)(2,1)} %copy-done.8), calls=%async_computation.2 | async-start | bytes 786432 | tf_op jit(solution)/shard_map/all_to_all | solution.py:325
  149.0 39.5 %copy-start.20 = (s32[64]{0:T(128)S(1)}, s32[64]{0:T(128)}, u32[]{:S(2)}) copy-start(s32[64]{0:T(128)} %param.21) | copy-start | bytes 772
  149.0 39.8 %collective-permute-start.22 = (bf16[128,5120]{1,0:T(8,128)(2,1)S(1)}, bf16[128,5120]{1,0:T(8,128)(2,1)S(1)}, u32[]{:S(2)}, u32[]{:S(2)}) collective-permute-start(bf16[128,5120]{1,0:T(8,128)(2,1)S(1)} %copy-done.1), channel_id=1, source_target_pairs={{0,32},{32,0},{1,33},{33,1},{2,34},{34,2},{3,35},{35,3},{4,36},{36... | collective-permute-start | bytes 3932168 | tf_op jit(solution)/shard_map/ppermute | solution.py:466
  151.4 10.0 %collective-permute-start.19 = (bf16[384,128]{1,0:T(8,128)(2,1)S(1)}, bf16[384,128]{1,0:T(8,128)(2,1)S(1)}, u32[]{:S(2)}, u32[]{:S(2)}) collective-permute-start(bf16[384,128]{1,0:T(8,128)(2,1)S(1)} %get-tuple-element.57.refs_0_), channel_id=1, source_target_pairs={{8,0},{16,8},{24,16},{0,24},{9,1},{17,9},{25,17},{1,25},{10,2},{18... | collective-permute-start | bytes 294920 | tf_op jit(solution)/shard_map/ppermute | solution.py:336
  155.8 7.7 %collective-permute-start.20 = (bf16[384,128]{1,0:T(8,128)(2,1)S(1)}, bf16[384,128]{1,0:T(8,128)(2,1)S(1)}, u32[]{:S(2)}, u32[]{:S(2)}) collective-permute-start(bf16[384,128]{1,0:T(8,128)(2,1)S(1)} %get-tuple-element.57.refs_0_), channel_id=1, source_target_pairs={{24,0},{0,8},{8,16},{16,24},{25,1},{1,9},{9,17},{17,25},{26,2},{2,... | collective-permute-start | bytes 294920 | tf_op jit(solution)/shard_map/ppermute | solution.py:336
  157.7 7.5 %collective-permute-start.21 = (bf16[384,128]{1,0:T(8,128)(2,1)S(1)}, bf16[384,128]{1,0:T(8,128)(2,1)S(1)}, u32[]{:S(2)}, u32[]{:S(2)}) collective-permute-start(bf16[384,128]{1,0:T(8,128)(2,1)S(1)} %get-tuple-element.57.refs_0_), channel_id=1, source_target_pairs={{16,0},{24,8},{0,16},{8,24},{17,1},{25,9},{1,17},{9,25},{18,2},{26... | collective-permute-start | bytes 294920 | tf_op jit(solution)/shard_map/ppermute | solution.py:336
  165.3 1.0 copy-start.7
  167.7 15.2 %all-to-all-start.3 = ((bf16[16,4,160]{2,1,0:T(4,128)(2,1)}), bf16[16,4,160]{2,1,0:T(4,128)(2,1)S(1)}, u32[]{:S(2)}, u32[]{:S(2)}) async-start(bf16[16,4,160]{2,1,0:T(4,128)(2,1)} %get-tuple-element.59), calls=%async_computation.3 | async-start | bytes 65536 | tf_op jit(solution)/shard_map/all_to_all | solution.py:325
  184.0 14.9 %all-to-all-start.4 = ((bf16[32,40,128]{2,1,0:T(8,128)(2,1)}), bf16[32,40,128]{2,1,0:T(8,128)(2,1)S(1)}, u32[]{:S(2)}, u32[]{:S(2)}) async-start(bf16[32,40,128]{2,1,0:T(8,128)(2,1)} %shard_map.127), calls=%async_computation.4 | async-start | bytes 655360 | tf_op jit(solution)/shard_map/all_to_all | solution.py:325

commit v8 on v7

--- a/solution.py
+++ b/solution.py
@@ -199,10 +199,11 @@
     fold = Fold(width, lanes, near)
     pairs = []
     for n, weight in enumerate(weights):
-        pairs.append((weight.at[:lanes, :], down_ref.at[n, :lanes, :]))
+        base = 2 * n * lanes
+        pairs.append((weight.at[:lanes, :], down_ref.at[base : base + lanes, :]))
         for q in range(fold.parts):
-            at = lanes + q * fold.rest
-            pairs.append((weight.at[lanes:, :], down_ref.at[n, at : at + fold.rest, :]))
+            at = base + lanes + q * fold.rest
+            pairs.append((weight.at[lanes:, :], down_ref.at[at : at + fold.rest, :]))
     copies = fetch(pairs, sems)
     ny = hidden_ref.shape[0]
     units = flat_ref.shape[0] // (nx * ny)
@@ -222,8 +223,9 @@
     own_part = lax.div(iota(dims, 0), fold.rest) == fold.part_of(iota(dims, 1))
     for copy in copies:
         copy.wait()
+    outs = nn(down_ref[...], flat_ref[...])
     for n in range(nx):
-        out = nn(down_ref[n], flat_ref[...])
+        out = outs[2 * n * lanes : 2 * (n + 1) * lanes]
         full = nt(eye, out[:lanes].astype(BF16)).astype(BF16)
         rest = nt(lines, jnp.where(own_part, out[lanes:], 0.0).astype(BF16))
         for g in range(count // near):
@@ -231,8 +233,9 @@
             out_ref[g * nx + own[n], near:, :] = rest[g * EIGHT : (g + 1) * EIGHT, :].astype(BF16)
 
 
-def combine_body(x_ref, slot_ref, gate_ref, back_ref, tok_ref, down_ref, *refs):
-    *hidden, out_ref, scored_ref = refs
+def combine_body(x_ref, down_far, slot_ref, gate_ref, back_ref, tok_ref, *refs):
+    *hidden, out_ref, scored_ref, down_ref, sems = refs
+    copies = fetch([(down_far, down_ref)], sems)
     experts, rows = slot_ref.shape
     width = tok_ref.shape[0]
     lanes = back_ref.shape[2]
@@ -271,6 +274,7 @@
             part = got[q * fold.rest : (q + 1) * fold.rest]
             rest = rest + part[:, 2 * q * rows : (2 * q + 1) * rows] + part[:, (2 * q + 1) * rows : (2 * q + 2) * rows]
     routed = jnp.concatenate([full, rest], axis=0)
+    copies[0].wait()
     shared = jnp.zeros((width, rows), F32)
     for shift, units in zip(SHIFTS, hidden):
         depth = units.shape[0]
@@ -429,7 +433,8 @@
         ],
         limit=56,
     )
-    hidden, d1, d3 = lax.optimization_barrier((hidden, after["d1"], after["d3"]))
+    hidden, d3 = lax.optimization_barrier((hidden, after["d3"]))
+    d1 = after["d1"]
     d2 = from_shift(d3, "x", nx - 1)
     all_hidden = exchange(hidden, "y")
     returned, own_shared = call(
@@ -440,7 +445,7 @@
         far=range(2, 2 + nx),
         scratch=[
             pltpu.VMEM((lanes * units, count), BF16),
-            pltpu.VMEM((nx, 2 * rows, lanes * units), BF16),
+            pltpu.VMEM((2 * nx * rows, lanes * units), BF16),
             pltpu.SemaphoreType.DMA((nx * (1 + rows // (width - rows)),)),
         ],
         limit=40,
@@ -450,9 +455,13 @@
     layer_out, scored = call(
         combine_body,
         [shape((width, rows)), shape((groups, SCORE_E, width))],
-        [x_at, slot, gate, back, tok, shared_down.T, *near_shared],
+        [x_at, shared_down.T, slot, gate, back, tok, *near_shared],
         scalars=1,
-    )
+        far=(1,),
+        scratch=[pltpu.VMEM((width, lanes * units), BF16), pltpu.SemaphoreType.DMA((1,))],
+    )
+    scored, moved = lax.optimization_barrier((scored, vocab))
+    other_vocab = lax.ppermute(moved, "core", [(0, 1), (1, 0)])
     line_rows = exchange(scored, LINE).reshape(groups * SCORE_E, width)
     count = groups * SCORE_E // nc
     core = lax.axis_index("core").astype(jnp.int32)
@@ -463,7 +472,6 @@
         scalars=1,
     )
     every = exchange(packed, PLANE)
-    other_vocab = lax.ppermute(vocab, "core", [(0, 1), (1, 0)])
     place = lax.axis_index("x") * ny + lax.axis_index("y")
     first = [
         (((lax.axis_index("z") * nc + c) * lanes + place) * vocab.shape[0]).astype(jnp.int32)

time: 230 us -> 226 us (0.983)
  local copies, waits for them, and re-layouts: 7.03 us -> 2.4 us
    ppermute x22, waiting for transfers between devices: 24.8 us -> 31.7 us  [from_shift(): lax.ppermute(value, axis, [((i + shift) % count, i) for i in range(count)])]
    all_to_all x5, waiting for transfers between devices: 28.6 us -> 23.8 us  [exchange(): return lax.all_to_all(value, axes, 0, 0, tiled=True)]
    unnamed x42 -> x36, local copies, waits for them, and re-layouts: 6.21 us -> 1.58 us
  transfers between devices with their start and end apart: 28 -> 28, of which waited for: 16 -> 18; matrix products, arithmetic and copies ran while one was open for 0% -> 0% of each run, Pallas kernels for 4% -> 4%
where the time goes in v8:
time: 226 us; the launch traced here: 225 us
  starting transfers between devices  118 us (52%)
  waiting for transfers between devices  55.5 us (25%)
  blocking collectives  27.8 us (12%)
  Pallas kernels  19.4 us (9%)
  local copies, waits for them, and re-layouts  2.4 us (1%)
    ppermute x22, starting transfers between devices, from_shift(): lax.ppermute(value, axis, [((i + shift) % count, i) for i in range(count)])  72.3 us
    all_to_all x5, starting transfers between devices, exchange(): return lax.all_to_all(value, axes, 0, 0, tiled=True)  42.7 us
    ppermute x22, waiting for transfers between devices, from_shift(): lax.ppermute(value, axis, [((i + shift) % count, i) for i in range(count)])  31.7 us
    all_to_all x2, blocking collectives, spread_all(): lax.all_to_all(jnp.broadcast_to(value[None], (count, *value.shape)), axes...  27.8 us
    all_to_all x5, waiting for transfers between devices, exchange(): return lax.all_to_all(value, axes, 0, 0, tiled=True)  23.8 us
    pallas_call x7, Pallas kernels, call(): pl.pallas_call(body, out_shape=outs, in_specs=specs, out_specs=[pl.BlockS...  19.4 us
  transfers between devices with their start and end apart: 28, of which 18 were waited for; matrix products, arithmetic and copies ran while one was open for 0% of the time, Pallas kernels for 4%

profile of v8, /device:TPU:1, one launch (start us, length us, event | category | flops | bytes accessed | tf_op | source)
XLA Modules:
  0.0 224.8 jit_solution(447255494522674983)
XLA Ops:
  0.6 2.6 %shard_map.122 = (bf16[64,24,128]{2,1,0:T(8,128)(2,1)}, s32[16,128]{1,0:T(8,128)}, f32[16,128]{1,0:T(8,128)}) custom-call(s32[6,128]{1,0:T(8,128)} %bitcast.37, f32[6,128]{1,0:T(8,128)} %bitcast.38, bf16[160,128]{1,0:T(8,128)(2,1)} %bitcast.23), custom_call_target="tpu_custom_call" | custom-call | bytes 456704 | tf_op jit(solution)/shard_map/pallas_call | solution.py:25
  3.3 14.8 %all-to-all-start = ((bf16[64,24,128]{2,1,0:T(8,128)(2,1)}), bf16[64,24,128]{2,1,0:T(8,128)(2,1)S(1)}, u32[]{:S(2)}, u32[]{:S(2)}) async-start(bf16[64,24,128]{2,1,0:T(8,128)(2,1)} %get-tuple-element.34), calls=%async_computation | async-start | bytes 786432 | tf_op jit(solution)/shard_map/all_to_all | solution.py:329
  18.1 4.5 %collective-permute-start = (bf16[160,128]{1,0:T(8,128)(2,1)}, bf16[160,128]{1,0:T(8,128)(2,1)S(1)}, u32[]{:S(2)}, u32[]{:S(2)}) collective-permute-start(bf16[160,128]{1,0:T(8,128)(2,1)} %bitcast.24), channel_id=1, source_target_pairs={{8,0},{16,8},{24,16},{0,24},{9,1},{17,9},{25,17},{1,25},{10,2},{18... | collective-permute-start | bytes 122888 | tf_op jit(solution)/shard_map/ppermute | solution.py:340
  22.6 1.9 collective-permute-start.1
  24.6 3.7 %collective-permute-start.2 = (bf16[160,128]{1,0:T(8,128)(2,1)}, bf16[160,128]{1,0:T(8,128)(2,1)S(1)}, u32[]{:S(2)}, u32[]{:S(2)}) collective-permute-start(bf16[160,128]{1,0:T(8,128)(2,1)} %bitcast.26), channel_id=1, source_target_pairs={{16,0},{24,8},{0,16},{8,24},{17,1},{25,9},{1,17},{9,25},{18,2},{26... | collective-permute-start | bytes 122888 | tf_op jit(solution)/shard_map/ppermute | solution.py:340
  28.2 1.1 collective-permute-done.1.refs_2_
  29.4 2.2 collective-permute-done.2.refs_3_
  31.6 1.2 all-to-all-done.in_ref
  32.7 0.8 copy-done.5
  33.5 0.5 shard_map.123.refs_0_
  34.1 3.2 %collective-permute-start.3 = (bf16[640,384]{1,0:T(8,128)(2,1)S(1)}, bf16[640,384]{1,0:T(8,128)(2,1)S(1)}, u32[]{:S(2)}, u32[]{:S(2)}) collective-permute-start(bf16[640,384]{1,0:T(8,128)(2,1)S(1)} %shard_map.123.refs_0_), channel_id=1, source_target_pairs={{7,0},{0,1},{1,2},{2,3},{3,4},{4,5},{5,6},{6,7},{15,8},{8,9},{9,10... | collective-permute-start | bytes 1474568 | tf_op jit(solution)/shard_map/ppermute | solution.py:340
  37.3 3.8 %collective-permute-start.4 = (bf16[640,384]{1,0:T(8,128)(2,1)S(1)}, bf16[640,384]{1,0:T(8,128)(2,1)S(1)}, u32[]{:S(2)}, u32[]{:S(2)}) collective-permute-start(bf16[640,384]{1,0:T(8,128)(2,1)S(1)} %shard_map.123.refs_0_), channel_id=1, source_target_pairs={{1,0},{2,1},{3,2},{4,3},{5,4},{6,5},{7,6},{0,7},{9,8},{10,9},{11,1... | collective-permute-start | bytes 1474568 | tf_op jit(solution)/shard_map/ppermute | solution.py:340
  41.1 3.8 %collective-permute-start.7 = (bf16[48,5120]{1,0:T(8,128)(2,1)}, bf16[48,5120]{1,0:T(8,128)(2,1)S(1)}, u32[]{:S(2)}, u32[]{:S(2)}) collective-permute-start(bf16[48,5120]{1,0:T(8,128)(2,1)} %bitcast.29), channel_id=1, source_target_pairs={{8,0},{16,8},{24,16},{0,24},{9,1},{17,9},{25,17},{1,25},{10,2},{18... | collective-permute-start | bytes 1474568 | tf_op jit(solution)/shard_map/ppermute | solution.py:340
  45.0 1.9 collective-permute-start.8
  46.9 2.0 collective-permute-done.3.refs_1_
  48.9 0.9 collective-permute-done.4.refs_2_
  49.8 3.2 %collective-permute-start.5 = (bf16[640,384]{1,0:T(8,128)(2,1)S(1)}, bf16[640,384]{1,0:T(8,128)(2,1)S(1)}, u32[]{:S(2)}, u32[]{:S(2)}) collective-permute-start(bf16[640,384]{1,0:T(8,128)(2,1)S(1)} %collective-permute-done.3.refs_1_), channel_id=1, source_target_pairs={{7,0},{0,1},{1,2},{2,3},{3,4},{4,5},{5,6},{6,7},{15,8},{8,9},{9,10... | collective-permute-start | bytes 1474568 | tf_op jit(solution)/shard_map/ppermute | solution.py:340
  53.0 4.0 %collective-permute-start.6 = (bf16[640,384]{1,0:T(8,128)(2,1)S(1)}, bf16[640,384]{1,0:T(8,128)(2,1)S(1)}, u32[]{:S(2)}, u32[]{:S(2)}) collective-permute-start(bf16[640,384]{1,0:T(8,128)(2,1)S(1)} %collective-permute-done.4.refs_2_), channel_id=1, source_target_pairs={{1,0},{2,1},{3,2},{4,3},{5,4},{6,5},{7,6},{0,7},{9,8},{10,9},{11,1... | collective-permute-start | bytes 1474568 | tf_op jit(solution)/shard_map/ppermute | solution.py:340
  57.0 2.3 %collective-permute-start.11 = (bf16[48,5120]{1,0:T(8,128)(2,1)}, bf16[48,5120]{1,0:T(8,128)(2,1)S(1)}, u32[]{:S(2)}, u32[]{:S(2)}) collective-permute-start(bf16[48,5120]{1,0:T(8,128)(2,1)} %bitcast.30), channel_id=1, source_target_pairs={{24,0},{0,8},{8,16},{16,24},{25,1},{1,9},{9,17},{17,25},{26,2},{2,... | collective-permute-start | bytes 1474568 | tf_op jit(solution)/shard_map/ppermute | solution.py:340
  59.3 4.2 %collective-permute-start.12 = (bf16[48,5120]{1,0:T(8,128)(2,1)}, bf16[48,5120]{1,0:T(8,128)(2,1)S(1)}, u32[]{:S(2)}, u32[]{:S(2)}) collective-permute-start(bf16[48,5120]{1,0:T(8,128)(2,1)} %bitcast.33), channel_id=1, source_target_pairs={{8,0},{16,8},{24,16},{0,24},{9,1},{17,9},{25,17},{1,25},{10,2},{18... | collective-permute-start | bytes 1474568 | tf_op jit(solution)/shard_map/ppermute | solution.py:340
  63.6 0.3 collective-permute-done.5.refs_3_
  63.8 2.2 collective-permute-done.6.refs_4_
  66.0 4.0 %collective-permute-start.9 = (bf16[640,384]{1,0:T(8,128)(2,1)S(1)}, bf16[640,384]{1,0:T(8,128)(2,1)}, u32[]{:S(2)}, u32[]{:S(2)}) collective-permute-start(bf16[640,384]{1,0:T(8,128)(2,1)S(1)} %collective-permute-done.5.refs_3_), channel_id=1, source_target_pairs={{7,0},{0,1},{1,2},{2,3},{3,4},{4,5},{5,6},{6,7},{15,8},{8,9},{9,10... | collective-permute-start | bytes 1474568 | tf_op jit(solution)/shard_map/ppermute | solution.py:340
  70.0 2.5 %collective-permute-start.10 = (bf16[640,384]{1,0:T(8,128)(2,1)S(1)}, bf16[640,384]{1,0:T(8,128)(2,1)S(1)}, u32[]{:S(2)}, u32[]{:S(2)}) collective-permute-start(bf16[640,384]{1,0:T(8,128)(2,1)S(1)} %collective-permute-done.6.refs_4_), channel_id=1, source_target_pairs={{1,0},{2,1},{3,2},{4,3},{5,4},{6,5},{7,6},{0,7},{9,8},{10,9},{11,1... | collective-permute-start | bytes 1474568 | tf_op jit(solution)/shard_map/ppermute | solution.py:340
  72.5 5.5 %collective-permute-start.14 = (bf16[48,5120]{1,0:T(8,128)(2,1)S(1)}, bf16[48,5120]{1,0:T(8,128)(2,1)}, u32[]{:S(2)}, u32[]{:S(2)}) collective-permute-start(bf16[48,5120]{1,0:T(8,128)(2,1)S(1)} %collective-permute-done.7.refs_10_), channel_id=1, source_target_pairs={{8,0},{16,8},{24,16},{0,24},{9,1},{17,9},{25,17},{1,25},{10,2},{18... | collective-permute-start | bytes 1474568 | tf_op jit(solution)/shard_map/ppermute | solution.py:340
  78.0 1.9 collective-permute-start.15
  79.9 0.5 collective-permute-done.10.refs_6_
  80.4 2.9 %collective-permute-start.13 = (bf16[640,384]{1,0:T(8,128)(2,1)}, bf16[640,384]{1,0:T(8,128)(2,1)}, u32[]{:S(2)}, u32[]{:S(2)}) collective-permute-start(bf16[640,384]{1,0:T(8,128)(2,1)} %collective-permute-done.9.refs_5_), channel_id=1, source_target_pairs={{7,0},{0,1},{1,2},{2,3},{3,4},{4,5},{5,6},{6,7},{15,8},{8,9},{9,10... | collective-permute-start | bytes 1474568 | tf_op jit(solution)/shard_map/ppermute | solution.py:340
  83.4 2.2 collective-permute-start.16
  85.6 4.7 %collective-permute-done.15.refs_15_ = bf16[48,5120]{1,0:T(8,128)(2,1)} collective-permute-done((bf16[48,5120]{1,0:T(8,128)(2,1)}, bf16[48,5120]{1,0:T(8,128)(2,1)}, u32[]{:S(2)}, u32[]{:S(2)}) %collective-permute-start.15) | collective-permute-done | bytes 491552 | tf_op jit(solution)/shard_map/ppermute | solution.py:340
  90.4 1.4 collective-permute-done.13.refs_7_
  91.9 7.2 %shard_map.124 = bf16[8,224,256]{2,1,0:T(8,128)(2,1)} custom-call(s32[1]{0:T(128)} %bitcast.5.y_ref, bf16[640,384]{1,0:T(8,128)(2,1)} %copy-done, bf16[640,384]{1,0:T(8,128)(2,1)} %copy-done.9, bf16[640,384]{1,0:T(8,128)(2,1)} %copy-done.10, bf16[640,384]{1,0:T(8,128)(2,1)} %copy-done.12, bf16[640,384]{1,0:T(8,128)(2,1)} %copy-done.13, ...), custom_call_target="tpu_custom_call" | custom-call | bytes 9764868 | tf_op jit(solution)/shard_map/pallas_call | solution.py:25
  99.0 2.2 collective-permute-done.16.refs_2_
  101.2 4.5 %all-to-all-start.1 = ((bf16[8,224,256]{2,1,0:T(8,128)(2,1)}), bf16[8,224,256]{2,1,0:T(8,128)(2,1)S(1)}, u32[]{:S(2)}, u32[]{:S(2)}) async-start(bf16[8,224,256]{2,1,0:T(8,128)(2,1)} %shard_map.124), calls=%async_computation.1 | async-start | bytes 1835008 | tf_op jit(solution)/shard_map/all_to_all | solution.py:329
  105.7 0.0 copy-start.6
  105.7 0.0 copy-start.7
  105.8 4.8 %collective-permute-start.17 = (bf16[160,1536]{1,0:T(8,128)(2,1)S(1)}, bf16[160,1536]{1,0:T(8,128)(2,1)S(1)}, u32[]{:S(2)}, u32[]{:S(2)}) collective-permute-start(bf16[160,1536]{1,0:T(8,128)(2,1)S(1)} %bitcast.20), channel_id=1, source_target_pairs={{8,0},{16,8},{24,16},{0,24},{9,1},{17,9},{25,17},{1,25},{10,2},{18... | collective-permute-start | bytes 1474568 | tf_op jit(solution)/shard_map/ppermute | solution.py:340
  110.5 1.9 collective-permute-start.18
  112.5 3.8 %collective-permute-done.17.refs_1_ = bf16[160,1536]{1,0:T(8,128)(2,1)S(1)} collective-permute-done((bf16[160,1536]{1,0:T(8,128)(2,1)S(1)}, bf16[160,1536]{1,0:T(8,128)(2,1)S(1)}, u32[]{:S(2)}, u32[]{:S(2)}) %collective-permute-start.17) | collective-permute-done | bytes 491552 | tf_op jit(solution)/shard_map/ppermute | solution.py:340
  116.3 5.3 %collective-permute-done.18.refs_3_ = bf16[160,1536]{1,0:T(8,128)(2,1)S(1)} collective-permute-done((bf16[160,1536]{1,0:T(8,128)(2,1)S(1)}, bf16[160,1536]{1,0:T(8,128)(2,1)S(1)}, u32[]{:S(2)}, u32[]{:S(2)}) %collective-permute-start.18) | collective-permute-done | bytes 491552 | tf_op jit(solution)/shard_map/ppermute | solution.py:340
  121.6 5.1 %all-to-all-done.1.hidden_ref = bf16[8,224,256]{2,1,0:T(8,128)(2,1)S(1)} async-done(((bf16[8,224,256]{2,1,0:T(8,128)(2,1)}), bf16[8,224,256]{2,1,0:T(8,128)(2,1)S(1)}, u32[]{:S(2)}, u32[]{:S(2)}) %all-to-all-start.1) | async-done | bytes 917536 | tf_op jit(solution)/shard_map/all_to_all | solution.py:329
  126.7 4.5 %shard_map.125 = (bf16[64,24,128]{2,1,0:T(8,128)(2,1)S(1)}, bf16[384,128]{1,0:T(8,128)(2,1)S(1)}) custom-call(s32[1]{0:T(128)} %bitcast.x_ref, bf16[8,224,256]{2,1,0:T(8,128)(2,1)S(1)} %all-to-all-done.1.hidden_ref, bf16[160,1536]{1,0:T(8,128)(2,1)S(1)} %bitcast.21, bf16[160,1536]{1,0:T(8,128)(2,1)S(1)} %collective-permute-done.17.refs_1_, ...), custom_call_target="tpu_custom_call" | custom-call | bytes 3375108 | tf_op jit(solution)/shard_map/pallas_call | solution.py:25
  131.3 0.7 copy-done.4
  132.0 13.2 %all-to-all-start.2 = ((bf16[64,24,128]{2,1,0:T(8,128)(2,1)}), bf16[64,24,128]{2,1,0:T(8,128)(2,1)S(1)}, u32[]{:S(2)}, u32[]{:S(2)}) async-start(bf16[64,24,128]{2,1,0:T(8,128)(2,1)} %copy-done.4), calls=%async_computation.2 | async-start | bytes 786432 | tf_op jit(solution)/shard_map/all_to_all | solution.py:329
  145.2 4.5 %collective-permute-start.19 = (bf16[384,128]{1,0:T(8,128)(2,1)S(1)}, bf16[384,128]{1,0:T(8,128)(2,1)S(1)}, u32[]{:S(2)}, u32[]{:S(2)}) collective-permute-start(bf16[384,128]{1,0:T(8,128)(2,1)S(1)} %get-tuple-element.57.refs_0_), channel_id=1, source_target_pairs={{8,0},{16,8},{24,16},{0,24},{9,1},{17,9},{25,17},{1,25},{10,2},{18... | collective-permute-start | bytes 294920 | tf_op jit(solution)/shard_map/ppermute | solution.py:340
  149.8 1.9 collective-permute-start.20
  151.7 3.7 %collective-permute-start.21 = (bf16[384,128]{1,0:T(8,128)(2,1)S(1)}, bf16[384,128]{1,0:T(8,128)(2,1)S(1)}, u32[]{:S(2)}, u32[]{:S(2)}) collective-permute-start(bf16[384,128]{1,0:T(8,128)(2,1)S(1)} %get-tuple-element.57.refs_0_), channel_id=1, source_target_pairs={{16,0},{24,8},{0,16},{8,24},{17,1},{25,9},{1,17},{9,25},{18,2},{26... | collective-permute-start | bytes 294920 | tf_op jit(solution)/shard_map/ppermute | solution.py:340
  155.4 2.5 %collective-permute-done.20.refs_2_ = bf16[384,128]{1,0:T(8,128)(2,1)S(1)} collective-permute-done((bf16[384,128]{1,0:T(8,128)(2,1)S(1)}, bf16[384,128]{1,0:T(8,128)(2,1)S(1)}, u32[]{:S(2)}, u32[]{:S(2)}) %collective-permute-start.20) | collective-permute-done | bytes 98336 | tf_op jit(solution)/shard_map/ppermute | solution.py:340
  157.9 2.5 %collective-permute-done.21.refs_3_ = bf16[384,128]{1,0:T(8,128)(2,1)S(1)} collective-permute-done((bf16[384,128]{1,0:T(8,128)(2,1)S(1)}, bf16[384,128]{1,0:T(8,128)(2,1)S(1)}, u32[]{:S(2)}, u32[]{:S(2)}) %collective-permute-start.21) | collective-permute-done | bytes 98336 | tf_op jit(solution)/shard_map/ppermute | solution.py:340
  160.4 1.9 shard_map.126
  162.3 3.3 %collective-permute-start.22 = (bf16[128,5120]{1,0:T(8,128)(2,1)S(1)}, bf16[128,5120]{1,0:T(8,128)(2,1)S(1)}, u32[]{:S(2)}, u32[]{:S(2)}) collective-permute-start(bf16[128,5120]{1,0:T(8,128)(2,1)S(1)} %copy-done.1), channel_id=1, source_target_pairs={{0,32},{32,0},{1,33},{33,1},{2,34},{34,2},{3,35},{35,3},{4,36},{36... | collective-permute-start | bytes 3932168 | tf_op jit(solution)/shard_map/ppermute | solution.py:464
  165.7 6.0 %all-to-all-start.3 = ((bf16[16,4,160]{2,1,0:T(4,128)(2,1)}), bf16[16,4,160]{2,1,0:T(4,128)(2,1)S(1)}, u32[]{:S(2)}, u32[]{:S(2)}) async-start(bf16[16,4,160]{2,1,0:T(4,128)(2,1)} %get-tuple-element.60), calls=%async_computation.3 | async-start | bytes 65536 | tf_op jit(solution)/shard_map/all_to_all | solution.py:329
  171.7 7.4 %all-to-all-done.3 = bf16[16,4,160]{2,1,0:T(4,128)(2,1)S(1)} async-done(((bf16[16,4,160]{2,1,0:T(4,128)(2,1)}), bf16[16,4,160]{2,1,0:T(4,128)(2,1)S(1)}, u32[]{:S(2)}, u32[]{:S(2)}) %all-to-all-start.3) | async-done | bytes 20512 | tf_op jit(solution)/shard_map/all_to_all | solution.py:329
  179.1 1.0 shard_map.127
  180.1 4.1 %all-to-all-start.4 = ((bf16[32,40,128]{2,1,0:T(8,128)(2,1)}), bf16[32,40,128]{2,1,0:T(8,128)(2,1)S(1)}, u32[]{:S(2)}, u32[]{:S(2)}) async-start(bf16[32,40,128]{2,1,0:T(8,128)(2,1)} %shard_map.127), calls=%async_computation.4 | async-start | bytes 655360 | tf_op jit(solution)/shard_map/all_to_all | solution.py:329
  184.2 0.1 tile.10
  184.3 0.1 tile.12.targets_ref
  184.4 0.1 pad_add_fusion.at_ref
  184.5 10.2 %all-to-all-done.4.rows_ref = bf16[32,40,128]{2,1,0:T(8,128)(2,1)S(1)} async-done(((bf16[32,40,128]{2,1,0:T(8,128)(2,1)}), bf16[32,40,128]{2,1,0:T(8,128)(2,1)S(1)}, u32[]{:S(2)}, u32[]{:S(2)}) %all-to-all-start.4) | async-done | bytes 327712 | tf_op jit(solution)/shard_map/all_to_all | solution.py:329
  194.6 1.6 shard_map.128
  196.2 16.0 %all_to_all.35 = f32[32,1,128]{2,1,0:T(1,128)S(1)} all-to-all(f32[32,1,128]{2,1,0:T(1,128)S(1)} %broadcast_in_dim.7), channel_id=1, replica_groups=mesh['z'=8,'core'=2,'x'=4,'y'=8] {'x','y'}, dimensions={0} | all-to-all | bytes 32768 | tf_op jit(solution)/shard_map/all_to_all | solution.py:333
  212.2 11.8 %all_to_all.36 = f32[16,1,128]{2,1,0:T(1,128)S(1)} all-to-all(f32[16,1,128]{2,1,0:T(1,128)S(1)} %broadcast_in_dim.16), channel_id=1, replica_groups=mesh['z'=8,'core'=2,'x'=4,'y'=8] {'z','core'}, dimensions={0} | all-to-all | bytes 16384 | tf_op jit(solution)/shard_map/all_to_all | solution.py:333
  224.1 0.1 log_subtract_fusion
  224.2 0.6 reshape.36
  (49 shorter events, 0.2 us)
Async XLA Ops:
  0.6 82.8 %copy-start.2 = (bf16[1,1536,160]{1,2,0:T(8,128)(2,1)S(1)}, bf16[1,1536,160]{1,2,0:T(8,128)(2,1)}, u32[]{:S(2)}) copy-start(bf16[1,1536,160]{1,2,0:T(8,128)(2,1)} %param.16) | copy-start | bytes 1474564
  3.3 29.5 %all-to-all-start = ((bf16[64,24,128]{2,1,0:T(8,128)(2,1)}), bf16[64,24,128]{2,1,0:T(8,128)(2,1)S(1)}, u32[]{:S(2)}, u32[]{:S(2)}) async-start(bf16[64,24,128]{2,1,0:T(8,128)(2,1)} %get-tuple-element.34), calls=%async_computation | async-start | bytes 786432 | tf_op jit(solution)/shard_map/all_to_all | solution.py:329
  18.1 10.1 %collective-permute-start = (bf16[160,128]{1,0:T(8,128)(2,1)}, bf16[160,128]{1,0:T(8,128)(2,1)S(1)}, u32[]{:S(2)}, u32[]{:S(2)}) collective-permute-start(bf16[160,128]{1,0:T(8,128)(2,1)} %bitcast.24), channel_id=1, source_target_pairs={{8,0},{16,8},{24,16},{0,24},{9,1},{17,9},{25,17},{1,25},{10,2},{18... | collective-permute-start | bytes 122888 | tf_op jit(solution)/shard_map/ppermute | solution.py:340
  22.6 6.8 %collective-permute-start.1 = (bf16[160,128]{1,0:T(8,128)(2,1)}, bf16[160,128]{1,0:T(8,128)(2,1)S(1)}, u32[]{:S(2)}, u32[]{:S(2)}) collective-permute-start(bf16[160,128]{1,0:T(8,128)(2,1)} %bitcast.25), channel_id=1, source_target_pairs={{24,0},{0,8},{8,16},{16,24},{25,1},{1,9},{9,17},{17,25},{26,2},{2,... | collective-permute-start | bytes 122888 | tf_op jit(solution)/shard_map/ppermute | solution.py:340
  24.6 7.0 %collective-permute-start.2 = (bf16[160,128]{1,0:T(8,128)(2,1)}, bf16[160,128]{1,0:T(8,128)(2,1)S(1)}, u32[]{:S(2)}, u32[]{:S(2)}) collective-permute-start(bf16[160,128]{1,0:T(8,128)(2,1)} %bitcast.26), channel_id=1, source_target_pairs={{16,0},{24,8},{0,16},{8,24},{17,1},{25,9},{1,17},{9,25},{18,2},{26... | collective-permute-start | bytes 122888 | tf_op jit(solution)/shard_map/ppermute | solution.py:340
  32.7 0.8 copy-start.5
  34.1 57.8 %copy-start = (bf16[640,384]{1,0:T(8,128)(2,1)}, bf16[640,384]{1,0:T(8,128)(2,1)S(1)}, u32[]{:S(2)}) copy-start(bf16[640,384]{1,0:T(8,128)(2,1)S(1)} %shard_map.123.refs_0_) | copy-start | bytes 1474564
  34.1 14.8 %collective-permute-start.3 = (bf16[640,384]{1,0:T(8,128)(2,1)S(1)}, bf16[640,384]{1,0:T(8,128)(2,1)S(1)}, u32[]{:S(2)}, u32[]{:S(2)}) collective-permute-start(bf16[640,384]{1,0:T(8,128)(2,1)S(1)} %shard_map.123.refs_0_), channel_id=1, source_target_pairs={{7,0},{0,1},{1,2},{2,3},{3,4},{4,5},{5,6},{6,7},{15,8},{8,9},{9,10... | collective-permute-start | bytes 1474568 | tf_op jit(solution)/shard_map/ppermute | solution.py:340
  37.3 12.5 %collective-permute-start.4 = (bf16[640,384]{1,0:T(8,128)(2,1)S(1)}, bf16[640,384]{1,0:T(8,128)(2,1)S(1)}, u32[]{:S(2)}, u32[]{:S(2)}) collective-permute-start(bf16[640,384]{1,0:T(8,128)(2,1)S(1)} %shard_map.123.refs_0_), channel_id=1, source_target_pairs={{1,0},{2,1},{3,2},{4,3},{5,4},{6,5},{7,6},{0,7},{9,8},{10,9},{11,1... | collective-permute-start | bytes 1474568 | tf_op jit(solution)/shard_map/ppermute | solution.py:340
  41.1 18.2 %collective-permute-start.7 = (bf16[48,5120]{1,0:T(8,128)(2,1)}, bf16[48,5120]{1,0:T(8,128)(2,1)S(1)}, u32[]{:S(2)}, u32[]{:S(2)}) collective-permute-start(bf16[48,5120]{1,0:T(8,128)(2,1)} %bitcast.29), channel_id=1, source_target_pairs={{8,0},{16,8},{24,16},{0,24},{9,1},{17,9},{25,17},{1,25},{10,2},{18... | collective-permute-start | bytes 1474568 | tf_op jit(solution)/shard_map/ppermute | solution.py:340
  45.0 18.6 %collective-permute-start.8 = (bf16[48,5120]{1,0:T(8,128)(2,1)}, bf16[48,5120]{1,0:T(8,128)(2,1)}, u32[]{:S(2)}, u32[]{:S(2)}) collective-permute-start(bf16[48,5120]{1,0:T(8,128)(2,1)} %bitcast.32), channel_id=1, source_target_pairs={{24,0},{0,8},{8,16},{16,24},{25,1},{1,9},{9,17},{17,25},{26,2},{2,... | collective-permute-start | bytes 1474568 | tf_op jit(solution)/shard_map/ppermute | solution.py:340
  48.9 43.0 %copy-start.9 = (bf16[640,384]{1,0:T(8,128)(2,1)}, bf16[640,384]{1,0:T(8,128)(2,1)S(1)}, u32[]{:S(2)}) copy-start(bf16[640,384]{1,0:T(8,128)(2,1)S(1)} %collective-permute-done.3.refs_1_) | copy-start | bytes 1474564
  49.8 42.1 %copy-start.10 = (bf16[640,384]{1,0:T(8,128)(2,1)}, bf16[640,384]{1,0:T(8,128)(2,1)S(1)}, u32[]{:S(2)}) copy-start(bf16[640,384]{1,0:T(8,128)(2,1)S(1)} %collective-permute-done.4.refs_2_) | copy-start | bytes 1474564
  49.8 14.0 %collective-permute-start.5 = (bf16[640,384]{1,0:T(8,128)(2,1)S(1)}, bf16[640,384]{1,0:T(8,128)(2,1)S(1)}, u32[]{:S(2)}, u32[]{:S(2)}) collective-permute-start(bf16[640,384]{1,0:T(8,128)(2,1)S(1)} %collective-permute-done.3.refs_1_), channel_id=1, source_target_pairs={{7,0},{0,1},{1,2},{2,3},{3,4},{4,5},{5,6},{6,7},{15,8},{8,9},{9,10... | collective-permute-start | bytes 1474568 | tf_op jit(solution)/shard_map/ppermute | solution.py:340
  53.0 13.0 %collective-permute-start.6 = (bf16[640,384]{1,0:T(8,128)(2,1)S(1)}, bf16[640,384]{1,0:T(8,128)(2,1)S(1)}, u32[]{:S(2)}, u32[]{:S(2)}) collective-permute-start(bf16[640,384]{1,0:T(8,128)(2,1)S(1)} %collective-permute-done.4.refs_2_), channel_id=1, source_target_pairs={{1,0},{2,1},{3,2},{4,3},{5,4},{6,5},{7,6},{0,7},{9,8},{10,9},{11,1... | collective-permute-start | bytes 1474568 | tf_op jit(solution)/shard_map/ppermute | solution.py:340
  57.0 21.0 %collective-permute-start.11 = (bf16[48,5120]{1,0:T(8,128)(2,1)}, bf16[48,5120]{1,0:T(8,128)(2,1)S(1)}, u32[]{:S(2)}, u32[]{:S(2)}) collective-permute-start(bf16[48,5120]{1,0:T(8,128)(2,1)} %bitcast.30), channel_id=1, source_target_pairs={{24,0},{0,8},{8,16},{16,24},{25,1},{1,9},{9,17},{17,25},{26,2},{2,... | collective-permute-start | bytes 1474568 | tf_op jit(solution)/shard_map/ppermute | solution.py:340
  59.3 32.6 %copy-start.11 = (bf16[48,5120]{1,0:T(8,128)(2,1)}, bf16[48,5120]{1,0:T(8,128)(2,1)S(1)}, u32[]{:S(2)}) copy-start(bf16[48,5120]{1,0:T(8,128)(2,1)S(1)} %collective-permute-done.7.refs_10_) | copy-start | bytes 1474564
  59.3 20.6 %collective-permute-start.12 = (bf16[48,5120]{1,0:T(8,128)(2,1)}, bf16[48,5120]{1,0:T(8,128)(2,1)S(1)}, u32[]{:S(2)}, u32[]{:S(2)}) collective-permute-start(bf16[48,5120]{1,0:T(8,128)(2,1)} %bitcast.33), channel_id=1, source_target_pairs={{8,0},{16,8},{24,16},{0,24},{9,1},{17,9},{25,17},{1,25},{10,2},{18... | collective-permute-start | bytes 1474568 | tf_op jit(solution)/shard_map/ppermute | solution.py:340
  63.8 16.6 %copy-start.12 = (bf16[640,384]{1,0:T(8,128)(2,1)}, bf16[640,384]{1,0:T(8,128)(2,1)S(1)}, u32[]{:S(2)}) copy-start(bf16[640,384]{1,0:T(8,128)(2,1)S(1)} %collective-permute-done.5.refs_3_) | copy-start | bytes 1474564
  66.0 17.4 %copy-start.13 = (bf16[640,384]{1,0:T(8,128)(2,1)}, bf16[640,384]{1,0:T(8,128)(2,1)S(1)}, u32[]{:S(2)}) copy-start(bf16[640,384]{1,0:T(8,128)(2,1)S(1)} %collective-permute-done.6.refs_4_) | copy-start | bytes 1474564
  66.0 13.9 %collective-permute-start.9 = (bf16[640,384]{1,0:T(8,128)(2,1)S(1)}, bf16[640,384]{1,0:T(8,128)(2,1)}, u32[]{:S(2)}, u32[]{:S(2)}) collective-permute-start(bf16[640,384]{1,0:T(8,128)(2,1)S(1)} %collective-permute-done.5.refs_3_), channel_id=1, source_target_pairs={{7,0},{0,1},{1,2},{2,3},{3,4},{4,5},{5,6},{6,7},{15,8},{8,9},{9,10... | collective-permute-start | bytes 1474568 | tf_op jit(solution)/shard_map/ppermute | solution.py:340
  70.0 10.5 %collective-permute-start.10 = (bf16[640,384]{1,0:T(8,128)(2,1)S(1)}, bf16[640,384]{1,0:T(8,128)(2,1)S(1)}, u32[]{:S(2)}, u32[]{:S(2)}) collective-permute-start(bf16[640,384]{1,0:T(8,128)(2,1)S(1)} %collective-permute-done.6.refs_4_), channel_id=1, source_target_pairs={{1,0},{2,1},{3,2},{4,3},{5,4},{6,5},{7,6},{0,7},{9,8},{10,9},{11,1... | collective-permute-start | bytes 1474568 | tf_op jit(solution)/shard_map/ppermute | solution.py:340
  72.5 13.2 %collective-permute-start.14 = (bf16[48,5120]{1,0:T(8,128)(2,1)S(1)}, bf16[48,5120]{1,0:T(8,128)(2,1)}, u32[]{:S(2)}, u32[]{:S(2)}) collective-permute-start(bf16[48,5120]{1,0:T(8,128)(2,1)S(1)} %collective-permute-done.7.refs_10_), channel_id=1, source_target_pairs={{8,0},{16,8},{24,16},{0,24},{9,1},{17,9},{25,17},{1,25},{10,2},{18... | collective-permute-start | bytes 1474568 | tf_op jit(solution)/shard_map/ppermute | solution.py:340
  78.0 5.4 %copy-start.14 = (bf16[48,5120]{1,0:T(8,128)(2,1)}, bf16[48,5120]{1,0:T(8,128)(2,1)S(1)}, u32[]{:S(2)}) copy-start(bf16[48,5120]{1,0:T(8,128)(2,1)S(1)} %collective-permute-done.11.refs_12_) | copy-start | bytes 1474564
  78.0 12.4 %collective-permute-start.15 = (bf16[48,5120]{1,0:T(8,128)(2,1)}, bf16[48,5120]{1,0:T(8,128)(2,1)}, u32[]{:S(2)}, u32[]{:S(2)}) collective-permute-start(bf16[48,5120]{1,0:T(8,128)(2,1)} %collective-permute-done.8.refs_13_), channel_id=1, source_target_pairs={{24,0},{0,8},{8,16},{16,24},{25,1},{1,9},{9,17},{17,25},{26,2},{2,... | collective-permute-start | bytes 1474568 | tf_op jit(solution)/shard_map/ppermute | solution.py:340
  79.9 3.5 %copy-start.15 = (bf16[48,5120]{1,0:T(8,128)(2,1)}, bf16[48,5120]{1,0:T(8,128)(2,1)S(1)}, u32[]{:S(2)}) copy-start(bf16[48,5120]{1,0:T(8,128)(2,1)S(1)} %collective-permute-done.12.refs_11_) | copy-start | bytes 1474564
  80.4 2.9 %copy-start.16 = (bf16[640,384]{1,0:T(8,128)(2,1)}, bf16[640,384]{1,0:T(8,128)(2,1)S(1)}, u32[]{:S(2)}) copy-start(bf16[640,384]{1,0:T(8,128)(2,1)S(1)} %collective-permute-done.10.refs_6_) | copy-start | bytes 1474564
  80.4 11.4 %collective-permute-start.13 = (bf16[640,384]{1,0:T(8,128)(2,1)}, bf16[640,384]{1,0:T(8,128)(2,1)}, u32[]{:S(2)}, u32[]{:S(2)}) collective-permute-start(bf16[640,384]{1,0:T(8,128)(2,1)} %collective-permute-done.9.refs_5_), channel_id=1, source_target_pairs={{7,0},{0,1},{1,2},{2,3},{3,4},{4,5},{5,6},{6,7},{15,8},{8,9},{9,10... | collective-permute-start | bytes 1474568 | tf_op jit(solution)/shard_map/ppermute | solution.py:340
  83.4 17.8 %collective-permute-start.16 = (bf16[160,1536]{1,0:T(8,128)(2,1)S(1)}, bf16[160,1536]{1,0:T(8,128)(2,1)S(1)}, u32[]{:S(2)}, u32[]{:S(2)}) collective-permute-start(bf16[160,1536]{1,0:T(8,128)(2,1)S(1)} %bitcast.19), channel_id=1, source_target_pairs={{24,0},{0,8},{8,16},{16,24},{25,1},{1,9},{9,17},{17,25},{26,2},{2,... | collective-permute-start | bytes 1474568 | tf_op jit(solution)/shard_map/ppermute | solution.py:340
  101.2 25.5 %all-to-all-start.1 = ((bf16[8,224,256]{2,1,0:T(8,128)(2,1)}), bf16[8,224,256]{2,1,0:T(8,128)(2,1)S(1)}, u32[]{:S(2)}, u32[]{:S(2)}) async-start(bf16[8,224,256]{2,1,0:T(8,128)(2,1)} %shard_map.124), calls=%async_computation.1 | async-start | bytes 1835008 | tf_op jit(solution)/shard_map/all_to_all | solution.py:329
  105.7 54.7 %copy-start.3 = (bf16[1536,160]{0,1:T(8,128)(2,1)S(1)}, bf16[1536,160]{0,1:T(8,128)(2,1)}, u32[]{:S(2)}) copy-start(bf16[1536,160]{0,1:T(8,128)(2,1)} %param.19) | copy-start | bytes 1474564
  105.7 54.6 %copy-start.6 = (bf16[128,160]{0,1:T(8,128)(2,1)S(1)}, bf16[128,160]{0,1:T(8,128)(2,1)}, u32[]{:S(2)}) copy-start(bf16[128,160]{0,1:T(8,128)(2,1)} %param.11) | copy-start | bytes 122884
  105.7 54.6 %copy-start.7 = (s32[16,128]{1,0:T(8,128)S(1)}, s32[16,128]{1,0:T(8,128)}, u32[]{:S(2)}) copy-start(s32[16,128]{1,0:T(8,128)} %get-tuple-element.32.slot_ref) | copy-start | bytes 24580
  105.8 54.6 %copy-start.8 = (f32[16,128]{1,0:T(8,128)S(1)}, f32[16,128]{1,0:T(8,128)}, u32[]{:S(2)}) copy-start(f32[16,128]{1,0:T(8,128)} %get-tuple-element.33.gate_ref) | copy-start | bytes 24580
  105.8 10.5 %collective-permute-start.17 = (bf16[160,1536]{1,0:T(8,128)(2,1)S(1)}, bf16[160,1536]{1,0:T(8,128)(2,1)S(1)}, u32[]{:S(2)}, u32[]{:S(2)}) collective-permute-start(bf16[160,1536]{1,0:T(8,128)(2,1)S(1)} %bitcast.20), channel_id=1, source_target_pairs={{8,0},{16,8},{24,16},{0,24},{9,1},{17,9},{25,17},{1,25},{10,2},{18... | collective-permute-start | bytes 1474568 | tf_op jit(solution)/shard_map/ppermute | solution.py:340
  110.5 11.1 %collective-permute-start.18 = (bf16[160,1536]{1,0:T(8,128)(2,1)S(1)}, bf16[160,1536]{1,0:T(8,128)(2,1)S(1)}, u32[]{:S(2)}, u32[]{:S(2)}) collective-permute-start(bf16[160,1536]{1,0:T(8,128)(2,1)S(1)} %collective-permute-done.16.refs_2_), channel_id=1, source_target_pairs={{24,0},{0,8},{8,16},{16,24},{25,1},{1,9},{9,17},{17,25},{26,2},{2,... | collective-permute-start | bytes 1474568 | tf_op jit(solution)/shard_map/ppermute | solution.py:340
  131.3 0.7 copy-start.4
  132.0 30.3 %copy-start.1 = (bf16[128,5120]{1,0:T(8,128)(2,1)S(1)}, bf16[128,5120]{1,0:T(8,128)(2,1)}, u32[]{:S(2)}) copy-start(bf16[128,5120]{1,0:T(8,128)(2,1)} %vocab_ref.1) | copy-start | bytes 3932164
  132.0 28.4 %all-to-all-start.2 = ((bf16[64,24,128]{2,1,0:T(8,128)(2,1)}), bf16[64,24,128]{2,1,0:T(8,128)(2,1)S(1)}, u32[]{:S(2)}, u32[]{:S(2)}) async-start(bf16[64,24,128]{2,1,0:T(8,128)(2,1)} %copy-done.4), calls=%async_computation.2 | async-start | bytes 786432 | tf_op jit(solution)/shard_map/all_to_all | solution.py:329
  145.2 39.0 %copy-start.17 = (s32[64]{0:T(128)S(1)}, s32[64]{0:T(128)}, u32[]{:S(2)}) copy-start(s32[64]{0:T(128)} %param.21) | copy-start | bytes 772
  145.2 10.1 %collective-permute-start.19 = (bf16[384,128]{1,0:T(8,128)(2,1)S(1)}, bf16[384,128]{1,0:T(8,128)(2,1)S(1)}, u32[]{:S(2)}, u32[]{:S(2)}) collective-permute-start(bf16[384,128]{1,0:T(8,128)(2,1)S(1)} %get-tuple-element.57.refs_0_), channel_id=1, source_target_pairs={{8,0},{16,8},{24,16},{0,24},{9,1},{17,9},{25,17},{1,25},{10,2},{18... | collective-permute-start | bytes 294920 | tf_op jit(solution)/shard_map/ppermute | solution.py:340
  149.8 8.1 %collective-permute-start.20 = (bf16[384,128]{1,0:T(8,128)(2,1)S(1)}, bf16[384,128]{1,0:T(8,128)(2,1)S(1)}, u32[]{:S(2)}, u32[]{:S(2)}) collective-permute-start(bf16[384,128]{1,0:T(8,128)(2,1)S(1)} %get-tuple-element.57.refs_0_), channel_id=1, source_target_pairs={{24,0},{0,8},{8,16},{16,24},{25,1},{1,9},{9,17},{17,25},{26,2},{2,... | collective-permute-start | bytes 294920 | tf_op jit(solution)/shard_map/ppermute | solution.py:340
  151.7 8.7 %collective-permute-start.21 = (bf16[384,128]{1,0:T(8,128)(2,1)S(1)}, bf16[384,128]{1,0:T(8,128)(2,1)S(1)}, u32[]{:S(2)}, u32[]{:S(2)}) collective-permute-start(bf16[384,128]{1,0:T(8,128)(2,1)S(1)} %get-tuple-element.57.refs_0_), channel_id=1, source_target_pairs={{16,0},{24,8},{0,16},{8,24},{17,1},{25,9},{1,17},{9,25},{18,2},{26... | collective-permute-start | bytes 294920 | tf_op jit(solution)/shard_map/ppermute | solution.py:340
  162.3 32.3 %collective-permute-start.22 = (bf16[128,5120]{1,0:T(8,128)(2,1)S(1)}, bf16[128,5120]{1,0:T(8,128)(2,1)S(1)}, u32[]{:S(2)}, u32[]{:S(2)}) collective-permute-start(bf16[128,5120]{1,0:T(8,128)(2,1)S(1)} %copy-done.1), channel_id=1, source_target_pairs={{0,32},{32,0},{1,33},{33,1},{2,34},{34,2},{3,35},{35,3},{4,36},{36... | collective-permute-start | bytes 3932168 | tf_op jit(solution)/shard_map/ppermute | solution.py:464
  165.7 13.4 %all-to-all-start.3 = ((bf16[16,4,160]{2,1,0:T(4,128)(2,1)}), bf16[16,4,160]{2,1,0:T(4,128)(2,1)S(1)}, u32[]{:S(2)}, u32[]{:S(2)}) async-start(bf16[16,4,160]{2,1,0:T(4,128)(2,1)} %get-tuple-element.60), calls=%async_computation.3 | async-start | bytes 65536 | tf_op jit(solution)/shard_map/all_to_all | solution.py:329
  180.1 14.5 %all-to-all-start.4 = ((bf16[32,40,128]{2,1,0:T(8,128)(2,1)}), bf16[32,40,128]{2,1,0:T(8,128)(2,1)S(1)}, u32[]{:S(2)}, u32[]{:S(2)}) async-start(bf16[32,40,128]{2,1,0:T(8,128)(2,1)} %shard_map.127), calls=%async_computation.4 | async-start | bytes 655360 | tf_op jit(solution)/shard_map/all_to_all | solution.py:329

commit v9 on v8

--- a/solution.py
+++ b/solution.py
@@ -167,22 +167,29 @@
     width = blocks[0].shape[0] // nx
     ny = flat_ref.shape[0] // (nx * width)
     top = nx * units
+    depth = ny * width
     pairs = []
-    for n, weight in enumerate(weights):
-        at = n // 2 * units + (n % 2) * top if n < 2 * nx else n * units
-        pairs.append((weight, weight_ref.at[at : at + units, :]))
-    for block, shift in zip(blocks, RING):
-        y = lax.rem(y_ref[0] + shift, ny)
-        for n in range(nx):
-            at = pl.multiple_of((n * ny + y) * width, width)
-            pairs.append((block.at[n * width : (n + 1) * width, :], flat_ref.at[pl.ds(at, width), :]))
-    for copy in fetch(pairs, sems):
-        copy.wait()
+    for x in range(nx):
+        span = slice(x * depth, (x + 1) * depth)
+        for n, weight in enumerate(weights):
+            at = n // 2 * units + (n % 2) * top if n < 2 * nx else n * units
+            pairs.append((weight.at[:, span], weight_ref.at[at : at + units, span]))
+        for block, shift in zip(blocks, RING):
+            at = pl.multiple_of(x * depth + lax.rem(y_ref[0] + shift, ny) * width, width)
+            pairs.append((block.at[x * width : (x + 1) * width, :], flat_ref.at[pl.ds(at, width), :]))
+    copies = fetch(pairs, sems)
     cols = out_ref.shape[2]
-    both = nn(weight_ref[: 2 * top, :], flat_ref[:, :cols])
-    routed = glu(both[:top], both[top:])
-    both = nn(weight_ref[2 * top :, :], flat_ref[:, cols:])
-    own = glu(both[:units], both[units:])
+    routed = jnp.zeros((2 * top, cols), F32)
+    own = jnp.zeros((2 * units, flat_ref.shape[1] - cols), F32)
+    each = len(copies) // nx
+    for x in range(nx):
+        for copy in copies[x * each : (x + 1) * each]:
+            copy.wait()
+        span = slice(x * depth, (x + 1) * depth)
+        routed = routed + nn(weight_ref[: 2 * top, span], flat_ref[span, :cols])
+        own = own + nn(weight_ref[2 * top :, span], flat_ref[span, cols:])
+    routed = glu(routed[:top], routed[top:])
+    own = glu(own[:units], own[units:])
     fold = units // 2
     folded = jnp.concatenate([own[:fold], own[fold:]], axis=1)
     for y in range(ny):
@@ -429,7 +436,7 @@
         scratch=[
             pltpu.VMEM((lanes * width, count + rows), BF16),
             pltpu.VMEM((2 * (nx + 1) * units, lanes * width), BF16),
-            pltpu.SemaphoreType.DMA((2 * nx + 2 + lanes,)),
+            pltpu.SemaphoreType.DMA((nx * (2 * nx + 2 + ny),)),
         ],
         limit=56,
     )

time: 226 us -> 226 us (level)
  no operation moved by 1% of the time
where the time goes in v9:
time: 226 us; the launch traced here: 225 us
  starting transfers between devices  119 us (53%)
  waiting for transfers between devices  54.5 us (24%)
  blocking collectives  27.8 us (12%)
  Pallas kernels  19.5 us (9%)
  local copies, waits for them, and re-layouts  2.4 us (1%)
    ppermute x22, starting transfers between devices, from_shift(): lax.ppermute(value, axis, [((i + shift) % count, i) for i in range(count)])  72.5 us
    all_to_all x5, starting transfers between devices, exchange(): return lax.all_to_all(value, axes, 0, 0, tiled=True)  43.5 us
    ppermute x22, waiting for transfers between devices, from_shift(): lax.ppermute(value, axis, [((i + shift) % count, i) for i in range(count)])  31.5 us
    all_to_all x2, blocking collectives, spread_all(): lax.all_to_all(jnp.broadcast_to(value[None], (count, *value.shape)), axes...  27.8 us
    all_to_all x5, waiting for transfers between devices, exchange(): return lax.all_to_all(value, axes, 0, 0, tiled=True)  23 us
    pallas_call x7, Pallas kernels, call(): pl.pallas_call(body, out_shape=outs, in_specs=specs, out_specs=[pl.BlockS...  19.5 us
  transfers between devices with their start and end apart: 28, of which 18 were waited for; matrix products, arithmetic and copies ran while one was open for 0% of the time, Pallas kernels for 4%

profile of v9, /device:TPU:1, one launch (start us, length us, event | category | flops | bytes accessed | tf_op | source)
XLA Modules:
  0.0 224.9 jit_solution(14903965093828096460)
XLA Ops:
  0.6 2.6 %shard_map.122 = (bf16[64,24,128]{2,1,0:T(8,128)(2,1)}, s32[16,128]{1,0:T(8,128)}, f32[16,128]{1,0:T(8,128)}) custom-call(s32[6,128]{1,0:T(8,128)} %bitcast.37, f32[6,128]{1,0:T(8,128)} %bitcast.38, bf16[160,128]{1,0:T(8,128)(2,1)} %bitcast.23), custom_call_target="tpu_custom_call" | custom-call | bytes 456704 | tf_op jit(solution)/shard_map/pallas_call | solution.py:25
  3.3 14.8 %all-to-all-start = ((bf16[64,24,128]{2,1,0:T(8,128)(2,1)}), bf16[64,24,128]{2,1,0:T(8,128)(2,1)S(1)}, u32[]{:S(2)}, u32[]{:S(2)}) async-start(bf16[64,24,128]{2,1,0:T(8,128)(2,1)} %get-tuple-element.34), calls=%async_computation | async-start | bytes 786432 | tf_op jit(solution)/shard_map/all_to_all | solution.py:336
  18.1 4.5 %collective-permute-start = (bf16[160,128]{1,0:T(8,128)(2,1)}, bf16[160,128]{1,0:T(8,128)(2,1)S(1)}, u32[]{:S(2)}, u32[]{:S(2)}) collective-permute-start(bf16[160,128]{1,0:T(8,128)(2,1)} %bitcast.24), channel_id=1, source_target_pairs={{8,0},{16,8},{24,16},{0,24},{9,1},{17,9},{25,17},{1,25},{10,2},{18... | collective-permute-start | bytes 122888 | tf_op jit(solution)/shard_map/ppermute | solution.py:347
  22.6 1.9 collective-permute-start.1
  24.6 3.7 %collective-permute-start.2 = (bf16[160,128]{1,0:T(8,128)(2,1)}, bf16[160,128]{1,0:T(8,128)(2,1)S(1)}, u32[]{:S(2)}, u32[]{:S(2)}) collective-permute-start(bf16[160,128]{1,0:T(8,128)(2,1)} %bitcast.26), channel_id=1, source_target_pairs={{16,0},{24,8},{0,16},{8,24},{17,1},{25,9},{1,17},{9,25},{18,2},{26... | collective-permute-start | bytes 122888 | tf_op jit(solution)/shard_map/ppermute | solution.py:347
  28.2 1.1 collective-permute-done.1.refs_2_
  29.4 2.2 collective-permute-done.2.refs_3_
  31.6 1.2 all-to-all-done.in_ref
  32.7 0.8 copy-done.5
  33.5 0.5 shard_map.123.refs_0_
  34.1 3.2 %collective-permute-start.3 = (bf16[640,384]{1,0:T(8,128)(2,1)S(1)}, bf16[640,384]{1,0:T(8,128)(2,1)S(1)}, u32[]{:S(2)}, u32[]{:S(2)}) collective-permute-start(bf16[640,384]{1,0:T(8,128)(2,1)S(1)} %shard_map.123.refs_0_), channel_id=1, source_target_pairs={{7,0},{0,1},{1,2},{2,3},{3,4},{4,5},{5,6},{6,7},{15,8},{8,9},{9,10... | collective-permute-start | bytes 1474568 | tf_op jit(solution)/shard_map/ppermute | solution.py:347
  37.3 3.8 %collective-permute-start.4 = (bf16[640,384]{1,0:T(8,128)(2,1)S(1)}, bf16[640,384]{1,0:T(8,128)(2,1)S(1)}, u32[]{:S(2)}, u32[]{:S(2)}) collective-permute-start(bf16[640,384]{1,0:T(8,128)(2,1)S(1)} %shard_map.123.refs_0_), channel_id=1, source_target_pairs={{1,0},{2,1},{3,2},{4,3},{5,4},{6,5},{7,6},{0,7},{9,8},{10,9},{11,1... | collective-permute-start | bytes 1474568 | tf_op jit(solution)/shard_map/ppermute | solution.py:347
  41.1 3.8 %collective-permute-start.7 = (bf16[48,5120]{1,0:T(8,128)(2,1)}, bf16[48,5120]{1,0:T(8,128)(2,1)S(1)}, u32[]{:S(2)}, u32[]{:S(2)}) collective-permute-start(bf16[48,5120]{1,0:T(8,128)(2,1)} %bitcast.29), channel_id=1, source_target_pairs={{8,0},{16,8},{24,16},{0,24},{9,1},{17,9},{25,17},{1,25},{10,2},{18... | collective-permute-start | bytes 1474568 | tf_op jit(solution)/shard_map/ppermute | solution.py:347
  45.0 1.9 collective-permute-start.8
  46.9 2.0 collective-permute-done.3.refs_1_
  48.9 0.9 collective-permute-done.4.refs_2_
  49.8 3.2 %collective-permute-start.5 = (bf16[640,384]{1,0:T(8,128)(2,1)S(1)}, bf16[640,384]{1,0:T(8,128)(2,1)S(1)}, u32[]{:S(2)}, u32[]{:S(2)}) collective-permute-start(bf16[640,384]{1,0:T(8,128)(2,1)S(1)} %collective-permute-done.3.refs_1_), channel_id=1, source_target_pairs={{7,0},{0,1},{1,2},{2,3},{3,4},{4,5},{5,6},{6,7},{15,8},{8,9},{9,10... | collective-permute-start | bytes 1474568 | tf_op jit(solution)/shard_map/ppermute | solution.py:347
  53.0 4.0 %collective-permute-start.6 = (bf16[640,384]{1,0:T(8,128)(2,1)S(1)}, bf16[640,384]{1,0:T(8,128)(2,1)S(1)}, u32[]{:S(2)}, u32[]{:S(2)}) collective-permute-start(bf16[640,384]{1,0:T(8,128)(2,1)S(1)} %collective-permute-done.4.refs_2_), channel_id=1, source_target_pairs={{1,0},{2,1},{3,2},{4,3},{5,4},{6,5},{7,6},{0,7},{9,8},{10,9},{11,1... | collective-permute-start | bytes 1474568 | tf_op jit(solution)/shard_map/ppermute | solution.py:347
  57.0 2.3 %collective-permute-start.11 = (bf16[48,5120]{1,0:T(8,128)(2,1)}, bf16[48,5120]{1,0:T(8,128)(2,1)S(1)}, u32[]{:S(2)}, u32[]{:S(2)}) collective-permute-start(bf16[48,5120]{1,0:T(8,128)(2,1)} %bitcast.30), channel_id=1, source_target_pairs={{24,0},{0,8},{8,16},{16,24},{25,1},{1,9},{9,17},{17,25},{26,2},{2,... | collective-permute-start | bytes 1474568 | tf_op jit(solution)/shard_map/ppermute | solution.py:347
  59.3 4.2 %collective-permute-start.12 = (bf16[48,5120]{1,0:T(8,128)(2,1)}, bf16[48,5120]{1,0:T(8,128)(2,1)S(1)}, u32[]{:S(2)}, u32[]{:S(2)}) collective-permute-start(bf16[48,5120]{1,0:T(8,128)(2,1)} %bitcast.33), channel_id=1, source_target_pairs={{8,0},{16,8},{24,16},{0,24},{9,1},{17,9},{25,17},{1,25},{10,2},{18... | collective-permute-start | bytes 1474568 | tf_op jit(solution)/shard_map/ppermute | solution.py:347
  63.6 0.3 collective-permute-done.5.refs_3_
  63.8 2.2 collective-permute-done.6.refs_4_
  66.0 4.0 %collective-permute-start.9 = (bf16[640,384]{1,0:T(8,128)(2,1)S(1)}, bf16[640,384]{1,0:T(8,128)(2,1)}, u32[]{:S(2)}, u32[]{:S(2)}) collective-permute-start(bf16[640,384]{1,0:T(8,128)(2,1)S(1)} %collective-permute-done.5.refs_3_), channel_id=1, source_target_pairs={{7,0},{0,1},{1,2},{2,3},{3,4},{4,5},{5,6},{6,7},{15,8},{8,9},{9,10... | collective-permute-start | bytes 1474568 | tf_op jit(solution)/shard_map/ppermute | solution.py:347
  70.0 2.5 %collective-permute-start.10 = (bf16[640,384]{1,0:T(8,128)(2,1)S(1)}, bf16[640,384]{1,0:T(8,128)(2,1)S(1)}, u32[]{:S(2)}, u32[]{:S(2)}) collective-permute-start(bf16[640,384]{1,0:T(8,128)(2,1)S(1)} %collective-permute-done.6.refs_4_), channel_id=1, source_target_pairs={{1,0},{2,1},{3,2},{4,3},{5,4},{6,5},{7,6},{0,7},{9,8},{10,9},{11,1... | collective-permute-start | bytes 1474568 | tf_op jit(solution)/shard_map/ppermute | solution.py:347
  72.5 5.5 %collective-permute-start.14 = (bf16[48,5120]{1,0:T(8,128)(2,1)S(1)}, bf16[48,5120]{1,0:T(8,128)(2,1)}, u32[]{:S(2)}, u32[]{:S(2)}) collective-permute-start(bf16[48,5120]{1,0:T(8,128)(2,1)S(1)} %collective-permute-done.7.refs_10_), channel_id=1, source_target_pairs={{8,0},{16,8},{24,16},{0,24},{9,1},{17,9},{25,17},{1,25},{10,2},{18... | collective-permute-start | bytes 1474568 | tf_op jit(solution)/shard_map/ppermute | solution.py:347
  78.0 1.9 collective-permute-start.15
  79.9 0.5 collective-permute-done.10.refs_6_
  80.4 2.9 %collective-permute-start.13 = (bf16[640,384]{1,0:T(8,128)(2,1)}, bf16[640,384]{1,0:T(8,128)(2,1)}, u32[]{:S(2)}, u32[]{:S(2)}) collective-permute-start(bf16[640,384]{1,0:T(8,128)(2,1)} %collective-permute-done.9.refs_5_), channel_id=1, source_target_pairs={{7,0},{0,1},{1,2},{2,3},{3,4},{4,5},{5,6},{6,7},{15,8},{8,9},{9,10... | collective-permute-start | bytes 1474568 | tf_op jit(solution)/shard_map/ppermute | solution.py:347
  83.4 2.2 collective-permute-start.16
  85.6 4.7 %collective-permute-done.15.refs_15_ = bf16[48,5120]{1,0:T(8,128)(2,1)} collective-permute-done((bf16[48,5120]{1,0:T(8,128)(2,1)}, bf16[48,5120]{1,0:T(8,128)(2,1)}, u32[]{:S(2)}, u32[]{:S(2)}) %collective-permute-start.15) | collective-permute-done | bytes 491552 | tf_op jit(solution)/shard_map/ppermute | solution.py:347
  90.4 1.4 collective-permute-done.13.refs_7_
  91.9 7.3 %shard_map.124 = bf16[8,224,256]{2,1,0:T(8,128)(2,1)} custom-call(s32[1]{0:T(128)} %bitcast.5.y_ref, bf16[640,384]{1,0:T(8,128)(2,1)} %copy-done, bf16[640,384]{1,0:T(8,128)(2,1)} %copy-done.9, bf16[640,384]{1,0:T(8,128)(2,1)} %copy-done.10, bf16[640,384]{1,0:T(8,128)(2,1)} %copy-done.12, bf16[640,384]{1,0:T(8,128)(2,1)} %copy-done.13, ...), custom_call_target="tpu_custom_call" | custom-call | bytes 9764868 | tf_op jit(solution)/shard_map/pallas_call | solution.py:25
  99.2 2.0 collective-permute-done.16.refs_2_
  101.2 4.5 %all-to-all-start.1 = ((bf16[8,224,256]{2,1,0:T(8,128)(2,1)}), bf16[8,224,256]{2,1,0:T(8,128)(2,1)S(1)}, u32[]{:S(2)}, u32[]{:S(2)}) async-start(bf16[8,224,256]{2,1,0:T(8,128)(2,1)} %shard_map.124), calls=%async_computation.1 | async-start | bytes 1835008 | tf_op jit(solution)/shard_map/all_to_all | solution.py:336
  105.7 0.0 copy-start.6
  105.7 0.0 copy-start.7
  105.8 4.9 %collective-permute-start.17 = (bf16[160,1536]{1,0:T(8,128)(2,1)S(1)}, bf16[160,1536]{1,0:T(8,128)(2,1)S(1)}, u32[]{:S(2)}, u32[]{:S(2)}) collective-permute-start(bf16[160,1536]{1,0:T(8,128)(2,1)S(1)} %bitcast.20), channel_id=1, source_target_pairs={{8,0},{16,8},{24,16},{0,24},{9,1},{17,9},{25,17},{1,25},{10,2},{18... | collective-permute-start | bytes 1474568 | tf_op jit(solution)/shard_map/ppermute | solution.py:347
  110.7 1.9 collective-permute-start.18
  112.6 3.8 %collective-permute-done.17.refs_1_ = bf16[160,1536]{1,0:T(8,128)(2,1)S(1)} collective-permute-done((bf16[160,1536]{1,0:T(8,128)(2,1)S(1)}, bf16[160,1536]{1,0:T(8,128)(2,1)S(1)}, u32[]{:S(2)}, u32[]{:S(2)}) %collective-permute-start.17) | collective-permute-done | bytes 491552 | tf_op jit(solution)/shard_map/ppermute | solution.py:347
  116.5 5.3 %collective-permute-done.18.refs_3_ = bf16[160,1536]{1,0:T(8,128)(2,1)S(1)} collective-permute-done((bf16[160,1536]{1,0:T(8,128)(2,1)S(1)}, bf16[160,1536]{1,0:T(8,128)(2,1)S(1)}, u32[]{:S(2)}, u32[]{:S(2)}) %collective-permute-start.18) | collective-permute-done | bytes 491552 | tf_op jit(solution)/shard_map/ppermute | solution.py:347
  121.8 4.3 %all-to-all-done.1.hidden_ref = bf16[8,224,256]{2,1,0:T(8,128)(2,1)S(1)} async-done(((bf16[8,224,256]{2,1,0:T(8,128)(2,1)}), bf16[8,224,256]{2,1,0:T(8,128)(2,1)S(1)}, u32[]{:S(2)}, u32[]{:S(2)}) %all-to-all-start.1) | async-done | bytes 917536 | tf_op jit(solution)/shard_map/all_to_all | solution.py:336
  126.1 4.5 %shard_map.125 = (bf16[64,24,128]{2,1,0:T(8,128)(2,1)S(1)}, bf16[384,128]{1,0:T(8,128)(2,1)S(1)}) custom-call(s32[1]{0:T(128)} %bitcast.x_ref, bf16[8,224,256]{2,1,0:T(8,128)(2,1)S(1)} %all-to-all-done.1.hidden_ref, bf16[160,1536]{1,0:T(8,128)(2,1)S(1)} %bitcast.21, bf16[160,1536]{1,0:T(8,128)(2,1)S(1)} %collective-permute-done.17.refs_1_, ...), custom_call_target="tpu_custom_call" | custom-call | bytes 3375108 | tf_op jit(solution)/shard_map/pallas_call | solution.py:25
  130.6 0.7 copy-done.4
  131.3 14.1 %all-to-all-start.2 = ((bf16[64,24,128]{2,1,0:T(8,128)(2,1)}), bf16[64,24,128]{2,1,0:T(8,128)(2,1)S(1)}, u32[]{:S(2)}, u32[]{:S(2)}) async-start(bf16[64,24,128]{2,1,0:T(8,128)(2,1)} %copy-done.4), calls=%async_computation.2 | async-start | bytes 786432 | tf_op jit(solution)/shard_map/all_to_all | solution.py:336
  145.4 4.5 %collective-permute-start.19 = (bf16[384,128]{1,0:T(8,128)(2,1)S(1)}, bf16[384,128]{1,0:T(8,128)(2,1)S(1)}, u32[]{:S(2)}, u32[]{:S(2)}) collective-permute-start(bf16[384,128]{1,0:T(8,128)(2,1)S(1)} %get-tuple-element.57.refs_0_), channel_id=1, source_target_pairs={{8,0},{16,8},{24,16},{0,24},{9,1},{17,9},{25,17},{1,25},{10,2},{18... | collective-permute-start | bytes 294920 | tf_op jit(solution)/shard_map/ppermute | solution.py:347
  149.9 1.9 collective-permute-start.20
  151.9 3.7 %collective-permute-start.21 = (bf16[384,128]{1,0:T(8,128)(2,1)S(1)}, bf16[384,128]{1,0:T(8,128)(2,1)S(1)}, u32[]{:S(2)}, u32[]{:S(2)}) collective-permute-start(bf16[384,128]{1,0:T(8,128)(2,1)S(1)} %get-tuple-element.57.refs_0_), channel_id=1, source_target_pairs={{16,0},{24,8},{0,16},{8,24},{17,1},{25,9},{1,17},{9,25},{18,2},{26... | collective-permute-start | bytes 294920 | tf_op jit(solution)/shard_map/ppermute | solution.py:347
  155.5 2.5 %collective-permute-done.20.refs_2_ = bf16[384,128]{1,0:T(8,128)(2,1)S(1)} collective-permute-done((bf16[384,128]{1,0:T(8,128)(2,1)S(1)}, bf16[384,128]{1,0:T(8,128)(2,1)S(1)}, u32[]{:S(2)}, u32[]{:S(2)}) %collective-permute-start.20) | collective-permute-done | bytes 98336 | tf_op jit(solution)/shard_map/ppermute | solution.py:347
  158.0 2.5 %collective-permute-done.21.refs_3_ = bf16[384,128]{1,0:T(8,128)(2,1)S(1)} collective-permute-done((bf16[384,128]{1,0:T(8,128)(2,1)S(1)}, bf16[384,128]{1,0:T(8,128)(2,1)S(1)}, u32[]{:S(2)}, u32[]{:S(2)}) %collective-permute-start.21) | collective-permute-done | bytes 98336 | tf_op jit(solution)/shard_map/ppermute | solution.py:347
  160.6 1.9 shard_map.126
  162.5 3.3 %collective-permute-start.22 = (bf16[128,5120]{1,0:T(8,128)(2,1)S(1)}, bf16[128,5120]{1,0:T(8,128)(2,1)S(1)}, u32[]{:S(2)}, u32[]{:S(2)}) collective-permute-start(bf16[128,5120]{1,0:T(8,128)(2,1)S(1)} %copy-done.1), channel_id=1, source_target_pairs={{0,32},{32,0},{1,33},{33,1},{2,34},{34,2},{3,35},{35,3},{4,36},{36... | collective-permute-start | bytes 3932168 | tf_op jit(solution)/shard_map/ppermute | solution.py:471
  165.8 6.0 %all-to-all-start.3 = ((bf16[16,4,160]{2,1,0:T(4,128)(2,1)}), bf16[16,4,160]{2,1,0:T(4,128)(2,1)S(1)}, u32[]{:S(2)}, u32[]{:S(2)}) async-start(bf16[16,4,160]{2,1,0:T(4,128)(2,1)} %get-tuple-element.60), calls=%async_computation.3 | async-start | bytes 65536 | tf_op jit(solution)/shard_map/all_to_all | solution.py:336
  171.8 7.4 %all-to-all-done.3 = bf16[16,4,160]{2,1,0:T(4,128)(2,1)S(1)} async-done(((bf16[16,4,160]{2,1,0:T(4,128)(2,1)}), bf16[16,4,160]{2,1,0:T(4,128)(2,1)S(1)}, u32[]{:S(2)}, u32[]{:S(2)}) %all-to-all-start.3) | async-done | bytes 20512 | tf_op jit(solution)/shard_map/all_to_all | solution.py:336
  179.3 1.0 shard_map.127
  180.3 4.1 %all-to-all-start.4 = ((bf16[32,40,128]{2,1,0:T(8,128)(2,1)}), bf16[32,40,128]{2,1,0:T(8,128)(2,1)S(1)}, u32[]{:S(2)}, u32[]{:S(2)}) async-start(bf16[32,40,128]{2,1,0:T(8,128)(2,1)} %shard_map.127), calls=%async_computation.4 | async-start | bytes 655360 | tf_op jit(solution)/shard_map/all_to_all | solution.py:336
  184.4 0.1 tile.10
  184.5 0.1 tile.12.targets_ref
  184.6 0.1 pad_add_fusion.at_ref
  184.6 10.2 %all-to-all-done.4.rows_ref = bf16[32,40,128]{2,1,0:T(8,128)(2,1)S(1)} async-done(((bf16[32,40,128]{2,1,0:T(8,128)(2,1)}), bf16[32,40,128]{2,1,0:T(8,128)(2,1)S(1)}, u32[]{:S(2)}, u32[]{:S(2)}) %all-to-all-start.4) | async-done | bytes 327712 | tf_op jit(solution)/shard_map/all_to_all | solution.py:336
  194.8 1.6 shard_map.128
  196.4 16.0 %all_to_all.35 = f32[32,1,128]{2,1,0:T(1,128)S(1)} all-to-all(f32[32,1,128]{2,1,0:T(1,128)S(1)} %broadcast_in_dim.7), channel_id=1, replica_groups=mesh['z'=8,'core'=2,'x'=4,'y'=8] {'x','y'}, dimensions={0} | all-to-all | bytes 32768 | tf_op jit(solution)/shard_map/all_to_all | solution.py:340
  212.4 11.8 %all_to_all.36 = f32[16,1,128]{2,1,0:T(1,128)S(1)} all-to-all(f32[16,1,128]{2,1,0:T(1,128)S(1)} %broadcast_in_dim.16), channel_id=1, replica_groups=mesh['z'=8,'core'=2,'x'=4,'y'=8] {'z','core'}, dimensions={0} | all-to-all | bytes 16384 | tf_op jit(solution)/shard_map/all_to_all | solution.py:340
  224.3 0.1 log_subtract_fusion
  224.3 0.6 reshape.36
  (49 shorter events, 0.2 us)
Async XLA Ops:
  0.6 82.8 %copy-start.2 = (bf16[1,1536,160]{1,2,0:T(8,128)(2,1)S(1)}, bf16[1,1536,160]{1,2,0:T(8,128)(2,1)}, u32[]{:S(2)}) copy-start(bf16[1,1536,160]{1,2,0:T(8,128)(2,1)} %param.16) | copy-start | bytes 1474564
  3.3 29.5 %all-to-all-start = ((bf16[64,24,128]{2,1,0:T(8,128)(2,1)}), bf16[64,24,128]{2,1,0:T(8,128)(2,1)S(1)}, u32[]{:S(2)}, u32[]{:S(2)}) async-start(bf16[64,24,128]{2,1,0:T(8,128)(2,1)} %get-tuple-element.34), calls=%async_computation | async-start | bytes 786432 | tf_op jit(solution)/shard_map/all_to_all | solution.py:336
  18.1 10.1 %collective-permute-start = (bf16[160,128]{1,0:T(8,128)(2,1)}, bf16[160,128]{1,0:T(8,128)(2,1)S(1)}, u32[]{:S(2)}, u32[]{:S(2)}) collective-permute-start(bf16[160,128]{1,0:T(8,128)(2,1)} %bitcast.24), channel_id=1, source_target_pairs={{8,0},{16,8},{24,16},{0,24},{9,1},{17,9},{25,17},{1,25},{10,2},{18... | collective-permute-start | bytes 122888 | tf_op jit(solution)/shard_map/ppermute | solution.py:347
  22.6 6.8 %collective-permute-start.1 = (bf16[160,128]{1,0:T(8,128)(2,1)}, bf16[160,128]{1,0:T(8,128)(2,1)S(1)}, u32[]{:S(2)}, u32[]{:S(2)}) collective-permute-start(bf16[160,128]{1,0:T(8,128)(2,1)} %bitcast.25), channel_id=1, source_target_pairs={{24,0},{0,8},{8,16},{16,24},{25,1},{1,9},{9,17},{17,25},{26,2},{2,... | collective-permute-start | bytes 122888 | tf_op jit(solution)/shard_map/ppermute | solution.py:347
  24.6 7.0 %collective-permute-start.2 = (bf16[160,128]{1,0:T(8,128)(2,1)}, bf16[160,128]{1,0:T(8,128)(2,1)S(1)}, u32[]{:S(2)}, u32[]{:S(2)}) collective-permute-start(bf16[160,128]{1,0:T(8,128)(2,1)} %bitcast.26), channel_id=1, source_target_pairs={{16,0},{24,8},{0,16},{8,24},{17,1},{25,9},{1,17},{9,25},{18,2},{26... | collective-permute-start | bytes 122888 | tf_op jit(solution)/shard_map/ppermute | solution.py:347
  32.7 0.8 copy-start.5
  34.1 57.8 %copy-start = (bf16[640,384]{1,0:T(8,128)(2,1)}, bf16[640,384]{1,0:T(8,128)(2,1)S(1)}, u32[]{:S(2)}) copy-start(bf16[640,384]{1,0:T(8,128)(2,1)S(1)} %shard_map.123.refs_0_) | copy-start | bytes 1474564
  34.1 14.8 %collective-permute-start.3 = (bf16[640,384]{1,0:T(8,128)(2,1)S(1)}, bf16[640,384]{1,0:T(8,128)(2,1)S(1)}, u32[]{:S(2)}, u32[]{:S(2)}) collective-permute-start(bf16[640,384]{1,0:T(8,128)(2,1)S(1)} %shard_map.123.refs_0_), channel_id=1, source_target_pairs={{7,0},{0,1},{1,2},{2,3},{3,4},{4,5},{5,6},{6,7},{15,8},{8,9},{9,10... | collective-permute-start | bytes 1474568 | tf_op jit(solution)/shard_map/ppermute | solution.py:347
  37.3 12.5 %collective-permute-start.4 = (bf16[640,384]{1,0:T(8,128)(2,1)S(1)}, bf16[640,384]{1,0:T(8,128)(2,1)S(1)}, u32[]{:S(2)}, u32[]{:S(2)}) collective-permute-start(bf16[640,384]{1,0:T(8,128)(2,1)S(1)} %shard_map.123.refs_0_), channel_id=1, source_target_pairs={{1,0},{2,1},{3,2},{4,3},{5,4},{6,5},{7,6},{0,7},{9,8},{10,9},{11,1... | collective-permute-start | bytes 1474568 | tf_op jit(solution)/shard_map/ppermute | solution.py:347
  41.1 18.2 %collective-permute-start.7 = (bf16[48,5120]{1,0:T(8,128)(2,1)}, bf16[48,5120]{1,0:T(8,128)(2,1)S(1)}, u32[]{:S(2)}, u32[]{:S(2)}) collective-permute-start(bf16[48,5120]{1,0:T(8,128)(2,1)} %bitcast.29), channel_id=1, source_target_pairs={{8,0},{16,8},{24,16},{0,24},{9,1},{17,9},{25,17},{1,25},{10,2},{18... | collective-permute-start | bytes 1474568 | tf_op jit(solution)/shard_map/ppermute | solution.py:347
  45.0 18.6 %collective-permute-start.8 = (bf16[48,5120]{1,0:T(8,128)(2,1)}, bf16[48,5120]{1,0:T(8,128)(2,1)}, u32[]{:S(2)}, u32[]{:S(2)}) collective-permute-start(bf16[48,5120]{1,0:T(8,128)(2,1)} %bitcast.32), channel_id=1, source_target_pairs={{24,0},{0,8},{8,16},{16,24},{25,1},{1,9},{9,17},{17,25},{26,2},{2,... | collective-permute-start | bytes 1474568 | tf_op jit(solution)/shard_map/ppermute | solution.py:347
  48.9 43.0 %copy-start.9 = (bf16[640,384]{1,0:T(8,128)(2,1)}, bf16[640,384]{1,0:T(8,128)(2,1)S(1)}, u32[]{:S(2)}) copy-start(bf16[640,384]{1,0:T(8,128)(2,1)S(1)} %collective-permute-done.3.refs_1_) | copy-start | bytes 1474564
  49.8 42.1 %copy-start.10 = (bf16[640,384]{1,0:T(8,128)(2,1)}, bf16[640,384]{1,0:T(8,128)(2,1)S(1)}, u32[]{:S(2)}) copy-start(bf16[640,384]{1,0:T(8,128)(2,1)S(1)} %collective-permute-done.4.refs_2_) | copy-start | bytes 1474564
  49.8 14.0 %collective-permute-start.5 = (bf16[640,384]{1,0:T(8,128)(2,1)S(1)}, bf16[640,384]{1,0:T(8,128)(2,1)S(1)}, u32[]{:S(2)}, u32[]{:S(2)}) collective-permute-start(bf16[640,384]{1,0:T(8,128)(2,1)S(1)} %collective-permute-done.3.refs_1_), channel_id=1, source_target_pairs={{7,0},{0,1},{1,2},{2,3},{3,4},{4,5},{5,6},{6,7},{15,8},{8,9},{9,10... | collective-permute-start | bytes 1474568 | tf_op jit(solution)/shard_map/ppermute | solution.py:347
  53.0 13.0 %collective-permute-start.6 = (bf16[640,384]{1,0:T(8,128)(2,1)S(1)}, bf16[640,384]{1,0:T(8,128)(2,1)S(1)}, u32[]{:S(2)}, u32[]{:S(2)}) collective-permute-start(bf16[640,384]{1,0:T(8,128)(2,1)S(1)} %collective-permute-done.4.refs_2_), channel_id=1, source_target_pairs={{1,0},{2,1},{3,2},{4,3},{5,4},{6,5},{7,6},{0,7},{9,8},{10,9},{11,1... | collective-permute-start | bytes 1474568 | tf_op jit(solution)/shard_map/ppermute | solution.py:347
  57.0 21.0 %collective-permute-start.11 = (bf16[48,5120]{1,0:T(8,128)(2,1)}, bf16[48,5120]{1,0:T(8,128)(2,1)S(1)}, u32[]{:S(2)}, u32[]{:S(2)}) collective-permute-start(bf16[48,5120]{1,0:T(8,128)(2,1)} %bitcast.30), channel_id=1, source_target_pairs={{24,0},{0,8},{8,16},{16,24},{25,1},{1,9},{9,17},{17,25},{26,2},{2,... | collective-permute-start | bytes 1474568 | tf_op jit(solution)/shard_map/ppermute | solution.py:347
  59.3 32.6 %copy-start.11 = (bf16[48,5120]{1,0:T(8,128)(2,1)}, bf16[48,5120]{1,0:T(8,128)(2,1)S(1)}, u32[]{:S(2)}) copy-start(bf16[48,5120]{1,0:T(8,128)(2,1)S(1)} %collective-permute-done.7.refs_10_) | copy-start | bytes 1474564
  59.3 20.6 %collective-permute-start.12 = (bf16[48,5120]{1,0:T(8,128)(2,1)}, bf16[48,5120]{1,0:T(8,128)(2,1)S(1)}, u32[]{:S(2)}, u32[]{:S(2)}) collective-permute-start(bf16[48,5120]{1,0:T(8,128)(2,1)} %bitcast.33), channel_id=1, source_target_pairs={{8,0},{16,8},{24,16},{0,24},{9,1},{17,9},{25,17},{1,25},{10,2},{18... | collective-permute-start | bytes 1474568 | tf_op jit(solution)/shard_map/ppermute | solution.py:347
  63.8 16.6 %copy-start.12 = (bf16[640,384]{1,0:T(8,128)(2,1)}, bf16[640,384]{1,0:T(8,128)(2,1)S(1)}, u32[]{:S(2)}) copy-start(bf16[640,384]{1,0:T(8,128)(2,1)S(1)} %collective-permute-done.5.refs_3_) | copy-start | bytes 1474564
  66.0 17.4 %copy-start.13 = (bf16[640,384]{1,0:T(8,128)(2,1)}, bf16[640,384]{1,0:T(8,128)(2,1)S(1)}, u32[]{:S(2)}) copy-start(bf16[640,384]{1,0:T(8,128)(2,1)S(1)} %collective-permute-done.6.refs_4_) | copy-start | bytes 1474564
  66.0 13.9 %collective-permute-start.9 = (bf16[640,384]{1,0:T(8,128)(2,1)S(1)}, bf16[640,384]{1,0:T(8,128)(2,1)}, u32[]{:S(2)}, u32[]{:S(2)}) collective-permute-start(bf16[640,384]{1,0:T(8,128)(2,1)S(1)} %collective-permute-done.5.refs_3_), channel_id=1, source_target_pairs={{7,0},{0,1},{1,2},{2,3},{3,4},{4,5},{5,6},{6,7},{15,8},{8,9},{9,10... | collective-permute-start | bytes 1474568 | tf_op jit(solution)/shard_map/ppermute | solution.py:347
  70.0 10.5 %collective-permute-start.10 = (bf16[640,384]{1,0:T(8,128)(2,1)S(1)}, bf16[640,384]{1,0:T(8,128)(2,1)S(1)}, u32[]{:S(2)}, u32[]{:S(2)}) collective-permute-start(bf16[640,384]{1,0:T(8,128)(2,1)S(1)} %collective-permute-done.6.refs_4_), channel_id=1, source_target_pairs={{1,0},{2,1},{3,2},{4,3},{5,4},{6,5},{7,6},{0,7},{9,8},{10,9},{11,1... | collective-permute-start | bytes 1474568 | tf_op jit(solution)/shard_map/ppermute | solution.py:347
  72.5 13.2 %collective-permute-start.14 = (bf16[48,5120]{1,0:T(8,128)(2,1)S(1)}, bf16[48,5120]{1,0:T(8,128)(2,1)}, u32[]{:S(2)}, u32[]{:S(2)}) collective-permute-start(bf16[48,5120]{1,0:T(8,128)(2,1)S(1)} %collective-permute-done.7.refs_10_), channel_id=1, source_target_pairs={{8,0},{16,8},{24,16},{0,24},{9,1},{17,9},{25,17},{1,25},{10,2},{18... | collective-permute-start | bytes 1474568 | tf_op jit(solution)/shard_map/ppermute | solution.py:347
  78.0 5.4 %copy-start.14 = (bf16[48,5120]{1,0:T(8,128)(2,1)}, bf16[48,5120]{1,0:T(8,128)(2,1)S(1)}, u32[]{:S(2)}) copy-start(bf16[48,5120]{1,0:T(8,128)(2,1)S(1)} %collective-permute-done.11.refs_12_) | copy-start | bytes 1474564
  78.0 12.4 %collective-permute-start.15 = (bf16[48,5120]{1,0:T(8,128)(2,1)}, bf16[48,5120]{1,0:T(8,128)(2,1)}, u32[]{:S(2)}, u32[]{:S(2)}) collective-permute-start(bf16[48,5120]{1,0:T(8,128)(2,1)} %collective-permute-done.8.refs_13_), channel_id=1, source_target_pairs={{24,0},{0,8},{8,16},{16,24},{25,1},{1,9},{9,17},{17,25},{26,2},{2,... | collective-permute-start | bytes 1474568 | tf_op jit(solution)/shard_map/ppermute | solution.py:347
  79.9 3.5 %copy-start.15 = (bf16[48,5120]{1,0:T(8,128)(2,1)}, bf16[48,5120]{1,0:T(8,128)(2,1)S(1)}, u32[]{:S(2)}) copy-start(bf16[48,5120]{1,0:T(8,128)(2,1)S(1)} %collective-permute-done.12.refs_11_) | copy-start | bytes 1474564
  80.4 2.9 %copy-start.16 = (bf16[640,384]{1,0:T(8,128)(2,1)}, bf16[640,384]{1,0:T(8,128)(2,1)S(1)}, u32[]{:S(2)}) copy-start(bf16[640,384]{1,0:T(8,128)(2,1)S(1)} %collective-permute-done.10.refs_6_) | copy-start | bytes 1474564
  80.4 11.4 %collective-permute-start.13 = (bf16[640,384]{1,0:T(8,128)(2,1)}, bf16[640,384]{1,0:T(8,128)(2,1)}, u32[]{:S(2)}, u32[]{:S(2)}) collective-permute-start(bf16[640,384]{1,0:T(8,128)(2,1)} %collective-permute-done.9.refs_5_), channel_id=1, source_target_pairs={{7,0},{0,1},{1,2},{2,3},{3,4},{4,5},{5,6},{6,7},{15,8},{8,9},{9,10... | collective-permute-start | bytes 1474568 | tf_op jit(solution)/shard_map/ppermute | solution.py:347
  83.4 17.8 %collective-permute-start.16 = (bf16[160,1536]{1,0:T(8,128)(2,1)S(1)}, bf16[160,1536]{1,0:T(8,128)(2,1)S(1)}, u32[]{:S(2)}, u32[]{:S(2)}) collective-permute-start(bf16[160,1536]{1,0:T(8,128)(2,1)S(1)} %bitcast.19), channel_id=1, source_target_pairs={{24,0},{0,8},{8,16},{16,24},{25,1},{1,9},{9,17},{17,25},{26,2},{2,... | collective-permute-start | bytes 1474568 | tf_op jit(solution)/shard_map/ppermute | solution.py:347
  101.2 24.8 %all-to-all-start.1 = ((bf16[8,224,256]{2,1,0:T(8,128)(2,1)}), bf16[8,224,256]{2,1,0:T(8,128)(2,1)S(1)}, u32[]{:S(2)}, u32[]{:S(2)}) async-start(bf16[8,224,256]{2,1,0:T(8,128)(2,1)} %shard_map.124), calls=%async_computation.1 | async-start | bytes 1835008 | tf_op jit(solution)/shard_map/all_to_all | solution.py:336
  105.7 54.8 %copy-start.3 = (bf16[1536,160]{0,1:T(8,128)(2,1)S(1)}, bf16[1536,160]{0,1:T(8,128)(2,1)}, u32[]{:S(2)}) copy-start(bf16[1536,160]{0,1:T(8,128)(2,1)} %param.19) | copy-start | bytes 1474564
  105.7 54.8 %copy-start.6 = (bf16[128,160]{0,1:T(8,128)(2,1)S(1)}, bf16[128,160]{0,1:T(8,128)(2,1)}, u32[]{:S(2)}) copy-start(bf16[128,160]{0,1:T(8,128)(2,1)} %param.11) | copy-start | bytes 122884
  105.7 54.8 %copy-start.7 = (s32[16,128]{1,0:T(8,128)S(1)}, s32[16,128]{1,0:T(8,128)}, u32[]{:S(2)}) copy-start(s32[16,128]{1,0:T(8,128)} %get-tuple-element.32.slot_ref) | copy-start | bytes 24580
  105.8 54.8 %copy-start.8 = (f32[16,128]{1,0:T(8,128)S(1)}, f32[16,128]{1,0:T(8,128)}, u32[]{:S(2)}) copy-start(f32[16,128]{1,0:T(8,128)} %get-tuple-element.33.gate_ref) | copy-start | bytes 24580
  105.8 10.7 %collective-permute-start.17 = (bf16[160,1536]{1,0:T(8,128)(2,1)S(1)}, bf16[160,1536]{1,0:T(8,128)(2,1)S(1)}, u32[]{:S(2)}, u32[]{:S(2)}) collective-permute-start(bf16[160,1536]{1,0:T(8,128)(2,1)S(1)} %bitcast.20), channel_id=1, source_target_pairs={{8,0},{16,8},{24,16},{0,24},{9,1},{17,9},{25,17},{1,25},{10,2},{18... | collective-permute-start | bytes 1474568 | tf_op jit(solution)/shard_map/ppermute | solution.py:347
  110.7 11.1 %collective-permute-start.18 = (bf16[160,1536]{1,0:T(8,128)(2,1)S(1)}, bf16[160,1536]{1,0:T(8,128)(2,1)S(1)}, u32[]{:S(2)}, u32[]{:S(2)}) collective-permute-start(bf16[160,1536]{1,0:T(8,128)(2,1)S(1)} %collective-permute-done.16.refs_2_), channel_id=1, source_target_pairs={{24,0},{0,8},{8,16},{16,24},{25,1},{1,9},{9,17},{17,25},{26,2},{2,... | collective-permute-start | bytes 1474568 | tf_op jit(solution)/shard_map/ppermute | solution.py:347
  130.6 0.7 copy-start.4
  131.3 31.2 %copy-start.1 = (bf16[128,5120]{1,0:T(8,128)(2,1)S(1)}, bf16[128,5120]{1,0:T(8,128)(2,1)}, u32[]{:S(2)}) copy-start(bf16[128,5120]{1,0:T(8,128)(2,1)} %vocab_ref.1) | copy-start | bytes 3932164
  131.3 29.2 %all-to-all-start.2 = ((bf16[64,24,128]{2,1,0:T(8,128)(2,1)}), bf16[64,24,128]{2,1,0:T(8,128)(2,1)S(1)}, u32[]{:S(2)}, u32[]{:S(2)}) async-start(bf16[64,24,128]{2,1,0:T(8,128)(2,1)} %copy-done.4), calls=%async_computation.2 | async-start | bytes 786432 | tf_op jit(solution)/shard_map/all_to_all | solution.py:336
  145.4 39.0 %copy-start.17 = (s32[64]{0:T(128)S(1)}, s32[64]{0:T(128)}, u32[]{:S(2)}) copy-start(s32[64]{0:T(128)} %param.21) | copy-start | bytes 772
  145.4 10.1 %collective-permute-start.19 = (bf16[384,128]{1,0:T(8,128)(2,1)S(1)}, bf16[384,128]{1,0:T(8,128)(2,1)S(1)}, u32[]{:S(2)}, u32[]{:S(2)}) collective-permute-start(bf16[384,128]{1,0:T(8,128)(2,1)S(1)} %get-tuple-element.57.refs_0_), channel_id=1, source_target_pairs={{8,0},{16,8},{24,16},{0,24},{9,1},{17,9},{25,17},{1,25},{10,2},{18... | collective-permute-start | bytes 294920 | tf_op jit(solution)/shard_map/ppermute | solution.py:347
  149.9 8.1 %collective-permute-start.20 = (bf16[384,128]{1,0:T(8,128)(2,1)S(1)}, bf16[384,128]{1,0:T(8,128)(2,1)S(1)}, u32[]{:S(2)}, u32[]{:S(2)}) collective-permute-start(bf16[384,128]{1,0:T(8,128)(2,1)S(1)} %get-tuple-element.57.refs_0_), channel_id=1, source_target_pairs={{24,0},{0,8},{8,16},{16,24},{25,1},{1,9},{9,17},{17,25},{26,2},{2,... | collective-permute-start | bytes 294920 | tf_op jit(solution)/shard_map/ppermute | solution.py:347
  151.9 8.7 %collective-permute-start.21 = (bf16[384,128]{1,0:T(8,128)(2,1)S(1)}, bf16[384,128]{1,0:T(8,128)(2,1)S(1)}, u32[]{:S(2)}, u32[]{:S(2)}) collective-permute-start(bf16[384,128]{1,0:T(8,128)(2,1)S(1)} %get-tuple-element.57.refs_0_), channel_id=1, source_target_pairs={{16,0},{24,8},{0,16},{8,24},{17,1},{25,9},{1,17},{9,25},{18,2},{26... | collective-permute-start | bytes 294920 | tf_op jit(solution)/shard_map/ppermute | solution.py:347
  162.5 32.3 %collective-permute-start.22 = (bf16[128,5120]{1,0:T(8,128)(2,1)S(1)}, bf16[128,5120]{1,0:T(8,128)(2,1)S(1)}, u32[]{:S(2)}, u32[]{:S(2)}) collective-permute-start(bf16[128,5120]{1,0:T(8,128)(2,1)S(1)} %copy-done.1), channel_id=1, source_target_pairs={{0,32},{32,0},{1,33},{33,1},{2,34},{34,2},{3,35},{35,3},{4,36},{36... | collective-permute-start | bytes 3932168 | tf_op jit(solution)/shard_map/ppermute | solution.py:471
  165.8 13.4 %all-to-all-start.3 = ((bf16[16,4,160]{2,1,0:T(4,128)(2,1)}), bf16[16,4,160]{2,1,0:T(4,128)(2,1)S(1)}, u32[]{:S(2)}, u32[]{:S(2)}) async-start(bf16[16,4,160]{2,1,0:T(4,128)(2,1)} %get-tuple-element.60), calls=%async_computation.3 | async-start | bytes 65536 | tf_op jit(solution)/shard_map/all_to_all | solution.py:336
  180.3 14.5 %all-to-all-start.4 = ((bf16[32,40,128]{2,1,0:T(8,128)(2,1)}), bf16[32,40,128]{2,1,0:T(8,128)(2,1)S(1)}, u32[]{:S(2)}, u32[]{:S(2)}) async-start(bf16[32,40,128]{2,1,0:T(8,128)(2,1)} %shard_map.127), calls=%async_computation.4 | async-start | bytes 655360 | tf_op jit(solution)/shard_map/all_to_all | solution.py:336

commit v10 on v8

--- a/solution.py
+++ b/solution.py
@@ -490,8 +490,8 @@
         scalars=1,
         scratch=[pltpu.VMEM((lanes * width, 2 * cap), BF16)],
     )
-    sums = jnp.sum(spread_all(sums[:1], PLANE, lanes), axis=0)
-    sums = jnp.sum(spread_all(sums, LINE, groups).reshape(nz, nc, 2 * cap), axis=0)
+    sums = jnp.sum(spread_all(sums[:1], ("z", "x"), nz * nx), axis=0)
+    sums = jnp.sum(spread_all(sums, ("core", "y"), nc * ny).reshape(nc, ny, 2 * cap), axis=1)
     return layer_out.T, (sums[:, count : 2 * count] - jnp.log(sums[:, :count])).reshape(-1)
 
 

time: 226 us -> 225 us (level)
  no operation moved by 1% of the time
where the time goes in v10:
time: 225 us; the launch traced here: 224 us
  starting transfers between devices  118 us (52%)
  waiting for transfers between devices  55.5 us (25%)
  blocking collectives  27.1 us (12%)
  Pallas kernels  19.4 us (9%)
  local copies, waits for them, and re-layouts  2.4 us (1%)
    ppermute x22, starting transfers between devices, from_shift(): lax.ppermute(value, axis, [((i + shift) % count, i) for i in range(count)])  72.3 us
    all_to_all x5, starting transfers between devices, exchange(): return lax.all_to_all(value, axes, 0, 0, tiled=True)  42.7 us
    ppermute x22, waiting for transfers between devices, from_shift(): lax.ppermute(value, axis, [((i + shift) % count, i) for i in range(count)])  31.7 us
    all_to_all x2, blocking collectives, spread_all(): lax.all_to_all(jnp.broadcast_to(value[None], (count, *value.shape)), axes...  27.1 us
    all_to_all x5, waiting for transfers between devices, exchange(): return lax.all_to_all(value, axes, 0, 0, tiled=True)  23.8 us
    pallas_call x7, Pallas kernels, call(): pl.pallas_call(body, out_shape=outs, in_specs=specs, out_specs=[pl.BlockS...  19.4 us
  transfers between devices with their start and end apart: 28, of which 18 were waited for; matrix products, arithmetic and copies ran while one was open for 0% of the time, Pallas kernels for 4%

profile of v10, /device:TPU:1, one launch (start us, length us, event | category | flops | bytes accessed | tf_op | source)
XLA Modules:
  0.0 224.1 jit_solution(3665226473478585767)
XLA Ops:
  0.6 2.6 %shard_map.122 = (bf16[64,24,128]{2,1,0:T(8,128)(2,1)}, s32[16,128]{1,0:T(8,128)}, f32[16,128]{1,0:T(8,128)}) custom-call(s32[6,128]{1,0:T(8,128)} %bitcast.39, f32[6,128]{1,0:T(8,128)} %bitcast.40, bf16[160,128]{1,0:T(8,128)(2,1)} %bitcast.25), custom_call_target="tpu_custom_call" | custom-call | bytes 456704 | tf_op jit(solution)/shard_map/pallas_call | solution.py:25
  3.3 14.8 %all-to-all-start = ((bf16[64,24,128]{2,1,0:T(8,128)(2,1)}), bf16[64,24,128]{2,1,0:T(8,128)(2,1)S(1)}, u32[]{:S(2)}, u32[]{:S(2)}) async-start(bf16[64,24,128]{2,1,0:T(8,128)(2,1)} %get-tuple-element.34), calls=%async_computation | async-start | bytes 786432 | tf_op jit(solution)/shard_map/all_to_all | solution.py:329
  18.1 4.5 %collective-permute-start = (bf16[160,128]{1,0:T(8,128)(2,1)}, bf16[160,128]{1,0:T(8,128)(2,1)S(1)}, u32[]{:S(2)}, u32[]{:S(2)}) collective-permute-start(bf16[160,128]{1,0:T(8,128)(2,1)} %bitcast.26), channel_id=1, source_target_pairs={{8,0},{16,8},{24,16},{0,24},{9,1},{17,9},{25,17},{1,25},{10,2},{18... | collective-permute-start | bytes 122888 | tf_op jit(solution)/shard_map/ppermute | solution.py:340
  22.6 1.9 collective-permute-start.1
  24.6 3.7 %collective-permute-start.2 = (bf16[160,128]{1,0:T(8,128)(2,1)}, bf16[160,128]{1,0:T(8,128)(2,1)S(1)}, u32[]{:S(2)}, u32[]{:S(2)}) collective-permute-start(bf16[160,128]{1,0:T(8,128)(2,1)} %bitcast.28), channel_id=1, source_target_pairs={{16,0},{24,8},{0,16},{8,24},{17,1},{25,9},{1,17},{9,25},{18,2},{26... | collective-permute-start | bytes 122888 | tf_op jit(solution)/shard_map/ppermute | solution.py:340
  28.2 1.1 collective-permute-done.1.refs_2_
  29.4 2.2 collective-permute-done.2.refs_3_
  31.6 1.2 all-to-all-done.in_ref
  32.7 0.8 copy-done.5
  33.5 0.5 shard_map.123.refs_0_
  34.1 3.2 %collective-permute-start.3 = (bf16[640,384]{1,0:T(8,128)(2,1)S(1)}, bf16[640,384]{1,0:T(8,128)(2,1)S(1)}, u32[]{:S(2)}, u32[]{:S(2)}) collective-permute-start(bf16[640,384]{1,0:T(8,128)(2,1)S(1)} %shard_map.123.refs_0_), channel_id=1, source_target_pairs={{7,0},{0,1},{1,2},{2,3},{3,4},{4,5},{5,6},{6,7},{15,8},{8,9},{9,10... | collective-permute-start | bytes 1474568 | tf_op jit(solution)/shard_map/ppermute | solution.py:340
  37.3 3.8 %collective-permute-start.4 = (bf16[640,384]{1,0:T(8,128)(2,1)S(1)}, bf16[640,384]{1,0:T(8,128)(2,1)S(1)}, u32[]{:S(2)}, u32[]{:S(2)}) collective-permute-start(bf16[640,384]{1,0:T(8,128)(2,1)S(1)} %shard_map.123.refs_0_), channel_id=1, source_target_pairs={{1,0},{2,1},{3,2},{4,3},{5,4},{6,5},{7,6},{0,7},{9,8},{10,9},{11,1... | collective-permute-start | bytes 1474568 | tf_op jit(solution)/shard_map/ppermute | solution.py:340
  41.1 3.8 %collective-permute-start.7 = (bf16[48,5120]{1,0:T(8,128)(2,1)}, bf16[48,5120]{1,0:T(8,128)(2,1)S(1)}, u32[]{:S(2)}, u32[]{:S(2)}) collective-permute-start(bf16[48,5120]{1,0:T(8,128)(2,1)} %bitcast.31), channel_id=1, source_target_pairs={{8,0},{16,8},{24,16},{0,24},{9,1},{17,9},{25,17},{1,25},{10,2},{18... | collective-permute-start | bytes 1474568 | tf_op jit(solution)/shard_map/ppermute | solution.py:340
  45.0 1.9 collective-permute-start.8
  46.9 2.0 collective-permute-done.3.refs_1_
  48.9 0.9 collective-permute-done.4.refs_2_
  49.8 3.2 %collective-permute-start.5 = (bf16[640,384]{1,0:T(8,128)(2,1)S(1)}, bf16[640,384]{1,0:T(8,128)(2,1)S(1)}, u32[]{:S(2)}, u32[]{:S(2)}) collective-permute-start(bf16[640,384]{1,0:T(8,128)(2,1)S(1)} %collective-permute-done.3.refs_1_), channel_id=1, source_target_pairs={{7,0},{0,1},{1,2},{2,3},{3,4},{4,5},{5,6},{6,7},{15,8},{8,9},{9,10... | collective-permute-start | bytes 1474568 | tf_op jit(solution)/shard_map/ppermute | solution.py:340
  53.0 4.0 %collective-permute-start.6 = (bf16[640,384]{1,0:T(8,128)(2,1)S(1)}, bf16[640,384]{1,0:T(8,128)(2,1)S(1)}, u32[]{:S(2)}, u32[]{:S(2)}) collective-permute-start(bf16[640,384]{1,0:T(8,128)(2,1)S(1)} %collective-permute-done.4.refs_2_), channel_id=1, source_target_pairs={{1,0},{2,1},{3,2},{4,3},{5,4},{6,5},{7,6},{0,7},{9,8},{10,9},{11,1... | collective-permute-start | bytes 1474568 | tf_op jit(solution)/shard_map/ppermute | solution.py:340
  57.0 2.3 %collective-permute-start.11 = (bf16[48,5120]{1,0:T(8,128)(2,1)}, bf16[48,5120]{1,0:T(8,128)(2,1)S(1)}, u32[]{:S(2)}, u32[]{:S(2)}) collective-permute-start(bf16[48,5120]{1,0:T(8,128)(2,1)} %bitcast.32), channel_id=1, source_target_pairs={{24,0},{0,8},{8,16},{16,24},{25,1},{1,9},{9,17},{17,25},{26,2},{2,... | collective-permute-start | bytes 1474568 | tf_op jit(solution)/shard_map/ppermute | solution.py:340
  59.3 4.2 %collective-permute-start.12 = (bf16[48,5120]{1,0:T(8,128)(2,1)}, bf16[48,5120]{1,0:T(8,128)(2,1)S(1)}, u32[]{:S(2)}, u32[]{:S(2)}) collective-permute-start(bf16[48,5120]{1,0:T(8,128)(2,1)} %bitcast.35), channel_id=1, source_target_pairs={{8,0},{16,8},{24,16},{0,24},{9,1},{17,9},{25,17},{1,25},{10,2},{18... | collective-permute-start | bytes 1474568 | tf_op jit(solution)/shard_map/ppermute | solution.py:340
  63.6 0.3 collective-permute-done.5.refs_3_
  63.8 2.2 collective-permute-done.6.refs_4_
  66.0 4.0 %collective-permute-start.9 = (bf16[640,384]{1,0:T(8,128)(2,1)S(1)}, bf16[640,384]{1,0:T(8,128)(2,1)}, u32[]{:S(2)}, u32[]{:S(2)}) collective-permute-start(bf16[640,384]{1,0:T(8,128)(2,1)S(1)} %collective-permute-done.5.refs_3_), channel_id=1, source_target_pairs={{7,0},{0,1},{1,2},{2,3},{3,4},{4,5},{5,6},{6,7},{15,8},{8,9},{9,10... | collective-permute-start | bytes 1474568 | tf_op jit(solution)/shard_map/ppermute | solution.py:340
  70.0 2.5 %collective-permute-start.10 = (bf16[640,384]{1,0:T(8,128)(2,1)S(1)}, bf16[640,384]{1,0:T(8,128)(2,1)S(1)}, u32[]{:S(2)}, u32[]{:S(2)}) collective-permute-start(bf16[640,384]{1,0:T(8,128)(2,1)S(1)} %collective-permute-done.6.refs_4_), channel_id=1, source_target_pairs={{1,0},{2,1},{3,2},{4,3},{5,4},{6,5},{7,6},{0,7},{9,8},{10,9},{11,1... | collective-permute-start | bytes 1474568 | tf_op jit(solution)/shard_map/ppermute | solution.py:340
  72.5 5.5 %collective-permute-start.14 = (bf16[48,5120]{1,0:T(8,128)(2,1)S(1)}, bf16[48,5120]{1,0:T(8,128)(2,1)}, u32[]{:S(2)}, u32[]{:S(2)}) collective-permute-start(bf16[48,5120]{1,0:T(8,128)(2,1)S(1)} %collective-permute-done.7.refs_10_), channel_id=1, source_target_pairs={{8,0},{16,8},{24,16},{0,24},{9,1},{17,9},{25,17},{1,25},{10,2},{18... | collective-permute-start | bytes 1474568 | tf_op jit(solution)/shard_map/ppermute | solution.py:340
  78.0 1.9 collective-permute-start.15
  79.9 0.5 collective-permute-done.10.refs_6_
  80.4 2.9 %collective-permute-start.13 = (bf16[640,384]{1,0:T(8,128)(2,1)}, bf16[640,384]{1,0:T(8,128)(2,1)}, u32[]{:S(2)}, u32[]{:S(2)}) collective-permute-start(bf16[640,384]{1,0:T(8,128)(2,1)} %collective-permute-done.9.refs_5_), channel_id=1, source_target_pairs={{7,0},{0,1},{1,2},{2,3},{3,4},{4,5},{5,6},{6,7},{15,8},{8,9},{9,10... | collective-permute-start | bytes 1474568 | tf_op jit(solution)/shard_map/ppermute | solution.py:340
  83.4 2.2 collective-permute-start.16
  85.6 4.7 %collective-permute-done.15.refs_15_ = bf16[48,5120]{1,0:T(8,128)(2,1)} collective-permute-done((bf16[48,5120]{1,0:T(8,128)(2,1)}, bf16[48,5120]{1,0:T(8,128)(2,1)}, u32[]{:S(2)}, u32[]{:S(2)}) %collective-permute-start.15) | collective-permute-done | bytes 491552 | tf_op jit(solution)/shard_map/ppermute | solution.py:340
  90.4 1.4 collective-permute-done.13.refs_7_
  91.9 7.2 %shard_map.124 = bf16[8,224,256]{2,1,0:T(8,128)(2,1)} custom-call(s32[1]{0:T(128)} %bitcast.5.y_ref, bf16[640,384]{1,0:T(8,128)(2,1)} %copy-done, bf16[640,384]{1,0:T(8,128)(2,1)} %copy-done.9, bf16[640,384]{1,0:T(8,128)(2,1)} %copy-done.10, bf16[640,384]{1,0:T(8,128)(2,1)} %copy-done.12, bf16[640,384]{1,0:T(8,128)(2,1)} %copy-done.13, ...), custom_call_target="tpu_custom_call" | custom-call | bytes 9764868 | tf_op jit(solution)/shard_map/pallas_call | solution.py:25
  99.0 2.2 collective-permute-done.16.refs_2_
  101.2 4.5 %all-to-all-start.1 = ((bf16[8,224,256]{2,1,0:T(8,128)(2,1)}), bf16[8,224,256]{2,1,0:T(8,128)(2,1)S(1)}, u32[]{:S(2)}, u32[]{:S(2)}) async-start(bf16[8,224,256]{2,1,0:T(8,128)(2,1)} %shard_map.124), calls=%async_computation.1 | async-start | bytes 1835008 | tf_op jit(solution)/shard_map/all_to_all | solution.py:329
  105.7 0.0 copy-start.6
  105.7 0.0 copy-start.7
  105.8 4.8 %collective-permute-start.17 = (bf16[160,1536]{1,0:T(8,128)(2,1)S(1)}, bf16[160,1536]{1,0:T(8,128)(2,1)S(1)}, u32[]{:S(2)}, u32[]{:S(2)}) collective-permute-start(bf16[160,1536]{1,0:T(8,128)(2,1)S(1)} %bitcast.22), channel_id=1, source_target_pairs={{8,0},{16,8},{24,16},{0,24},{9,1},{17,9},{25,17},{1,25},{10,2},{18... | collective-permute-start | bytes 1474568 | tf_op jit(solution)/shard_map/ppermute | solution.py:340
  110.5 1.9 collective-permute-start.18
  112.5 3.8 %collective-permute-done.17.refs_1_ = bf16[160,1536]{1,0:T(8,128)(2,1)S(1)} collective-permute-done((bf16[160,1536]{1,0:T(8,128)(2,1)S(1)}, bf16[160,1536]{1,0:T(8,128)(2,1)S(1)}, u32[]{:S(2)}, u32[]{:S(2)}) %collective-permute-start.17) | collective-permute-done | bytes 491552 | tf_op jit(solution)/shard_map/ppermute | solution.py:340
  116.3 5.3 %collective-permute-done.18.refs_3_ = bf16[160,1536]{1,0:T(8,128)(2,1)S(1)} collective-permute-done((bf16[160,1536]{1,0:T(8,128)(2,1)S(1)}, bf16[160,1536]{1,0:T(8,128)(2,1)S(1)}, u32[]{:S(2)}, u32[]{:S(2)}) %collective-permute-start.18) | collective-permute-done | bytes 491552 | tf_op jit(solution)/shard_map/ppermute | solution.py:340
  121.6 5.1 %all-to-all-done.1.hidden_ref = bf16[8,224,256]{2,1,0:T(8,128)(2,1)S(1)} async-done(((bf16[8,224,256]{2,1,0:T(8,128)(2,1)}), bf16[8,224,256]{2,1,0:T(8,128)(2,1)S(1)}, u32[]{:S(2)}, u32[]{:S(2)}) %all-to-all-start.1) | async-done | bytes 917536 | tf_op jit(solution)/shard_map/all_to_all | solution.py:329
  126.7 4.5 %shard_map.125 = (bf16[64,24,128]{2,1,0:T(8,128)(2,1)S(1)}, bf16[384,128]{1,0:T(8,128)(2,1)S(1)}) custom-call(s32[1]{0:T(128)} %bitcast.x_ref, bf16[8,224,256]{2,1,0:T(8,128)(2,1)S(1)} %all-to-all-done.1.hidden_ref, bf16[160,1536]{1,0:T(8,128)(2,1)S(1)} %bitcast.23, bf16[160,1536]{1,0:T(8,128)(2,1)S(1)} %collective-permute-done.17.refs_1_, ...), custom_call_target="tpu_custom_call" | custom-call | bytes 3375108 | tf_op jit(solution)/shard_map/pallas_call | solution.py:25
  131.3 0.7 copy-done.4
  132.0 13.2 %all-to-all-start.2 = ((bf16[64,24,128]{2,1,0:T(8,128)(2,1)}), bf16[64,24,128]{2,1,0:T(8,128)(2,1)S(1)}, u32[]{:S(2)}, u32[]{:S(2)}) async-start(bf16[64,24,128]{2,1,0:T(8,128)(2,1)} %copy-done.4), calls=%async_computation.2 | async-start | bytes 786432 | tf_op jit(solution)/shard_map/all_to_all | solution.py:329
  145.2 4.5 %collective-permute-start.19 = (bf16[384,128]{1,0:T(8,128)(2,1)S(1)}, bf16[384,128]{1,0:T(8,128)(2,1)S(1)}, u32[]{:S(2)}, u32[]{:S(2)}) collective-permute-start(bf16[384,128]{1,0:T(8,128)(2,1)S(1)} %get-tuple-element.57.refs_0_), channel_id=1, source_target_pairs={{8,0},{16,8},{24,16},{0,24},{9,1},{17,9},{25,17},{1,25},{10,2},{18... | collective-permute-start | bytes 294920 | tf_op jit(solution)/shard_map/ppermute | solution.py:340
  149.8 1.9 collective-permute-start.20
  151.7 3.7 %collective-permute-start.21 = (bf16[384,128]{1,0:T(8,128)(2,1)S(1)}, bf16[384,128]{1,0:T(8,128)(2,1)S(1)}, u32[]{:S(2)}, u32[]{:S(2)}) collective-permute-start(bf16[384,128]{1,0:T(8,128)(2,1)S(1)} %get-tuple-element.57.refs_0_), channel_id=1, source_target_pairs={{16,0},{24,8},{0,16},{8,24},{17,1},{25,9},{1,17},{9,25},{18,2},{26... | collective-permute-start | bytes 294920 | tf_op jit(solution)/shard_map/ppermute | solution.py:340
  155.4 2.5 %collective-permute-done.20.refs_2_ = bf16[384,128]{1,0:T(8,128)(2,1)S(1)} collective-permute-done((bf16[384,128]{1,0:T(8,128)(2,1)S(1)}, bf16[384,128]{1,0:T(8,128)(2,1)S(1)}, u32[]{:S(2)}, u32[]{:S(2)}) %collective-permute-start.20) | collective-permute-done | bytes 98336 | tf_op jit(solution)/shard_map/ppermute | solution.py:340
  157.9 2.5 %collective-permute-done.21.refs_3_ = bf16[384,128]{1,0:T(8,128)(2,1)S(1)} collective-permute-done((bf16[384,128]{1,0:T(8,128)(2,1)S(1)}, bf16[384,128]{1,0:T(8,128)(2,1)S(1)}, u32[]{:S(2)}, u32[]{:S(2)}) %collective-permute-start.21) | collective-permute-done | bytes 98336 | tf_op jit(solution)/shard_map/ppermute | solution.py:340
  160.4 1.9 shard_map.126
  162.3 3.3 %collective-permute-start.22 = (bf16[128,5120]{1,0:T(8,128)(2,1)S(1)}, bf16[128,5120]{1,0:T(8,128)(2,1)S(1)}, u32[]{:S(2)}, u32[]{:S(2)}) collective-permute-start(bf16[128,5120]{1,0:T(8,128)(2,1)S(1)} %copy-done.1), channel_id=1, source_target_pairs={{0,32},{32,0},{1,33},{33,1},{2,34},{34,2},{3,35},{35,3},{4,36},{36... | collective-permute-start | bytes 3932168 | tf_op jit(solution)/shard_map/ppermute | solution.py:464
  165.7 6.0 %all-to-all-start.3 = ((bf16[16,4,160]{2,1,0:T(4,128)(2,1)}), bf16[16,4,160]{2,1,0:T(4,128)(2,1)S(1)}, u32[]{:S(2)}, u32[]{:S(2)}) async-start(bf16[16,4,160]{2,1,0:T(4,128)(2,1)} %get-tuple-element.60), calls=%async_computation.3 | async-start | bytes 65536 | tf_op jit(solution)/shard_map/all_to_all | solution.py:329
  171.7 7.4 %all-to-all-done.3 = bf16[16,4,160]{2,1,0:T(4,128)(2,1)S(1)} async-done(((bf16[16,4,160]{2,1,0:T(4,128)(2,1)}), bf16[16,4,160]{2,1,0:T(4,128)(2,1)S(1)}, u32[]{:S(2)}, u32[]{:S(2)}) %all-to-all-start.3) | async-done | bytes 20512 | tf_op jit(solution)/shard_map/all_to_all | solution.py:329
  179.1 1.0 shard_map.127
  180.1 4.1 %all-to-all-start.4 = ((bf16[32,40,128]{2,1,0:T(8,128)(2,1)}), bf16[32,40,128]{2,1,0:T(8,128)(2,1)S(1)}, u32[]{:S(2)}, u32[]{:S(2)}) async-start(bf16[32,40,128]{2,1,0:T(8,128)(2,1)} %shard_map.127), calls=%async_computation.4 | async-start | bytes 655360 | tf_op jit(solution)/shard_map/all_to_all | solution.py:329
  184.2 0.1 tile.10
  184.3 0.1 tile.12.targets_ref
  184.4 0.1 pad_add_fusion.at_ref
  184.5 10.2 %all-to-all-done.4.rows_ref = bf16[32,40,128]{2,1,0:T(8,128)(2,1)S(1)} async-done(((bf16[32,40,128]{2,1,0:T(8,128)(2,1)}), bf16[32,40,128]{2,1,0:T(8,128)(2,1)S(1)}, u32[]{:S(2)}, u32[]{:S(2)}) %all-to-all-start.4) | async-done | bytes 327712 | tf_op jit(solution)/shard_map/all_to_all | solution.py:329
  194.6 1.6 shard_map.128
  196.2 12.1 %all_to_all.35 = f32[32,1,128]{2,1,0:T(1,128)S(1)} all-to-all(f32[32,1,128]{2,1,0:T(1,128)S(1)} %broadcast_in_dim.7), channel_id=1, replica_groups=mesh['z'=8,'core'=2,'x'=4,'y'=8] {'z','x'}, dimensions={0} | all-to-all | bytes 32768 | tf_op jit(solution)/shard_map/all_to_all | solution.py:333
  208.4 15.0 %all_to_all.36 = f32[16,1,128]{2,1,0:T(1,128)S(1)} all-to-all(f32[16,1,128]{2,1,0:T(1,128)S(1)} %broadcast_in_dim.16), channel_id=1, replica_groups=mesh['z'=8,'core'=2,'x'=4,'y'=8] {'core','y'}, dimensions={0} | all-to-all | bytes 16384 | tf_op jit(solution)/shard_map/all_to_all | solution.py:333
  223.4 0.1 log_subtract_fusion
  223.5 0.6 reshape.36
  (49 shorter events, 0.2 us)
Async XLA Ops:
  0.6 82.8 %copy-start.2 = (bf16[1,1536,160]{1,2,0:T(8,128)(2,1)S(1)}, bf16[1,1536,160]{1,2,0:T(8,128)(2,1)}, u32[]{:S(2)}) copy-start(bf16[1,1536,160]{1,2,0:T(8,128)(2,1)} %param.16) | copy-start | bytes 1474564
  3.3 29.5 %all-to-all-start = ((bf16[64,24,128]{2,1,0:T(8,128)(2,1)}), bf16[64,24,128]{2,1,0:T(8,128)(2,1)S(1)}, u32[]{:S(2)}, u32[]{:S(2)}) async-start(bf16[64,24,128]{2,1,0:T(8,128)(2,1)} %get-tuple-element.34), calls=%async_computation | async-start | bytes 786432 | tf_op jit(solution)/shard_map/all_to_all | solution.py:329
  18.1 10.1 %collective-permute-start = (bf16[160,128]{1,0:T(8,128)(2,1)}, bf16[160,128]{1,0:T(8,128)(2,1)S(1)}, u32[]{:S(2)}, u32[]{:S(2)}) collective-permute-start(bf16[160,128]{1,0:T(8,128)(2,1)} %bitcast.26), channel_id=1, source_target_pairs={{8,0},{16,8},{24,16},{0,24},{9,1},{17,9},{25,17},{1,25},{10,2},{18... | collective-permute-start | bytes 122888 | tf_op jit(solution)/shard_map/ppermute | solution.py:340
  22.6 6.8 %collective-permute-start.1 = (bf16[160,128]{1,0:T(8,128)(2,1)}, bf16[160,128]{1,0:T(8,128)(2,1)S(1)}, u32[]{:S(2)}, u32[]{:S(2)}) collective-permute-start(bf16[160,128]{1,0:T(8,128)(2,1)} %bitcast.27), channel_id=1, source_target_pairs={{24,0},{0,8},{8,16},{16,24},{25,1},{1,9},{9,17},{17,25},{26,2},{2,... | collective-permute-start | bytes 122888 | tf_op jit(solution)/shard_map/ppermute | solution.py:340
  24.6 7.0 %collective-permute-start.2 = (bf16[160,128]{1,0:T(8,128)(2,1)}, bf16[160,128]{1,0:T(8,128)(2,1)S(1)}, u32[]{:S(2)}, u32[]{:S(2)}) collective-permute-start(bf16[160,128]{1,0:T(8,128)(2,1)} %bitcast.28), channel_id=1, source_target_pairs={{16,0},{24,8},{0,16},{8,24},{17,1},{25,9},{1,17},{9,25},{18,2},{26... | collective-permute-start | bytes 122888 | tf_op jit(solution)/shard_map/ppermute | solution.py:340
  32.7 0.8 copy-start.5
  34.1 57.8 %copy-start = (bf16[640,384]{1,0:T(8,128)(2,1)}, bf16[640,384]{1,0:T(8,128)(2,1)S(1)}, u32[]{:S(2)}) copy-start(bf16[640,384]{1,0:T(8,128)(2,1)S(1)} %shard_map.123.refs_0_) | copy-start | bytes 1474564
  34.1 14.8 %collective-permute-start.3 = (bf16[640,384]{1,0:T(8,128)(2,1)S(1)}, bf16[640,384]{1,0:T(8,128)(2,1)S(1)}, u32[]{:S(2)}, u32[]{:S(2)}) collective-permute-start(bf16[640,384]{1,0:T(8,128)(2,1)S(1)} %shard_map.123.refs_0_), channel_id=1, source_target_pairs={{7,0},{0,1},{1,2},{2,3},{3,4},{4,5},{5,6},{6,7},{15,8},{8,9},{9,10... | collective-permute-start | bytes 1474568 | tf_op jit(solution)/shard_map/ppermute | solution.py:340
  37.3 12.5 %collective-permute-start.4 = (bf16[640,384]{1,0:T(8,128)(2,1)S(1)}, bf16[640,384]{1,0:T(8,128)(2,1)S(1)}, u32[]{:S(2)}, u32[]{:S(2)}) collective-permute-start(bf16[640,384]{1,0:T(8,128)(2,1)S(1)} %shard_map.123.refs_0_), channel_id=1, source_target_pairs={{1,0},{2,1},{3,2},{4,3},{5,4},{6,5},{7,6},{0,7},{9,8},{10,9},{11,1... | collective-permute-start | bytes 1474568 | tf_op jit(solution)/shard_map/ppermute | solution.py:340
  41.1 18.2 %collective-permute-start.7 = (bf16[48,5120]{1,0:T(8,128)(2,1)}, bf16[48,5120]{1,0:T(8,128)(2,1)S(1)}, u32[]{:S(2)}, u32[]{:S(2)}) collective-permute-start(bf16[48,5120]{1,0:T(8,128)(2,1)} %bitcast.31), channel_id=1, source_target_pairs={{8,0},{16,8},{24,16},{0,24},{9,1},{17,9},{25,17},{1,25},{10,2},{18... | collective-permute-start | bytes 1474568 | tf_op jit(solution)/shard_map/ppermute | solution.py:340
  45.0 18.6 %collective-permute-start.8 = (bf16[48,5120]{1,0:T(8,128)(2,1)}, bf16[48,5120]{1,0:T(8,128)(2,1)}, u32[]{:S(2)}, u32[]{:S(2)}) collective-permute-start(bf16[48,5120]{1,0:T(8,128)(2,1)} %bitcast.34), channel_id=1, source_target_pairs={{24,0},{0,8},{8,16},{16,24},{25,1},{1,9},{9,17},{17,25},{26,2},{2,... | collective-permute-start | bytes 1474568 | tf_op jit(solution)/shard_map/ppermute | solution.py:340
  48.9 43.0 %copy-start.9 = (bf16[640,384]{1,0:T(8,128)(2,1)}, bf16[640,384]{1,0:T(8,128)(2,1)S(1)}, u32[]{:S(2)}) copy-start(bf16[640,384]{1,0:T(8,128)(2,1)S(1)} %collective-permute-done.3.refs_1_) | copy-start | bytes 1474564
  49.8 42.1 %copy-start.10 = (bf16[640,384]{1,0:T(8,128)(2,1)}, bf16[640,384]{1,0:T(8,128)(2,1)S(1)}, u32[]{:S(2)}) copy-start(bf16[640,384]{1,0:T(8,128)(2,1)S(1)} %collective-permute-done.4.refs_2_) | copy-start | bytes 1474564
  49.8 14.0 %collective-permute-start.5 = (bf16[640,384]{1,0:T(8,128)(2,1)S(1)}, bf16[640,384]{1,0:T(8,128)(2,1)S(1)}, u32[]{:S(2)}, u32[]{:S(2)}) collective-permute-start(bf16[640,384]{1,0:T(8,128)(2,1)S(1)} %collective-permute-done.3.refs_1_), channel_id=1, source_target_pairs={{7,0},{0,1},{1,2},{2,3},{3,4},{4,5},{5,6},{6,7},{15,8},{8,9},{9,10... | collective-permute-start | bytes 1474568 | tf_op jit(solution)/shard_map/ppermute | solution.py:340
  53.0 13.0 %collective-permute-start.6 = (bf16[640,384]{1,0:T(8,128)(2,1)S(1)}, bf16[640,384]{1,0:T(8,128)(2,1)S(1)}, u32[]{:S(2)}, u32[]{:S(2)}) collective-permute-start(bf16[640,384]{1,0:T(8,128)(2,1)S(1)} %collective-permute-done.4.refs_2_), channel_id=1, source_target_pairs={{1,0},{2,1},{3,2},{4,3},{5,4},{6,5},{7,6},{0,7},{9,8},{10,9},{11,1... | collective-permute-start | bytes 1474568 | tf_op jit(solution)/shard_map/ppermute | solution.py:340
  57.0 21.0 %collective-permute-start.11 = (bf16[48,5120]{1,0:T(8,128)(2,1)}, bf16[48,5120]{1,0:T(8,128)(2,1)S(1)}, u32[]{:S(2)}, u32[]{:S(2)}) collective-permute-start(bf16[48,5120]{1,0:T(8,128)(2,1)} %bitcast.32), channel_id=1, source_target_pairs={{24,0},{0,8},{8,16},{16,24},{25,1},{1,9},{9,17},{17,25},{26,2},{2,... | collective-permute-start | bytes 1474568 | tf_op jit(solution)/shard_map/ppermute | solution.py:340
  59.3 32.6 %copy-start.11 = (bf16[48,5120]{1,0:T(8,128)(2,1)}, bf16[48,5120]{1,0:T(8,128)(2,1)S(1)}, u32[]{:S(2)}) copy-start(bf16[48,5120]{1,0:T(8,128)(2,1)S(1)} %collective-permute-done.7.refs_10_) | copy-start | bytes 1474564
  59.3 20.6 %collective-permute-start.12 = (bf16[48,5120]{1,0:T(8,128)(2,1)}, bf16[48,5120]{1,0:T(8,128)(2,1)S(1)}, u32[]{:S(2)}, u32[]{:S(2)}) collective-permute-start(bf16[48,5120]{1,0:T(8,128)(2,1)} %bitcast.35), channel_id=1, source_target_pairs={{8,0},{16,8},{24,16},{0,24},{9,1},{17,9},{25,17},{1,25},{10,2},{18... | collective-permute-start | bytes 1474568 | tf_op jit(solution)/shard_map/ppermute | solution.py:340
  63.8 16.6 %copy-start.12 = (bf16[640,384]{1,0:T(8,128)(2,1)}, bf16[640,384]{1,0:T(8,128)(2,1)S(1)}, u32[]{:S(2)}) copy-start(bf16[640,384]{1,0:T(8,128)(2,1)S(1)} %collective-permute-done.5.refs_3_) | copy-start | bytes 1474564
  66.0 17.4 %copy-start.13 = (bf16[640,384]{1,0:T(8,128)(2,1)}, bf16[640,384]{1,0:T(8,128)(2,1)S(1)}, u32[]{:S(2)}) copy-start(bf16[640,384]{1,0:T(8,128)(2,1)S(1)} %collective-permute-done.6.refs_4_) | copy-start | bytes 1474564
  66.0 13.9 %collective-permute-start.9 = (bf16[640,384]{1,0:T(8,128)(2,1)S(1)}, bf16[640,384]{1,0:T(8,128)(2,1)}, u32[]{:S(2)}, u32[]{:S(2)}) collective-permute-start(bf16[640,384]{1,0:T(8,128)(2,1)S(1)} %collective-permute-done.5.refs_3_), channel_id=1, source_target_pairs={{7,0},{0,1},{1,2},{2,3},{3,4},{4,5},{5,6},{6,7},{15,8},{8,9},{9,10... | collective-permute-start | bytes 1474568 | tf_op jit(solution)/shard_map/ppermute | solution.py:340
  70.0 10.5 %collective-permute-start.10 = (bf16[640,384]{1,0:T(8,128)(2,1)S(1)}, bf16[640,384]{1,0:T(8,128)(2,1)S(1)}, u32[]{:S(2)}, u32[]{:S(2)}) collective-permute-start(bf16[640,384]{1,0:T(8,128)(2,1)S(1)} %collective-permute-done.6.refs_4_), channel_id=1, source_target_pairs={{1,0},{2,1},{3,2},{4,3},{5,4},{6,5},{7,6},{0,7},{9,8},{10,9},{11,1... | collective-permute-start | bytes 1474568 | tf_op jit(solution)/shard_map/ppermute | solution.py:340
  72.5 13.2 %collective-permute-start.14 = (bf16[48,5120]{1,0:T(8,128)(2,1)S(1)}, bf16[48,5120]{1,0:T(8,128)(2,1)}, u32[]{:S(2)}, u32[]{:S(2)}) collective-permute-start(bf16[48,5120]{1,0:T(8,128)(2,1)S(1)} %collective-permute-done.7.refs_10_), channel_id=1, source_target_pairs={{8,0},{16,8},{24,16},{0,24},{9,1},{17,9},{25,17},{1,25},{10,2},{18... | collective-permute-start | bytes 1474568 | tf_op jit(solution)/shard_map/ppermute | solution.py:340
  78.0 5.4 %copy-start.14 = (bf16[48,5120]{1,0:T(8,128)(2,1)}, bf16[48,5120]{1,0:T(8,128)(2,1)S(1)}, u32[]{:S(2)}) copy-start(bf16[48,5120]{1,0:T(8,128)(2,1)S(1)} %collective-permute-done.11.refs_12_) | copy-start | bytes 1474564
  78.0 12.4 %collective-permute-start.15 = (bf16[48,5120]{1,0:T(8,128)(2,1)}, bf16[48,5120]{1,0:T(8,128)(2,1)}, u32[]{:S(2)}, u32[]{:S(2)}) collective-permute-start(bf16[48,5120]{1,0:T(8,128)(2,1)} %collective-permute-done.8.refs_13_), channel_id=1, source_target_pairs={{24,0},{0,8},{8,16},{16,24},{25,1},{1,9},{9,17},{17,25},{26,2},{2,... | collective-permute-start | bytes 1474568 | tf_op jit(solution)/shard_map/ppermute | solution.py:340
  79.9 3.5 %copy-start.15 = (bf16[48,5120]{1,0:T(8,128)(2,1)}, bf16[48,5120]{1,0:T(8,128)(2,1)S(1)}, u32[]{:S(2)}) copy-start(bf16[48,5120]{1,0:T(8,128)(2,1)S(1)} %collective-permute-done.12.refs_11_) | copy-start | bytes 1474564
  80.4 2.9 %copy-start.16 = (bf16[640,384]{1,0:T(8,128)(2,1)}, bf16[640,384]{1,0:T(8,128)(2,1)S(1)}, u32[]{:S(2)}) copy-start(bf16[640,384]{1,0:T(8,128)(2,1)S(1)} %collective-permute-done.10.refs_6_) | copy-start | bytes 1474564
  80.4 11.4 %collective-permute-start.13 = (bf16[640,384]{1,0:T(8,128)(2,1)}, bf16[640,384]{1,0:T(8,128)(2,1)}, u32[]{:S(2)}, u32[]{:S(2)}) collective-permute-start(bf16[640,384]{1,0:T(8,128)(2,1)} %collective-permute-done.9.refs_5_), channel_id=1, source_target_pairs={{7,0},{0,1},{1,2},{2,3},{3,4},{4,5},{5,6},{6,7},{15,8},{8,9},{9,10... | collective-permute-start | bytes 1474568 | tf_op jit(solution)/shard_map/ppermute | solution.py:340
  83.4 17.8 %collective-permute-start.16 = (bf16[160,1536]{1,0:T(8,128)(2,1)S(1)}, bf16[160,1536]{1,0:T(8,128)(2,1)S(1)}, u32[]{:S(2)}, u32[]{:S(2)}) collective-permute-start(bf16[160,1536]{1,0:T(8,128)(2,1)S(1)} %bitcast.21), channel_id=1, source_target_pairs={{24,0},{0,8},{8,16},{16,24},{25,1},{1,9},{9,17},{17,25},{26,2},{2,... | collective-permute-start | bytes 1474568 | tf_op jit(solution)/shard_map/ppermute | solution.py:340
  101.2 25.5 %all-to-all-start.1 = ((bf16[8,224,256]{2,1,0:T(8,128)(2,1)}), bf16[8,224,256]{2,1,0:T(8,128)(2,1)S(1)}, u32[]{:S(2)}, u32[]{:S(2)}) async-start(bf16[8,224,256]{2,1,0:T(8,128)(2,1)} %shard_map.124), calls=%async_computation.1 | async-start | bytes 1835008 | tf_op jit(solution)/shard_map/all_to_all | solution.py:329
  105.7 54.7 %copy-start.3 = (bf16[1536,160]{0,1:T(8,128)(2,1)S(1)}, bf16[1536,160]{0,1:T(8,128)(2,1)}, u32[]{:S(2)}) copy-start(bf16[1536,160]{0,1:T(8,128)(2,1)} %param.19) | copy-start | bytes 1474564
  105.7 54.6 %copy-start.6 = (bf16[128,160]{0,1:T(8,128)(2,1)S(1)}, bf16[128,160]{0,1:T(8,128)(2,1)}, u32[]{:S(2)}) copy-start(bf16[128,160]{0,1:T(8,128)(2,1)} %param.11) | copy-start | bytes 122884
  105.7 54.6 %copy-start.7 = (s32[16,128]{1,0:T(8,128)S(1)}, s32[16,128]{1,0:T(8,128)}, u32[]{:S(2)}) copy-start(s32[16,128]{1,0:T(8,128)} %get-tuple-element.32.slot_ref) | copy-start | bytes 24580
  105.8 54.6 %copy-start.8 = (f32[16,128]{1,0:T(8,128)S(1)}, f32[16,128]{1,0:T(8,128)}, u32[]{:S(2)}) copy-start(f32[16,128]{1,0:T(8,128)} %get-tuple-element.33.gate_ref) | copy-start | bytes 24580
  105.8 10.5 %collective-permute-start.17 = (bf16[160,1536]{1,0:T(8,128)(2,1)S(1)}, bf16[160,1536]{1,0:T(8,128)(2,1)S(1)}, u32[]{:S(2)}, u32[]{:S(2)}) collective-permute-start(bf16[160,1536]{1,0:T(8,128)(2,1)S(1)} %bitcast.22), channel_id=1, source_target_pairs={{8,0},{16,8},{24,16},{0,24},{9,1},{17,9},{25,17},{1,25},{10,2},{18... | collective-permute-start | bytes 1474568 | tf_op jit(solution)/shard_map/ppermute | solution.py:340
  110.5 11.1 %collective-permute-start.18 = (bf16[160,1536]{1,0:T(8,128)(2,1)S(1)}, bf16[160,1536]{1,0:T(8,128)(2,1)S(1)}, u32[]{:S(2)}, u32[]{:S(2)}) collective-permute-start(bf16[160,1536]{1,0:T(8,128)(2,1)S(1)} %collective-permute-done.16.refs_2_), channel_id=1, source_target_pairs={{24,0},{0,8},{8,16},{16,24},{25,1},{1,9},{9,17},{17,25},{26,2},{2,... | collective-permute-start | bytes 1474568 | tf_op jit(solution)/shard_map/ppermute | solution.py:340
  131.3 0.7 copy-start.4
  132.0 30.3 %copy-start.1 = (bf16[128,5120]{1,0:T(8,128)(2,1)S(1)}, bf16[128,5120]{1,0:T(8,128)(2,1)}, u32[]{:S(2)}) copy-start(bf16[128,5120]{1,0:T(8,128)(2,1)} %vocab_ref.1) | copy-start | bytes 3932164
  132.0 28.4 %all-to-all-start.2 = ((bf16[64,24,128]{2,1,0:T(8,128)(2,1)}), bf16[64,24,128]{2,1,0:T(8,128)(2,1)S(1)}, u32[]{:S(2)}, u32[]{:S(2)}) async-start(bf16[64,24,128]{2,1,0:T(8,128)(2,1)} %copy-done.4), calls=%async_computation.2 | async-start | bytes 786432 | tf_op jit(solution)/shard_map/all_to_all | solution.py:329
  145.2 39.0 %copy-start.17 = (s32[64]{0:T(128)S(1)}, s32[64]{0:T(128)}, u32[]{:S(2)}) copy-start(s32[64]{0:T(128)} %param.21) | copy-start | bytes 772
  145.2 10.1 %collective-permute-start.19 = (bf16[384,128]{1,0:T(8,128)(2,1)S(1)}, bf16[384,128]{1,0:T(8,128)(2,1)S(1)}, u32[]{:S(2)}, u32[]{:S(2)}) collective-permute-start(bf16[384,128]{1,0:T(8,128)(2,1)S(1)} %get-tuple-element.57.refs_0_), channel_id=1, source_target_pairs={{8,0},{16,8},{24,16},{0,24},{9,1},{17,9},{25,17},{1,25},{10,2},{18... | collective-permute-start | bytes 294920 | tf_op jit(solution)/shard_map/ppermute | solution.py:340
  149.8 8.1 %collective-permute-start.20 = (bf16[384,128]{1,0:T(8,128)(2,1)S(1)}, bf16[384,128]{1,0:T(8,128)(2,1)S(1)}, u32[]{:S(2)}, u32[]{:S(2)}) collective-permute-start(bf16[384,128]{1,0:T(8,128)(2,1)S(1)} %get-tuple-element.57.refs_0_), channel_id=1, source_target_pairs={{24,0},{0,8},{8,16},{16,24},{25,1},{1,9},{9,17},{17,25},{26,2},{2,... | collective-permute-start | bytes 294920 | tf_op jit(solution)/shard_map/ppermute | solution.py:340
  151.7 8.7 %collective-permute-start.21 = (bf16[384,128]{1,0:T(8,128)(2,1)S(1)}, bf16[384,128]{1,0:T(8,128)(2,1)S(1)}, u32[]{:S(2)}, u32[]{:S(2)}) collective-permute-start(bf16[384,128]{1,0:T(8,128)(2,1)S(1)} %get-tuple-element.57.refs_0_), channel_id=1, source_target_pairs={{16,0},{24,8},{0,16},{8,24},{17,1},{25,9},{1,17},{9,25},{18,2},{26... | collective-permute-start | bytes 294920 | tf_op jit(solution)/shard_map/ppermute | solution.py:340
  162.3 32.3 %collective-permute-start.22 = (bf16[128,5120]{1,0:T(8,128)(2,1)S(1)}, bf16[128,5120]{1,0:T(8,128)(2,1)S(1)}, u32[]{:S(2)}, u32[]{:S(2)}) collective-permute-start(bf16[128,5120]{1,0:T(8,128)(2,1)S(1)} %copy-done.1), channel_id=1, source_target_pairs={{0,32},{32,0},{1,33},{33,1},{2,34},{34,2},{3,35},{35,3},{4,36},{36... | collective-permute-start | bytes 3932168 | tf_op jit(solution)/shard_map/ppermute | solution.py:464
  165.7 13.4 %all-to-all-start.3 = ((bf16[16,4,160]{2,1,0:T(4,128)(2,1)}), bf16[16,4,160]{2,1,0:T(4,128)(2,1)S(1)}, u32[]{:S(2)}, u32[]{:S(2)}) async-start(bf16[16,4,160]{2,1,0:T(4,128)(2,1)} %get-tuple-element.60), calls=%async_computation.3 | async-start | bytes 65536 | tf_op jit(solution)/shard_map/all_to_all | solution.py:329
  180.1 14.5 %all-to-all-start.4 = ((bf16[32,40,128]{2,1,0:T(8,128)(2,1)}), bf16[32,40,128]{2,1,0:T(8,128)(2,1)S(1)}, u32[]{:S(2)}, u32[]{:S(2)}) async-start(bf16[32,40,128]{2,1,0:T(8,128)(2,1)} %shard_map.127), calls=%async_computation.4 | async-start | bytes 655360 | tf_op jit(solution)/shard_map/all_to_all | solution.py:329
